TPU v7x, 32 devices: a whole 2x2x4 slice. The times are simulated.
32 devices in a mesh: shard: 2 (over y), ctx: 4 (over x, core), tp: 4 (over z).
Axes of the slice: x: 2, y: 2, z: 4, core: 2. Of those that a mesh axis runs over, the one named last changes fastest.
Arguments:
- tokens: bfloat16 [2, 2, 2560, 1280], P(None, 'shard', ('ctx', 'tp')), may hold values from -0.16992188 to 0.16992188
- parents: int32 [2, 2, 40], P(None, 'shard'), may hold values from 0 to 38, as said below
- slot_segment: int32 [2, 2, 40], P(None, 'shard'), may hold values from 0 to 39, each once within a row
- w_query: bfloat16 [1280, 1280], P(('shard', 'ctx'), 'tp'), may hold values from -0.15625 to 0.15625
- w_key: bfloat16 [1280, 1280], P(('shard', 'ctx'), 'tp'), may hold values from -0.15625 to 0.15625
- w_value: bfloat16 [1280, 1280], P(('shard', 'ctx'), 'tp'), may hold values from -0.15625 to 0.15625
- w_attn_out: bfloat16 [1280, 1280], P('tp', ('shard', 'ctx')), may hold values from -0.15625 to 0.15625
- w_up: bfloat16 [1280, 5120], P(('shard', 'ctx'), 'tp'), may hold values from -0.15625 to 0.15625
- w_gate: bfloat16 [1280, 5120], P(('shard', 'ctx'), 'tp'), may hold values from -0.15625 to 0.15625
- w_down: bfloat16 [5120, 1280], P('tp', ('shard', 'ctx')), may hold values from -0.078125 to 0.078125
- alpha_attn: float32 [1280], replicated, may hold values from 0.15 to 0.6
- alpha_mlp: float32 [1280], replicated, may hold values from 0.15 to 0.6
- scale_qk: float32 [1280], P('tp'), may hold values from 0.7 to 1.4
- scale_up: float32 [5120], P('tp'), may hold values from 0.5 to 2
- scale_gate: float32 [5120], P('tp'), may hold values from 0.5 to 2
- cotangent: bfloat16 [2, 2, 2560, 1280], P(None, 'shard', ('ctx', 'tp')), may hold values from -6 to 6
Outputs:
- block_out: bfloat16 [2, 2, 2560, 1280], P(None, 'shard', ('ctx', 'tp'))
- grad_tokens: float32 [2, 2, 2560, 1280], P(None, 'shard', ('ctx', 'tp'))
- grad_w_query: float32 [1280, 1280], P(('shard', 'ctx'), 'tp')
- grad_w_key: float32 [1280, 1280], P(('shard', 'ctx'), 'tp')
- grad_w_value: float32 [1280, 1280], P(('shard', 'ctx'), 'tp')
- grad_w_attn_out: float32 [1280, 1280], P('tp', ('shard', 'ctx'))
- grad_w_up: float32 [1280, 5120], P(('shard', 'ctx'), 'tp')
- grad_w_gate: float32 [1280, 5120], P(('shard', 'ctx'), 'tp')
- grad_w_down: float32 [5120, 1280], P('tp', ('shard', 'ctx'))
- grad_alpha_attn: float32 [1280], replicated
- grad_alpha_mlp: float32 [1280], replicated
- grad_scale_qk: float32 [1280], P('tp')
- grad_scale_up: float32 [5120], P('tp')
- grad_scale_gate: float32 [5120], P('tp')
Inputs may be any that keep to these rules, and one draw needn't show every extreme that they name: `parents`: segment 0 of each tree is its root and names itself; every other segment names a segment with a lower number; every segment has 64 tokens. `slot_segment`: each tree's 40 slots hold its segments, each once.
All inputs are finite; a program needn't handle non-finite values.
Results may differ from a plain program's by a relative error of at most 0.019.
Values may be sent and summed in bfloat16 or wider, within the bound.
No kernel may reach another device: no remote copies, remote signals or barrier semaphores. Data moves between devices by JAX's collectives and lax.ppermute only.
A program may use at most 120 MiB of HBM per device.

v0:
```python
import math

import jax
import jax.numpy as jnp
from jax import lax
from jax.sharding import PartitionSpec as P

D = 1280
HDIM = 64
SEG = 64
SEGS = 40
TREE_TOK = 2560


EPSILON = 1e-06
MASKED = -1e30
HIGHEST = lax.Precision.HIGHEST


def unit_rows(values):
    return values * lax.rsqrt(jnp.sum(values * values, axis=-1, keepdims=True) + EPSILON)


def unit_heads(values):
    shaped = values.reshape(values.shape[0], values.shape[1] // HDIM, HDIM)
    return unit_rows(shaped).reshape(values.shape)


def contract_rows(former, latter):
    return lax.dot_general(
        former, latter, (((0,), (0,)), ((), ())), preferred_element_type=jnp.float32
    )


def contract_cols(former, latter):
    return lax.dot_general(
        former, latter, (((1,), (1,)), ((), ())), preferred_element_type=jnp.float32
    )


def split_heads(values):
    return values.reshape(values.shape[0], values.shape[1] // HDIM, HDIM).transpose(1, 0, 2)


def merge_heads(values):
    return values.transpose(1, 0, 2).reshape(values.shape[1], values.shape[0] * values.shape[2])


def mix_rows(residual, branch, mixing):
    return unit_rows(residual + mixing * (unit_rows(branch) - residual))


def query_key(query_raw, key_raw, gain_qk):
    return (unit_heads(query_raw) * gain_qk, unit_heads(key_raw) * gain_qk)


def middle(up_raw, gate_raw, scale_up, scale_gate):
    return up_raw * scale_up * jax.nn.silu(gate_raw * (scale_gate * math.sqrt(D)))


def group_rows(own_block):
    return lax.all_gather(own_block, "tp", axis=0, tiled=True)


def group_grads(own_block):
    return lax.all_gather(own_block, "tp", axis=0, tiled=True)


def own_rows(partial_value):
    return lax.psum_scatter(partial_value, "tp", scatter_dimension=0, tiled=True)


def own_grads(partial_value):
    return lax.psum_scatter(
        partial_value.astype(jnp.bfloat16), "tp", scatter_dimension=0, tiled=True
    ).astype(jnp.float32)


def visibility(parents, slots, group_size):
    labels = jnp.arange(SEGS, dtype=jnp.int32)
    linked = (parents[:, None] == labels[None, :]).astype(jnp.float32)
    reachable = jnp.maximum(linked, jnp.eye(SEGS, dtype=jnp.float32))
    for doubling in range(SEGS.bit_length()):
        reachable = jnp.minimum(jnp.dot(reachable, reachable, precision=HIGHEST), 1.0)
    segment = jnp.broadcast_to(slots[:, None], (SEGS, SEG)).reshape(TREE_TOK)
    offset = lax.broadcasted_iota(jnp.int32, (SEGS, SEG), 1).reshape(TREE_TOK)
    first_row = lax.axis_index("ctx") * group_size
    seg_query = lax.dynamic_slice_in_dim(segment, first_row, group_size)
    off_query = lax.dynamic_slice_in_dim(offset, first_row, group_size)
    key_onehot = (segment[:, None] == labels[None, :]).astype(jnp.float32)
    query_onehot = (seg_query[:, None] == labels[None, :]).astype(jnp.float32)
    linked_rows = jnp.dot(query_onehot, reachable, precision=HIGHEST)
    seen = (
        lax.dot_general(linked_rows, key_onehot, (((1,), (1,)), ((), ())), precision=HIGHEST) > 0.5
    )
    return seen & (
        (seg_query[:, None] != segment[None, :]) | (offset[None, :] <= off_query[:, None])
    )


def micro_step(gathered, vectors, tokens_own, cotangent_own, parents, slots):
    w_query, w_key, w_value, w_attn_out, w_up, w_gate, w_down = gathered
    alpha_attn, alpha_mlp, scale_qk, scale_up, scale_gate = vectors
    score_scale = math.sqrt(HDIM)
    hidden_group = group_rows(tokens_own)
    visible = visibility(parents, slots, hidden_group.shape[0])
    query_raw = jnp.dot(hidden_group, w_query, preferred_element_type=jnp.float32)
    key_raw = jnp.dot(hidden_group, w_key, preferred_element_type=jnp.float32)
    value_low = jnp.dot(hidden_group, w_value, preferred_element_type=jnp.float32).astype(
        jnp.bfloat16
    )
    query_unit, key_unit = query_key(query_raw, key_raw, scale_qk)
    queries = query_unit.astype(jnp.bfloat16)
    keys_own = key_unit.astype(jnp.bfloat16)
    keys_tree, values_tree = (
        lax.all_gather(keys_own, "ctx", axis=0, tiled=True),
        lax.all_gather(value_low, "ctx", axis=0, tiled=True),
    )
    query_heads = split_heads(queries)
    key_heads = split_heads(keys_tree)
    value_heads = split_heads(values_tree)

    def head_forward(record):
        query_one, key_one, value_one = record
        scores = jnp.where(visible, contract_cols(query_one, key_one) * score_scale, MASKED)
        row_peak = jnp.max(scores, axis=-1, keepdims=True)
        lifted = jnp.exp(scores - row_peak)
        row_total = jnp.sum(lifted, axis=-1, keepdims=True)
        soft_weights = lifted / row_total
        head_value = jnp.dot(
            soft_weights.astype(jnp.bfloat16), value_one, preferred_element_type=jnp.float32
        )
        return (head_value, (row_peak + jnp.log(row_total))[:, 0])

    head_values, log_totals = lax.map(head_forward, (query_heads, key_heads, value_heads))
    heads_low = merge_heads(head_values).astype(jnp.bfloat16)
    tokens_wide = tokens_own.astype(jnp.float32)
    branch_one = own_rows(jnp.dot(heads_low, w_attn_out, preferred_element_type=jnp.float32))
    hidden_one = mix_rows(tokens_wide, branch_one, alpha_attn)
    hidden_one_group = group_rows(hidden_one.astype(jnp.bfloat16))
    up_raw = jnp.dot(hidden_one_group, w_up, preferred_element_type=jnp.float32)
    gate_raw = jnp.dot(hidden_one_group, w_gate, preferred_element_type=jnp.float32)
    mixed_low = middle(up_raw, gate_raw, scale_up, scale_gate).astype(jnp.bfloat16)
    branch_two = own_rows(jnp.dot(mixed_low, w_down, preferred_element_type=jnp.float32))
    output_wide, pull_out = jax.vjp(mix_rows, hidden_one, branch_two, alpha_mlp)
    upstream = cotangent_own.astype(jnp.float32)
    hidden_one_direct, branch_two_grad, grad_alpha_mlp = pull_out(upstream)
    branch_two_group = group_grads(branch_two_grad.astype(jnp.bfloat16))
    grad_down = contract_rows(mixed_low, branch_two_group)
    mixed_grad = contract_cols(branch_two_group, w_down).astype(jnp.bfloat16).astype(jnp.float32)
    middle_value, pull_mid = jax.vjp(middle, up_raw, gate_raw, scale_up, scale_gate)
    up_grad, gate_grad, grad_scale_up, grad_scale_gate = pull_mid(mixed_grad)
    up_low = up_grad.astype(jnp.bfloat16)
    gate_low = gate_grad.astype(jnp.bfloat16)
    grad_up = contract_rows(hidden_one_group, up_low)
    grad_gate = contract_rows(hidden_one_group, gate_low)
    hidden_one_grad = hidden_one_direct + own_grads(
        contract_cols(up_low, w_up) + contract_cols(gate_low, w_gate)
    )
    hidden_again, pull_in = jax.vjp(mix_rows, tokens_wide, branch_one, alpha_attn)
    tokens_direct, branch_one_grad, grad_alpha_attn = pull_in(hidden_one_grad)
    branch_one_group = group_grads(branch_one_grad.astype(jnp.bfloat16))
    grad_attn_out = contract_rows(heads_low, branch_one_group)
    heads_grad = split_heads(contract_cols(branch_one_group, w_attn_out).astype(jnp.bfloat16))

    def head_backward(record):
        query_one, key_one, value_one, upstream_one, log_total = record
        scores = jnp.where(visible, contract_cols(query_one, key_one) * score_scale, MASKED)
        soft_weights = jnp.exp(scores - log_total[:, None])
        weight_grad = contract_cols(upstream_one, value_one)
        row_inner = jnp.sum(soft_weights * weight_grad, axis=-1, keepdims=True)
        score_grad = (soft_weights * (weight_grad - row_inner)).astype(jnp.bfloat16)
        query_grad = jnp.dot(score_grad, key_one, preferred_element_type=jnp.float32) * score_scale
        key_grad = contract_rows(score_grad, query_one) * score_scale
        value_grad = contract_rows(soft_weights.astype(jnp.bfloat16), upstream_one)
        return (query_grad, key_grad, value_grad)

    query_grads, key_grads, value_grads = lax.map(
        head_backward, (query_heads, key_heads, value_heads, heads_grad, log_totals)
    )
    key_own_grad, value_own_grad = (
        lax.psum_scatter(
            merge_heads(key_grads).astype(jnp.bfloat16), "ctx", scatter_dimension=0, tiled=True
        ).astype(jnp.float32),
        lax.psum_scatter(
            merge_heads(value_grads).astype(jnp.bfloat16), "ctx", scatter_dimension=0, tiled=True
        ).astype(jnp.float32),
    )
    unit_again, pull_qk = jax.vjp(query_key, query_raw, key_raw, scale_qk)
    query_raw_grad, key_raw_grad, grad_scale_qk = pull_qk((merge_heads(query_grads), key_own_grad))
    query_low = query_raw_grad.astype(jnp.bfloat16)
    key_low = key_raw_grad.astype(jnp.bfloat16)
    value_grad_low = value_own_grad.astype(jnp.bfloat16)
    grad_query = contract_rows(hidden_group, query_low)
    grad_key = contract_rows(hidden_group, key_low)
    grad_value = contract_rows(hidden_group, value_grad_low)
    input_part = (
        contract_cols(query_low, w_query)
        + contract_cols(key_low, w_key)
        + contract_cols(value_grad_low, w_value)
    )
    grad_tokens = tokens_direct + own_grads(input_part)
    weight_grads = (grad_query, grad_key, grad_value, grad_attn_out, grad_up, grad_gate, grad_down)
    vector_grads = (grad_alpha_attn, grad_alpha_mlp, grad_scale_qk, grad_scale_up, grad_scale_gate)
    return (output_wide.astype(jnp.bfloat16), grad_tokens, weight_grads, vector_grads)


def per_device(
    tokens,
    parents,
    slot_segment,
    w_query,
    w_key,
    w_value,
    w_attn_out,
    w_up,
    w_gate,
    w_down,
    alpha_attn,
    alpha_mlp,
    scale_qk,
    scale_up,
    scale_gate,
    cotangent,
):
    width = tokens.shape[-1]
    local_heads = w_query.shape[1]
    local_hidden = w_up.shape[1]
    vectors = (alpha_attn, alpha_mlp, scale_qk, scale_up, scale_gate)
    zero_weights = (
        jnp.zeros((width, local_heads), jnp.float32),
        jnp.zeros((width, local_heads), jnp.float32),
        jnp.zeros((width, local_heads), jnp.float32),
        jnp.zeros((local_heads, width), jnp.float32),
        jnp.zeros((width, local_hidden), jnp.float32),
        jnp.zeros((width, local_hidden), jnp.float32),
        jnp.zeros((local_hidden, width), jnp.float32),
    )
    zero_vectors = (
        jnp.zeros((width,), jnp.float32),
        jnp.zeros((width,), jnp.float32),
        jnp.zeros((local_heads,), jnp.float32),
        jnp.zeros((local_hidden,), jnp.float32),
        jnp.zeros((local_hidden,), jnp.float32),
    )

    def one_micro(totals, record):
        tokens_one, cotangent_one, parents_one, slots_one = record
        gathered = (
            lax.all_gather(w_query, ("shard", "ctx"), axis=0, tiled=True),
            lax.all_gather(w_key, ("shard", "ctx"), axis=0, tiled=True),
            lax.all_gather(w_value, ("shard", "ctx"), axis=0, tiled=True),
            lax.all_gather(w_attn_out, ("shard", "ctx"), axis=1, tiled=True),
            lax.all_gather(w_up, ("shard", "ctx"), axis=0, tiled=True),
            lax.all_gather(w_gate, ("shard", "ctx"), axis=0, tiled=True),
            lax.all_gather(w_down, ("shard", "ctx"), axis=1, tiled=True),
        )
        output_one, input_grad, weight_grads, vector_grads = micro_step(
            gathered, vectors, tokens_one, cotangent_one, parents_one[0], slots_one[0]
        )
        weight_totals = tuple((former + latter for former, latter in zip(totals[0], weight_grads)))
        vector_totals = tuple((former + latter for former, latter in zip(totals[1], vector_grads)))
        return ((weight_totals, vector_totals), (output_one, input_grad))

    totals, stacked = lax.scan(
        one_micro,
        (zero_weights, zero_vectors),
        (tokens[:, 0], cotangent[:, 0], parents, slot_segment),
    )
    weight_totals, vector_totals = totals
    grad_q, grad_k, grad_v, grad_o, grad_u, grad_g, grad_d = weight_totals
    weight_totals = (
        lax.psum_scatter(grad_q, ("shard", "ctx"), scatter_dimension=0, tiled=True),
        lax.psum_scatter(grad_k, ("shard", "ctx"), scatter_dimension=0, tiled=True),
        lax.psum_scatter(grad_v, ("shard", "ctx"), scatter_dimension=0, tiled=True),
        lax.psum_scatter(grad_o, ("shard", "ctx"), scatter_dimension=1, tiled=True),
        lax.psum_scatter(grad_u, ("shard", "ctx"), scatter_dimension=0, tiled=True),
        lax.psum_scatter(grad_g, ("shard", "ctx"), scatter_dimension=0, tiled=True),
        lax.psum_scatter(grad_d, ("shard", "ctx"), scatter_dimension=1, tiled=True),
    )
    tp_count = lax.axis_size("tp")
    tp_place = lax.axis_index("tp")
    qk_padded = lax.dynamic_update_slice_in_dim(
        jnp.zeros((local_heads * tp_count,), jnp.float32),
        vector_totals[2],
        tp_place * local_heads,
        0,
    )
    up_padded = lax.dynamic_update_slice_in_dim(
        jnp.zeros((local_hidden * tp_count,), jnp.float32),
        vector_totals[3],
        tp_place * local_hidden,
        0,
    )
    gate_padded = lax.dynamic_update_slice_in_dim(
        jnp.zeros((local_hidden * tp_count,), jnp.float32),
        vector_totals[4],
        tp_place * local_hidden,
        0,
    )
    alpha_attn_sum, alpha_mlp_sum, qk_sum, up_sum, gate_sum = lax.psum(
        (vector_totals[0], vector_totals[1], qk_padded, up_padded, gate_padded),
        ("shard", "ctx", "tp"),
    )
    outputs_all, input_grads_all = stacked
    return (
        outputs_all[:, None],
        input_grads_all[:, None],
        weight_totals[0],
        weight_totals[1],
        weight_totals[2],
        weight_totals[3],
        weight_totals[4],
        weight_totals[5],
        weight_totals[6],
        alpha_attn_sum,
        alpha_mlp_sum,
        lax.dynamic_slice_in_dim(qk_sum, tp_place * local_heads, local_heads),
        lax.dynamic_slice_in_dim(up_sum, tp_place * local_hidden, local_hidden),
        lax.dynamic_slice_in_dim(gate_sum, tp_place * local_hidden, local_hidden),
    )


def solution(mesh):
    return jax.shard_map(
        per_device,
        mesh=mesh,
        in_specs=(
            P(None, "shard", ("ctx", "tp"), None),
            P(None, "shard", None),
            P(None, "shard", None),
            P(("shard", "ctx"), "tp"),
            P(("shard", "ctx"), "tp"),
            P(("shard", "ctx"), "tp"),
            P("tp", ("shard", "ctx")),
            P(("shard", "ctx"), "tp"),
            P(("shard", "ctx"), "tp"),
            P("tp", ("shard", "ctx")),
            P(),
            P(),
            P("tp"),
            P("tp"),
            P("tp"),
            P(None, "shard", ("ctx", "tp"), None),
        ),
        out_specs=(
            P(None, "shard", ("ctx", "tp"), None),
            P(None, "shard", ("ctx", "tp"), None),
            P(("shard", "ctx"), "tp"),
            P(("shard", "ctx"), "tp"),
            P(("shard", "ctx"), "tp"),
            P("tp", ("shard", "ctx")),
            P(("shard", "ctx"), "tp"),
            P(("shard", "ctx"), "tp"),
            P("tp", ("shard", "ctx")),
            P(),
            P(),
            P("tp"),
            P("tp"),
            P("tp"),
        ),
        check_vma=False,
    )
```

profile of v0, /device:TPU:0, one launch (start us, length us, event | category | flops | bytes accessed | tf_op | source)
XLA Modules:
  0.0 1824.4 jit_solution(9787138842484749526)
XLA Ops:
  8.1 1430.4 %while.72 = (s32[]{:T(128)}, f32[1280,320]{0,1:T(8,128)}, f32[1280,320]{0,1:T(8,128)}, f32[1280,320]{0,1:T(8,128)}, f32[320,1280]{1,0:T(8,128)}, /*index=5*/f32[...) while((s32[]{:T(128)}, f32[1280,320]{0,1:T(8,128)}, ...), condition=%wide.region_32.33_spmd.clone.clone, body=%wide.region_0.32_spmd.clone.sunk.clone | while | flops 27549972480 | bytes 720861376 | solution.py:265
  10.4 12.8 all_gather.78
  23.1 29.2 %all-gather.15.cloned.1.call-done = bf16[1,640,1280]{2,1,0:T(8,128)(2,1)} async-done(((bf16[1,160,1280]{2,1,0:T(8,128)(2,1)}), bf16[1,640,1280]{2,1,0:T(8,128)(2,1)}) %all-gather.15.cloned.1.call-update) | async-done | bytes 1638416 | tf_op jit(solution)/shard_map/while/body/eval_jaxpr/all_gather | solution.py:62
  56.9 13.5 all_gather.76
  70.4 12.4 all_gather.75
  89.6 14.8 all_gather.80
  120.1 31.5 %while.70 = (s32[]{:T(128)}, bf16[5,640,64]{1,2,0:T(8,128)(2,1)}, f32[5,640]{1,0:T(8,128)S(1)}, bf16[5,640,64]{2,1,0:T(8,128)(2,1)}, bf16[5,2560,64]{2,1,0:T(8,1...) while((s32[]{:T(128)}, bf16[5,640,64]{1,2,0:T(8,128)(2,1)}, ...), condition=%wide.region_6.6_spmd, body=%wide.region_3.5_spmd.sunk | while | flops 432536960 | bytes 22973544 | solution.py:135
  157.4 60.2 %reduce-scatter.38.cloned.1.call-done = f32[160,1280]{1,0:T(8,128)} async-done(((f32[640,1280]{1,0:T(8,128)}), f32[160,1280]{1,0:T(8,128)}) %reduce-scatter.38.cloned.1.call-update) | async-done | bytes 819216 | tf_op jit(solution)/shard_map/while/body/eval_jaxpr/reduce_scatter | solution.py:70
  223.2 36.4 %all-gather.21.cloned.1.call-done = bf16[640,1280]{1,0:T(8,128)(2,1)} async-done(((bf16[160,1280]{1,0:T(8,128)(2,1)}), bf16[640,1280]{1,0:T(8,128)(2,1)}) %all-gather.21.cloned.1.call-update) | async-done | bytes 1638416 | tf_op jit(solution)/shard_map/while/body/eval_jaxpr/all_gather | solution.py:62
  266.1 27.0 %all-gather.25.cloned.1.call-done = bf16[1280,1280]{1,0:T(8,128)(2,1)} async-done(((bf16[160,1280]{1,0:T(8,128)(2,1)}), bf16[1280,1280]{1,0:T(8,128)(2,1)}) %all-gather.25.cloned.1.call-update) | async-done | bytes 3276816 | tf_op jit(solution)/shard_map/while/body/eval_jaxpr/all_gather | solution.py:254
  300.7 27.2 %all-gather.27.cloned.1.call-done = bf16[1280,1280]{0,1:T(8,128)(2,1)} async-done(((bf16[1280,160]{0,1:T(8,128)(2,1)}), bf16[1280,1280]{0,1:T(8,128)(2,1)}) %all-gather.27.cloned.1.call-update) | async-done | bytes 3276816 | tf_op jit(solution)/shard_map/while/body/eval_jaxpr/all_gather | solution.py:256
  334.4 62.4 %reduce-scatter.40.cloned.1.call-done = f32[160,1280]{1,0:T(8,128)} async-done(((f32[640,1280]{1,0:T(8,128)}), f32[160,1280]{1,0:T(8,128)}) %reduce-scatter.40.cloned.1.call-update) | async-done | bytes 819216 | tf_op jit(solution)/shard_map/while/body/eval_jaxpr/reduce_scatter | solution.py:70
  402.4 37.6 %all-gather.29.cloned.1.call-done = bf16[640,1280]{1,0:T(8,128)(2,1)} async-done(((bf16[160,1280]{1,0:T(8,128)(2,1)}), bf16[640,1280]{1,0:T(8,128)(2,1)}) %all-gather.29.cloned.1.call-update) | async-done | bytes 1638416 | tf_op jit(solution)/shard_map/while/body/eval_jaxpr/all_gather | solution.py:66
  439.9 8.3 multiply_reduce_fusion.45
  455.6 35.3 %reduce-scatter.42.cloned.1.call-done = bf16[160,1280]{1,0:T(8,128)(2,1)} async-done(((bf16[640,1280]{1,0:T(8,128)(2,1)}), bf16[160,1280]{1,0:T(8,128)(2,1)}) %reduce-scatter.42.cloned.1.call-update) | async-done | bytes 409616 | tf_op jit(solution)/shard_map/while/body/eval_jaxpr/reduce_scatter | solution.py:74
  497.1 36.9 %all-gather.31.cloned.1.call-done = bf16[640,1280]{1,0:T(8,128)(2,1)} async-done(((bf16[160,1280]{1,0:T(8,128)(2,1)}), bf16[640,1280]{1,0:T(8,128)(2,1)}) %all-gather.31.cloned.1.call-update) | async-done | bytes 1638416 | tf_op jit(solution)/shard_map/while/body/eval_jaxpr/all_gather | solution.py:66
  537.7 75.6 %while.71 = (s32[]{:T(128)}, f32[5,640,64]{1,2,0:T(8,128)}, bf16[5,2560,64]{1,2,0:T(8,128)(2,1)}, bf16[5,2560,64]{1,2,0:T(8,128)(2,1)}, bf16[5,640,64]{2,1,0:T(8...) while((s32[]{:T(128)}, f32[5,640,64]{1,2,0:T(8,128)}, ...), condition=%wide.region_20.20_spmd, body=%wide.region_18.19_spmd.sunk | while | flops 1063525760 | bytes 68011696 | solution.py:178
  634.8 12.1 reduce-scatter.44.cloned.1.call-done
  658.0 22.2 %reduce-scatter.46.cloned.1.call-done = bf16[640,320]{1,0:T(8,128)(2,1)} async-done(((bf16[2560,320]{1,0:T(8,128)(2,1)}), bf16[640,320]{1,0:T(8,128)(2,1)}) %reduce-scatter.46.cloned.1.call-update) | async-done | bytes 409616 | tf_op jit(solution)/shard_map/while
  706.9 14.6 reduce-scatter.48.cloned.1.call-done
  725.9 11.2 all_gather.78
  737.2 27.0 %all-gather.15.cloned.1.call-done = bf16[1,640,1280]{2,1,0:T(8,128)(2,1)} async-done(((bf16[1,160,1280]{2,1,0:T(8,128)(2,1)}), bf16[1,640,1280]{2,1,0:T(8,128)(2,1)}) %all-gather.15.cloned.1.call-update) | async-done | bytes 1638416 | tf_op jit(solution)/shard_map/while/body/eval_jaxpr/all_gather | solution.py:62
  768.6 13.5 all_gather.76
  782.2 12.4 all_gather.75
  801.3 14.5 all_gather.80
  831.6 31.5 %while.70 = (s32[]{:T(128)}, bf16[5,640,64]{1,2,0:T(8,128)(2,1)}, f32[5,640]{1,0:T(8,128)S(1)}, bf16[5,640,64]{2,1,0:T(8,128)(2,1)}, bf16[5,2560,64]{2,1,0:T(8,1...) while((s32[]{:T(128)}, bf16[5,640,64]{1,2,0:T(8,128)(2,1)}, ...), condition=%wide.region_6.6_spmd, body=%wide.region_3.5_spmd.sunk | while | flops 432536960 | bytes 22973544 | solution.py:135
  868.9 60.2 %reduce-scatter.38.cloned.1.call-done = f32[160,1280]{1,0:T(8,128)} async-done(((f32[640,1280]{1,0:T(8,128)}), f32[160,1280]{1,0:T(8,128)}) %reduce-scatter.38.cloned.1.call-update) | async-done | bytes 819216 | tf_op jit(solution)/shard_map/while/body/eval_jaxpr/reduce_scatter | solution.py:70
  934.5 36.6 %all-gather.21.cloned.1.call-done = bf16[640,1280]{1,0:T(8,128)(2,1)} async-done(((bf16[160,1280]{1,0:T(8,128)(2,1)}), bf16[640,1280]{1,0:T(8,128)(2,1)}) %all-gather.21.cloned.1.call-update) | async-done | bytes 1638416 | tf_op jit(solution)/shard_map/while/body/eval_jaxpr/all_gather | solution.py:62
  977.6 27.1 %all-gather.25.cloned.1.call-done = bf16[1280,1280]{1,0:T(8,128)(2,1)} async-done(((bf16[160,1280]{1,0:T(8,128)(2,1)}), bf16[1280,1280]{1,0:T(8,128)(2,1)}) %all-gather.25.cloned.1.call-update) | async-done | bytes 3276816 | tf_op jit(solution)/shard_map/while/body/eval_jaxpr/all_gather | solution.py:254
  1012.3 27.1 %all-gather.27.cloned.1.call-done = bf16[1280,1280]{0,1:T(8,128)(2,1)} async-done(((bf16[1280,160]{0,1:T(8,128)(2,1)}), bf16[1280,1280]{0,1:T(8,128)(2,1)}) %all-gather.27.cloned.1.call-update) | async-done | bytes 3276816 | tf_op jit(solution)/shard_map/while/body/eval_jaxpr/all_gather | solution.py:256
  1045.9 62.4 %reduce-scatter.40.cloned.1.call-done = f32[160,1280]{1,0:T(8,128)} async-done(((f32[640,1280]{1,0:T(8,128)}), f32[160,1280]{1,0:T(8,128)}) %reduce-scatter.40.cloned.1.call-update) | async-done | bytes 819216 | tf_op jit(solution)/shard_map/while/body/eval_jaxpr/reduce_scatter | solution.py:70
  1113.4 37.9 %all-gather.29.cloned.1.call-done = bf16[640,1280]{1,0:T(8,128)(2,1)} async-done(((bf16[160,1280]{1,0:T(8,128)(2,1)}), bf16[640,1280]{1,0:T(8,128)(2,1)}) %all-gather.29.cloned.1.call-update) | async-done | bytes 1638416 | tf_op jit(solution)/shard_map/while/body/eval_jaxpr/all_gather | solution.py:66
  1167.0 35.3 %reduce-scatter.42.cloned.1.call-done = bf16[160,1280]{1,0:T(8,128)(2,1)} async-done(((bf16[640,1280]{1,0:T(8,128)(2,1)}), bf16[160,1280]{1,0:T(8,128)(2,1)}) %reduce-scatter.42.cloned.1.call-update) | async-done | bytes 409616 | tf_op jit(solution)/shard_map/while/body/eval_jaxpr/reduce_scatter | solution.py:74
  1208.8 36.6 %all-gather.31.cloned.1.call-done = bf16[640,1280]{1,0:T(8,128)(2,1)} async-done(((bf16[160,1280]{1,0:T(8,128)(2,1)}), bf16[640,1280]{1,0:T(8,128)(2,1)}) %all-gather.31.cloned.1.call-update) | async-done | bytes 1638416 | tf_op jit(solution)/shard_map/while/body/eval_jaxpr/all_gather | solution.py:66
  1249.2 75.6 %while.71 = (s32[]{:T(128)}, f32[5,640,64]{1,2,0:T(8,128)}, bf16[5,2560,64]{1,2,0:T(8,128)(2,1)}, bf16[5,2560,64]{1,2,0:T(8,128)(2,1)}, bf16[5,640,64]{2,1,0:T(8...) while((s32[]{:T(128)}, f32[5,640,64]{1,2,0:T(8,128)}, ...), condition=%wide.region_20.20_spmd, body=%wide.region_18.19_spmd.sunk | while | flops 1063525760 | bytes 68011696 | solution.py:178
  1334.2 10.0 convolution_add_fusion.30
  1348.4 9.9 reduce-scatter.44.cloned.1.call-done
  1369.6 22.0 %reduce-scatter.46.cloned.1.call-done = bf16[640,320]{1,0:T(8,128)(2,1)} async-done(((bf16[2560,320]{1,0:T(8,128)(2,1)}), bf16[640,320]{1,0:T(8,128)(2,1)}) %reduce-scatter.46.cloned.1.call-update) | async-done | bytes 409616 | tf_op jit(solution)/shard_map/while
  1396.4 9.4 convolution_add_fusion.32
  1420.1 12.7 reduce-scatter.48.cloned.1.call-done
  1448.5 8.3 copy.47
  1458.4 40.7 %all-reduce = (f32[1280]{0:T(1024)}, f32[1280]{0:T(1024)}, f32[1280]{0:T(1024)S(1)}, f32[5120]{0:T(1024)S(1)}, f32[5120]{0:T(1024)S(1)}) all-reduce(f32[1280]{0:T(1024)S(1)} %copy-done.73, f32[1280]{0:T(1024)S(1)} %copy-done.70, f32[1280]{0:T(1024)S(1)} %dynamic_update_slice.35, ...), channel_id=1, replica_groups=mesh['shard'=2,'ctx'=4,'tp'=4] {'shard','ctx','tp'}, use_global_device_ids=true, to_apply=%region_40.41 | all-reduce | flops 14080 | bytes 112640 | tf_op jit(solution)/shard_map/psum | solution.py:301
  1501.1 26.2 %reduce-scatter.26.cloned.1.call-done = f32[160,320]{1,0:T(8,128)} async-done(((f32[1280,320]{1,0:T(8,128)}), f32[160,320]{1,0:T(8,128)}) %reduce-scatter.26.cloned.1.call-update) | async-done | bytes 204816 | tf_op jit(solution)/shard_map/reduce_scatter | solution.py:274
  1527.3 44.2 %reduce-scatter.28.cloned.1.call-done = f32[160,320]{1,0:T(8,128)} async-done(((f32[1280,320]{1,0:T(8,128)}), f32[160,320]{1,0:T(8,128)}) %reduce-scatter.28.cloned.1.call-update) | async-done | bytes 204816 | tf_op jit(solution)/shard_map/reduce_scatter | solution.py:275
  1571.5 44.6 %reduce-scatter.30.cloned.1.call-done = f32[320,160]{0,1:T(8,128)} async-done(((f32[320,1280]{0,1:T(8,128)}), f32[320,160]{0,1:T(8,128)}) %reduce-scatter.30.cloned.1.call-update) | async-done | bytes 204816 | tf_op jit(solution)/shard_map/reduce_scatter | solution.py:276
  1616.1 66.8 %reduce-scatter.32.cloned.1.call-done = f32[160,1280]{1,0:T(8,128)} async-done(((f32[1280,1280]{1,0:T(8,128)}), f32[160,1280]{1,0:T(8,128)}) %reduce-scatter.32.cloned.1.call-update) | async-done | bytes 819216 | tf_op jit(solution)/shard_map/reduce_scatter | solution.py:277
  1682.8 67.3 %reduce-scatter.34.cloned.1.call-done = f32[160,1280]{1,0:T(8,128)} async-done(((f32[1280,1280]{1,0:T(8,128)}), f32[160,1280]{1,0:T(8,128)}) %reduce-scatter.34.cloned.1.call-update) | async-done | bytes 819216 | tf_op jit(solution)/shard_map/reduce_scatter | solution.py:278
  1750.1 66.8 %reduce-scatter.36.cloned.1.call-done = f32[1280,160]{0,1:T(8,128)} async-done(((f32[1280,1280]{0,1:T(8,128)}), f32[1280,160]{0,1:T(8,128)}) %reduce-scatter.36.cloned.1.call-update) | async-done | bytes 819216 | tf_op jit(solution)/shard_map/reduce_scatter | solution.py:279
  (775 shorter events, 507.6 us)
Async XLA Ops:
  8.4 44.0 %all-gather.15.cloned.1.call-start = ((), (), s32[]{:S(2)}) async-start(), calls=%async_computation.20 | async-start | bytes 2048000 | tf_op jit(solution)/shard_map/while/body/eval_jaxpr/all_gather | solution.py:62
  10.3 102.0 %all-gather.19.cloned.1.call-start = ((), (), s32[]{:S(2)}) async-start(), calls=%async_computation.22 | async-start | bytes 2048000 | tf_op jit(solution)/shard_map/while/body/eval_jaxpr/all_gather | solution.py:117
  10.3 60.0 %copy-start.57 = (bf16[160,320]{1,0:T(8,128)(2,1)S(1)}, bf16[160,320]{1,0:T(8,128)(2,1)}, u32[]{:S(2)}) copy-start(bf16[160,320]{1,0:T(8,128)(2,1)} %get-tuple-element.1199) | copy-start | bytes 307204 | tf_op jit(solution)/shard_map/while
  55.6 60.0 %all-gather.17.cloned.1.call-start = ((), (), s32[]{:S(2)}) async-start(), calls=%async_computation.21 | async-start | bytes 2048000 | tf_op jit(solution)/shard_map/while/body/eval_jaxpr/all_gather | solution.py:116
  89.5 128.1 %reduce-scatter.38.cloned.1.call-start = ((), (), s32[]{:S(2)}) async-start(), calls=%async_computation.23 | async-start | bytes 4096000 | tf_op jit(solution)/shard_map/while/body/eval_jaxpr/reduce_scatter | solution.py:70
  156.7 62.2 %copy-start.56 = (f32[1280]{0:T(1024)S(1)}, f32[1280]{0:T(1024)}, u32[]{:S(2)}) copy-start(f32[1280]{0:T(1024)} %get-tuple-element.1203) | copy-start | bytes 15364 | tf_op jit(solution)/shard_map/while
  156.7 66.4 %copy-start.74 = (f32[1280]{0:T(1024)S(1)}, f32[1280]{0:T(1024)}, u32[]{:S(2)}) copy-start(f32[1280]{0:T(1024)} %get-tuple-element.1212) | copy-start | bytes 15364 | tf_op jit(solution)/shard_map/while
  156.8 66.4 %all-gather.23.cloned.1.call-start = ((), (), s32[]{:S(2)}) async-start(), calls=%async_computation.25 | async-start | bytes 3686400 | tf_op jit(solution)/shard_map/while/body/eval_jaxpr/all_gather | solution.py:255
  157.3 102.3 %all-gather.21.cloned.1.call-start = ((), (), s32[]{:S(2)}) async-start(), calls=%async_computation.24 | async-start | bytes 2048000 | tf_op jit(solution)/shard_map/while/body/eval_jaxpr/all_gather | solution.py:62
  221.4 71.7 %all-gather.25.cloned.1.call-start = ((), (), s32[]{:S(2)}) async-start(), calls=%async_computation.26 | async-start | bytes 3686400 | tf_op jit(solution)/shard_map/while/body/eval_jaxpr/all_gather | solution.py:254
  222.0 105.9 %all-gather.27.cloned.1.call-start = ((), (), s32[]{:S(2)}) async-start(), calls=%async_computation.27 | async-start | bytes 3686400 | tf_op jit(solution)/shard_map/while/body/eval_jaxpr/all_gather | solution.py:256
  222.7 174.1 %reduce-scatter.40.cloned.1.call-start = ((), (), s32[]{:S(2)}) async-start(), calls=%async_computation.28 | async-start | bytes 4096000 | tf_op jit(solution)/shard_map/while/body/eval_jaxpr/reduce_scatter | solution.py:70
  223.2 70.0 %copy-start.82 = (f32[1280]{0:T(1024)S(1)}, f32[1280]{0:T(1024)}, u32[]{:S(2)}) copy-start(f32[1280]{0:T(1024)} %get-tuple-element.1210) | copy-start | bytes 15364 | tf_op jit(solution)/shard_map/while
  334.4 63.8 %copy-start.34 = (bf16[2,160,1280]{2,1,0:T(8,128)(2,1)S(1)}, bf16[2,160,1280]{2,1,0:T(8,128)(2,1)}, u32[]{:S(2)}) copy-start(bf16[2,160,1280]{2,1,0:T(8,128)(2,1)} %get-tuple-element.1204) | copy-start | bytes 2457604 | tf_op jit(solution)/shard_map/while
  334.4 63.8 %copy-start.47 = (f32[1280]{0:T(1024)S(1)}, f32[1280]{0:T(1024)}, u32[]{:S(2)}) copy-start(f32[1280]{0:T(1024)} %get-tuple-element.1208) | copy-start | bytes 15364 | tf_op jit(solution)/shard_map/while
  334.4 105.5 %all-gather.29.cloned.1.call-start = ((), (), s32[]{:S(2)}) async-start(), calls=%async_computation.29 | async-start | bytes 2048000 | tf_op jit(solution)/shard_map/while/body/eval_jaxpr/all_gather | solution.py:66
  401.7 89.1 %reduce-scatter.42.cloned.1.call-start = ((), (), s32[]{:S(2)}) async-start(), calls=%async_computation.30 | async-start | bytes 2048000 | tf_op jit(solution)/shard_map/while/body/eval_jaxpr/reduce_scatter | solution.py:74
  455.5 78.4 %all-gather.31.cloned.1.call-start = ((), (), s32[]{:S(2)}) async-start(), calls=%async_computation.31 | async-start | bytes 2048000 | tf_op jit(solution)/shard_map/while/body/eval_jaxpr/all_gather | solution.py:66
  496.8 150.1 %reduce-scatter.44.cloned.1.call-start = ((), (), s32[]{:S(2)}) async-start(), calls=%async_computation.32 | async-start | bytes 2457600 | tf_op jit(solution)/shard_map/while
  617.3 63.0 %reduce-scatter.46.cloned.1.call-start = ((), (), s32[]{:S(2)}) async-start(), calls=%async_computation.33 | async-start | bytes 2457600 | tf_op jit(solution)/shard_map/while
  621.3 100.2 %reduce-scatter.48.cloned.1.call-start = ((), (), s32[]{:S(2)}) async-start(), calls=%async_computation.34 | async-start | bytes 2048000 | tf_op jit(solution)/shard_map/while/body/eval_jaxpr/reduce_scatter | solution.py:74
  723.9 40.2 %all-gather.15.cloned.1.call-start = ((), (), s32[]{:S(2)}) async-start(), calls=%async_computation.20 | async-start | bytes 2048000 | tf_op jit(solution)/shard_map/while/body/eval_jaxpr/all_gather | solution.py:62
  725.8 97.9 %all-gather.19.cloned.1.call-start = ((), (), s32[]{:S(2)}) async-start(), calls=%async_computation.22 | async-start | bytes 2048000 | tf_op jit(solution)/shard_map/while/body/eval_jaxpr/all_gather | solution.py:117
  767.4 59.7 %all-gather.17.cloned.1.call-start = ((), (), s32[]{:S(2)}) async-start(), calls=%async_computation.21 | async-start | bytes 2048000 | tf_op jit(solution)/shard_map/while/body/eval_jaxpr/all_gather | solution.py:116
  801.2 127.8 %reduce-scatter.38.cloned.1.call-start = ((), (), s32[]{:S(2)}) async-start(), calls=%async_computation.23 | async-start | bytes 4096000 | tf_op jit(solution)/shard_map/while/body/eval_jaxpr/reduce_scatter | solution.py:70
  868.2 62.1 %copy-start.56 = (f32[1280]{0:T(1024)S(1)}, f32[1280]{0:T(1024)}, u32[]{:S(2)}) copy-start(f32[1280]{0:T(1024)} %get-tuple-element.1203) | copy-start | bytes 15364 | tf_op jit(solution)/shard_map/while
  868.2 66.2 %copy-start.74 = (f32[1280]{0:T(1024)S(1)}, f32[1280]{0:T(1024)}, u32[]{:S(2)}) copy-start(f32[1280]{0:T(1024)} %get-tuple-element.1212) | copy-start | bytes 15364 | tf_op jit(solution)/shard_map/while
  868.2 66.3 %all-gather.23.cloned.1.call-start = ((), (), s32[]{:S(2)}) async-start(), calls=%async_computation.25 | async-start | bytes 3686400 | tf_op jit(solution)/shard_map/while/body/eval_jaxpr/all_gather | solution.py:255
  868.8 102.2 %all-gather.21.cloned.1.call-start = ((), (), s32[]{:S(2)}) async-start(), calls=%async_computation.24 | async-start | bytes 2048000 | tf_op jit(solution)/shard_map/while/body/eval_jaxpr/all_gather | solution.py:62
  932.9 71.9 %all-gather.25.cloned.1.call-start = ((), (), s32[]{:S(2)}) async-start(), calls=%async_computation.26 | async-start | bytes 3686400 | tf_op jit(solution)/shard_map/while/body/eval_jaxpr/all_gather | solution.py:254
  933.6 105.7 %all-gather.27.cloned.1.call-start = ((), (), s32[]{:S(2)}) async-start(), calls=%async_computation.27 | async-start | bytes 3686400 | tf_op jit(solution)/shard_map/while/body/eval_jaxpr/all_gather | solution.py:256
  934.2 174.1 %reduce-scatter.40.cloned.1.call-start = ((), (), s32[]{:S(2)}) async-start(), calls=%async_computation.28 | async-start | bytes 4096000 | tf_op jit(solution)/shard_map/while/body/eval_jaxpr/reduce_scatter | solution.py:70
  934.5 70.2 %copy-start.82 = (f32[1280]{0:T(1024)S(1)}, f32[1280]{0:T(1024)}, u32[]{:S(2)}) copy-start(f32[1280]{0:T(1024)} %get-tuple-element.1210) | copy-start | bytes 15364 | tf_op jit(solution)/shard_map/while
  1045.8 63.8 %copy-start.34 = (bf16[2,160,1280]{2,1,0:T(8,128)(2,1)S(1)}, bf16[2,160,1280]{2,1,0:T(8,128)(2,1)}, u32[]{:S(2)}) copy-start(bf16[2,160,1280]{2,1,0:T(8,128)(2,1)} %get-tuple-element.1204) | copy-start | bytes 2457604 | tf_op jit(solution)/shard_map/while
  1045.8 63.8 %copy-start.47 = (f32[1280]{0:T(1024)S(1)}, f32[1280]{0:T(1024)}, u32[]{:S(2)}) copy-start(f32[1280]{0:T(1024)} %get-tuple-element.1208) | copy-start | bytes 15364 | tf_op jit(solution)/shard_map/while
  1045.8 105.5 %all-gather.29.cloned.1.call-start = ((), (), s32[]{:S(2)}) async-start(), calls=%async_computation.29 | async-start | bytes 2048000 | tf_op jit(solution)/shard_map/while/body/eval_jaxpr/all_gather | solution.py:66
  1113.1 89.1 %reduce-scatter.42.cloned.1.call-start = ((), (), s32[]{:S(2)}) async-start(), calls=%async_computation.30 | async-start | bytes 2048000 | tf_op jit(solution)/shard_map/while/body/eval_jaxpr/reduce_scatter | solution.py:74
  1166.9 78.4 %all-gather.31.cloned.1.call-start = ((), (), s32[]{:S(2)}) async-start(), calls=%async_computation.31 | async-start | bytes 2048000 | tf_op jit(solution)/shard_map/while/body/eval_jaxpr/all_gather | solution.py:66
  1208.2 150.1 %reduce-scatter.44.cloned.1.call-start = ((), (), s32[]{:S(2)}) async-start(), calls=%async_computation.32 | async-start | bytes 2457600 | tf_op jit(solution)/shard_map/while
  1328.7 62.9 %reduce-scatter.46.cloned.1.call-start = ((), (), s32[]{:S(2)}) async-start(), calls=%async_computation.33 | async-start | bytes 2457600 | tf_op jit(solution)/shard_map/while
  1332.7 100.0 %reduce-scatter.48.cloned.1.call-start = ((), (), s32[]{:S(2)}) async-start(), calls=%async_computation.34 | async-start | bytes 2048000 | tf_op jit(solution)/shard_map/while/body/eval_jaxpr/reduce_scatter | solution.py:74
  1438.5 62.5 %reduce-scatter.24.cloned.1.call-start = ((), (), s32[]{:S(2)}) async-start(), calls=%async_computation.13 | async-start | bytes 2211840 | tf_op jit(solution)/shard_map/reduce_scatter | solution.py:273
  1441.5 85.8 %reduce-scatter.26.cloned.1.call-start = ((), (), s32[]{:S(2)}) async-start(), calls=%async_computation.14 | async-start | bytes 2211840 | tf_op jit(solution)/shard_map/reduce_scatter | solution.py:274
  1443.4 128.1 %reduce-scatter.28.cloned.1.call-start = ((), (), s32[]{:S(2)}) async-start(), calls=%async_computation.15 | async-start | bytes 2211840 | tf_op jit(solution)/shard_map/reduce_scatter | solution.py:275
  1445.3 170.8 %reduce-scatter.30.cloned.1.call-start = ((), (), s32[]{:S(2)}) async-start(), calls=%async_computation.16 | async-start | bytes 2211840 | tf_op jit(solution)/shard_map/reduce_scatter | solution.py:276
  1447.1 235.7 %reduce-scatter.32.cloned.1.call-start = ((), (), s32[]{:S(2)}) async-start(), calls=%async_computation.17 | async-start | bytes 7372800 | tf_op jit(solution)/shard_map/reduce_scatter | solution.py:277
  1447.7 302.4 %reduce-scatter.34.cloned.1.call-start = ((), (), s32[]{:S(2)}) async-start(), calls=%async_computation.18 | async-start | bytes 7372800 | tf_op jit(solution)/shard_map/reduce_scatter | solution.py:278
  1448.5 368.5 %reduce-scatter.36.cloned.1.call-start = ((), (), s32[]{:S(2)}) async-start(), calls=%async_computation.19 | async-start | bytes 7372800 | tf_op jit(solution)/shard_map/reduce_scatter | solution.py:279
  (171 other events, 1420.6 us)
Sparse Core Ops, SparseCore 0:
  11.4 40.8 all-gather.14
  55.7 20.9 all-gather.18
  89.6 20.8 all-gather.16
  156.9 60.6 reduce-scatter.37
  334.5 62.2 reduce-scatter.39
  455.6 35.1 reduce-scatter.41
  617.4 29.4 reduce-scatter.43
  649.6 30.6 reduce-scatter.45
  727.0 37.0 all-gather.14
  767.5 20.9 all-gather.18
  801.4 20.6 all-gather.16
  868.3 60.6 reduce-scatter.37
  1045.9 62.2 reduce-scatter.39
  1167.0 35.1 reduce-scatter.41
  1328.8 29.4 reduce-scatter.43
  1360.9 30.6 reduce-scatter.45
Sparse Core Ops, SparseCore 1:
  159.3 31.0 all-gather.22
  221.5 38.1 all-gather.20
  261.5 31.5 all-gather.24
  295.2 32.7 all-gather.26
  401.7 38.1 all-gather.28
  496.9 37.0 all-gather.30
  685.1 36.3 reduce-scatter.47
  870.8 31.0 all-gather.22
  932.9 38.1 all-gather.20
  973.1 31.5 all-gather.24
  1006.6 32.7 all-gather.26
  1113.2 38.1 all-gather.28
  1208.3 37.0 all-gather.30
  1396.4 36.3 reduce-scatter.47
  1443.3 39.3 reduce-scatter.23
  1487.1 40.1 reduce-scatter.25
  1531.3 40.1 reduce-scatter.27
  1575.9 40.2 reduce-scatter.29
  1620.0 62.8 reduce-scatter.31
  1687.3 62.8 reduce-scatter.33
  1754.0 62.8 reduce-scatter.35
where the time goes:
time: 1830 us; the launch traced here: 1820 us
  waiting for transfers between devices  1120 us (61%)
  matrix products  371 us (20%)
  blocking collectives  146 us (8%)
  local copies, waits for them, and re-layouts  95.6 us (5%)
  other arithmetic  67.2 us (4%)
    reduce_scatter x4, waiting for transfers between devices, own_rows(): lax.psum_scatter(partial_value, 'tp', scatter_dimension=0, tiled=True)  245 us
    dot_general x44, matrix products, contract_cols(): lax.dot_general(former, latter, (((1,), (1,)), ((), ())), preferred_eleme...  152 us
    all_gather x4, waiting for transfers between devices, group_grads(): return lax.all_gather(own_block, 'tp', axis=0, tiled=True)  149 us
    all_gather x4, waiting for transfers between devices, group_rows(): return lax.all_gather(own_block, 'tp', axis=0, tiled=True)  129 us
    reduce_scatter x4, waiting for transfers between devices, own_grads(): lax.psum_scatter(partial_value.astype(jnp.bfloat16), 'tp', scatter_dimens...  97.7 us
    dot_general x34, matrix products, contract_rows(): lax.dot_general(former, latter, (((0,), (0,)), ((), ())), preferred_eleme...  92.1 us
    while x34, waiting for transfers between devices  70.1 us
    reduce_scatter x1, waiting for transfers between devices, per_device(): lax.psum_scatter(grad_g, ('shard', 'ctx'), scatter_dimension=0, tiled=True)  67.3 us
  transfers between devices with their start and end apart: 37, of which 30 were waited for; matrix products, arithmetic and copies ran while one was open for 10% of the time, Pallas kernels for 0%

commit v1 on v0

--- a/solution.py
+++ b/solution.py
@@ -67,7 +67,7 @@
 
 
 def own_rows(partial_value):
-    return lax.psum_scatter(partial_value, "tp", scatter_dimension=0, tiled=True)
+    return own_grads(partial_value)
 
 
 def own_grads(partial_value):
@@ -98,8 +98,8 @@
     )
 
 
-def micro_step(gathered, vectors, tokens_own, cotangent_own, parents, slots):
-    w_query, w_key, w_value, w_attn_out, w_up, w_gate, w_down = gathered
+def forward_attention(gathered, vectors, tokens_own, parents, slots):
+    w_query, w_key, w_value, w_attn_out = gathered[:4]
     alpha_attn, alpha_mlp, scale_qk, scale_up, scale_gate = vectors
     score_scale = math.sqrt(HDIM)
     hidden_group = group_rows(tokens_own)
@@ -112,10 +112,10 @@
     query_unit, key_unit = query_key(query_raw, key_raw, scale_qk)
     queries = query_unit.astype(jnp.bfloat16)
     keys_own = key_unit.astype(jnp.bfloat16)
-    keys_tree, values_tree = (
-        lax.all_gather(keys_own, "ctx", axis=0, tiled=True),
-        lax.all_gather(value_low, "ctx", axis=0, tiled=True),
-    )
+    keys_values = lax.all_gather(
+        jnp.concatenate([keys_own, value_low], axis=1), "ctx", axis=0, tiled=True
+    )
+    keys_tree, values_tree = jnp.split(keys_values, 2, axis=1)
     query_heads = split_heads(queries)
     key_heads = split_heads(keys_tree)
     value_heads = split_heads(values_tree)
@@ -134,8 +134,25 @@
 
     head_values, log_totals = lax.map(head_forward, (query_heads, key_heads, value_heads))
     heads_low = merge_heads(head_values).astype(jnp.bfloat16)
+    branch_one = own_rows(jnp.dot(heads_low, w_attn_out, preferred_element_type=jnp.float32))
+    kept = (
+        hidden_group,
+        visible,
+        query_raw,
+        key_raw,
+        query_heads,
+        key_heads,
+        value_heads,
+        log_totals,
+        heads_low,
+    )
+    return branch_one, kept
+
+
+def feed_forward(gathered, vectors, tokens_own, branch_one, cotangent_own):
+    w_up, w_gate, w_down = gathered[4:]
+    alpha_attn, alpha_mlp, scale_qk, scale_up, scale_gate = vectors
     tokens_wide = tokens_own.astype(jnp.float32)
-    branch_one = own_rows(jnp.dot(heads_low, w_attn_out, preferred_element_type=jnp.float32))
     hidden_one = mix_rows(tokens_wide, branch_one, alpha_attn)
     hidden_one_group = group_rows(hidden_one.astype(jnp.bfloat16))
     up_raw = jnp.dot(hidden_one_group, w_up, preferred_element_type=jnp.float32)
@@ -146,21 +163,37 @@
     upstream = cotangent_own.astype(jnp.float32)
     hidden_one_direct, branch_two_grad, grad_alpha_mlp = pull_out(upstream)
     branch_two_group = group_grads(branch_two_grad.astype(jnp.bfloat16))
-    grad_down = contract_rows(mixed_low, branch_two_group)
     mixed_grad = contract_cols(branch_two_group, w_down).astype(jnp.bfloat16).astype(jnp.float32)
     middle_value, pull_mid = jax.vjp(middle, up_raw, gate_raw, scale_up, scale_gate)
     up_grad, gate_grad, grad_scale_up, grad_scale_gate = pull_mid(mixed_grad)
     up_low = up_grad.astype(jnp.bfloat16)
     gate_low = gate_grad.astype(jnp.bfloat16)
-    grad_up = contract_rows(hidden_one_group, up_low)
-    grad_gate = contract_rows(hidden_one_group, gate_low)
     hidden_one_grad = hidden_one_direct + own_grads(
         contract_cols(up_low, w_up) + contract_cols(gate_low, w_gate)
     )
     hidden_again, pull_in = jax.vjp(mix_rows, tokens_wide, branch_one, alpha_attn)
     tokens_direct, branch_one_grad, grad_alpha_attn = pull_in(hidden_one_grad)
+    factors = (mixed_low, branch_two_group, hidden_one_group, up_low, gate_low)
+    sums = (grad_alpha_attn, grad_alpha_mlp, grad_scale_up, grad_scale_gate)
+    return output_wide.astype(jnp.bfloat16), tokens_direct, branch_one_grad, factors, sums
+
+
+def backward_attention(gathered, vectors, kept, branch_one_grad, tokens_direct):
+    w_query, w_key, w_value, w_attn_out = gathered[:4]
+    scale_qk = vectors[2]
+    score_scale = math.sqrt(HDIM)
+    (
+        hidden_group,
+        visible,
+        query_raw,
+        key_raw,
+        query_heads,
+        key_heads,
+        value_heads,
+        log_totals,
+        heads_low,
+    ) = kept
     branch_one_group = group_grads(branch_one_grad.astype(jnp.bfloat16))
-    grad_attn_out = contract_rows(heads_low, branch_one_group)
     heads_grad = split_heads(contract_cols(branch_one_group, w_attn_out).astype(jnp.bfloat16))
 
     def head_backward(record):
@@ -178,31 +211,28 @@
     query_grads, key_grads, value_grads = lax.map(
         head_backward, (query_heads, key_heads, value_heads, heads_grad, log_totals)
     )
-    key_own_grad, value_own_grad = (
-        lax.psum_scatter(
-            merge_heads(key_grads).astype(jnp.bfloat16), "ctx", scatter_dimension=0, tiled=True
-        ).astype(jnp.float32),
-        lax.psum_scatter(
-            merge_heads(value_grads).astype(jnp.bfloat16), "ctx", scatter_dimension=0, tiled=True
-        ).astype(jnp.float32),
-    )
+    both = lax.psum_scatter(
+        jnp.concatenate([merge_heads(key_grads), merge_heads(value_grads)], axis=1).astype(
+            jnp.bfloat16
+        ),
+        "ctx",
+        scatter_dimension=0,
+        tiled=True,
+    ).astype(jnp.float32)
+    key_own_grad, value_own_grad = jnp.split(both, 2, axis=1)
     unit_again, pull_qk = jax.vjp(query_key, query_raw, key_raw, scale_qk)
     query_raw_grad, key_raw_grad, grad_scale_qk = pull_qk((merge_heads(query_grads), key_own_grad))
     query_low = query_raw_grad.astype(jnp.bfloat16)
     key_low = key_raw_grad.astype(jnp.bfloat16)
     value_grad_low = value_own_grad.astype(jnp.bfloat16)
-    grad_query = contract_rows(hidden_group, query_low)
-    grad_key = contract_rows(hidden_group, key_low)
-    grad_value = contract_rows(hidden_group, value_grad_low)
     input_part = (
         contract_cols(query_low, w_query)
         + contract_cols(key_low, w_key)
         + contract_cols(value_grad_low, w_value)
     )
     grad_tokens = tokens_direct + own_grads(input_part)
-    weight_grads = (grad_query, grad_key, grad_value, grad_attn_out, grad_up, grad_gate, grad_down)
-    vector_grads = (grad_alpha_attn, grad_alpha_mlp, grad_scale_qk, grad_scale_up, grad_scale_gate)
-    return (output_wide.astype(jnp.bfloat16), grad_tokens, weight_grads, vector_grads)
+    factors = (hidden_group, query_low, key_low, value_grad_low, heads_low, branch_one_group)
+    return grad_tokens, factors, grad_scale_qk
 
 
 def per_device(
@@ -223,96 +253,84 @@
     scale_gate,
     cotangent,
 ):
-    width = tokens.shape[-1]
     local_heads = w_query.shape[1]
     local_hidden = w_up.shape[1]
     vectors = (alpha_attn, alpha_mlp, scale_qk, scale_up, scale_gate)
-    zero_weights = (
-        jnp.zeros((width, local_heads), jnp.float32),
-        jnp.zeros((width, local_heads), jnp.float32),
-        jnp.zeros((width, local_heads), jnp.float32),
-        jnp.zeros((local_heads, width), jnp.float32),
-        jnp.zeros((width, local_hidden), jnp.float32),
-        jnp.zeros((width, local_hidden), jnp.float32),
-        jnp.zeros((local_hidden, width), jnp.float32),
-    )
-    zero_vectors = (
-        jnp.zeros((width,), jnp.float32),
-        jnp.zeros((width,), jnp.float32),
-        jnp.zeros((local_heads,), jnp.float32),
-        jnp.zeros((local_hidden,), jnp.float32),
-        jnp.zeros((local_hidden,), jnp.float32),
-    )
-
-    def one_micro(totals, record):
-        tokens_one, cotangent_one, parents_one, slots_one = record
-        gathered = (
-            lax.all_gather(w_query, ("shard", "ctx"), axis=0, tiled=True),
-            lax.all_gather(w_key, ("shard", "ctx"), axis=0, tiled=True),
-            lax.all_gather(w_value, ("shard", "ctx"), axis=0, tiled=True),
-            lax.all_gather(w_attn_out, ("shard", "ctx"), axis=1, tiled=True),
-            lax.all_gather(w_up, ("shard", "ctx"), axis=0, tiled=True),
-            lax.all_gather(w_gate, ("shard", "ctx"), axis=0, tiled=True),
-            lax.all_gather(w_down, ("shard", "ctx"), axis=1, tiled=True),
+    spread = ("shard", "ctx")
+    gathered = (
+        lax.all_gather(w_query, spread, axis=0, tiled=True),
+        lax.all_gather(w_key, spread, axis=0, tiled=True),
+        lax.all_gather(w_value, spread, axis=0, tiled=True),
+        lax.all_gather(w_attn_out, spread, axis=1, tiled=True),
+        lax.all_gather(w_up, spread, axis=0, tiled=True),
+        lax.all_gather(w_gate, spread, axis=0, tiled=True),
+        lax.all_gather(w_down, spread, axis=1, tiled=True),
+    )
+    micros = range(tokens.shape[0])
+    front = [
+        forward_attention(gathered, vectors, tokens[m, 0], parents[m, 0], slot_segment[m, 0])
+        for m in micros
+    ]
+    mid = [
+        feed_forward(gathered, vectors, tokens[m, 0], front[m][0], cotangent[m, 0]) for m in micros
+    ]
+    back = [
+        backward_attention(gathered, vectors, front[m][1], mid[m][2], mid[m][1]) for m in micros
+    ]
+
+    def stack(pick):
+        return jnp.concatenate([pick(m) for m in micros], axis=0)
+
+    mixed_all, top_all, hidden_all, up_all, gate_all = (
+        stack(lambda m: mid[m][3][place]) for place in range(5)
+    )
+    tokens_all, query_all, key_all, value_all, heads_all, branch_all = (
+        stack(lambda m: back[m][1][place]) for place in range(6)
+    )
+
+    def to_owner(former, latter, axis):
+        product = contract_rows(former, latter).astype(jnp.bfloat16)
+        return lax.psum_scatter(product, spread, scatter_dimension=axis, tiled=True).astype(
+            jnp.float32
         )
-        output_one, input_grad, weight_grads, vector_grads = micro_step(
-            gathered, vectors, tokens_one, cotangent_one, parents_one[0], slots_one[0]
-        )
-        weight_totals = tuple((former + latter for former, latter in zip(totals[0], weight_grads)))
-        vector_totals = tuple((former + latter for former, latter in zip(totals[1], vector_grads)))
-        return ((weight_totals, vector_totals), (output_one, input_grad))
-
-    totals, stacked = lax.scan(
-        one_micro,
-        (zero_weights, zero_vectors),
-        (tokens[:, 0], cotangent[:, 0], parents, slot_segment),
-    )
-    weight_totals, vector_totals = totals
-    grad_q, grad_k, grad_v, grad_o, grad_u, grad_g, grad_d = weight_totals
-    weight_totals = (
-        lax.psum_scatter(grad_q, ("shard", "ctx"), scatter_dimension=0, tiled=True),
-        lax.psum_scatter(grad_k, ("shard", "ctx"), scatter_dimension=0, tiled=True),
-        lax.psum_scatter(grad_v, ("shard", "ctx"), scatter_dimension=0, tiled=True),
-        lax.psum_scatter(grad_o, ("shard", "ctx"), scatter_dimension=1, tiled=True),
-        lax.psum_scatter(grad_u, ("shard", "ctx"), scatter_dimension=0, tiled=True),
-        lax.psum_scatter(grad_g, ("shard", "ctx"), scatter_dimension=0, tiled=True),
-        lax.psum_scatter(grad_d, ("shard", "ctx"), scatter_dimension=1, tiled=True),
-    )
+
+    grad_d = to_owner(mixed_all, top_all, 1)
+    grad_u = to_owner(hidden_all, up_all, 0)
+    grad_g = to_owner(hidden_all, gate_all, 0)
+    grad_o = to_owner(heads_all, branch_all, 1)
+    grad_q = to_owner(tokens_all, query_all, 0)
+    grad_k = to_owner(tokens_all, key_all, 0)
+    grad_v = to_owner(tokens_all, value_all, 0)
+
+    sum_attn, sum_mlp, sum_up, sum_gate = (
+        sum(mid[m][4][place] for m in micros) for place in range(4)
+    )
+    sum_qk = sum(back[m][2] for m in micros)
     tp_count = lax.axis_size("tp")
     tp_place = lax.axis_index("tp")
-    qk_padded = lax.dynamic_update_slice_in_dim(
-        jnp.zeros((local_heads * tp_count,), jnp.float32),
-        vector_totals[2],
-        tp_place * local_heads,
-        0,
-    )
-    up_padded = lax.dynamic_update_slice_in_dim(
-        jnp.zeros((local_hidden * tp_count,), jnp.float32),
-        vector_totals[3],
-        tp_place * local_hidden,
-        0,
-    )
-    gate_padded = lax.dynamic_update_slice_in_dim(
-        jnp.zeros((local_hidden * tp_count,), jnp.float32),
-        vector_totals[4],
-        tp_place * local_hidden,
-        0,
-    )
+
+    def padded(vector):
+        return lax.dynamic_update_slice_in_dim(
+            jnp.zeros((vector.shape[0] * tp_count,), jnp.float32),
+            vector,
+            tp_place * vector.shape[0],
+            0,
+        )
+
     alpha_attn_sum, alpha_mlp_sum, qk_sum, up_sum, gate_sum = lax.psum(
-        (vector_totals[0], vector_totals[1], qk_padded, up_padded, gate_padded),
+        (sum_attn, sum_mlp, padded(sum_qk), padded(sum_up), padded(sum_gate)),
         ("shard", "ctx", "tp"),
     )
-    outputs_all, input_grads_all = stacked
     return (
-        outputs_all[:, None],
-        input_grads_all[:, None],
-        weight_totals[0],
-        weight_totals[1],
-        weight_totals[2],
-        weight_totals[3],
-        weight_totals[4],
-        weight_totals[5],
-        weight_totals[6],
+        jnp.stack([mid[m][0] for m in micros])[:, None],
+        jnp.stack([back[m][0] for m in micros])[:, None],
+        grad_q,
+        grad_k,
+        grad_v,
+        grad_o,
+        grad_u,
+        grad_g,
+        grad_d,
         alpha_attn_sum,
         alpha_mlp_sum,
         lax.dynamic_slice_in_dim(qk_sum, tp_place * local_heads, local_heads),

time: 1830 us -> 1380 us (0.75)
  waiting for transfers between devices: 1120 us -> 707 us
  blocking collectives: 146 us -> 92.6 us
    reduce_scatter x11 -> x7, waiting for transfers between devices: 561 us -> 210 us  [to_owner(): lax.psum_scatter(product, spread, scatter_dimension=axis, tiled=True)]
    reduce_scatter x4 -> x8, waiting for transfers between devices: 97.7 us -> 234 us  [own_grads(): lax.psum_scatter(partial_value.astype(jnp.bfloat16), 'tp', scatter_dimens...]
    all_gather x4, waiting for transfers between devices: 149 us -> 71.4 us  [group_grads(): return lax.all_gather(own_block, 'tp', axis=0, tiled=True)]
    while x34 -> x0, waiting for transfers between devices: 70.1 us -> none
    all_gather x8 -> x4, blocking collectives: 105 us -> 51.7 us  [the longest x1 15.2 us: per_device(): lax.all_gather(w_attn_out, spread, axis=1, tiled=True)]
    while x359 -> x40, local copies, waits for them, and re-layouts: 66.3 us -> 16.9 us
    unnamed x16 -> x248, local copies, waits for them, and re-layouts: 0.66 us -> 39.8 us
    all_gather x10 -> x5, waiting for transfers between devices: 109 us -> 79.3 us  [the longest x1 27.2 us: per_device(): lax.all_gather(w_down, spread, axis=1, tiled=True)]
  transfers between devices with their start and end apart: 37 -> 30, of which waited for: 30 -> 23; matrix products, arithmetic and copies ran while one was open for 10% -> 27% of each run, Pallas kernels for 0% -> 0%
where the time goes in v1:
time: 1380 us; the launch traced here: 1370 us
  waiting for transfers between devices  707 us (51%)
  matrix products  354 us (26%)
  local copies, waits for them, and re-layouts  111 us (8%)
  blocking collectives  92.6 us (7%)
  other arithmetic  84.3 us (6%)
  between operations  17.7 us (1%)
    reduce_scatter x8, waiting for transfers between devices, own_grads(): lax.psum_scatter(partial_value.astype(jnp.bfloat16), 'tp', scatter_dimens...  234 us
    reduce_scatter x7, waiting for transfers between devices, to_owner(): lax.psum_scatter(product, spread, scatter_dimension=axis, tiled=True)  210 us
    dot_general x44, matrix products, contract_cols(): lax.dot_general(former, latter, (((1,), (1,)), ((), ())), preferred_eleme...  127 us
    all_gather x4, waiting for transfers between devices, group_rows(): return lax.all_gather(own_block, 'tp', axis=0, tiled=True)  110 us
    dot_general x27, matrix products, contract_rows(): lax.dot_general(former, latter, (((0,), (0,)), ((), ())), preferred_eleme...  88.9 us
    all_gather x4, waiting for transfers between devices, group_grads(): return lax.all_gather(own_block, 'tp', axis=0, tiled=True)  71.4 us
    dot_general x10, matrix products, head_forward(): jnp.dot(soft_weights.astype(jnp.bfloat16), value_one, preferred_element_t...  49.6 us
    psum x1, blocking collectives, per_device(): lax.psum((sum_attn, sum_mlp, padded(sum_qk), padded(sum_up), padded(sum_g...  40.9 us
  transfers between devices with their start and end apart: 30, of which 23 were waited for; matrix products, arithmetic and copies ran while one was open for 27% of the time, Pallas kernels for 0%

profile of v1, /device:TPU:0, one launch (start us, length us, event | category | flops | bytes accessed | tf_op | source)
XLA Modules:
  0.0 1370.7 jit_solution(1674269570403214196)
XLA Ops:
  11.0 14.3 %all_gather.52 = bf16[1280,320]{1,0:T(8,128)(2,1)} all-gather(bf16[160,320]{1,0:T(8,128)(2,1)} %param.27), channel_id=1, replica_groups=mesh['shard'=2,'ctx'=4,'tp'=4] {'shard','ctx'}, dimensions={0}, use_global_device_ids=true | all-gather | bytes 921600 | tf_op jit(solution)/shard_map/all_gather | solution.py:261
  25.3 10.2 all_gather.53
  35.4 12.0 all_gather.54
  54.6 36.5 %all-gather.38.cloned.1.call-done = bf16[1,1,640,1280]{3,2,1,0:T(8,128)(2,1)} async-done(((bf16[1,1,160,1280]{3,2,1,0:T(8,128)(2,1)}), bf16[1,1,640,1280]{3,2,1,0:T(8,128)(2,1)}) %all-gather.38.cloned.1.call-update) | async-done | bytes 1638416 | tf_op jit(solution)/shard_map/all_gather | solution.py:62
  109.7 15.2 %all_gather.56 = bf16[320,1280]{0,1:T(8,128)(2,1)} all-gather(bf16[320,160]{0,1:T(8,128)(2,1)S(1)} %copy-done.91), channel_id=1, replica_groups=mesh['shard'=2,'ctx'=4,'tp'=4] {'shard','ctx'}, dimensions={1}, use_global_device_ids=true | all-gather | bytes 921600 | tf_op jit(solution)/shard_map/all_gather | solution.py:264
  131.7 7.4 all-gather.16.cloned.1.call-done
  150.4 57.9 %while.52 = (s32[]{:T(128)}, bf16[5,640,64]{1,2,0:T(8,128)(2,1)}, f32[5,640]{1,0:T(8,128)}, bf16[5,640,64]{2,1,0:T(8,128)(2,1)}, bf16[5,2560,64]{2,1,0:T(8,128)(...) while((s32[]{:T(128)}, bf16[5,640,64]{1,2,0:T(8,128)(2,1)}, ...), condition=%wide.region_5.6_spmd, body=%wide.region_2.5_spmd.sunk | while | flops 432536960 | bytes 49184892 | solution.py:135
  180.2 4.9 fusion.305
  213.1 33.7 %reduce-scatter.22.cloned.1.call-done = bf16[160,1280]{1,0:T(8,128)(2,1)} async-done(((bf16[640,1280]{1,0:T(8,128)(2,1)}), bf16[160,1280]{1,0:T(8,128)(2,1)}) %reduce-scatter.22.cloned.1.call-update) | async-done | bytes 409616 | tf_op jit(solution)/shard_map/reduce_scatter | solution.py:74
  257.4 32.3 %all-gather.18.cloned.1.call-done = bf16[640,1280]{1,0:T(8,128)(2,1)} async-done(((bf16[160,1280]{1,0:T(8,128)(2,1)}), bf16[640,1280]{1,0:T(8,128)(2,1)}) %all-gather.18.cloned.1.call-update) | async-done | bytes 1638416 | tf_op jit(solution)/shard_map/all_gather | solution.py:62
  289.8 6.5 fusion.186
  296.3 27.0 %all-gather.20.cloned.1.call-done = bf16[1280,1280]{1,0:T(8,128)(2,1)} async-done(((bf16[160,1280]{1,0:T(8,128)(2,1)}), bf16[1280,1280]{1,0:T(8,128)(2,1)}) %all-gather.20.cloned.1.call-update) | async-done | bytes 3276816 | tf_op jit(solution)/shard_map/all_gather | solution.py:265
  323.3 7.6 multiply_convert_fusion.7
  330.9 27.2 %all-gather.24.cloned.1.call-done = bf16[1280,1280]{0,1:T(8,128)(2,1)} async-done(((bf16[1280,160]{0,1:T(8,128)(2,1)}), bf16[1280,1280]{0,1:T(8,128)(2,1)}) %all-gather.24.cloned.1.call-update) | async-done | bytes 3276816 | tf_op jit(solution)/shard_map/all_gather | solution.py:267
  358.0 5.9 convolution_convert_fusion.7
  371.1 17.7 %all-gather.26.cloned.1.call-done = bf16[2560,640]{0,1:T(8,128)(2,1)} async-done(((bf16[640,640]{0,1:T(8,128)(2,1)}), bf16[2560,640]{0,1:T(8,128)(2,1)}) %all-gather.26.cloned.1.call-update) | async-done | bytes 3276816 | tf_op jit(solution)/shard_map/all_gather | solution.py:115
  409.0 51.8 %while.53 = (s32[]{:T(128)}, bf16[5,640,64]{1,2,0:T(8,128)(2,1)}, f32[5,640]{1,0:T(8,128)S(1)}, bf16[5,640,64]{2,1,0:T(8,128)(2,1)}, bf16[5,2560,64]{2,1,0:T(8,1...) while((s32[]{:T(128)}, bf16[5,640,64]{1,2,0:T(8,128)(2,1)}, ...), condition=%wide.region_17.18_spmd, body=%wide.region_14.17_spmd.sunk | while | flops 432536960 | bytes 49184892 | solution.py:135
  414.4 5.2 fusion.309
  425.0 5.0 fusion.309
  435.3 5.0 fusion.309
  445.6 4.9 fusion.309
  455.9 4.9 fusion.309
  465.3 8.9 multiply_reduce_fusion.3
  483.8 17.6 %reduce-scatter.26.cloned.1.call-done = bf16[160,1280]{1,0:T(8,128)(2,1)} async-done(((bf16[640,1280]{1,0:T(8,128)(2,1)}), bf16[160,1280]{1,0:T(8,128)(2,1)}) %reduce-scatter.26.cloned.1.call-update) | async-done | bytes 409616 | tf_op jit(solution)/shard_map/reduce_scatter | solution.py:74
  502.6 36.5 %reduce-scatter.30.cloned.1.call-done = bf16[160,1280]{1,0:T(8,128)(2,1)} async-done(((bf16[640,1280]{1,0:T(8,128)(2,1)}), bf16[160,1280]{1,0:T(8,128)(2,1)}) %reduce-scatter.30.cloned.1.call-update) | async-done | bytes 409616 | tf_op jit(solution)/shard_map/reduce_scatter | solution.py:74
  543.0 37.1 %all-gather.28.cloned.1.call-done = bf16[640,1280]{1,0:T(8,128)(2,1)} async-done(((bf16[160,1280]{1,0:T(8,128)(2,1)}), bf16[640,1280]{1,0:T(8,128)(2,1)}) %all-gather.28.cloned.1.call-update) | async-done | bytes 1638416 | tf_op jit(solution)/shard_map/all_gather | solution.py:62
  594.0 35.3 %reduce-scatter.28.cloned.1.call-done = bf16[160,1280]{1,0:T(8,128)(2,1)} async-done(((bf16[640,1280]{1,0:T(8,128)(2,1)}), bf16[160,1280]{1,0:T(8,128)(2,1)}) %reduce-scatter.28.cloned.1.call-update) | async-done | bytes 409616 | tf_op jit(solution)/shard_map/reduce_scatter | solution.py:74
  636.0 36.7 %all-gather.34.cloned.1.call-done = bf16[640,1280]{1,0:T(8,128)(2,1)} async-done(((bf16[160,1280]{1,0:T(8,128)(2,1)}), bf16[640,1280]{1,0:T(8,128)(2,1)}) %all-gather.34.cloned.1.call-update) | async-done | bytes 1638416 | tf_op jit(solution)/shard_map/all_gather | solution.py:66
  672.7 8.8 multiply_reduce_fusion.2
  690.5 35.2 %reduce-scatter.34.cloned.1.call-done = bf16[160,1280]{1,0:T(8,128)(2,1)} async-done(((bf16[640,1280]{1,0:T(8,128)(2,1)}), bf16[160,1280]{1,0:T(8,128)(2,1)}) %reduce-scatter.34.cloned.1.call-update) | async-done | bytes 409616 | tf_op jit(solution)/shard_map/reduce_scatter | solution.py:74
  734.0 34.7 %all-gather.32.cloned.1.call-done = bf16[640,1280]{1,0:T(8,128)(2,1)} async-done(((bf16[160,1280]{1,0:T(8,128)(2,1)}), bf16[640,1280]{1,0:T(8,128)(2,1)}) %all-gather.32.cloned.1.call-update) | async-done | bytes 1638416 | tf_op jit(solution)/shard_map/all_gather | solution.py:66
  775.3 71.4 %while.54 = (s32[]{:T(128)}, f32[5,640,64]{1,2,0:T(8,128)S(1)}, bf16[5,2560,64]{1,2,0:T(8,128)(2,1)}, bf16[5,2560,64]{1,2,0:T(8,128)(2,1)}, bf16[5,640,64]{2,1,0...) while((s32[]{:T(128)}, f32[5,640,64]{1,2,0:T(8,128)S(1)}, ...), condition=%wide.region_31.32_spmd, body=%wide.region_29.31_spmd.sunk | while | flops 1063525760 | bytes 61458068 | solution.py:211
  860.6 71.4 %while.55 = (s32[]{:T(128)}, f32[5,640,64]{1,2,0:T(8,128)S(1)}, bf16[5,2560,64]{1,2,0:T(8,128)(2,1)}, bf16[5,2560,64]{1,2,0:T(8,128)(2,1)}, bf16[5,640,64]{2,1,0...) while((s32[]{:T(128)}, f32[5,640,64]{1,2,0:T(8,128)S(1)}, ...), condition=%wide.region_43.44_spmd, body=%wide.region_41.43_spmd.sunk | while | flops 1063525760 | bytes 61458068 | solution.py:211
  940.4 7.9 convolution_convert_fusion
  953.0 6.0 convolution_convert_fusion.1
  960.9 7.9 convolution_convert_fusion.2
  968.9 5.2 fusion.104
  985.2 5.1 convolution_convert_fusion.9
  1002.4 5.0 convolution_convert_fusion.10
  1020.0 6.6 reduce-scatter.50.cloned.1.call-done
  1028.6 48.3 %reduce-scatter.48.cloned.1.call-done = bf16[160,1280]{1,0:T(8,128)(2,1)} async-done(((bf16[1280,1280]{1,0:T(8,128)(2,1)}), bf16[160,1280]{1,0:T(8,128)(2,1)}) %reduce-scatter.48.cloned.1.call-update) | async-done | bytes 409616 | tf_op jit(solution)/shard_map/reduce_scatter | solution.py:293
  1078.8 48.2 %reduce-scatter.46.cloned.1.call-done = bf16[160,1280]{1,0:T(8,128)(2,1)} async-done(((bf16[1280,1280]{1,0:T(8,128)(2,1)}), bf16[160,1280]{1,0:T(8,128)(2,1)}) %reduce-scatter.46.cloned.1.call-update) | async-done | bytes 409616 | tf_op jit(solution)/shard_map/reduce_scatter | solution.py:293
  1129.1 36.7 %reduce-scatter.44.cloned.1.call-done = bf16[320,160]{0,1:T(8,128)(2,1)} async-done(((bf16[320,1280]{0,1:T(8,128)(2,1)}), bf16[320,160]{0,1:T(8,128)(2,1)}) %reduce-scatter.44.cloned.1.call-update) | async-done | bytes 102416 | tf_op jit(solution)/shard_map/reduce_scatter | solution.py:293
  1167.5 37.6 %reduce-scatter.38.cloned.1.call-done = bf16[160,320]{1,0:T(8,128)(2,1)} async-done(((bf16[1280,320]{1,0:T(8,128)(2,1)}), bf16[160,320]{1,0:T(8,128)(2,1)}) %reduce-scatter.38.cloned.1.call-update) | async-done | bytes 102416 | tf_op jit(solution)/shard_map/reduce_scatter | solution.py:293
  1206.7 40.9 %all-reduce = (f32[1280]{0:T(1024)}, f32[1280]{0:T(1024)}, f32[1280]{0:T(1024)S(1)}, f32[5120]{0:T(1024)S(1)}, f32[5120]{0:T(1024)S(1)}) all-reduce(f32[1280]{0:T(1024)S(1)} %add.328, f32[1280]{0:T(1024)S(1)} %add.329, f32[1280]{0:T(1024)S(1)} %add_dynamic-update-slice_fusion.1, ...), channel_id=1, replica_groups=mesh['shard'=2,'ctx'=4,'tp'=4] {'shard','ctx','tp'}, use_global_device_ids=true, to_apply=%region_57.58 | all-reduce | flops 14080 | bytes 112640 | tf_op jit(solution)/shard_map/psum | solution.py:320
  1251.3 32.1 %reduce-scatter.40.cloned.1.call-done = bf16[160,320]{1,0:T(8,128)(2,1)} async-done(((bf16[1280,320]{1,0:T(8,128)(2,1)}), bf16[160,320]{1,0:T(8,128)(2,1)}) %reduce-scatter.40.cloned.1.call-update) | async-done | bytes 102416 | tf_op jit(solution)/shard_map/reduce_scatter | solution.py:293
  1285.0 36.9 %reduce-scatter.36.cloned.1.call-done = bf16[160,1280]{1,0:T(8,128)(2,1)} async-done(((bf16[640,1280]{1,0:T(8,128)(2,1)}), bf16[160,1280]{1,0:T(8,128)(2,1)}) %reduce-scatter.36.cloned.1.call-update) | async-done | bytes 409616 | tf_op jit(solution)/shard_map/reduce_scatter | solution.py:74
  1321.9 38.3 %reduce-scatter.32.cloned.1.call-done = bf16[160,1280]{1,0:T(8,128)(2,1)} async-done(((bf16[640,1280]{1,0:T(8,128)(2,1)}), bf16[160,1280]{1,0:T(8,128)(2,1)}) %reduce-scatter.32.cloned.1.call-update) | async-done | bytes 409616 | tf_op jit(solution)/shard_map/reduce_scatter | solution.py:74
  (632 shorter events, 455.7 us)
Async XLA Ops:
  8.0 43.9 %all-gather.40.cloned.1.call-start = ((), (), s32[]{:S(2)}) async-start(), calls=%async_computation.44 | async-start | bytes 2048000 | tf_op jit(solution)/shard_map/all_gather | solution.py:62
  10.2 80.9 %all-gather.38.cloned.1.call-start = ((), (), s32[]{:S(2)}) async-start(), calls=%async_computation.43 | async-start | bytes 2048000 | tf_op jit(solution)/shard_map/all_gather | solution.py:62
  11.0 128.2 %all-gather.16.cloned.1.call-start = ((), (), s32[]{:S(2)}) async-start(), calls=%async_computation.17 | async-start | bytes 4096000 | tf_op jit(solution)/shard_map/all_gather | solution.py:115
  35.4 62.4 %copy-start.9 = (bf16[1280,320]{1,0:T(8,128)(2,1)}, bf16[1280,320]{1,0:T(8,128)(2,1)S(1)}, u32[]{:S(2)}) copy-start(bf16[1280,320]{1,0:T(8,128)(2,1)S(1)} %all_gather.53) | copy-start | bytes 2457604
  54.5 48.1 %copy-start.15 = (f32[640,320]{0,1:T(8,128)}, f32[640,320]{0,1:T(8,128)S(1)}, u32[]{:S(2)}) copy-start(f32[640,320]{0,1:T(8,128)S(1)} %fusion.165) | copy-start | bytes 2457604
  54.6 39.2 %copy-start.83 = (f32[640,5]{0,1:T(8,128)}, f32[640,5]{0,1:T(8,128)S(1)}, u32[]{:S(2)}) copy-start(f32[640,5]{0,1:T(8,128)S(1)} %multiply_reduce_fusion.18) | copy-start | bytes 38404
  54.6 48.0 %copy-start.73 = (f32[640,5]{0,1:T(8,128)}, f32[640,5]{0,1:T(8,128)S(1)}, u32[]{:S(2)}) copy-start(f32[640,5]{0,1:T(8,128)S(1)} %add_rsqrt_fusion.1) | copy-start | bytes 38404
  108.4 138.4 %reduce-scatter.22.cloned.1.call-start = ((), (), s32[]{:S(2)}) async-start(), calls=%async_computation.18 | async-start | bytes 2048000 | tf_op jit(solution)/shard_map/reduce_scatter | solution.py:74
  150.4 57.9 %copy-start.66 = (bf16[320,1280]{0,1:T(8,128)(2,1)S(1)}, bf16[320,1280]{0,1:T(8,128)(2,1)}, u32[]{:S(2)}) copy-start(bf16[320,1280]{0,1:T(8,128)(2,1)} %all_gather.56) | copy-start | bytes 2457604
  208.3 44.3 %copy-start.2 = (pred[640,2560]{1,0:T(32,128)(4,1)}, pred[640,2560]{1,0:T(32,128)(4,1)S(1)}, u32[]{:S(2)}) copy-start(pred[640,2560]{1,0:T(32,128)(4,1)S(1)} %get-tuple-element.781) | copy-start | bytes 4915204
  208.3 40.2 %copy-start.8 = (bf16[2,1,160,1280]{3,2,1,0:T(8,128)(2,1)S(1)}, bf16[2,1,160,1280]{3,2,1,0:T(8,128)(2,1)}, u32[]{:S(2)}) copy-start(bf16[2,1,160,1280]{3,2,1,0:T(8,128)(2,1)} %param.24) | copy-start | bytes 2457604
  208.3 40.2 %copy-start.68 = (f32[1280]{0:T(1024)S(1)}, f32[1280]{0:T(1024)}, u32[]{:S(2)}) copy-start(f32[1280]{0:T(1024)} %param.34) | copy-start | bytes 15364
  211.9 42.1 %copy-start.29 = (bf16[1280,320]{1,0:T(8,128)(2,1)S(1)}, bf16[1280,320]{1,0:T(8,128)(2,1)}, u32[]{:S(2)}) copy-start(bf16[1280,320]{1,0:T(8,128)(2,1)} %all_gather.54) | copy-start | bytes 2457604
  211.9 45.5 %all-gather.22.cloned.1.call-start = ((), (), s32[]{:S(2)}) async-start(), calls=%async_computation.21 | async-start | bytes 3686400 | tf_op jit(solution)/shard_map/all_gather | solution.py:266
  212.5 77.3 %all-gather.18.cloned.1.call-start = ((), (), s32[]{:S(2)}) async-start(), calls=%async_computation.19 | async-start | bytes 2048000 | tf_op jit(solution)/shard_map/all_gather | solution.py:62
  252.7 70.6 %all-gather.20.cloned.1.call-start = ((), (), s32[]{:S(2)}) async-start(), calls=%async_computation.20 | async-start | bytes 3686400 | tf_op jit(solution)/shard_map/all_gather | solution.py:265
  253.2 104.8 %all-gather.24.cloned.1.call-start = ((), (), s32[]{:S(2)}) async-start(), calls=%async_computation.22 | async-start | bytes 3686400 | tf_op jit(solution)/shard_map/all_gather | solution.py:267
  254.0 134.9 %all-gather.26.cloned.1.call-start = ((), (), s32[]{:S(2)}) async-start(), calls=%async_computation.24 | async-start | bytes 4096000 | tf_op jit(solution)/shard_map/all_gather | solution.py:115
  257.3 144.4 %reduce-scatter.24.cloned.1.call-start = ((), (), s32[]{:S(2)}) async-start(), calls=%async_computation.23 | async-start | bytes 2048000 | tf_op jit(solution)/shard_map/reduce_scatter | solution.py:74
  257.4 65.9 %copy-start.118 = (f32[1280]{0:T(1024)S(1)}, f32[1280]{0:T(1024)}, u32[]{:S(2)}) copy-start(f32[1280]{0:T(1024)} %param.37) | copy-start | bytes 15364
  364.0 101.3 %all-gather.30.cloned.1.call-start = ((), (), s32[]{:S(2)}) async-start(), calls=%async_computation.28 | async-start | bytes 2048000 | tf_op jit(solution)/shard_map/all_gather | solution.py:66
  409.0 92.4 %reduce-scatter.26.cloned.1.call-start = ((), (), s32[]{:S(2)}) async-start(), calls=%async_computation.25 | async-start | bytes 2048000 | tf_op jit(solution)/shard_map/reduce_scatter | solution.py:74
  465.0 74.1 %reduce-scatter.30.cloned.1.call-start = ((), (), s32[]{:S(2)}) async-start(), calls=%async_computation.29 | async-start | bytes 2048000 | tf_op jit(solution)/shard_map/reduce_scatter | solution.py:74
  480.3 58.9 %copy-start.23 = (f32[160,1280]{1,0:T(8,128)S(1)}, f32[160,1280]{1,0:T(8,128)}, u32[]{:S(2)}) copy-start(f32[160,1280]{1,0:T(8,128)} %copy-done.22) | copy-start | bytes 2457604
  483.8 96.4 %all-gather.28.cloned.1.call-start = ((), (), s32[]{:S(2)}) async-start(), calls=%async_computation.26 | async-start | bytes 2048000 | tf_op jit(solution)/shard_map/all_gather | solution.py:62
  501.4 40.4 %copy-start.12 = (bf16[160,1280]{1,0:T(8,128)(2,1)S(1)}, bf16[160,1280]{1,0:T(8,128)(2,1)}, u32[]{:S(2)}) copy-start(bf16[160,1280]{1,0:T(8,128)(2,1)} %reduce-scatter.26.cloned.1.call-done) | copy-start | bytes 1228804
  543.0 86.3 %reduce-scatter.28.cloned.1.call-start = ((), (), s32[]{:S(2)}) async-start(), calls=%async_computation.27 | async-start | bytes 2048000 | tf_op jit(solution)/shard_map/reduce_scatter | solution.py:74
  590.4 40.1 %copy-start.37 = (bf16[2,1,160,1280]{3,2,1,0:T(8,128)(2,1)S(1)}, bf16[2,1,160,1280]{3,2,1,0:T(8,128)(2,1)}, u32[]{:S(2)}) copy-start(bf16[2,1,160,1280]{3,2,1,0:T(8,128)(2,1)} %param.39) | copy-start | bytes 2457604
  594.0 78.7 %all-gather.34.cloned.1.call-start = ((), (), s32[]{:S(2)}) async-start(), calls=%async_computation.32 | async-start | bytes 2048000 | tf_op jit(solution)/shard_map/all_gather | solution.py:66
  635.5 90.2 %reduce-scatter.34.cloned.1.call-start = ((), (), s32[]{:S(2)}) async-start(), calls=%async_computation.33 | async-start | bytes 2048000 | tf_op jit(solution)/shard_map/reduce_scatter | solution.py:74
  686.9 38.9 %copy-start.62 = (bf16[160,1280]{1,0:T(8,128)(2,1)S(1)}, bf16[160,1280]{1,0:T(8,128)(2,1)}, u32[]{:S(2)}) copy-start(bf16[160,1280]{1,0:T(8,128)(2,1)} %reduce-scatter.30.cloned.1.call-done) | copy-start | bytes 1228804
  690.5 78.2 %all-gather.32.cloned.1.call-start = ((), (), s32[]{:S(2)}) async-start(), calls=%async_computation.30 | async-start | bytes 2048000 | tf_op jit(solution)/shard_map/all_gather | solution.py:66
  731.5 121.9 %all-gather.36.cloned.1.call-start = ((), (), s32[]{:S(2)}) async-start(), calls=%async_computation.34 | async-start | bytes 2048000 | tf_op jit(solution)/shard_map/all_gather | solution.py:66
  733.7 245.9 %reduce-scatter.52.cloned.1.call-start = ((), (), s32[]{:S(2)}) async-start(), calls=%async_computation.45 | async-start | bytes 4096000
  853.2 128.9 %reduce-scatter.54.cloned.1.call-start = ((), (), s32[]{:S(2)}) async-start(), calls=%async_computation.46 | async-start | bytes 4096000
  938.5 88.2 %reduce-scatter.50.cloned.1.call-start = ((), (), s32[]{:S(2)}) async-start(), calls=%async_computation.42 | async-start | bytes 3686400 | tf_op jit(solution)/shard_map/reduce_scatter | solution.py:293
  948.3 128.6 %reduce-scatter.48.cloned.1.call-start = ((), (), s32[]{:S(2)}) async-start(), calls=%async_computation.41 | async-start | bytes 3686400 | tf_op jit(solution)/shard_map/reduce_scatter | solution.py:293
  959.0 168.0 %reduce-scatter.46.cloned.1.call-start = ((), (), s32[]{:S(2)}) async-start(), calls=%async_computation.40 | async-start | bytes 3686400 | tf_op jit(solution)/shard_map/reduce_scatter | solution.py:293
  968.8 197.0 %reduce-scatter.44.cloned.1.call-start = ((), (), s32[]{:S(2)}) async-start(), calls=%async_computation.39 | async-start | bytes 1105920 | tf_op jit(solution)/shard_map/reduce_scatter | solution.py:293
  974.1 230.9 %reduce-scatter.38.cloned.1.call-start = ((), (), s32[]{:S(2)}) async-start(), calls=%async_computation.36 | async-start | bytes 1105920 | tf_op jit(solution)/shard_map/reduce_scatter | solution.py:293
  979.1 270.6 %reduce-scatter.42.cloned.1.call-start = ((), (), s32[]{:S(2)}) async-start(), calls=%async_computation.38 | async-start | bytes 1105920 | tf_op jit(solution)/shard_map/reduce_scatter | solution.py:293
  990.3 293.1 %reduce-scatter.40.cloned.1.call-start = ((), (), s32[]{:S(2)}) async-start(), calls=%async_computation.37 | async-start | bytes 1105920 | tf_op jit(solution)/shard_map/reduce_scatter | solution.py:293
  1007.4 314.5 %reduce-scatter.36.cloned.1.call-start = ((), (), s32[]{:S(2)}) async-start(), calls=%async_computation.35 | async-start | bytes 2048000 | tf_op jit(solution)/shard_map/reduce_scatter | solution.py:74
  1012.5 347.7 %reduce-scatter.32.cloned.1.call-start = ((), (), s32[]{:S(2)}) async-start(), calls=%async_computation.31 | async-start | bytes 2048000 | tf_op jit(solution)/shard_map/reduce_scatter | solution.py:74
  1018.6 110.4 %copy-start.36 = (f32[640,320]{0,1:T(8,128)S(1)}, f32[640,320]{0,1:T(8,128)}, u32[]{:S(2)}) copy-start(f32[640,320]{0,1:T(8,128)} %get-tuple-element.387) | copy-start | bytes 2457604
  1019.9 340.3 %copy-start.32 = (f32[160,1280]{1,0:T(8,128)S(1)}, f32[160,1280]{1,0:T(8,128)}, u32[]{:S(2)}) copy-start(f32[160,1280]{1,0:T(8,128)} %get-tuple-element.332) | copy-start | bytes 2457604
  1020.0 340.3 %copy-start.34 = (f32[160,1280]{1,0:T(8,128)S(1)}, f32[160,1280]{1,0:T(8,128)}, u32[]{:S(2)}) copy-start(f32[160,1280]{1,0:T(8,128)} %copy-done.33) | copy-start | bytes 2457604
  1020.0 340.3 %copy-start.69 = (f32[1280]{0:T(1024)S(1)}, f32[1280]{0:T(1024)}, u32[]{:S(2)}) copy-start(f32[1280]{0:T(1024)} %param.34) | copy-start | bytes 15364
  (121 other events, 541.9 us)
Sparse Core Ops, SparseCore 0:
  11.0 40.8 all-gather.39
  54.0 37.0 all-gather.37
  108.5 30.6 all-gather.15
  212.1 34.6 reduce-scatter.21
  364.1 36.2 reduce-scatter.23
  409.1 38.1 all-gather.29
  465.2 36.1 reduce-scatter.25
  503.8 35.3 reduce-scatter.29
  594.1 35.1 reduce-scatter.27
  690.6 35.1 reduce-scatter.33
  853.3 37.6 reduce-scatter.51
  938.6 37.6 reduce-scatter.53
  979.7 46.8 reduce-scatter.49
  1029.9 46.9 reduce-scatter.47
  1080.1 46.8 reduce-scatter.45
  1130.1 35.7 reduce-scatter.43
  1169.2 35.7 reduce-scatter.37
  1208.1 35.8 reduce-scatter.41
  1247.5 35.8 reduce-scatter.39
  1285.5 36.3 reduce-scatter.35
  1324.9 35.2 reduce-scatter.31
Sparse Core Ops, SparseCore 1:
  214.4 31.0 all-gather.21
  252.7 37.0 all-gather.17
  291.7 31.5 all-gather.19
  325.3 32.7 all-gather.23
  359.6 29.1 all-gather.25
  543.1 37.0 all-gather.27
  635.6 37.0 all-gather.33
  731.6 37.0 all-gather.31
  770.2 36.8 all-gather.35

commit v2 on v1

--- a/solution.py
+++ b/solution.py
@@ -58,22 +58,138 @@
     return up_raw * scale_up * jax.nn.silu(gate_raw * (scale_gate * math.sqrt(D)))
 
 
-def group_rows(own_block):
-    return lax.all_gather(own_block, "tp", axis=0, tiled=True)
-
-
-def group_grads(own_block):
-    return lax.all_gather(own_block, "tp", axis=0, tiled=True)
-
-
-def own_rows(partial_value):
-    return own_grads(partial_value)
-
-
-def own_grads(partial_value):
-    return lax.psum_scatter(
-        partial_value.astype(jnp.bfloat16), "tp", scatter_dimension=0, tiled=True
-    ).astype(jnp.float32)
+def swap(value, axis, bit):
+    size = lax.axis_size(axis)
+    return lax.ppermute(value, axis, [(place, place ^ bit) for place in range(size)])
+
+
+def add_low(former, latter):
+    return (former.astype(jnp.float32) + latter.astype(jnp.float32)).astype(jnp.bfloat16)
+
+
+def butterfly(value, axes):
+    for axis in axes:
+        bit = 1
+        while bit < lax.axis_size(axis):
+            value = value + swap(value, axis, bit)
+            bit *= 2
+    return value
+
+
+def line_order():
+    size = lax.axis_size("tp")
+    places = jnp.arange(size, dtype=jnp.int32)
+    if size != 4:
+        return places
+    return (places + lax.axis_index("tp")) % size
+
+
+def line_gather(own_block):
+    if lax.axis_size("tp") != 4:
+        return lax.all_gather(own_block, "tp", axis=0, tiled=True)
+    right_one = lax.ppermute(own_block, "tp", [(0, 1), (1, 2), (2, 3)])
+    left_one = lax.ppermute(own_block, "tp", [(3, 2), (2, 1), (1, 0)])
+    right_two = lax.ppermute(right_one, "tp", [(1, 2), (2, 3)])
+    left_two = lax.ppermute(left_one, "tp", [(2, 1), (1, 0)])
+    right_three = lax.ppermute(right_two, "tp", [(2, 3)])
+    left_three = lax.ppermute(left_two, "tp", [(1, 0)])
+    return jnp.concatenate(
+        [own_block, left_one + right_three, left_two + right_two, left_three + right_one], axis=0
+    )
+
+
+def line_scatter(partial_low):
+    if lax.axis_size("tp") != 4:
+        return lax.psum_scatter(partial_low, "tp", scatter_dimension=0, tiled=True).astype(
+            jnp.float32
+        )
+    own, one, two, three = jnp.split(partial_low, 4, axis=0)
+    right = lax.ppermute(three, "tp", [(0, 1)])
+    left = lax.ppermute(one, "tp", [(3, 2)])
+    right = lax.ppermute(add_low(right, two), "tp", [(0, 1), (1, 2)])
+    left = lax.ppermute(add_low(left, two), "tp", [(3, 2), (2, 1)])
+    right = lax.ppermute(add_low(right, one), "tp", [(0, 1), (1, 2), (2, 3)])
+    left = lax.ppermute(add_low(left, three), "tp", [(3, 2), (2, 1), (1, 0)])
+    return own.astype(jnp.float32) + right.astype(jnp.float32) + left.astype(jnp.float32)
+
+
+def tree_order():
+    size = lax.axis_size("ctx")
+    places = jnp.arange(size, dtype=jnp.int32)
+    if size != 4:
+        return places
+    return places ^ lax.axis_index("ctx")
+
+
+def tree_gather(own_block):
+    if lax.axis_size("ctx") != 4:
+        return lax.all_gather(own_block, "ctx", axis=0, tiled=True)
+    across = swap(own_block, "ctx", 2)
+    beside = swap(own_block, "ctx", 1)
+    return jnp.concatenate([own_block, beside, across, swap(across, "ctx", 1)], axis=0)
+
+
+def tree_scatter(partial_low):
+    if lax.axis_size("ctx") != 4:
+        return lax.psum_scatter(partial_low, "ctx", scatter_dimension=0, tiled=True).astype(
+            jnp.float32
+        )
+    own, beside, across, far = jnp.split(partial_low, 4, axis=0)
+    across = add_low(across, swap(far, "ctx", 1))
+    beside = swap(beside, "ctx", 1)
+    across = swap(across, "ctx", 2)
+    return own.astype(jnp.float32) + beside.astype(jnp.float32) + across.astype(jnp.float32)
+
+
+def owner_scatter(product_low):
+    if lax.axis_size("ctx") != 4 or lax.axis_size("shard") != 2:
+        return lax.psum_scatter(
+            product_low, ("shard", "ctx"), scatter_dimension=0, tiled=True
+        ).astype(jnp.float32)
+    place = lax.axis_index("ctx")
+    core, along = place % 2, place // 2
+    plane = lax.axis_index("shard")
+    rows, width = product_low.shape
+    blocks = product_low.reshape(2, 2, 2, rows // 8, width)
+
+    def pick(value, index, axis):
+        return lax.dynamic_index_in_dim(value, index, axis, keepdims=False)
+
+    blocks = add_low(pick(blocks, core, 2), swap(pick(blocks, 1 - core, 2), "ctx", 1))
+    former, latter = blocks[..., : width // 2], blocks[..., width // 2 :]
+    former_in = swap(pick(former, 1 - along, 1), "ctx", 2)
+    latter_in = swap(pick(latter, 1 - plane, 0), "shard", 1)
+    former = add_low(pick(former, along, 1), former_in)
+    latter = add_low(pick(latter, plane, 0), latter_in)
+    former_in = swap(pick(former, 1 - plane, 0), "shard", 1)
+    latter_in = swap(pick(latter, 1 - along, 0), "ctx", 2)
+    return jnp.concatenate(
+        [
+            pick(former, plane, 0).astype(jnp.float32) + former_in.astype(jnp.float32),
+            pick(latter, along, 0).astype(jnp.float32) + latter_in.astype(jnp.float32),
+        ],
+        axis=1,
+    )
+
+
+def row_labels(slots, group_size):
+    tree_rows = group_size * lax.axis_size("ctx")
+    chunk = group_size // lax.axis_size("tp")
+    within = (line_order()[:, None] * chunk + jnp.arange(chunk, dtype=jnp.int32)).reshape(-1)
+    keys = (tree_order()[:, None] * group_size + within[None, :]).reshape(-1)
+    onehot = (keys[:, None] // SEG == jnp.arange(tree_rows // SEG, dtype=jnp.int32)[None, :])
+    segment = jnp.sum(jnp.where(onehot, slots[None, :], 0), axis=1)
+    offset = keys % SEG
+    if lax.axis_size("ctx") != 4:
+        first = lax.axis_index("ctx") * group_size
+    else:
+        first = 0
+    return (
+        lax.dynamic_slice_in_dim(segment, first, group_size),
+        lax.dynamic_slice_in_dim(offset, first, group_size),
+        segment,
+        offset,
+    )
 
 
 def visibility(parents, slots, group_size):
@@ -82,11 +198,7 @@
     reachable = jnp.maximum(linked, jnp.eye(SEGS, dtype=jnp.float32))
     for doubling in range(SEGS.bit_length()):
         reachable = jnp.minimum(jnp.dot(reachable, reachable, precision=HIGHEST), 1.0)
-    segment = jnp.broadcast_to(slots[:, None], (SEGS, SEG)).reshape(TREE_TOK)
-    offset = lax.broadcasted_iota(jnp.int32, (SEGS, SEG), 1).reshape(TREE_TOK)
-    first_row = lax.axis_index("ctx") * group_size
-    seg_query = lax.dynamic_slice_in_dim(segment, first_row, group_size)
-    off_query = lax.dynamic_slice_in_dim(offset, first_row, group_size)
+    seg_query, off_query, segment, offset = row_labels(slots, group_size)
     key_onehot = (segment[:, None] == labels[None, :]).astype(jnp.float32)
     query_onehot = (seg_query[:, None] == labels[None, :]).astype(jnp.float32)
     linked_rows = jnp.dot(query_onehot, reachable, precision=HIGHEST)
@@ -102,7 +214,7 @@
     w_query, w_key, w_value, w_attn_out = gathered[:4]
     alpha_attn, alpha_mlp, scale_qk, scale_up, scale_gate = vectors
     score_scale = math.sqrt(HDIM)
-    hidden_group = group_rows(tokens_own)
+    hidden_group = line_gather(tokens_own)
     visible = visibility(parents, slots, hidden_group.shape[0])
     query_raw = jnp.dot(hidden_group, w_query, preferred_element_type=jnp.float32)
     key_raw = jnp.dot(hidden_group, w_key, preferred_element_type=jnp.float32)
@@ -112,9 +224,7 @@
     query_unit, key_unit = query_key(query_raw, key_raw, scale_qk)
     queries = query_unit.astype(jnp.bfloat16)
     keys_own = key_unit.astype(jnp.bfloat16)
-    keys_values = lax.all_gather(
-        jnp.concatenate([keys_own, value_low], axis=1), "ctx", axis=0, tiled=True
-    )
+    keys_values = tree_gather(jnp.concatenate([keys_own, value_low], axis=1))
     keys_tree, values_tree = jnp.split(keys_values, 2, axis=1)
     query_heads = split_heads(queries)
     key_heads = split_heads(keys_tree)
@@ -134,7 +244,7 @@
 
     head_values, log_totals = lax.map(head_forward, (query_heads, key_heads, value_heads))
     heads_low = merge_heads(head_values).astype(jnp.bfloat16)
-    branch_one = own_rows(jnp.dot(heads_low, w_attn_out, preferred_element_type=jnp.float32))
+    branch_one = line_scatter(contract_cols(heads_low, w_attn_out).astype(jnp.bfloat16))
     kept = (
         hidden_group,
         visible,
@@ -154,22 +264,26 @@
     alpha_attn, alpha_mlp, scale_qk, scale_up, scale_gate = vectors
     tokens_wide = tokens_own.astype(jnp.float32)
     hidden_one = mix_rows(tokens_wide, branch_one, alpha_attn)
-    hidden_one_group = group_rows(hidden_one.astype(jnp.bfloat16))
+    hidden_one_group = line_gather(hidden_one.astype(jnp.bfloat16))
     up_raw = jnp.dot(hidden_one_group, w_up, preferred_element_type=jnp.float32)
     gate_raw = jnp.dot(hidden_one_group, w_gate, preferred_element_type=jnp.float32)
     mixed_low = middle(up_raw, gate_raw, scale_up, scale_gate).astype(jnp.bfloat16)
-    branch_two = own_rows(jnp.dot(mixed_low, w_down, preferred_element_type=jnp.float32))
+    branch_two = line_scatter(contract_cols(mixed_low, w_down).astype(jnp.bfloat16))
     output_wide, pull_out = jax.vjp(mix_rows, hidden_one, branch_two, alpha_mlp)
     upstream = cotangent_own.astype(jnp.float32)
     hidden_one_direct, branch_two_grad, grad_alpha_mlp = pull_out(upstream)
-    branch_two_group = group_grads(branch_two_grad.astype(jnp.bfloat16))
-    mixed_grad = contract_cols(branch_two_group, w_down).astype(jnp.bfloat16).astype(jnp.float32)
+    branch_two_group = line_gather(branch_two_grad.astype(jnp.bfloat16))
+    mixed_grad = (
+        jnp.dot(branch_two_group, w_down, preferred_element_type=jnp.float32)
+        .astype(jnp.bfloat16)
+        .astype(jnp.float32)
+    )
     middle_value, pull_mid = jax.vjp(middle, up_raw, gate_raw, scale_up, scale_gate)
     up_grad, gate_grad, grad_scale_up, grad_scale_gate = pull_mid(mixed_grad)
     up_low = up_grad.astype(jnp.bfloat16)
     gate_low = gate_grad.astype(jnp.bfloat16)
-    hidden_one_grad = hidden_one_direct + own_grads(
-        contract_cols(up_low, w_up) + contract_cols(gate_low, w_gate)
+    hidden_one_grad = hidden_one_direct + line_scatter(
+        (contract_cols(up_low, w_up) + contract_cols(gate_low, w_gate)).astype(jnp.bfloat16)
     )
     hidden_again, pull_in = jax.vjp(mix_rows, tokens_wide, branch_one, alpha_attn)
     tokens_direct, branch_one_grad, grad_alpha_attn = pull_in(hidden_one_grad)
@@ -193,8 +307,12 @@
         log_totals,
         heads_low,
     ) = kept
-    branch_one_group = group_grads(branch_one_grad.astype(jnp.bfloat16))
-    heads_grad = split_heads(contract_cols(branch_one_group, w_attn_out).astype(jnp.bfloat16))
+    branch_one_group = line_gather(branch_one_grad.astype(jnp.bfloat16))
+    heads_grad = split_heads(
+        jnp.dot(branch_one_group, w_attn_out, preferred_element_type=jnp.float32).astype(
+            jnp.bfloat16
+        )
+    )
 
     def head_backward(record):
         query_one, key_one, value_one, upstream_one, log_total = record
@@ -211,14 +329,11 @@
     query_grads, key_grads, value_grads = lax.map(
         head_backward, (query_heads, key_heads, value_heads, heads_grad, log_totals)
     )
-    both = lax.psum_scatter(
+    both = tree_scatter(
         jnp.concatenate([merge_heads(key_grads), merge_heads(value_grads)], axis=1).astype(
             jnp.bfloat16
-        ),
-        "ctx",
-        scatter_dimension=0,
-        tiled=True,
-    ).astype(jnp.float32)
+        )
+    )
     key_own_grad, value_own_grad = jnp.split(both, 2, axis=1)
     unit_again, pull_qk = jax.vjp(query_key, query_raw, key_raw, scale_qk)
     query_raw_grad, key_raw_grad, grad_scale_qk = pull_qk((merge_heads(query_grads), key_own_grad))
@@ -230,7 +345,7 @@
         + contract_cols(key_low, w_key)
         + contract_cols(value_grad_low, w_value)
     )
-    grad_tokens = tokens_direct + own_grads(input_part)
+    grad_tokens = tokens_direct + line_scatter(input_part.astype(jnp.bfloat16))
     factors = (hidden_group, query_low, key_low, value_grad_low, heads_low, branch_one_group)
     return grad_tokens, factors, grad_scale_qk
 
@@ -257,14 +372,19 @@
     local_hidden = w_up.shape[1]
     vectors = (alpha_attn, alpha_mlp, scale_qk, scale_up, scale_gate)
     spread = ("shard", "ctx")
+
+    def spread_gather(own_block):
+        return lax.all_gather(own_block, spread, axis=0, tiled=True)
+
+    packed = spread_gather(jnp.concatenate([w_query, w_key, w_value, w_attn_out.T], axis=1))
     gathered = (
-        lax.all_gather(w_query, spread, axis=0, tiled=True),
-        lax.all_gather(w_key, spread, axis=0, tiled=True),
-        lax.all_gather(w_value, spread, axis=0, tiled=True),
-        lax.all_gather(w_attn_out, spread, axis=1, tiled=True),
-        lax.all_gather(w_up, spread, axis=0, tiled=True),
-        lax.all_gather(w_gate, spread, axis=0, tiled=True),
-        lax.all_gather(w_down, spread, axis=1, tiled=True),
+        packed[:, :local_heads],
+        packed[:, local_heads : 2 * local_heads],
+        packed[:, 2 * local_heads : 3 * local_heads],
+        packed[:, 3 * local_heads :],
+        spread_gather(w_up),
+        spread_gather(w_gate),
+        spread_gather(w_down.T),
     )
     micros = range(tokens.shape[0])
     front = [
@@ -288,54 +408,46 @@
         stack(lambda m: back[m][1][place]) for place in range(6)
     )
 
-    def to_owner(former, latter, axis):
-        product = contract_rows(former, latter).astype(jnp.bfloat16)
-        return lax.psum_scatter(product, spread, scatter_dimension=axis, tiled=True).astype(
-            jnp.float32
-        )
-
-    grad_d = to_owner(mixed_all, top_all, 1)
-    grad_u = to_owner(hidden_all, up_all, 0)
-    grad_g = to_owner(hidden_all, gate_all, 0)
-    grad_o = to_owner(heads_all, branch_all, 1)
-    grad_q = to_owner(tokens_all, query_all, 0)
-    grad_k = to_owner(tokens_all, key_all, 0)
-    grad_v = to_owner(tokens_all, value_all, 0)
+    def to_owner(former, latter):
+        return owner_scatter(contract_rows(former, latter).astype(jnp.bfloat16))
+
+    grad_d = to_owner(top_all, mixed_all).T
+    grad_u = to_owner(hidden_all, up_all)
+    grad_g = to_owner(hidden_all, gate_all)
+    attention_product = jnp.concatenate(
+        [
+            contract_rows(tokens_all, query_all),
+            contract_rows(tokens_all, key_all),
+            contract_rows(tokens_all, value_all),
+            contract_rows(branch_all, heads_all),
+        ],
+        axis=1,
+    )
+    grad_attention = owner_scatter(attention_product.astype(jnp.bfloat16))
+    grad_q, grad_k, grad_v, grad_o = jnp.split(grad_attention, 4, axis=1)
 
     sum_attn, sum_mlp, sum_up, sum_gate = (
         sum(mid[m][4][place] for m in micros) for place in range(4)
     )
-    sum_qk = sum(back[m][2] for m in micros)
-    tp_count = lax.axis_size("tp")
-    tp_place = lax.axis_index("tp")
-
-    def padded(vector):
-        return lax.dynamic_update_slice_in_dim(
-            jnp.zeros((vector.shape[0] * tp_count,), jnp.float32),
-            vector,
-            tp_place * vector.shape[0],
-            0,
-        )
-
-    alpha_attn_sum, alpha_mlp_sum, qk_sum, up_sum, gate_sum = lax.psum(
-        (sum_attn, sum_mlp, padded(sum_qk), padded(sum_up), padded(sum_gate)),
-        ("shard", "ctx", "tp"),
-    )
+    sum_qk = butterfly(sum(back[m][2] for m in micros), spread)
+    width = sum_attn.shape[0]
+    sums = butterfly(jnp.concatenate([sum_attn, sum_mlp, sum_up, sum_gate]), spread)
+    alphas = butterfly(sums[: 2 * width], ("tp",))
     return (
         jnp.stack([mid[m][0] for m in micros])[:, None],
         jnp.stack([back[m][0] for m in micros])[:, None],
         grad_q,
         grad_k,
         grad_v,
-        grad_o,
+        grad_o.T,
         grad_u,
         grad_g,
         grad_d,
-        alpha_attn_sum,
-        alpha_mlp_sum,
-        lax.dynamic_slice_in_dim(qk_sum, tp_place * local_heads, local_heads),
-        lax.dynamic_slice_in_dim(up_sum, tp_place * local_hidden, local_hidden),
-        lax.dynamic_slice_in_dim(gate_sum, tp_place * local_hidden, local_hidden),
+        alphas[:width],
+        alphas[width:],
+        sum_qk,
+        sums[2 * width : 2 * width + local_hidden],
+        sums[2 * width + local_hidden :],
     )
 
 

time: 1380 us -> 1130 us (0.82)
  waiting for transfers between devices: 707 us -> 331 us
  starting transfers between devices: 3.84 us -> 215 us
  blocking collectives: 92.6 us -> 0 us
  other arithmetic: 84.3 us -> 110 us
    reduce_scatter x15 -> x0, waiting for transfers between devices: 443 us -> none  [the longest x8 234 us: own_grads(): lax.psum_scatter(partial_value.astype(jnp.bfloat16), 'tp', scatter_dimens...]
    ppermute x0 -> x136, waiting for transfers between devices: none -> 330 us  [the longest x40 87.8 us: swap(): lax.ppermute(value, axis, [(place, place ^ bit) for place in range(size)])]
    all_gather x13 -> x4, waiting for transfers between devices: 261 us -> 0.01 us  [spread_gather(): return lax.all_gather(own_block, spread, axis=0, tiled=True)]
    ppermute x0 -> x136, starting transfers between devices: none -> 215 us  [the longest x8 43.9 us: line_scatter(): right = lax.ppermute(add_low(right, one), 'tp', [(0, 1), (1, 2), (2, 3)])]
    all_gather x4 -> x0, blocking collectives: 51.7 us -> none  [the longest x1 15.2 us: per_device(): lax.all_gather(w_attn_out, spread, axis=1, tiled=True)]
    psum x1 -> x0, blocking collectives: 40.9 us -> none  [per_device(): lax.psum((sum_attn, sum_mlp, padded(sum_qk), padded(sum_up), padded(sum_g...]
    unnamed x3 -> x29, other arithmetic: 2.27 us -> 31.4 us
    unnamed x248 -> x317, local copies, waits for them, and re-layouts: 39.8 us -> 13.9 us
  transfers between devices with their start and end apart: 30 -> 140, of which waited for: 23 -> 68; matrix products, arithmetic and copies ran while one was open for 27% -> 44% of each run, Pallas kernels for 0% -> 0%
where the time goes in v2:
time: 1130 us; the launch traced here: 1120 us
  matrix products  344 us (30%)
  waiting for transfers between devices  331 us (29%)
  starting transfers between devices  215 us (19%)
  other arithmetic  110 us (10%)
  local copies, waits for them, and re-layouts  97.6 us (9%)
  between operations  17.9 us (2%)
    dot_general x44, matrix products, contract_cols(): lax.dot_general(former, latter, (((1,), (1,)), ((), ())), preferred_eleme...  122 us
    ppermute x40, waiting for transfers between devices, swap(): lax.ppermute(value, axis, [(place, place ^ bit) for place in range(size)])  87.8 us
    dot_general x27, matrix products, contract_rows(): lax.dot_general(former, latter, (((0,), (0,)), ((), ())), preferred_eleme...  75.2 us
    ppermute x8, waiting for transfers between devices, line_gather(): left_two = lax.ppermute(left_one, 'tp', [(2, 1), (1, 0)])  52.3 us
    dot_general x10, matrix products, head_forward(): jnp.dot(soft_weights.astype(jnp.bfloat16), value_one, preferred_element_t...  49.6 us
    ppermute x8, waiting for transfers between devices, line_gather(): left_three = lax.ppermute(left_two, 'tp', [(1, 0)])  48.1 us
    ppermute x8, starting transfers between devices, line_scatter(): right = lax.ppermute(add_low(right, one), 'tp', [(0, 1), (1, 2), (2, 3)])  43.9 us
    ppermute x40, starting transfers between devices, swap(): lax.ppermute(value, axis, [(place, place ^ bit) for place in range(size)])  32.1 us
  transfers between devices with their start and end apart: 140, of which 68 were waited for; matrix products, arithmetic and copies ran while one was open for 44% of the time, Pallas kernels for 0%

profile of v2, /device:TPU:0, one launch (start us, length us, event | category | flops | bytes accessed | tf_op | source)
XLA Modules:
  0.0 1115.4 jit_solution(14823232031512173370)
XLA Ops:
  11.3 5.0 collective-permute-start.1
  40.8 10.9 collective-permute-done.4
  53.6 6.8 collective-permute-done.31
  103.0 25.9 %collective-permute-done.7 = bf16[640,640]{0,1:T(8,128)(2,1)} collective-permute-done((bf16[640,640]{0,1:T(8,128)(2,1)}, bf16[640,640]{0,1:T(8,128)(2,1)}, u32[]{:S(2)}, u32[]{:S(2)}) %collective-permute-start.7) | collective-permute-done | bytes 819232 | tf_op jit(solution)/shard_map/ppermute | solution.py:63
  129.3 5.0 fusion.77
  157.0 51.8 %while.52 = (s32[]{:T(128)}, bf16[5,640,64]{1,2,0:T(8,128)(2,1)}, f32[5,640]{1,0:T(8,128)S(1)}, bf16[5,640,64]{2,1,0:T(8,128)(2,1)}, bf16[5,2560,64]{2,1,0:T(8,1...) while((s32[]{:T(128)}, bf16[5,640,64]{1,2,0:T(8,128)(2,1)}, ...), condition=%wide.region_6.7_spmd, body=%wide.region_3.6_spmd.sunk | while | flops 432536960 | bytes 49184892 | solution.py:245
  172.7 4.9 fusion.375
  193.4 5.0 fusion.375
  203.8 4.9 fusion.375
  231.3 51.9 %while.53 = (s32[]{:T(128)}, bf16[5,640,64]{1,2,0:T(8,128)(2,1)}, f32[5,640]{1,0:T(8,128)S(1)}, bf16[5,640,64]{2,1,0:T(8,128)(2,1)}, bf16[5,2560,64]{2,1,0:T(8,1...) while((s32[]{:T(128)}, bf16[5,640,64]{1,2,0:T(8,128)(2,1)}, ...), condition=%wide.region_17.18_spmd, body=%wide.region_14.17_spmd.sunk | while | flops 432536960 | bytes 49184892 | solution.py:245
  236.7 5.0 fusion.379
  247.1 5.0 fusion.379
  257.5 5.0 fusion.379
  267.9 5.0 fusion.379
  278.2 5.0 fusion.379
  292.0 5.7 collective-permute-done.36
  315.5 5.1 collective-permute-start.38
  325.5 7.0 collective-permute-done.38
  341.1 6.5 collective-permute-done.16
  356.2 10.4 collective-permute-done.19
  372.3 5.8 collective-permute-done.20
  395.6 6.3 fusion.221
  409.3 6.4 collective-permute-done.47
  427.9 6.0 multiply_convert_fusion.7
  468.0 5.1 collective-permute-start.23
  476.8 5.1 collective-permute-start.50
  488.4 5.7 collective-permute-done.53
  507.2 7.8 collective-permute-done.54
  516.9 11.4 %collective-permute-done.58 = bf16[160,1280]{1,0:T(8,128)(2,1)S(1)} collective-permute-done((bf16[160,1280]{1,0:T(8,128)(2,1)S(1)}, bf16[160,1280]{1,0:T(8,128)(2,1)S(1)}, u32[]{:S(2)}, u32[]{:S(2)}) %collective-permute-start.58) | collective-permute-done | bytes 409632 | tf_op jit(solution)/shard_map/ppermute | solution.py:93
  531.4 6.8 collective-permute-done.59
  558.1 6.0 convolution_convert_fusion.4
  570.8 6.3 collective-permute-done.86
  578.2 11.5 %multiply_reduce_fusion.4 = (f32[1280]{0:T(1024)S(1)}, f32[1280]{0:T(1024)S(1)}, f32[1280]{0:T(1024)S(1)}, f32[1280]{0:T(1024)S(1)}, f32[640,1280]{1,0:T(8,128)S...) fusion(f32[640,1280]{1,0:T(8,128)} %copy-done.160, ...), kind=kOutput, calls=%fused_computation.154 | convolution fusion | flops 2138926080 | bytes 29521920 | tf_op jit(solution)/shard_map/dot_general | solution.py:277
  634.2 8.2 collective-permute-start.62
  644.0 7.1 collective-permute-start.89
  654.1 6.0 collective-permute-done.89
  680.0 5.6 collective-permute-done.131
  697.9 7.3 collective-permute-done.124
  737.2 7.0 collective-permute-done.71
  755.7 71.3 %while.54 = (s32[]{:T(128)}, f32[5,640,64]{1,2,0:T(8,128)S(1)}, bf16[5,2560,64]{1,2,0:T(8,128)(2,1)}, bf16[5,2560,64]{1,2,0:T(8,128)(2,1)}, bf16[5,640,64]{2,1,0...) while((s32[]{:T(128)}, f32[5,640,64]{1,2,0:T(8,128)S(1)}, ...), condition=%wide.region_28.29_spmd, body=%wide.region_26.28_spmd.sunk | while | flops 1063525760 | bytes 61458068 | solution.py:329
  835.9 8.7 collective-permute-done.93
  850.2 7.8 collective-permute-done.97
  861.1 9.4 collective-permute-done.98
  878.9 74.5 %while.55 = (s32[]{:T(128)}, f32[5,640,64]{1,2,0:T(8,128)}, bf16[5,2560,64]{1,2,0:T(8,128)(2,1)}, bf16[5,2560,64]{1,2,0:T(8,128)(2,1)}, bf16[5,640,64]{2,1,0:T(8...) while((s32[]{:T(128)}, f32[5,640,64]{1,2,0:T(8,128)}, ...), condition=%wide.region_37.38_spmd, body=%wide.region_35.37_spmd.sunk | while | flops 1063525760 | bytes 61458068 | solution.py:329
  982.6 14.0 %collective-permute-done.101 = bf16[640,640]{0,1:T(8,128)(2,1)} collective-permute-done((bf16[640,640]{0,1:T(8,128)(2,1)}, bf16[640,640]{0,1:T(8,128)(2,1)}, u32[]{:S(2)}, u32[]{:S(2)}) %collective-permute-start.101) | collective-permute-done | bytes 819232 | tf_op jit(solution)/shard_map/ppermute | solution.py:63
  1012.4 5.7 concatenate.134
  1048.2 6.3 collective-permute-done.103
  1059.9 5.3 collective-permute-done.76
  (999 shorter events, 780.5 us)
Async XLA Ops:
  7.2 69.7 %all-gather.5.cloned.1.call-start = ((), (), s32[]{:S(2)}) async-start(), calls=%async_computation | async-start | bytes 3686400 | tf_op jit(solution)/shard_map/all_gather | solution.py:377
  9.3 386.3 %all-gather.9.cloned.1.call-start = ((), (), s32[]{:S(2)}) async-start(), calls=%async_computation.2 | async-start | bytes 3686400 | tf_op jit(solution)/shard_map/all_gather | solution.py:377
  10.1 411.2 %all-gather.7.cloned.1.call-start = ((), (), s32[]{:S(2)}) async-start(), calls=%async_computation.1 | async-start | bytes 3686400 | tf_op jit(solution)/shard_map/all_gather | solution.py:377
  11.3 21.1 %collective-permute-start.1 = (bf16[160,1280]{1,0:T(8,128)(2,1)S(1)}, bf16[160,1280]{1,0:T(8,128)(2,1)S(1)}, u32[]{:S(2)}, u32[]{:S(2)}) collective-permute-start(bf16[160,1280]{1,0:T(8,128)(2,1)S(1)} %get-tuple-element.509), channel_id=1, source_target_pairs={{0,1},{1,2},{2,3},{4,5},{5,6},{6,7},{8,9},{9,10},{10,11},{12,13},{... | collective-permute-start | bytes 1228808 | tf_op jit(solution)/shard_map/ppermute | solution.py:90
  17.6 17.2 %collective-permute-start.28 = (bf16[160,1280]{1,0:T(8,128)(2,1)S(1)}, bf16[160,1280]{1,0:T(8,128)(2,1)S(1)}, u32[]{:S(2)}, u32[]{:S(2)}) collective-permute-start(bf16[160,1280]{1,0:T(8,128)(2,1)S(1)} %get-tuple-element.508), channel_id=1, source_target_pairs={{0,1},{1,2},{2,3},{4,5},{5,6},{6,7},{8,9},{9,10},{10,11},{12,13},{... | collective-permute-start | bytes 1228808 | tf_op jit(solution)/shard_map/ppermute | solution.py:90
  23.5 410.4 %all-gather.11.cloned.1.call-start = ((), (), s32[]{:S(2)}) async-start(), calls=%async_computation.3 | async-start | bytes 3686400 | tf_op jit(solution)/shard_map/all_gather | solution.py:377
  33.4 18.2 %collective-permute-start.4 = (bf16[160,1280]{1,0:T(8,128)(2,1)}, bf16[160,1280]{1,0:T(8,128)(2,1)S(1)}, u32[]{:S(2)}, u32[]{:S(2)}) collective-permute-start(bf16[160,1280]{1,0:T(8,128)(2,1)} %collective-permute-done), channel_id=1, source_target_pairs={{2,1},{1,0},{6,5},{5,4},{10,9},{9,8},{14,13},{13,12},{18,17},{17,1... | collective-permute-start | bytes 1228808 | tf_op jit(solution)/shard_map/ppermute | solution.py:93
  34.7 18.2 %collective-permute-start.29 = (bf16[160,1280]{1,0:T(8,128)(2,1)S(1)}, bf16[160,1280]{1,0:T(8,128)(2,1)S(1)}, u32[]{:S(2)}, u32[]{:S(2)}) collective-permute-start(bf16[160,1280]{1,0:T(8,128)(2,1)S(1)} %collective-permute-done.28), channel_id=1, source_target_pairs={{1,2},{2,3},{5,6},{6,7},{9,10},{10,11},{13,14},{14,15},{17,18},{18... | collective-permute-start | bytes 1228808 | tf_op jit(solution)/shard_map/ppermute | solution.py:92
  38.0 22.4 %collective-permute-start.31 = (bf16[160,1280]{1,0:T(8,128)(2,1)}, bf16[160,1280]{1,0:T(8,128)(2,1)S(1)}, u32[]{:S(2)}, u32[]{:S(2)}) collective-permute-start(bf16[160,1280]{1,0:T(8,128)(2,1)} %collective-permute-done.27), channel_id=1, source_target_pairs={{2,1},{1,0},{6,5},{5,4},{10,9},{9,8},{14,13},{13,12},{18,17},{17,1... | collective-permute-start | bytes 1228808 | tf_op jit(solution)/shard_map/ppermute | solution.py:93
  39.3 22.6 %collective-permute-start.3 = (bf16[160,1280]{1,0:T(8,128)(2,1)S(1)}, bf16[160,1280]{1,0:T(8,128)(2,1)S(1)}, u32[]{:S(2)}, u32[]{:S(2)}) collective-permute-start(bf16[160,1280]{1,0:T(8,128)(2,1)S(1)} %collective-permute-done.2), channel_id=1, source_target_pairs={{2,3},{6,7},{10,11},{14,15},{18,19},{22,23},{26,27},{30,31}} | collective-permute-start | bytes 1228808 | tf_op jit(solution)/shard_map/ppermute | solution.py:94
  51.6 17.6 %collective-permute-start.5 = (bf16[160,1280]{1,0:T(8,128)(2,1)S(1)}, bf16[160,1280]{1,0:T(8,128)(2,1)S(1)}, u32[]{:S(2)}, u32[]{:S(2)}) collective-permute-start(bf16[160,1280]{1,0:T(8,128)(2,1)S(1)} %collective-permute-done.4), channel_id=1, source_target_pairs={{1,0},{5,4},{9,8},{13,12},{17,16},{21,20},{25,24},{29,28}} | collective-permute-start | bytes 1228808 | tf_op jit(solution)/shard_map/ppermute | solution.py:95
  52.9 18.1 %collective-permute-start.30 = (bf16[160,1280]{1,0:T(8,128)(2,1)S(1)}, bf16[160,1280]{1,0:T(8,128)(2,1)S(1)}, u32[]{:S(2)}, u32[]{:S(2)}) collective-permute-start(bf16[160,1280]{1,0:T(8,128)(2,1)S(1)} %collective-permute-done.29), channel_id=1, source_target_pairs={{2,3},{6,7},{10,11},{14,15},{18,19},{22,23},{26,27},{30,31}} | collective-permute-start | bytes 1228808 | tf_op jit(solution)/shard_map/ppermute | solution.py:94
  98.6 30.3 %collective-permute-start.7 = (bf16[640,640]{0,1:T(8,128)(2,1)}, bf16[640,640]{0,1:T(8,128)(2,1)}, u32[]{:S(2)}, u32[]{:S(2)}) collective-permute-start(bf16[640,640]{0,1:T(8,128)(2,1)} %pad_maximum_fusion.8), channel_id=1, source_target_pairs={{0,8},{4,12},{8,0},{12,4},{1,9},{5,13},{9,1},{13,5},{2,10},{6,14},... | collective-permute-start | bytes 2457608 | tf_op jit(solution)/shard_map/ppermute | solution.py:63
  100.4 43.3 %collective-permute-start.6 = (bf16[640,640]{0,1:T(8,128)(2,1)}, bf16[640,640]{0,1:T(8,128)(2,1)}, u32[]{:S(2)}, u32[]{:S(2)}) collective-permute-start(bf16[640,640]{0,1:T(8,128)(2,1)} %pad_maximum_fusion.8), channel_id=1, source_target_pairs={{0,4},{4,0},{8,12},{12,8},{1,5},{5,1},{9,13},{13,9},{2,6},{6,2},{1... | collective-permute-start | bytes 2457608 | tf_op jit(solution)/shard_map/ppermute | solution.py:63
  102.4 41.2 %collective-permute-start.34 = (bf16[640,640]{0,1:T(8,128)(2,1)}, bf16[640,640]{0,1:T(8,128)(2,1)}, u32[]{:S(2)}, u32[]{:S(2)}) collective-permute-start(bf16[640,640]{0,1:T(8,128)(2,1)} %pad_maximum_fusion.9), channel_id=1, source_target_pairs={{0,8},{4,12},{8,0},{12,4},{1,9},{5,13},{9,1},{13,5},{2,10},{6,14},... | collective-permute-start | bytes 2457608 | tf_op jit(solution)/shard_map/ppermute | solution.py:63
  134.3 82.7 %collective-permute-start.33 = (bf16[640,640]{0,1:T(8,128)(2,1)}, bf16[640,640]{0,1:T(8,128)(2,1)}, u32[]{:S(2)}, u32[]{:S(2)}) collective-permute-start(bf16[640,640]{0,1:T(8,128)(2,1)} %pad_maximum_fusion.9), channel_id=1, source_target_pairs={{0,4},{4,0},{8,12},{12,8},{1,5},{5,1},{9,13},{13,9},{2,6},{6,2},{1... | collective-permute-start | bytes 2457608 | tf_op jit(solution)/shard_map/ppermute | solution.py:63
  143.6 73.4 %collective-permute-start.35 = (bf16[640,640]{0,1:T(8,128)(2,1)}, bf16[640,640]{0,1:T(8,128)(2,1)}, u32[]{:S(2)}, u32[]{:S(2)}) collective-permute-start(bf16[640,640]{0,1:T(8,128)(2,1)} %collective-permute-done.34), channel_id=1, source_target_pairs={{0,4},{4,0},{8,12},{12,8},{1,5},{5,1},{9,13},{13,9},{2,6},{6,2},{1... | collective-permute-start | bytes 2457608 | tf_op jit(solution)/shard_map/ppermute | solution.py:63
  213.1 75.5 %collective-permute-start.12 = (bf16[160,1280]{1,0:T(8,128)(2,1)}, bf16[160,1280]{1,0:T(8,128)(2,1)}, u32[]{:S(2)}, u32[]{:S(2)}) collective-permute-start(bf16[160,1280]{1,0:T(8,128)(2,1)} %get-tuple-element.501), channel_id=1, source_target_pairs={{3,2},{7,6},{11,10},{15,14},{19,18},{23,22},{27,26},{31,30}} | collective-permute-start | bytes 1228808 | tf_op jit(solution)/shard_map/ppermute | solution.py:108
  214.5 74.1 %collective-permute-start.9 = (bf16[160,1280]{1,0:T(8,128)(2,1)}, bf16[160,1280]{1,0:T(8,128)(2,1)}, u32[]{:S(2)}, u32[]{:S(2)}) collective-permute-start(bf16[160,1280]{1,0:T(8,128)(2,1)} %get-tuple-element.500), channel_id=1, source_target_pairs={{0,1},{4,5},{8,9},{12,13},{16,17},{20,21},{24,25},{28,29}} | collective-permute-start | bytes 1228808 | tf_op jit(solution)/shard_map/ppermute | solution.py:107
  297.9 17.4 %collective-permute-start.37 = (bf16[160,1280]{1,0:T(8,128)(2,1)S(1)}, bf16[160,1280]{1,0:T(8,128)(2,1)S(1)}, u32[]{:S(2)}, u32[]{:S(2)}) collective-permute-start(bf16[160,1280]{1,0:T(8,128)(2,1)S(1)} %get-tuple-element.492), channel_id=1, source_target_pairs={{0,1},{1,2},{4,5},{5,6},{8,9},{9,10},{12,13},{13,14},{16,17},{17,1... | collective-permute-start | bytes 1228808 | tf_op jit(solution)/shard_map/ppermute | solution.py:109
  306.7 17.3 %collective-permute-start.11 = (bf16[160,1280]{1,0:T(8,128)(2,1)S(1)}, bf16[160,1280]{1,0:T(8,128)(2,1)S(1)}, u32[]{:S(2)}, u32[]{:S(2)}) collective-permute-start(bf16[160,1280]{1,0:T(8,128)(2,1)S(1)} %get-tuple-element.496), channel_id=1, source_target_pairs={{0,1},{1,2},{2,3},{4,5},{5,6},{6,7},{8,9},{9,10},{10,11},{12,13},{... | collective-permute-start | bytes 1228808 | tf_op jit(solution)/shard_map/ppermute | solution.py:111
  450.5 17.4 %collective-permute-start.22 = (bf16[160,1280]{1,0:T(8,128)(2,1)S(1)}, bf16[160,1280]{1,0:T(8,128)(2,1)S(1)}, u32[]{:S(2)}, u32[]{:S(2)}) collective-permute-start(bf16[160,1280]{1,0:T(8,128)(2,1)S(1)} %get-tuple-element.480), channel_id=1, source_target_pairs={{0,1},{1,2},{4,5},{5,6},{8,9},{9,10},{12,13},{13,14},{16,17},{17,1... | collective-permute-start | bytes 1228808 | tf_op jit(solution)/shard_map/ppermute | solution.py:109
  459.2 17.4 %collective-permute-start.49 = (bf16[160,1280]{1,0:T(8,128)(2,1)S(1)}, bf16[160,1280]{1,0:T(8,128)(2,1)S(1)}, u32[]{:S(2)}, u32[]{:S(2)}) collective-permute-start(bf16[160,1280]{1,0:T(8,128)(2,1)S(1)} %get-tuple-element.486), channel_id=1, source_target_pairs={{0,1},{1,2},{4,5},{5,6},{8,9},{9,10},{12,13},{13,14},{16,17},{17,1... | collective-permute-start | bytes 1228808 | tf_op jit(solution)/shard_map/ppermute | solution.py:109
  596.9 25.8 %collective-permute-start.60 = (bf16[160,1280]{1,0:T(8,128)(2,1)S(1)}, bf16[160,1280]{1,0:T(8,128)(2,1)S(1)}, u32[]{:S(2)}, u32[]{:S(2)}) collective-permute-start(bf16[160,1280]{1,0:T(8,128)(2,1)S(1)} %get-tuple-element.476), channel_id=1, source_target_pairs={{0,1},{4,5},{8,9},{12,13},{16,17},{20,21},{24,25},{28,29}} | collective-permute-start | bytes 1228808 | tf_op jit(solution)/shard_map/ppermute | solution.py:107
  598.4 24.3 %collective-permute-start.63 = (bf16[160,1280]{1,0:T(8,128)(2,1)S(1)}, bf16[160,1280]{1,0:T(8,128)(2,1)S(1)}, u32[]{:S(2)}, u32[]{:S(2)}) collective-permute-start(bf16[160,1280]{1,0:T(8,128)(2,1)S(1)} %get-tuple-element.477), channel_id=1, source_target_pairs={{3,2},{7,6},{11,10},{15,14},{19,18},{23,22},{27,26},{31,30}} | collective-permute-start | bytes 1228808 | tf_op jit(solution)/shard_map/ppermute | solution.py:108
  622.4 69.7 %collective-permute-start.123 = (bf16[2,2,160,1280]{3,2,1,0:T(8,128)(2,1)S(1)}, bf16[2,2,160,1280]{3,2,1,0:T(8,128)(2,1)S(1)}, u32[]{:S(2)}, u32[]{:S(2)}) collective-permute-start(bf16[2,2,160,1280]{3,2,1,0:T(8,128)(2,1)S(1)} %dynamic-slice_bitcast_fusion), channel_id=1, source_target_pairs={{0,4},{4,0},{8,12},{12,8},{1,5},{5,1},{9,13},{13,9},{2,6},{6,2},{1... | collective-permute-start | bytes 4915208 | tf_op jit(solution)/shard_map/ppermute | solution.py:63
  625.1 18.7 %collective-permute-start.88 = (bf16[160,1280]{1,0:T(8,128)(2,1)S(1)}, bf16[160,1280]{1,0:T(8,128)(2,1)S(1)}, u32[]{:S(2)}, u32[]{:S(2)}) collective-permute-start(bf16[160,1280]{1,0:T(8,128)(2,1)S(1)} %get-tuple-element.468), channel_id=1, source_target_pairs={{0,1},{1,2},{4,5},{5,6},{8,9},{9,10},{12,13},{13,14},{16,17},{17,1... | collective-permute-start | bytes 1228808 | tf_op jit(solution)/shard_map/ppermute | solution.py:109
  634.2 18.6 %collective-permute-start.62 = (bf16[160,1280]{1,0:T(8,128)(2,1)S(1)}, bf16[160,1280]{1,0:T(8,128)(2,1)S(1)}, u32[]{:S(2)}, u32[]{:S(2)}) collective-permute-start(bf16[160,1280]{1,0:T(8,128)(2,1)S(1)} %get-tuple-element.472), channel_id=1, source_target_pairs={{0,1},{1,2},{2,3},{4,5},{5,6},{6,7},{8,9},{9,10},{10,11},{12,13},{... | collective-permute-start | bytes 1228808 | tf_op jit(solution)/shard_map/ppermute | solution.py:111
  652.8 41.8 %collective-permute-start.118 = (bf16[2,2,160,1280]{3,2,1,0:T(8,128)(2,1)S(1)}, bf16[2,2,160,1280]{3,2,1,0:T(8,128)(2,1)S(1)}, u32[]{:S(2)}, u32[]{:S(2)}) collective-permute-start(bf16[2,2,160,1280]{3,2,1,0:T(8,128)(2,1)S(1)} %dynamic-slice_bitcast_fusion.1), channel_id=1, source_target_pairs={{0,4},{4,0},{8,12},{12,8},{1,5},{5,1},{9,13},{13,9},{2,6},{6,2},{1... | collective-permute-start | bytes 4915208 | tf_op jit(solution)/shard_map/ppermute | solution.py:63
  654.1 42.4 %collective-permute-start.113 = (bf16[2,2,160,1280]{3,2,1,0:T(8,128)(2,1)S(1)}, bf16[2,2,160,1280]{3,2,1,0:T(8,128)(2,1)S(1)}, u32[]{:S(2)}, u32[]{:S(2)}) collective-permute-start(bf16[2,2,160,1280]{3,2,1,0:T(8,128)(2,1)S(1)} %dynamic-slice_bitcast_fusion.2), channel_id=1, source_target_pairs={{0,4},{4,0},{8,12},{12,8},{1,5},{5,1},{9,13},{13,9},{2,6},{6,2},{1... | collective-permute-start | bytes 4915208 | tf_op jit(solution)/shard_map/ppermute | solution.py:63
  671.2 42.2 %collective-permute-start.67 = (bf16[160,1280]{1,0:T(8,128)(2,1)S(1)}, bf16[160,1280]{1,0:T(8,128)(2,1)S(1)}, u32[]{:S(2)}, u32[]{:S(2)}) collective-permute-start(bf16[160,1280]{1,0:T(8,128)(2,1)S(1)} %get-tuple-element.391), channel_id=1, source_target_pairs={{0,1},{1,2},{2,3},{4,5},{5,6},{6,7},{8,9},{9,10},{10,11},{12,13},{... | collective-permute-start | bytes 1228808 | tf_op jit(solution)/shard_map/ppermute | solution.py:90
  690.2 24.5 %collective-permute-start.66 = (bf16[160,1280]{1,0:T(8,128)(2,1)S(1)}, bf16[160,1280]{1,0:T(8,128)(2,1)S(1)}, u32[]{:S(2)}, u32[]{:S(2)}) collective-permute-start(bf16[160,1280]{1,0:T(8,128)(2,1)S(1)} %get-tuple-element.391), channel_id=1, source_target_pairs={{3,2},{2,1},{1,0},{7,6},{6,5},{5,4},{11,10},{10,9},{9,8},{15,14},{... | collective-permute-start | bytes 1228808 | tf_op jit(solution)/shard_map/ppermute | solution.py:91
  694.5 20.9 %collective-permute-start.126 = (bf16[2,160,640]{2,1,0:T(8,128)(2,1)S(1)}, bf16[2,160,640]{2,1,0:T(8,128)(2,1)S(1)}, u32[]{:S(2)}, u32[]{:S(2)}) collective-permute-start(bf16[2,160,640]{2,1,0:T(8,128)(2,1)S(1)} %dynamic-slice_bitcast_fusion.4), channel_id=1, source_target_pairs={{0,16},{16,0},{1,17},{17,1},{2,18},{18,2},{3,19},{19,3},{4,20},{20... | collective-permute-start | bytes 1228808 | tf_op jit(solution)/shard_map/ppermute | solution.py:63
  714.7 17.6 %collective-permute-start.68 = (bf16[160,1280]{1,0:T(8,128)(2,1)S(1)}, bf16[160,1280]{1,0:T(8,128)(2,1)S(1)}, u32[]{:S(2)}, u32[]{:S(2)}) collective-permute-start(bf16[160,1280]{1,0:T(8,128)(2,1)S(1)} %collective-permute-done.67), channel_id=1, source_target_pairs={{1,2},{2,3},{5,6},{6,7},{9,10},{10,11},{13,14},{14,15},{17,18},{18... | collective-permute-start | bytes 1228808 | tf_op jit(solution)/shard_map/ppermute | solution.py:92
  715.4 17.7 %collective-permute-start.70 = (bf16[160,1280]{1,0:T(8,128)(2,1)S(1)}, bf16[160,1280]{1,0:T(8,128)(2,1)S(1)}, u32[]{:S(2)}, u32[]{:S(2)}) collective-permute-start(bf16[160,1280]{1,0:T(8,128)(2,1)S(1)} %collective-permute-done.66), channel_id=1, source_target_pairs={{2,1},{1,0},{6,5},{5,4},{10,9},{9,8},{14,13},{13,12},{18,17},{17,1... | collective-permute-start | bytes 1228808 | tf_op jit(solution)/shard_map/ppermute | solution.py:93
  729.2 100.4 %collective-permute-start.122 = (bf16[160,640]{1,0:T(8,128)(2,1)S(1)}, bf16[160,640]{1,0:T(8,128)(2,1)}, u32[]{:S(2)}, u32[]{:S(2)}) collective-permute-start(bf16[160,640]{1,0:T(8,128)(2,1)S(1)} %dynamic-slice_bitcast_fusion.14), channel_id=1, source_target_pairs={{0,8},{4,12},{8,0},{12,4},{1,9},{5,13},{9,1},{13,5},{2,10},{6,14},... | collective-permute-start | bytes 614408 | tf_op jit(solution)/shard_map/ppermute | solution.py:63
  730.6 102.2 %collective-permute-start.115 = (bf16[160,640]{1,0:T(8,128)(2,1)}, bf16[160,640]{1,0:T(8,128)(2,1)}, u32[]{:S(2)}, u32[]{:S(2)}) collective-permute-start(bf16[160,640]{1,0:T(8,128)(2,1)} %dynamic-slice_bitcast_fusion.17), channel_id=1, source_target_pairs={{0,16},{16,0},{1,17},{17,1},{2,18},{18,2},{3,19},{19,3},{4,20},{20... | collective-permute-start | bytes 614408 | tf_op jit(solution)/shard_map/ppermute | solution.py:63
  732.3 338.8 %collective-permute-start.117 = (bf16[160,640]{1,0:T(8,128)(2,1)}, bf16[160,640]{1,0:T(8,128)(2,1)}, u32[]{:S(2)}, u32[]{:S(2)}) collective-permute-start(bf16[160,640]{1,0:T(8,128)(2,1)} %dynamic-slice_bitcast_fusion.16), channel_id=1, source_target_pairs={{0,8},{4,12},{8,0},{12,4},{1,9},{5,13},{9,1},{13,5},{2,10},{6,14},... | collective-permute-start | bytes 614408 | tf_op jit(solution)/shard_map/ppermute | solution.py:63
  751.2 80.9 %collective-permute-start.94 = (bf16[160,1280]{1,0:T(8,128)(2,1)}, bf16[160,1280]{1,0:T(8,128)(2,1)S(1)}, u32[]{:S(2)}, u32[]{:S(2)}) collective-permute-start(bf16[160,1280]{1,0:T(8,128)(2,1)} %get-tuple-element.383), channel_id=1, source_target_pairs={{0,1},{1,2},{2,3},{4,5},{5,6},{6,7},{8,9},{9,10},{10,11},{12,13},{... | collective-permute-start | bytes 1228808 | tf_op jit(solution)/shard_map/ppermute | solution.py:90
  829.7 17.2 %collective-permute-start.73 = (bf16[640,640]{0,1:T(8,128)(2,1)S(1)}, bf16[640,640]{0,1:T(8,128)(2,1)S(1)}, u32[]{:S(2)}, u32[]{:S(2)}) collective-permute-start(bf16[640,640]{0,1:T(8,128)(2,1)S(1)} %get-tuple-element.435), channel_id=1, source_target_pairs={{0,4},{4,0},{8,12},{12,8},{1,5},{5,1},{9,13},{13,9},{2,6},{6,2},{1... | collective-permute-start | bytes 2457608 | tf_op jit(solution)/shard_map/ppermute | solution.py:63
  835.5 141.8 %collective-permute-start.72 = (bf16[640,640]{0,1:T(8,128)(2,1)}, bf16[640,640]{0,1:T(8,128)(2,1)}, u32[]{:S(2)}, u32[]{:S(2)}) collective-permute-start(bf16[640,640]{0,1:T(8,128)(2,1)} %get-tuple-element.434), channel_id=1, source_target_pairs={{0,4},{4,0},{8,12},{12,8},{1,5},{5,1},{9,13},{13,9},{2,6},{6,2},{1... | collective-permute-start | bytes 2457608 | tf_op jit(solution)/shard_map/ppermute | solution.py:63
  848.9 128.4 %collective-permute-start.74 = (bf16[640,640]{0,1:T(8,128)(2,1)}, bf16[640,640]{0,1:T(8,128)(2,1)}, u32[]{:S(2)}, u32[]{:S(2)}) collective-permute-start(bf16[640,640]{0,1:T(8,128)(2,1)} %add_convert_fusion.1), channel_id=1, source_target_pairs={{0,8},{4,12},{8,0},{12,4},{1,9},{5,13},{9,1},{13,5},{2,10},{6,14},... | collective-permute-start | bytes 2457608 | tf_op jit(solution)/shard_map/ppermute | solution.py:63
  956.3 17.3 %collective-permute-start.100 = (bf16[640,640]{0,1:T(8,128)(2,1)}, bf16[640,640]{0,1:T(8,128)(2,1)}, u32[]{:S(2)}, u32[]{:S(2)}) collective-permute-start(bf16[640,640]{0,1:T(8,128)(2,1)} %get-tuple-element.437), channel_id=1, source_target_pairs={{0,4},{4,0},{8,12},{12,8},{1,5},{5,1},{9,13},{13,9},{2,6},{6,2},{1... | collective-permute-start | bytes 2457608 | tf_op jit(solution)/shard_map/ppermute | solution.py:63
  956.3 26.3 %collective-permute-start.99 = (bf16[640,640]{0,1:T(8,128)(2,1)}, bf16[640,640]{0,1:T(8,128)(2,1)}, u32[]{:S(2)}, u32[]{:S(2)}) collective-permute-start(bf16[640,640]{0,1:T(8,128)(2,1)} %get-tuple-element.436), channel_id=1, source_target_pairs={{0,4},{4,0},{8,12},{12,8},{1,5},{5,1},{9,13},{13,9},{2,6},{6,2},{1... | collective-permute-start | bytes 2457608 | tf_op jit(solution)/shard_map/ppermute | solution.py:63
  976.1 20.5 %collective-permute-start.101 = (bf16[640,640]{0,1:T(8,128)(2,1)}, bf16[640,640]{0,1:T(8,128)(2,1)}, u32[]{:S(2)}, u32[]{:S(2)}) collective-permute-start(bf16[640,640]{0,1:T(8,128)(2,1)} %add_convert_fusion), channel_id=1, source_target_pairs={{0,8},{4,12},{8,0},{12,4},{1,9},{5,13},{9,1},{13,5},{2,10},{6,14},... | collective-permute-start | bytes 2457608 | tf_op jit(solution)/shard_map/ppermute | solution.py:63
  1000.1 29.1 %collective-permute-start.133 = (f32[320]{0:T(512)S(1)}, f32[320]{0:T(512)S(1)}, u32[]{:S(2)}, u32[]{:S(2)}) collective-permute-start(f32[320]{0:T(512)S(1)} %add_add_fusion.14), channel_id=1, source_target_pairs={{0,16},{16,0},{1,17},{17,1},{2,18},{18,2},{3,19},{19,3},{4,20},{20... | collective-permute-start | bytes 3848 | tf_op jit(solution)/shard_map/ppermute | solution.py:63
  1018.2 70.6 %collective-permute-start.108 = (bf16[2,2,160,1280]{3,2,1,0:T(8,128)(2,1)S(1)}, bf16[2,2,160,1280]{3,2,1,0:T(8,128)(2,1)S(1)}, u32[]{:S(2)}, u32[]{:S(2)}) collective-permute-start(bf16[2,2,160,1280]{3,2,1,0:T(8,128)(2,1)S(1)} %dynamic-slice_bitcast_fusion.3), channel_id=1, source_target_pairs={{0,4},{4,0},{8,12},{12,8},{1,5},{5,1},{9,13},{13,9},{2,6},{6,2},{1... | collective-permute-start | bytes 4915208 | tf_op jit(solution)/shard_map/ppermute | solution.py:63
  1036.5 39.3 %collective-permute-start.135 = (f32[320]{0:T(512)S(1)}, f32[320]{0:T(512)S(1)}, u32[]{:S(2)}, u32[]{:S(2)}) collective-permute-start(f32[320]{0:T(512)S(1)} %add.894), channel_id=1, source_target_pairs={{0,8},{4,12},{8,0},{12,4},{1,9},{5,13},{9,1},{13,5},{2,10},{6,14},... | collective-permute-start | bytes 3848 | tf_op jit(solution)/shard_map/ppermute | solution.py:63
  (269 other events, 2657.5 us)
Sparse Core Ops, SparseCore 0:
  10.5 35.5 all-gather.4
  48.0 32.8 all-gather.8
  82.8 41.6 all-gather.6
  356.3 42.9 all-gather.10

commit v3 on v2

--- a/solution.py
+++ b/solution.py
@@ -3,6 +3,8 @@
 import jax
 import jax.numpy as jnp
 from jax import lax
+from jax.experimental import pallas as pl
+from jax.experimental.pallas import tpu as pltpu
 from jax.sharding import PartitionSpec as P
 
 D = 1280
@@ -36,14 +38,6 @@
     return lax.dot_general(
         former, latter, (((1,), (1,)), ((), ())), preferred_element_type=jnp.float32
     )
-
-
-def split_heads(values):
-    return values.reshape(values.shape[0], values.shape[1] // HDIM, HDIM).transpose(1, 0, 2)
-
-
-def merge_heads(values):
-    return values.transpose(1, 0, 2).reshape(values.shape[1], values.shape[0] * values.shape[2])
 
 
 def mix_rows(residual, branch, mixing):
@@ -192,28 +186,208 @@
     )
 
 
+LOG2_SCALE = math.sqrt(HDIM) * math.log2(math.e)
+LANES = 128
+KEY_TILE = 256
+
+
+def half_kept(value, unit, axis):
+    place = lax.broadcasted_iota(jnp.int32, value.shape, axis)
+    inside = (place >= HDIM) if unit % 2 else (place < HDIM)
+    return jnp.where(inside, value, jnp.zeros_like(value))
+
+
+def seen_tile(hot_ref, side_ref):
+    hot = hot_ref[...]
+    strict = jnp.dot(hot, side_ref[0], preferred_element_type=jnp.float32)
+    same = jnp.dot(hot, side_ref[1], preferred_element_type=jnp.float32)
+    before = jnp.dot(hot, side_ref[2], preferred_element_type=jnp.float32)
+    return (strict + same * before).astype(jnp.bfloat16)
+
+
+def pair_of(unit):
+    return slice(unit // 2 * LANES, unit // 2 * LANES + LANES)
+
+
+def attend_body(query_ref, tree_ref, hot_ref, side_ref, out_ref, scale_ref, turned_ref, sum_ref):
+    heads = query_ref.shape[1] // HDIM
+    step = pl.program_id(0)
+
+    @pl.when(step == 0)
+    def prepare():
+        turned = query_ref[...].astype(jnp.float32).T.astype(jnp.bfloat16)
+        blank = jnp.zeros((HDIM, turned.shape[1]), jnp.bfloat16)
+        for head in range(heads):
+            own = turned[head * HDIM : (head + 1) * HDIM]
+            halves = [blank, own] if head % 2 else [own, blank]
+            turned_ref[head] = jnp.concatenate(halves, axis=0)
+        sum_ref[...] = jnp.zeros_like(sum_ref)
+
+    tree = tree_ref[...]
+    values_turned = tree[:, heads * HDIM :].astype(jnp.float32).T.astype(jnp.bfloat16)
+    seen = seen_tile(hot_ref, side_ref)
+    ones = jnp.ones((sum_ref.shape[1] - HDIM, tree.shape[0]), jnp.bfloat16)
+    for head in range(heads):
+        scores = jnp.dot(tree[:, pair_of(head)], turned_ref[head], preferred_element_type=jnp.float32)
+        lifted = jnp.exp2(scores * LOG2_SCALE).astype(jnp.bfloat16) * seen
+        own = jnp.concatenate([values_turned[head * HDIM : (head + 1) * HDIM], ones], axis=0)
+        sum_ref[head] += jnp.dot(own, lifted, preferred_element_type=jnp.float32)
+
+    @pl.when(step == pl.num_programs(0) - 1)
+    def finish():
+        parts = []
+        for head in range(heads):
+            inverse = 1.0 / sum_ref[head, HDIM : HDIM + 1]
+            scale_ref[head : head + 1] = inverse
+            parts.append(sum_ref[head, :HDIM] * inverse)
+        out_ref[...] = jnp.concatenate(parts, axis=0).T.astype(jnp.bfloat16)
+
+
+def attend(query, tree, hot, side):
+    rows, features = query.shape
+    keys, width = tree.shape
+    heads = features // HDIM
+    whole = lambda step: (0, 0)
+    return pl.pallas_call(
+        attend_body,
+        grid=(keys // KEY_TILE,),
+        in_specs=[
+            pl.BlockSpec((rows, features), whole),
+            pl.BlockSpec((KEY_TILE, width), lambda step: (step, 0)),
+            pl.BlockSpec((KEY_TILE, LANES), lambda step: (step, 0)),
+            pl.BlockSpec((3, LANES, rows), lambda step: (0, 0, 0)),
+        ],
+        out_specs=[
+            pl.BlockSpec((rows, features), whole),
+            pl.BlockSpec((8, rows), whole),
+        ],
+        out_shape=[
+            jax.ShapeDtypeStruct((rows, features), jnp.bfloat16),
+            jax.ShapeDtypeStruct((8, rows), jnp.float32),
+        ],
+        scratch_shapes=[
+            pltpu.VMEM((heads, LANES, rows), jnp.bfloat16),
+            pltpu.VMEM((heads, HDIM + 16, rows), jnp.float32),
+        ],
+        compiler_params=pltpu.CompilerParams(vmem_limit_bytes=48 << 20),
+        name="attend",
+    )(query, tree, hot, side)
+
+
+def attend_grad_body(
+    both_ref, heads_ref, tree_ref, hot_ref, side_ref, scale_ref,
+    query_out, tree_out, turned_ref, plain_ref, delta_ref, sum_ref,
+):
+    heads = heads_ref.shape[1] // HDIM
+    units = 2 * heads
+    step = pl.program_id(0)
+
+    @pl.when(step == 0)
+    def prepare():
+        both = both_ref[...]
+        turned = both.astype(jnp.float32).T
+        outs = heads_ref[...].astype(jnp.float32).T
+        blank = jnp.zeros((HDIM, turned.shape[1]), jnp.bfloat16)
+        for unit in range(units):
+            own = turned[unit * HDIM : (unit + 1) * HDIM].astype(jnp.bfloat16)
+            halves = [blank, own] if unit % 2 else [own, blank]
+            turned_ref[unit] = jnp.concatenate(halves, axis=0)
+            plain_ref[unit] = half_kept(both[:, pair_of(unit)], unit, 1)
+        for head in range(heads):
+            rows = slice(head * HDIM, (head + 1) * HDIM)
+            upstream = turned[(heads + head) * HDIM : (heads + head + 1) * HDIM]
+            delta_ref[head : head + 1] = jnp.sum(outs[rows] * upstream, axis=0, keepdims=True)
+        sum_ref[...] = jnp.zeros_like(sum_ref)
+
+    tree = tree_ref[...]
+    keys_turned = tree[:, : heads * HDIM].astype(jnp.float32).T.astype(jnp.bfloat16)
+    seen = seen_tile(hot_ref, side_ref)
+    weights, slopes = [], []
+    for head in range(heads):
+        scores = jnp.dot(tree[:, pair_of(head)], turned_ref[head], preferred_element_type=jnp.float32)
+        weight = jnp.exp2(scores * LOG2_SCALE) * scale_ref[head : head + 1]
+        pull = jnp.dot(
+            tree[:, pair_of(heads + head)], turned_ref[heads + head], preferred_element_type=jnp.float32
+        )
+        slope = (weight * (pull - delta_ref[head : head + 1])).astype(jnp.bfloat16) * seen
+        rows = slice(head * HDIM, (head + 1) * HDIM)
+        sum_ref[rows] += jnp.dot(keys_turned[rows], slope, preferred_element_type=jnp.float32)
+        weights.append(weight.astype(jnp.bfloat16) * seen)
+        slopes.append(slope)
+    terms = slopes + weights
+    score_scale = math.sqrt(HDIM)
+    for pair in range(heads):
+        total = 0.0
+        for unit in (2 * pair, 2 * pair + 1):
+            part = jnp.dot(terms[unit], plain_ref[unit], preferred_element_type=jnp.float32)
+            total = total + (part * score_scale if unit < heads else part)
+        tree_out[:, pair * LANES : (pair + 1) * LANES] = total.astype(jnp.bfloat16)
+
+    @pl.when(step == pl.num_programs(0) - 1)
+    def finish():
+        query_out[...] = sum_ref[...].T * score_scale
+
+
+def attend_grad(query, upstream, outs, tree, hot, side, scale):
+    rows, features = query.shape
+    keys, width = tree.shape
+    heads = features // HDIM
+    whole = lambda step: (0, 0)
+    return pl.pallas_call(
+        attend_grad_body,
+        grid=(keys // KEY_TILE,),
+        in_specs=[
+            pl.BlockSpec((rows, 2 * features), whole),
+            pl.BlockSpec((rows, features), whole),
+            pl.BlockSpec((KEY_TILE, width), lambda step: (step, 0)),
+            pl.BlockSpec((KEY_TILE, LANES), lambda step: (step, 0)),
+            pl.BlockSpec((3, LANES, rows), lambda step: (0, 0, 0)),
+            pl.BlockSpec((8, rows), whole),
+        ],
+        out_specs=[
+            pl.BlockSpec((rows, features), whole),
+            pl.BlockSpec((KEY_TILE, width), lambda step: (step, 0)),
+        ],
+        out_shape=[
+            jax.ShapeDtypeStruct((rows, features), jnp.float32),
+            jax.ShapeDtypeStruct((keys, width), jnp.bfloat16),
+        ],
+        scratch_shapes=[
+            pltpu.VMEM((2 * heads, LANES, rows), jnp.bfloat16),
+            pltpu.VMEM((2 * heads, rows, LANES), jnp.bfloat16),
+            pltpu.VMEM((8, rows), jnp.float32),
+            pltpu.VMEM((features, rows), jnp.float32),
+        ],
+        compiler_params=pltpu.CompilerParams(vmem_limit_bytes=48 << 20),
+        name="attend_grad",
+    )(jnp.concatenate([query, upstream], axis=1), outs, tree, hot, side, scale)
+
+
+def seen_factors(reachable, seg_query, off_query, segment, offset):
+    segs = reachable.shape[0]
+    labels = jnp.arange(LANES, dtype=jnp.int32)
+    key_mark = jnp.where(labels < HDIM, segment[:, None], offset[:, None] + HDIM)
+    hot = (key_mark == labels[None, :]).astype(jnp.bfloat16)
+    query_hot = (labels[:, None] == seg_query[None, :]).astype(jnp.float32)
+    wide = jnp.zeros((LANES, LANES), jnp.float32).at[:segs, :segs].set(reachable.T - jnp.eye(segs, dtype=jnp.float32))
+    strict = jnp.dot(wide, query_hot, preferred_element_type=jnp.float32)
+    same = query_hot
+    before = ((labels[:, None] >= HDIM) & (labels[:, None] - HDIM <= off_query[None, :])).astype(jnp.float32)
+    return hot, jnp.stack([strict, same, before]).astype(jnp.bfloat16)
+
+
 def visibility(parents, slots, group_size):
     labels = jnp.arange(SEGS, dtype=jnp.int32)
     linked = (parents[:, None] == labels[None, :]).astype(jnp.float32)
     reachable = jnp.maximum(linked, jnp.eye(SEGS, dtype=jnp.float32))
     for doubling in range(SEGS.bit_length()):
         reachable = jnp.minimum(jnp.dot(reachable, reachable, precision=HIGHEST), 1.0)
-    seg_query, off_query, segment, offset = row_labels(slots, group_size)
-    key_onehot = (segment[:, None] == labels[None, :]).astype(jnp.float32)
-    query_onehot = (seg_query[:, None] == labels[None, :]).astype(jnp.float32)
-    linked_rows = jnp.dot(query_onehot, reachable, precision=HIGHEST)
-    seen = (
-        lax.dot_general(linked_rows, key_onehot, (((1,), (1,)), ((), ())), precision=HIGHEST) > 0.5
-    )
-    return seen & (
-        (seg_query[:, None] != segment[None, :]) | (offset[None, :] <= off_query[:, None])
-    )
+    return seen_factors(reachable, *row_labels(slots, group_size))
 
 
 def forward_attention(gathered, vectors, tokens_own, parents, slots):
     w_query, w_key, w_value, w_attn_out = gathered[:4]
     alpha_attn, alpha_mlp, scale_qk, scale_up, scale_gate = vectors
-    score_scale = math.sqrt(HDIM)
     hidden_group = line_gather(tokens_own)
     visible = visibility(parents, slots, hidden_group.shape[0])
     query_raw = jnp.dot(hidden_group, w_query, preferred_element_type=jnp.float32)
@@ -225,35 +399,16 @@
     queries = query_unit.astype(jnp.bfloat16)
     keys_own = key_unit.astype(jnp.bfloat16)
     keys_values = tree_gather(jnp.concatenate([keys_own, value_low], axis=1))
-    keys_tree, values_tree = jnp.split(keys_values, 2, axis=1)
-    query_heads = split_heads(queries)
-    key_heads = split_heads(keys_tree)
-    value_heads = split_heads(values_tree)
-
-    def head_forward(record):
-        query_one, key_one, value_one = record
-        scores = jnp.where(visible, contract_cols(query_one, key_one) * score_scale, MASKED)
-        row_peak = jnp.max(scores, axis=-1, keepdims=True)
-        lifted = jnp.exp(scores - row_peak)
-        row_total = jnp.sum(lifted, axis=-1, keepdims=True)
-        soft_weights = lifted / row_total
-        head_value = jnp.dot(
-            soft_weights.astype(jnp.bfloat16), value_one, preferred_element_type=jnp.float32
-        )
-        return (head_value, (row_peak + jnp.log(row_total))[:, 0])
-
-    head_values, log_totals = lax.map(head_forward, (query_heads, key_heads, value_heads))
-    heads_low = merge_heads(head_values).astype(jnp.bfloat16)
+    heads_low, scale = attend(queries, keys_values, *visible)
     branch_one = line_scatter(contract_cols(heads_low, w_attn_out).astype(jnp.bfloat16))
     kept = (
         hidden_group,
         visible,
         query_raw,
         key_raw,
-        query_heads,
-        key_heads,
-        value_heads,
-        log_totals,
+        queries,
+        keys_values,
+        scale,
         heads_low,
     )
     return branch_one, kept
@@ -295,48 +450,26 @@
 def backward_attention(gathered, vectors, kept, branch_one_grad, tokens_direct):
     w_query, w_key, w_value, w_attn_out = gathered[:4]
     scale_qk = vectors[2]
-    score_scale = math.sqrt(HDIM)
     (
         hidden_group,
         visible,
         query_raw,
         key_raw,
-        query_heads,
-        key_heads,
-        value_heads,
-        log_totals,
+        queries,
+        keys_values,
+        scale,
         heads_low,
     ) = kept
     branch_one_group = line_gather(branch_one_grad.astype(jnp.bfloat16))
-    heads_grad = split_heads(
-        jnp.dot(branch_one_group, w_attn_out, preferred_element_type=jnp.float32).astype(
-            jnp.bfloat16
-        )
-    )
-
-    def head_backward(record):
-        query_one, key_one, value_one, upstream_one, log_total = record
-        scores = jnp.where(visible, contract_cols(query_one, key_one) * score_scale, MASKED)
-        soft_weights = jnp.exp(scores - log_total[:, None])
-        weight_grad = contract_cols(upstream_one, value_one)
-        row_inner = jnp.sum(soft_weights * weight_grad, axis=-1, keepdims=True)
-        score_grad = (soft_weights * (weight_grad - row_inner)).astype(jnp.bfloat16)
-        query_grad = jnp.dot(score_grad, key_one, preferred_element_type=jnp.float32) * score_scale
-        key_grad = contract_rows(score_grad, query_one) * score_scale
-        value_grad = contract_rows(soft_weights.astype(jnp.bfloat16), upstream_one)
-        return (query_grad, key_grad, value_grad)
-
-    query_grads, key_grads, value_grads = lax.map(
-        head_backward, (query_heads, key_heads, value_heads, heads_grad, log_totals)
-    )
-    both = tree_scatter(
-        jnp.concatenate([merge_heads(key_grads), merge_heads(value_grads)], axis=1).astype(
-            jnp.bfloat16
-        )
-    )
-    key_own_grad, value_own_grad = jnp.split(both, 2, axis=1)
+    heads_grad = jnp.dot(
+        branch_one_group, w_attn_out, preferred_element_type=jnp.float32
+    ).astype(jnp.bfloat16)
+    query_grads, tree_grads = attend_grad(
+        queries, heads_grad, heads_low, keys_values, *visible, scale
+    )
+    key_own_grad, value_own_grad = jnp.split(tree_scatter(tree_grads), 2, axis=1)
     unit_again, pull_qk = jax.vjp(query_key, query_raw, key_raw, scale_qk)
-    query_raw_grad, key_raw_grad, grad_scale_qk = pull_qk((merge_heads(query_grads), key_own_grad))
+    query_raw_grad, key_raw_grad, grad_scale_qk = pull_qk((query_grads, key_own_grad))
     query_low = query_raw_grad.astype(jnp.bfloat16)
     key_low = key_raw_grad.astype(jnp.bfloat16)
     value_grad_low = value_own_grad.astype(jnp.bfloat16)

time: 1130 us -> 1020 us (0.903)
  matrix products: 344 us -> 132 us
  Pallas kernels: 0 us -> 98.7 us
  waiting for transfers between devices: 331 us -> 349 us
    pallas_call x0 -> x4, Pallas kernels: none -> 98.7 us  [the longest x2 64.2 us: attend_grad(): pl.pallas_call(attend_grad_body, grid=(keys // KEY_TILE,), in_specs=[pl.B...]
    dot_general x44 -> x14, matrix products: 122 us -> 35.9 us  [contract_cols(): lax.dot_general(former, latter, (((1,), (1,)), ((), ())), preferred_eleme...]
    dot_general x24 -> x2, matrix products: 85.8 us -> 1.77 us  [seen_factors(): strict = jnp.dot(wide, query_hot, preferred_element_type=jnp.float32)]
    dot_general x27 -> x7, matrix products: 75.2 us -> 26.6 us  [contract_rows(): lax.dot_general(former, latter, (((0,), (0,)), ((), ())), preferred_eleme...]
    reshape x8 -> x0, local copies, waits for them, and re-layouts: 23.5 us -> none  [split_heads(): values.reshape(values.shape[0], values.shape[1] // HDIM, HDIM)]
    while x40 -> x0, local copies, waits for them, and re-layouts: 17.5 us -> none
    mul x1 -> x12, local copies, waits for them, and re-layouts: 0.66 us -> 16.8 us  [unit_rows(): values * lax.rsqrt(jnp.sum(values * values, axis=-1, keepdims=True) + EPS...]
    concatenate x2, other arithmetic: 6.99 us -> 19.2 us  [tree_gather(): jnp.concatenate([own_block, beside, across, swap(across, 'ctx', 1)], axis=0)]
  transfers between devices with their start and end apart: 140 -> 140, of which waited for: 68 -> 67; matrix products, arithmetic and copies ran while one was open for 44% -> 30% of each run, Pallas kernels for 0% -> 10%
where the time goes in v3:
time: 1020 us; the launch traced here: 1010 us
  waiting for transfers between devices  349 us (34%)
  starting transfers between devices  210 us (21%)
  matrix products  132 us (13%)
  other arithmetic  118 us (12%)
  Pallas kernels  98.7 us (10%)
  local copies, waits for them, and re-layouts  87.3 us (9%)
  between operations  17.4 us (2%)
    ppermute x40, waiting for transfers between devices, swap(): lax.ppermute(value, axis, [(place, place ^ bit) for place in range(size)])  83.1 us
    pallas_call x2, Pallas kernels, attend_grad(): pl.pallas_call(attend_grad_body, grid=(keys // KEY_TILE,), in_specs=[pl.B...  64.2 us
    ppermute x8, waiting for transfers between devices, line_gather(): left_two = lax.ppermute(left_one, 'tp', [(2, 1), (1, 0)])  58.6 us
    ppermute x8, waiting for transfers between devices, line_gather(): left_three = lax.ppermute(left_two, 'tp', [(1, 0)])  50 us
    ppermute x8, starting transfers between devices, line_scatter(): right = lax.ppermute(add_low(right, one), 'tp', [(0, 1), (1, 2), (2, 3)])  37.7 us
    dot_general x14, matrix products, contract_cols(): lax.dot_general(former, latter, (((1,), (1,)), ((), ())), preferred_eleme...  35.9 us
    pallas_call x2, Pallas kernels, attend(): pl.pallas_call(attend_body, grid=(keys // KEY_TILE,), in_specs=[pl.BlockS...  34.5 us
    ppermute x40, starting transfers between devices, swap(): lax.ppermute(value, axis, [(place, place ^ bit) for place in range(size)])  34.3 us
  transfers between devices with their start and end apart: 140, of which 67 were waited for; matrix products, arithmetic and copies ran while one was open for 30% of the time, Pallas kernels for 10%

profile of v3, /device:TPU:0, one launch (start us, length us, event | category | flops | bytes accessed | tf_op | source)
XLA Modules:
  0.0 1011.8 jit_solution(6986058034884303827)
XLA Ops:
  11.4 5.0 collective-permute-start.28
  28.3 5.5 collective-permute-done.1
  41.5 15.6 %collective-permute-done.31 = bf16[160,1280]{1,0:T(8,128)(2,1)S(1)} collective-permute-done((bf16[160,1280]{1,0:T(8,128)(2,1)S(1)}, bf16[160,1280]{1,0:T(8,128)(2,1)S(1)}, u32[]{:S(2)}, u32[]{:S(2)}) %collective-permute-start.31) | collective-permute-done | bytes 409632 | tf_op jit(solution)/shard_map/ppermute | solution.py:87
  58.3 7.5 collective-permute-done.4
  69.3 11.7 %collective-permute-done.5 = bf16[160,1280]{1,0:T(8,128)(2,1)S(1)} collective-permute-done((bf16[160,1280]{1,0:T(8,128)(2,1)S(1)}, bf16[160,1280]{1,0:T(8,128)(2,1)S(1)}, u32[]{:S(2)}, u32[]{:S(2)}) %collective-permute-start.5) | collective-permute-done | bytes 409632 | tf_op jit(solution)/shard_map/ppermute | solution.py:89
  130.0 5.0 multiply_convert_fusion.6
  146.1 11.6 %collective-permute-done.34 = bf16[640,640]{1,0:T(8,128)(2,1)} collective-permute-done((bf16[640,640]{1,0:T(8,128)(2,1)}, bf16[640,640]{1,0:T(8,128)(2,1)}, u32[]{:S(2)}, u32[]{:S(2)}) %collective-permute-start.34) | collective-permute-done | bytes 819232 | tf_op jit(solution)/shard_map/ppermute | solution.py:57
  160.3 11.8 %collective-permute-done.7 = bf16[640,640]{1,0:T(8,128)(2,1)S(1)} collective-permute-done((bf16[640,640]{1,0:T(8,128)(2,1)}, bf16[640,640]{1,0:T(8,128)(2,1)S(1)}, u32[]{:S(2)}, u32[]{:S(2)}) %collective-permute-start.7) | collective-permute-done | bytes 819232 | tf_op jit(solution)/shard_map/ppermute | solution.py:57
  172.2 8.9 pad_maximum_fusion.1.tree_ref
  181.1 17.3 %attend.3 = (bf16[640,320]{1,0:T(8,128)(2,1)S(1)}, f32[8,640]{1,0:T(8,128)S(1)}) custom-call(bf16[640,320]{1,0:T(8,128)(2,1)S(1)} %get-tuple-element.318.query_ref, bf16[2560,640]{1,0:T(8,128)(2,1)S(1)} %pad_maximum_fusion.1.tree_ref, bf16[2560,128]{1,0:T(8,128)(2,1)S(1)} %get-tuple-element.302.hot_ref, bf16[3,128,640]{2,1,0:T(8,128)(2,1)S(1)} %get-tuple-element.296.side_ref), custom_call_target="tpu_custom_call" | custom-call | tf_op jit(solution)/shard_map/attend/pallas_call | solution.py:251
  201.7 10.3 %pad_maximum_fusion.tree_ref = bf16[2560,640]{1,0:T(8,128)(2,1)S(1)} fusion(bf16[640,640]{1,0:T(8,128)(2,1)S(1)} %collective-permute-done.8, bf16[640,640]{1,0:T(8,128)(2,1)S(1)} %collective-permute-done.7, bf16[640,640]{1,0:T(8,128)(2,1)S(1)} %collective-permute-done.6, bf16[640,320]{1,0:T(8,128)(2,1)S(1)} %copy-done.62, bf16[640,320]{1,0:T(8,128)(2,1)S(1)} %copy-done.59), kind=kLoop, calls=%fused_computation.19 | loop fusion | flops 16384000 | bytes 6553600 | tf_op jit(solution)/shard_map/concatenate | solution.py:123
  212.0 17.3 %attend.2 = (bf16[640,320]{1,0:T(8,128)(2,1)S(1)}, f32[8,640]{1,0:T(8,128)S(1)}) custom-call(bf16[640,320]{1,0:T(8,128)(2,1)S(1)} %get-tuple-element.320.query_ref, bf16[2560,640]{1,0:T(8,128)(2,1)S(1)} %pad_maximum_fusion.tree_ref, bf16[2560,128]{1,0:T(8,128)(2,1)S(1)} %get-tuple-element.303.hot_ref, bf16[3,128,640]{2,1,0:T(8,128)(2,1)S(1)} %get-tuple-element.297.side_ref), custom_call_target="tpu_custom_call" | custom-call | tf_op jit(solution)/shard_map/attend/pallas_call | solution.py:251
  234.7 6.9 collective-permute-done.9
  268.2 8.3 collective-permute-done.11
  284.3 7.5 collective-permute-done.16
  298.8 9.5 collective-permute-done.19
  314.0 5.8 collective-permute-done.20
  337.3 6.2 fusion.139
  351.2 6.4 collective-permute-done.47
  370.0 6.0 multiply_convert_fusion.5
  410.1 5.5 collective-permute-start.23
  418.9 5.5 collective-permute-start.50
  430.8 5.3 collective-permute-done.53
  449.2 6.9 collective-permute-done.54
  458.1 12.1 %collective-permute-done.58 = bf16[160,1280]{1,0:T(8,128)(2,1)S(1)} collective-permute-done((bf16[160,1280]{1,0:T(8,128)(2,1)S(1)}, bf16[160,1280]{1,0:T(8,128)(2,1)S(1)}, u32[]{:S(2)}, u32[]{:S(2)}) %collective-permute-start.58) | collective-permute-done | bytes 409632 | tf_op jit(solution)/shard_map/ppermute | solution.py:87
  473.3 6.8 collective-permute-done.59
  492.5 6.3 collective-permute-done.81
  500.8 6.0 convolution_convert_fusion.4
  514.9 5.9 collective-permute-done.86
  528.7 11.6 %multiply_reduce_fusion.2 = (f32[1280]{0:T(1024)S(1)}, f32[1280]{0:T(1024)S(1)}, f32[1280]{0:T(1024)S(1)}, f32[1280]{0:T(1024)S(1)}, f32[640,1280]{1,0:T(8,128)S...) fusion(f32[640,1280]{1,0:T(8,128)} %copy-done.135, f32[640,1280]{1,0:T(8,128)} %fusion.137, ...), kind=kOutput, calls=%fused_computation.40 | convolution fusion | flops 2138926080 | bytes 29521920 | tf_op jit(solution)/shard_map/dot_general | solution.py:432
  547.1 5.0 convolution_convert_fusion.2
  552.1 6.1 fusion.200
  577.6 6.8 collective-permute-done.60
  611.3 6.1 collective-permute-done.62
  652.0 7.0 collective-permute-done.126
  687.7 8.8 collective-permute-done.71
  707.9 6.9 collective-permute-done.93
  721.2 7.5 collective-permute-done.97
  745.7 32.1 %attend_grad.3 = (f32[640,320]{1,0:T(8,128)S(1)}, bf16[2560,640]{1,0:T(8,128)(2,1)}) custom-call(bf16[640,640]{1,0:T(8,128)(2,1)S(1)} %get-tuple-element.340.both_ref, bf16[640,320]{1,0:T(8,128)(2,1)S(1)} %copy-done.16, bf16[2560,640]{1,0:T(8,128)(2,1)} %copy-done.1, bf16[2560,128]{1,0:T(8,128)(2,1)S(1)} %copy-done.5, bf16[3,128,640]{2,1,0:T(8,128)(2,1)S(1)} %copy-done.13, ...), custom_call_target="tpu_custom_call" | custom-call | tf_op jit(solution)/shard_map/attend_grad/pallas_call | solution.py:336
  787.8 32.1 %attend_grad.2 = (f32[640,320]{1,0:T(8,128)S(1)}, bf16[2560,640]{1,0:T(8,128)(2,1)}) custom-call(bf16[640,640]{1,0:T(8,128)(2,1)S(1)} %copy-done.14, bf16[640,320]{1,0:T(8,128)(2,1)S(1)} %copy-done.19, bf16[2560,640]{1,0:T(8,128)(2,1)} %copy-done, bf16[2560,128]{1,0:T(8,128)(2,1)S(1)} %copy-done.3, bf16[3,128,640]{2,1,0:T(8,128)(2,1)S(1)} %copy-done.11, ...), custom_call_target="tpu_custom_call" | custom-call | tf_op jit(solution)/shard_map/attend_grad/pallas_call | solution.py:336
  834.2 12.5 %collective-permute-done.101 = bf16[640,640]{1,0:T(8,128)(2,1)} collective-permute-done((bf16[640,640]{1,0:T(8,128)(2,1)}, bf16[640,640]{1,0:T(8,128)(2,1)}, u32[]{:S(2)}, u32[]{:S(2)}) %collective-permute-start.101) | collective-permute-done | bytes 819232 | tf_op jit(solution)/shard_map/ppermute | solution.py:57
  856.0 7.9 collective-permute-done.74
  881.5 6.5 multiply_reduce_fusion.4
  907.7 5.9 concatenate.136
  932.7 6.3 collective-permute-done.102
  944.5 7.0 collective-permute-done.76
  957.0 6.1 collective-permute-done.103
  990.2 6.2 collective-permute-done.109
  (803 shorter events, 561.6 us)
Async XLA Ops:
  7.2 78.6 %all-gather.5.cloned.1.call-start = ((), (), s32[]{:S(2)}) async-start(), calls=%async_computation | async-start | bytes 3686400 | tf_op jit(solution)/shard_map/all_gather | solution.py:510
  9.4 328.0 %all-gather.9.cloned.1.call-start = ((), (), s32[]{:S(2)}) async-start(), calls=%async_computation.2 | async-start | bytes 3686400 | tf_op jit(solution)/shard_map/all_gather | solution.py:510
  10.1 353.2 %all-gather.7.cloned.1.call-start = ((), (), s32[]{:S(2)}) async-start(), calls=%async_computation.1 | async-start | bytes 3686400 | tf_op jit(solution)/shard_map/all_gather | solution.py:510
  11.4 24.6 %collective-permute-start.28 = (bf16[160,1280]{1,0:T(8,128)(2,1)S(1)}, bf16[160,1280]{1,0:T(8,128)(2,1)S(1)}, u32[]{:S(2)}, u32[]{:S(2)}) collective-permute-start(bf16[160,1280]{1,0:T(8,128)(2,1)S(1)} %get-tuple-element.290), channel_id=1, source_target_pairs={{0,1},{1,2},{2,3},{4,5},{5,6},{6,7},{8,9},{9,10},{10,11},{12,13},{... | collective-permute-start | bytes 1228808 | tf_op jit(solution)/shard_map/ppermute | solution.py:84
  16.3 20.3 %collective-permute-start.27 = (bf16[160,1280]{1,0:T(8,128)(2,1)S(1)}, bf16[160,1280]{1,0:T(8,128)(2,1)S(1)}, u32[]{:S(2)}, u32[]{:S(2)}) collective-permute-start(bf16[160,1280]{1,0:T(8,128)(2,1)S(1)} %get-tuple-element.290), channel_id=1, source_target_pairs={{3,2},{2,1},{1,0},{7,6},{6,5},{5,4},{11,10},{10,9},{9,8},{15,14},{... | collective-permute-start | bytes 1228808 | tf_op jit(solution)/shard_map/ppermute | solution.py:85
  23.5 352.4 %all-gather.11.cloned.1.call-start = ((), (), s32[]{:S(2)}) async-start(), calls=%async_computation.3 | async-start | bytes 3686400 | tf_op jit(solution)/shard_map/all_gather | solution.py:510
  36.7 20.4 %collective-permute-start.31 = (bf16[160,1280]{1,0:T(8,128)(2,1)S(1)}, bf16[160,1280]{1,0:T(8,128)(2,1)S(1)}, u32[]{:S(2)}, u32[]{:S(2)}) collective-permute-start(bf16[160,1280]{1,0:T(8,128)(2,1)S(1)} %collective-permute-done.27), channel_id=1, source_target_pairs={{2,1},{1,0},{6,5},{5,4},{10,9},{9,8},{14,13},{13,12},{18,17},{17,1... | collective-permute-start | bytes 1228808 | tf_op jit(solution)/shard_map/ppermute | solution.py:87
  38.0 27.8 %collective-permute-start.4 = (bf16[160,1280]{1,0:T(8,128)(2,1)S(1)}, bf16[160,1280]{1,0:T(8,128)(2,1)S(1)}, u32[]{:S(2)}, u32[]{:S(2)}) collective-permute-start(bf16[160,1280]{1,0:T(8,128)(2,1)S(1)} %collective-permute-done), channel_id=1, source_target_pairs={{2,1},{1,0},{6,5},{5,4},{10,9},{9,8},{14,13},{13,12},{18,17},{17,1... | collective-permute-start | bytes 1228808 | tf_op jit(solution)/shard_map/ppermute | solution.py:87
  39.3 28.0 %collective-permute-start.3 = (bf16[160,1280]{1,0:T(8,128)(2,1)S(1)}, bf16[160,1280]{1,0:T(8,128)(2,1)S(1)}, u32[]{:S(2)}, u32[]{:S(2)}) collective-permute-start(bf16[160,1280]{1,0:T(8,128)(2,1)S(1)} %collective-permute-done.2), channel_id=1, source_target_pairs={{2,3},{6,7},{10,11},{14,15},{18,19},{22,23},{26,27},{30,31}} | collective-permute-start | bytes 1228808 | tf_op jit(solution)/shard_map/ppermute | solution.py:88
  40.8 42.0 %collective-permute-start.30 = (bf16[160,1280]{1,0:T(8,128)(2,1)S(1)}, bf16[160,1280]{1,0:T(8,128)(2,1)S(1)}, u32[]{:S(2)}, u32[]{:S(2)}) collective-permute-start(bf16[160,1280]{1,0:T(8,128)(2,1)S(1)} %collective-permute-done.29), channel_id=1, source_target_pairs={{2,3},{6,7},{10,11},{14,15},{18,19},{22,23},{26,27},{30,31}} | collective-permute-start | bytes 1228808 | tf_op jit(solution)/shard_map/ppermute | solution.py:88
  57.0 27.8 %collective-permute-start.32 = (bf16[160,1280]{1,0:T(8,128)(2,1)S(1)}, bf16[160,1280]{1,0:T(8,128)(2,1)S(1)}, u32[]{:S(2)}, u32[]{:S(2)}) collective-permute-start(bf16[160,1280]{1,0:T(8,128)(2,1)S(1)} %collective-permute-done.31), channel_id=1, source_target_pairs={{1,0},{5,4},{9,8},{13,12},{17,16},{21,20},{25,24},{29,28}} | collective-permute-start | bytes 1228808 | tf_op jit(solution)/shard_map/ppermute | solution.py:89
  136.2 21.5 %collective-permute-start.34 = (bf16[640,640]{1,0:T(8,128)(2,1)}, bf16[640,640]{1,0:T(8,128)(2,1)}, u32[]{:S(2)}, u32[]{:S(2)}) collective-permute-start(bf16[640,640]{1,0:T(8,128)(2,1)} %pad_maximum_fusion.7), channel_id=1, source_target_pairs={{0,8},{4,12},{8,0},{12,4},{1,9},{5,13},{9,1},{13,5},{2,10},{6,14},... | collective-permute-start | bytes 2457608 | tf_op jit(solution)/shard_map/ppermute | solution.py:57
  138.0 34.2 %collective-permute-start.33 = (bf16[640,640]{1,0:T(8,128)(2,1)}, bf16[640,640]{1,0:T(8,128)(2,1)}, u32[]{:S(2)}, u32[]{:S(2)}) collective-permute-start(bf16[640,640]{1,0:T(8,128)(2,1)} %pad_maximum_fusion.7), channel_id=1, source_target_pairs={{0,4},{4,0},{8,12},{12,8},{1,5},{5,1},{9,13},{13,9},{2,6},{6,2},{1... | collective-permute-start | bytes 2457608 | tf_op jit(solution)/shard_map/ppermute | solution.py:57
  145.6 26.6 %collective-permute-start.7 = (bf16[640,640]{1,0:T(8,128)(2,1)}, bf16[640,640]{1,0:T(8,128)(2,1)S(1)}, u32[]{:S(2)}, u32[]{:S(2)}) collective-permute-start(bf16[640,640]{1,0:T(8,128)(2,1)} %pad_maximum_fusion.6), channel_id=1, source_target_pairs={{0,8},{4,12},{8,0},{12,4},{1,9},{5,13},{9,1},{13,5},{2,10},{6,14},... | collective-permute-start | bytes 2457608 | tf_op jit(solution)/shard_map/ppermute | solution.py:57
  159.8 41.9 %collective-permute-start.6 = (bf16[640,640]{1,0:T(8,128)(2,1)}, bf16[640,640]{1,0:T(8,128)(2,1)S(1)}, u32[]{:S(2)}, u32[]{:S(2)}) collective-permute-start(bf16[640,640]{1,0:T(8,128)(2,1)} %pad_maximum_fusion.6), channel_id=1, source_target_pairs={{0,4},{4,0},{8,12},{12,8},{1,5},{5,1},{9,13},{13,9},{2,6},{6,2},{1... | collective-permute-start | bytes 2457608 | tf_op jit(solution)/shard_map/ppermute | solution.py:57
  172.1 29.5 %collective-permute-start.8 = (bf16[640,640]{1,0:T(8,128)(2,1)S(1)}, bf16[640,640]{1,0:T(8,128)(2,1)S(1)}, u32[]{:S(2)}, u32[]{:S(2)}) collective-permute-start(bf16[640,640]{1,0:T(8,128)(2,1)S(1)} %collective-permute-done.7), channel_id=1, source_target_pairs={{0,4},{4,0},{8,12},{12,8},{1,5},{5,1},{9,13},{13,9},{2,6},{6,2},{1... | collective-permute-start | bytes 2457608 | tf_op jit(solution)/shard_map/ppermute | solution.py:57
  199.6 32.9 %collective-permute-start.36 = (bf16[160,1280]{1,0:T(8,128)(2,1)S(1)}, bf16[160,1280]{1,0:T(8,128)(2,1)S(1)}, u32[]{:S(2)}, u32[]{:S(2)}) collective-permute-start(bf16[160,1280]{1,0:T(8,128)(2,1)S(1)} %get-tuple-element.272), channel_id=1, source_target_pairs={{0,1},{4,5},{8,9},{12,13},{16,17},{20,21},{24,25},{28,29}} | collective-permute-start | bytes 1228808 | tf_op jit(solution)/shard_map/ppermute | solution.py:101
  200.9 31.6 %collective-permute-start.39 = (bf16[160,1280]{1,0:T(8,128)(2,1)S(1)}, bf16[160,1280]{1,0:T(8,128)(2,1)S(1)}, u32[]{:S(2)}, u32[]{:S(2)}) collective-permute-start(bf16[160,1280]{1,0:T(8,128)(2,1)S(1)} %get-tuple-element.273), channel_id=1, source_target_pairs={{3,2},{7,6},{11,10},{15,14},{19,18},{23,22},{27,26},{31,30}} | collective-permute-start | bytes 1228808 | tf_op jit(solution)/shard_map/ppermute | solution.py:102
  232.7 17.7 %collective-permute-start.37 = (bf16[160,1280]{1,0:T(8,128)(2,1)S(1)}, bf16[160,1280]{1,0:T(8,128)(2,1)S(1)}, u32[]{:S(2)}, u32[]{:S(2)}) collective-permute-start(bf16[160,1280]{1,0:T(8,128)(2,1)S(1)} %get-tuple-element.270), channel_id=1, source_target_pairs={{0,1},{1,2},{4,5},{5,6},{8,9},{9,10},{12,13},{13,14},{16,17},{17,1... | collective-permute-start | bytes 1228808 | tf_op jit(solution)/shard_map/ppermute | solution.py:103
  234.0 16.4 %collective-permute-start.40 = (bf16[160,1280]{1,0:T(8,128)(2,1)S(1)}, bf16[160,1280]{1,0:T(8,128)(2,1)S(1)}, u32[]{:S(2)}, u32[]{:S(2)}) collective-permute-start(bf16[160,1280]{1,0:T(8,128)(2,1)S(1)} %get-tuple-element.271), channel_id=1, source_target_pairs={{3,2},{2,1},{7,6},{6,5},{11,10},{10,9},{15,14},{14,13},{19,18},{18... | collective-permute-start | bytes 1228808 | tf_op jit(solution)/shard_map/ppermute | solution.py:104
  241.8 17.4 %collective-permute-start.10 = (bf16[160,1280]{1,0:T(8,128)(2,1)S(1)}, bf16[160,1280]{1,0:T(8,128)(2,1)S(1)}, u32[]{:S(2)}, u32[]{:S(2)}) collective-permute-start(bf16[160,1280]{1,0:T(8,128)(2,1)S(1)} %get-tuple-element.276), channel_id=1, source_target_pairs={{0,1},{1,2},{4,5},{5,6},{8,9},{9,10},{12,13},{13,14},{16,17},{17,1... | collective-permute-start | bytes 1228808 | tf_op jit(solution)/shard_map/ppermute | solution.py:103
  250.6 17.4 %collective-permute-start.38 = (bf16[160,1280]{1,0:T(8,128)(2,1)S(1)}, bf16[160,1280]{1,0:T(8,128)(2,1)S(1)}, u32[]{:S(2)}, u32[]{:S(2)}) collective-permute-start(bf16[160,1280]{1,0:T(8,128)(2,1)S(1)} %get-tuple-element.268), channel_id=1, source_target_pairs={{0,1},{1,2},{2,3},{4,5},{5,6},{6,7},{8,9},{9,10},{10,11},{12,13},{... | collective-permute-start | bytes 1228808 | tf_op jit(solution)/shard_map/ppermute | solution.py:105
  259.4 17.2 %collective-permute-start.11 = (bf16[160,1280]{1,0:T(8,128)(2,1)S(1)}, bf16[160,1280]{1,0:T(8,128)(2,1)S(1)}, u32[]{:S(2)}, u32[]{:S(2)}) collective-permute-start(bf16[160,1280]{1,0:T(8,128)(2,1)S(1)} %get-tuple-element.274), channel_id=1, source_target_pairs={{0,1},{1,2},{2,3},{4,5},{5,6},{6,7},{8,9},{9,10},{10,11},{12,13},{... | collective-permute-start | bytes 1228808 | tf_op jit(solution)/shard_map/ppermute | solution.py:105
  392.5 17.4 %collective-permute-start.22 = (bf16[160,1280]{1,0:T(8,128)(2,1)S(1)}, bf16[160,1280]{1,0:T(8,128)(2,1)S(1)}, u32[]{:S(2)}, u32[]{:S(2)}) collective-permute-start(bf16[160,1280]{1,0:T(8,128)(2,1)S(1)} %get-tuple-element.258), channel_id=1, source_target_pairs={{0,1},{1,2},{4,5},{5,6},{8,9},{9,10},{12,13},{13,14},{16,17},{17,1... | collective-permute-start | bytes 1228808 | tf_op jit(solution)/shard_map/ppermute | solution.py:103
  401.3 17.4 %collective-permute-start.49 = (bf16[160,1280]{1,0:T(8,128)(2,1)S(1)}, bf16[160,1280]{1,0:T(8,128)(2,1)S(1)}, u32[]{:S(2)}, u32[]{:S(2)}) collective-permute-start(bf16[160,1280]{1,0:T(8,128)(2,1)S(1)} %get-tuple-element.264), channel_id=1, source_target_pairs={{0,1},{1,2},{4,5},{5,6},{8,9},{9,10},{12,13},{13,14},{16,17},{17,1... | collective-permute-start | bytes 1228808 | tf_op jit(solution)/shard_map/ppermute | solution.py:103
  526.9 119.0 %collective-permute-start.123 = (bf16[2,2,160,1280]{3,2,1,0:T(8,128)(2,1)S(1)}, bf16[2,2,160,1280]{3,2,1,0:T(8,128)(2,1)S(1)}, u32[]{:S(2)}, u32[]{:S(2)}) collective-permute-start(bf16[2,2,160,1280]{3,2,1,0:T(8,128)(2,1)S(1)} %dynamic-slice_bitcast_fusion), channel_id=1, source_target_pairs={{0,4},{4,0},{8,12},{12,8},{1,5},{5,1},{9,13},{13,9},{2,6},{6,2},{1... | collective-permute-start | bytes 4915208 | tf_op jit(solution)/shard_map/ppermute | solution.py:57
  575.6 17.6 %collective-permute-start.88 = (bf16[160,1280]{1,0:T(8,128)(2,1)S(1)}, bf16[160,1280]{1,0:T(8,128)(2,1)S(1)}, u32[]{:S(2)}, u32[]{:S(2)}) collective-permute-start(bf16[160,1280]{1,0:T(8,128)(2,1)S(1)} %get-tuple-element.246), channel_id=1, source_target_pairs={{0,1},{1,2},{4,5},{5,6},{8,9},{9,10},{12,13},{13,14},{16,17},{17,1... | collective-permute-start | bytes 1228808 | tf_op jit(solution)/shard_map/ppermute | solution.py:103
  577.0 16.3 %collective-permute-start.91 = (bf16[160,1280]{1,0:T(8,128)(2,1)S(1)}, bf16[160,1280]{1,0:T(8,128)(2,1)S(1)}, u32[]{:S(2)}, u32[]{:S(2)}) collective-permute-start(bf16[160,1280]{1,0:T(8,128)(2,1)S(1)} %get-tuple-element.247), channel_id=1, source_target_pairs={{3,2},{2,1},{7,6},{6,5},{11,10},{10,9},{15,14},{14,13},{19,18},{18... | collective-permute-start | bytes 1228808 | tf_op jit(solution)/shard_map/ppermute | solution.py:104
  584.7 17.4 %collective-permute-start.61 = (bf16[160,1280]{1,0:T(8,128)(2,1)S(1)}, bf16[160,1280]{1,0:T(8,128)(2,1)S(1)}, u32[]{:S(2)}, u32[]{:S(2)}) collective-permute-start(bf16[160,1280]{1,0:T(8,128)(2,1)S(1)} %get-tuple-element.252), channel_id=1, source_target_pairs={{0,1},{1,2},{4,5},{5,6},{8,9},{9,10},{12,13},{13,14},{16,17},{17,1... | collective-permute-start | bytes 1228808 | tf_op jit(solution)/shard_map/ppermute | solution.py:103
  593.5 17.3 %collective-permute-start.89 = (bf16[160,1280]{1,0:T(8,128)(2,1)S(1)}, bf16[160,1280]{1,0:T(8,128)(2,1)S(1)}, u32[]{:S(2)}, u32[]{:S(2)}) collective-permute-start(bf16[160,1280]{1,0:T(8,128)(2,1)S(1)} %get-tuple-element.244), channel_id=1, source_target_pairs={{0,1},{1,2},{2,3},{4,5},{5,6},{6,7},{8,9},{9,10},{10,11},{12,13},{... | collective-permute-start | bytes 1228808 | tf_op jit(solution)/shard_map/ppermute | solution.py:105
  610.8 37.5 %collective-permute-start.118 = (bf16[2,2,160,1280]{3,2,1,0:T(8,128)(2,1)S(1)}, bf16[2,2,160,1280]{3,2,1,0:T(8,128)(2,1)S(1)}, u32[]{:S(2)}, u32[]{:S(2)}) collective-permute-start(bf16[2,2,160,1280]{3,2,1,0:T(8,128)(2,1)S(1)} %dynamic-slice_bitcast_fusion.1), channel_id=1, source_target_pairs={{0,4},{4,0},{8,12},{12,8},{1,5},{5,1},{9,13},{13,9},{2,6},{6,2},{1... | collective-permute-start | bytes 4915208 | tf_op jit(solution)/shard_map/ppermute | solution.py:57
  610.8 39.6 %collective-permute-start.113 = (bf16[2,2,160,1280]{3,2,1,0:T(8,128)(2,1)S(1)}, bf16[2,2,160,1280]{3,2,1,0:T(8,128)(2,1)S(1)}, u32[]{:S(2)}, u32[]{:S(2)}) collective-permute-start(bf16[2,2,160,1280]{3,2,1,0:T(8,128)(2,1)S(1)} %dynamic-slice_bitcast_fusion.2), channel_id=1, source_target_pairs={{0,4},{4,0},{8,12},{12,8},{1,5},{5,1},{9,13},{13,9},{2,6},{6,2},{1... | collective-permute-start | bytes 4915208 | tf_op jit(solution)/shard_map/ppermute | solution.py:57
  625.1 42.0 %collective-permute-start.67 = (bf16[160,1280]{1,0:T(8,128)(2,1)S(1)}, bf16[160,1280]{1,0:T(8,128)(2,1)S(1)}, u32[]{:S(2)}, u32[]{:S(2)}) collective-permute-start(bf16[160,1280]{1,0:T(8,128)(2,1)S(1)} %get-tuple-element.181), channel_id=1, source_target_pairs={{0,1},{1,2},{2,3},{4,5},{5,6},{6,7},{8,9},{9,10},{10,11},{12,13},{... | collective-permute-start | bytes 1228808 | tf_op jit(solution)/shard_map/ppermute | solution.py:84
  643.7 24.9 %collective-permute-start.66 = (bf16[160,1280]{1,0:T(8,128)(2,1)S(1)}, bf16[160,1280]{1,0:T(8,128)(2,1)S(1)}, u32[]{:S(2)}, u32[]{:S(2)}) collective-permute-start(bf16[160,1280]{1,0:T(8,128)(2,1)S(1)} %get-tuple-element.181), channel_id=1, source_target_pairs={{3,2},{2,1},{1,0},{7,6},{6,5},{5,4},{11,10},{10,9},{9,8},{15,14},{... | collective-permute-start | bytes 1228808 | tf_op jit(solution)/shard_map/ppermute | solution.py:85
  648.3 21.0 %collective-permute-start.124 = (bf16[2,160,640]{2,1,0:T(8,128)(2,1)S(1)}, bf16[2,160,640]{2,1,0:T(8,128)(2,1)S(1)}, u32[]{:S(2)}, u32[]{:S(2)}) collective-permute-start(bf16[2,160,640]{2,1,0:T(8,128)(2,1)S(1)} %dynamic-slice_bitcast_fusion.5), channel_id=1, source_target_pairs={{0,8},{4,12},{8,0},{12,4},{1,9},{5,13},{9,1},{13,5},{2,10},{6,14},... | collective-permute-start | bytes 1228808 | tf_op jit(solution)/shard_map/ppermute | solution.py:57
  674.9 24.4 %collective-permute-start.125 = (bf16[160,640]{1,0:T(8,128)(2,1)S(1)}, bf16[160,640]{1,0:T(8,128)(2,1)S(1)}, u32[]{:S(2)}, u32[]{:S(2)}) collective-permute-start(bf16[160,640]{1,0:T(8,128)(2,1)S(1)} %dynamic-slice_bitcast_fusion.13), channel_id=1, source_target_pairs={{0,16},{16,0},{1,17},{17,1},{2,18},{18,2},{3,19},{19,3},{4,20},{20... | collective-permute-start | bytes 614408 | tf_op jit(solution)/shard_map/ppermute | solution.py:57
  679.6 21.3 %collective-permute-start.122 = (bf16[160,640]{1,0:T(8,128)(2,1)S(1)}, bf16[160,640]{1,0:T(8,128)(2,1)S(1)}, u32[]{:S(2)}, u32[]{:S(2)}) collective-permute-start(bf16[160,640]{1,0:T(8,128)(2,1)S(1)} %dynamic-slice_bitcast_fusion.14), channel_id=1, source_target_pairs={{0,8},{4,12},{8,0},{12,4},{1,9},{5,13},{9,1},{13,5},{2,10},{6,14},... | collective-permute-start | bytes 614408 | tf_op jit(solution)/shard_map/ppermute | solution.py:57
  683.3 23.7 %collective-permute-start.120 = (bf16[160,640]{1,0:T(8,128)(2,1)S(1)}, bf16[160,640]{1,0:T(8,128)(2,1)S(1)}, u32[]{:S(2)}, u32[]{:S(2)}) collective-permute-start(bf16[160,640]{1,0:T(8,128)(2,1)S(1)} %dynamic-slice_bitcast_fusion.15), channel_id=1, source_target_pairs={{0,16},{16,0},{1,17},{17,1},{2,18},{18,2},{3,19},{19,3},{4,20},{20... | collective-permute-start | bytes 614408 | tf_op jit(solution)/shard_map/ppermute | solution.py:57
  684.3 96.3 %collective-permute-start.117 = (bf16[160,640]{1,0:T(8,128)(2,1)}, bf16[160,640]{1,0:T(8,128)(2,1)}, u32[]{:S(2)}, u32[]{:S(2)}) collective-permute-start(bf16[160,640]{1,0:T(8,128)(2,1)} %dynamic-slice_bitcast_fusion.16), channel_id=1, source_target_pairs={{0,8},{4,12},{8,0},{12,4},{1,9},{5,13},{9,1},{13,5},{2,10},{6,14},... | collective-permute-start | bytes 614408 | tf_op jit(solution)/shard_map/ppermute | solution.py:57
  696.5 272.5 %collective-permute-start.115 = (bf16[160,640]{1,0:T(8,128)(2,1)}, bf16[160,640]{1,0:T(8,128)(2,1)}, u32[]{:S(2)}, u32[]{:S(2)}) collective-permute-start(bf16[160,640]{1,0:T(8,128)(2,1)} %dynamic-slice_bitcast_fusion.17), channel_id=1, source_target_pairs={{0,16},{16,0},{1,17},{17,1},{2,18},{18,2},{3,19},{19,3},{4,20},{20... | collective-permute-start | bytes 614408 | tf_op jit(solution)/shard_map/ppermute | solution.py:57
  780.6 42.2 %collective-permute-start.100 = (bf16[640,640]{1,0:T(8,128)(2,1)}, bf16[640,640]{1,0:T(8,128)(2,1)}, u32[]{:S(2)}, u32[]{:S(2)}) collective-permute-start(bf16[640,640]{1,0:T(8,128)(2,1)} %get-tuple-element.219), channel_id=1, source_target_pairs={{0,4},{4,0},{8,12},{12,8},{1,5},{5,1},{9,13},{13,9},{2,6},{6,2},{1... | collective-permute-start | bytes 2457608 | tf_op jit(solution)/shard_map/ppermute | solution.py:57
  785.1 49.1 %collective-permute-start.99 = (bf16[640,640]{1,0:T(8,128)(2,1)}, bf16[640,640]{1,0:T(8,128)(2,1)}, u32[]{:S(2)}, u32[]{:S(2)}) collective-permute-start(bf16[640,640]{1,0:T(8,128)(2,1)} %get-tuple-element.218), channel_id=1, source_target_pairs={{0,4},{4,0},{8,12},{12,8},{1,5},{5,1},{9,13},{13,9},{2,6},{6,2},{1... | collective-permute-start | bytes 2457608 | tf_op jit(solution)/shard_map/ppermute | solution.py:57
  825.3 21.4 %collective-permute-start.101 = (bf16[640,640]{1,0:T(8,128)(2,1)}, bf16[640,640]{1,0:T(8,128)(2,1)}, u32[]{:S(2)}, u32[]{:S(2)}) collective-permute-start(bf16[640,640]{1,0:T(8,128)(2,1)} %add_convert_fusion), channel_id=1, source_target_pairs={{0,8},{4,12},{8,0},{12,4},{1,9},{5,13},{9,1},{13,5},{2,10},{6,14},... | collective-permute-start | bytes 2457608 | tf_op jit(solution)/shard_map/ppermute | solution.py:57
  829.4 26.6 %collective-permute-start.72 = (bf16[640,640]{1,0:T(8,128)(2,1)}, bf16[640,640]{1,0:T(8,128)(2,1)}, u32[]{:S(2)}, u32[]{:S(2)}) collective-permute-start(bf16[640,640]{1,0:T(8,128)(2,1)} %get-tuple-element.216), channel_id=1, source_target_pairs={{0,4},{4,0},{8,12},{12,8},{1,5},{5,1},{9,13},{13,9},{2,6},{6,2},{1... | collective-permute-start | bytes 2457608 | tf_op jit(solution)/shard_map/ppermute | solution.py:57
  832.5 31.4 %collective-permute-start.74 = (bf16[640,640]{1,0:T(8,128)(2,1)}, bf16[640,640]{1,0:T(8,128)(2,1)}, u32[]{:S(2)}, u32[]{:S(2)}) collective-permute-start(bf16[640,640]{1,0:T(8,128)(2,1)} %add_convert_fusion.1), channel_id=1, source_target_pairs={{0,8},{4,12},{8,0},{12,4},{1,9},{5,13},{9,1},{13,5},{2,10},{6,14},... | collective-permute-start | bytes 2457608 | tf_op jit(solution)/shard_map/ppermute | solution.py:57
  888.0 38.2 %collective-permute-start.133 = (f32[320]{0:T(512)S(1)}, f32[320]{0:T(512)S(1)}, u32[]{:S(2)}, u32[]{:S(2)}) collective-permute-start(f32[320]{0:T(512)S(1)} %add_add_fusion.14), channel_id=1, source_target_pairs={{0,16},{16,0},{1,17},{17,1},{2,18},{18,2},{3,19},{19,3},{4,20},{20... | collective-permute-start | bytes 3848 | tf_op jit(solution)/shard_map/ppermute | solution.py:57
  913.8 73.4 %collective-permute-start.108 = (bf16[2,2,160,1280]{3,2,1,0:T(8,128)(2,1)S(1)}, bf16[2,2,160,1280]{3,2,1,0:T(8,128)(2,1)S(1)}, u32[]{:S(2)}, u32[]{:S(2)}) collective-permute-start(bf16[2,2,160,1280]{3,2,1,0:T(8,128)(2,1)S(1)} %dynamic-slice_bitcast_fusion.3), channel_id=1, source_target_pairs={{0,4},{4,0},{8,12},{12,8},{1,5},{5,1},{9,13},{13,9},{2,6},{6,2},{1... | collective-permute-start | bytes 4915208 | tf_op jit(solution)/shard_map/ppermute | solution.py:57
  931.8 41.8 %collective-permute-start.135 = (f32[320]{0:T(512)S(1)}, f32[320]{0:T(512)S(1)}, u32[]{:S(2)}, u32[]{:S(2)}) collective-permute-start(f32[320]{0:T(512)S(1)} %add.875), channel_id=1, source_target_pairs={{0,8},{4,12},{8,0},{12,4},{1,9},{5,13},{9,1},{13,5},{2,10},{6,14},... | collective-permute-start | bytes 3848 | tf_op jit(solution)/shard_map/ppermute | solution.py:57
  (228 other events, 2999.8 us)
Sparse Core Ops, SparseCore 0:
  10.5 35.5 all-gather.4
  48.0 32.8 all-gather.8
  82.8 32.8 all-gather.6
  298.9 41.5 all-gather.10

commit v4 on v3

--- a/solution.py
+++ b/solution.py
@@ -70,68 +70,29 @@
     return value
 
 
-def line_order():
-    size = lax.axis_size("tp")
+def group_order(axis):
+    size = lax.axis_size(axis)
     places = jnp.arange(size, dtype=jnp.int32)
-    if size != 4:
-        return places
-    return (places + lax.axis_index("tp")) % size
-
-
-def line_gather(own_block):
-    if lax.axis_size("tp") != 4:
-        return lax.all_gather(own_block, "tp", axis=0, tiled=True)
-    right_one = lax.ppermute(own_block, "tp", [(0, 1), (1, 2), (2, 3)])
-    left_one = lax.ppermute(own_block, "tp", [(3, 2), (2, 1), (1, 0)])
-    right_two = lax.ppermute(right_one, "tp", [(1, 2), (2, 3)])
-    left_two = lax.ppermute(left_one, "tp", [(2, 1), (1, 0)])
-    right_three = lax.ppermute(right_two, "tp", [(2, 3)])
-    left_three = lax.ppermute(left_two, "tp", [(1, 0)])
-    return jnp.concatenate(
-        [own_block, left_one + right_three, left_two + right_two, left_three + right_one], axis=0
-    )
-
-
-def line_scatter(partial_low):
-    if lax.axis_size("tp") != 4:
-        return lax.psum_scatter(partial_low, "tp", scatter_dimension=0, tiled=True).astype(
-            jnp.float32
-        )
-    own, one, two, three = jnp.split(partial_low, 4, axis=0)
-    right = lax.ppermute(three, "tp", [(0, 1)])
-    left = lax.ppermute(one, "tp", [(3, 2)])
-    right = lax.ppermute(add_low(right, two), "tp", [(0, 1), (1, 2)])
-    left = lax.ppermute(add_low(left, two), "tp", [(3, 2), (2, 1)])
-    right = lax.ppermute(add_low(right, one), "tp", [(0, 1), (1, 2), (2, 3)])
-    left = lax.ppermute(add_low(left, three), "tp", [(3, 2), (2, 1), (1, 0)])
-    return own.astype(jnp.float32) + right.astype(jnp.float32) + left.astype(jnp.float32)
-
-
-def tree_order():
-    size = lax.axis_size("ctx")
-    places = jnp.arange(size, dtype=jnp.int32)
-    if size != 4:
-        return places
-    return places ^ lax.axis_index("ctx")
-
-
-def tree_gather(own_block):
-    if lax.axis_size("ctx") != 4:
-        return lax.all_gather(own_block, "ctx", axis=0, tiled=True)
-    across = swap(own_block, "ctx", 2)
-    beside = swap(own_block, "ctx", 1)
-    return jnp.concatenate([own_block, beside, across, swap(across, "ctx", 1)], axis=0)
-
-
-def tree_scatter(partial_low):
-    if lax.axis_size("ctx") != 4:
-        return lax.psum_scatter(partial_low, "ctx", scatter_dimension=0, tiled=True).astype(
+    return places ^ lax.axis_index(axis) if size == 4 else places
+
+
+def group_gather(own_block, axis):
+    if lax.axis_size(axis) != 4:
+        return lax.all_gather(own_block, axis, axis=0, tiled=True)
+    across = swap(own_block, axis, 2)
+    beside = swap(own_block, axis, 1)
+    return jnp.concatenate([own_block, beside, across, swap(across, axis, 1)], axis=0)
+
+
+def group_scatter(partial_low, axis):
+    if lax.axis_size(axis) != 4:
+        return lax.psum_scatter(partial_low, axis, scatter_dimension=0, tiled=True).astype(
             jnp.float32
         )
     own, beside, across, far = jnp.split(partial_low, 4, axis=0)
-    across = add_low(across, swap(far, "ctx", 1))
-    beside = swap(beside, "ctx", 1)
-    across = swap(across, "ctx", 2)
+    far = swap(far, axis, 1)
+    beside = swap(beside, axis, 1)
+    across = swap(add_low(across, far), axis, 2)
     return own.astype(jnp.float32) + beside.astype(jnp.float32) + across.astype(jnp.float32)
 
 
@@ -169,8 +130,8 @@
 def row_labels(slots, group_size):
     tree_rows = group_size * lax.axis_size("ctx")
     chunk = group_size // lax.axis_size("tp")
-    within = (line_order()[:, None] * chunk + jnp.arange(chunk, dtype=jnp.int32)).reshape(-1)
-    keys = (tree_order()[:, None] * group_size + within[None, :]).reshape(-1)
+    within = (group_order("tp")[:, None] * chunk + jnp.arange(chunk, dtype=jnp.int32)).reshape(-1)
+    keys = (group_order("ctx")[:, None] * group_size + within[None, :]).reshape(-1)
     onehot = (keys[:, None] // SEG == jnp.arange(tree_rows // SEG, dtype=jnp.int32)[None, :])
     segment = jnp.sum(jnp.where(onehot, slots[None, :], 0), axis=1)
     offset = keys % SEG
@@ -388,7 +349,7 @@
 def forward_attention(gathered, vectors, tokens_own, parents, slots):
     w_query, w_key, w_value, w_attn_out = gathered[:4]
     alpha_attn, alpha_mlp, scale_qk, scale_up, scale_gate = vectors
-    hidden_group = line_gather(tokens_own)
+    hidden_group = group_gather(tokens_own, "tp")
     visible = visibility(parents, slots, hidden_group.shape[0])
     query_raw = jnp.dot(hidden_group, w_query, preferred_element_type=jnp.float32)
     key_raw = jnp.dot(hidden_group, w_key, preferred_element_type=jnp.float32)
@@ -398,9 +359,9 @@
     query_unit, key_unit = query_key(query_raw, key_raw, scale_qk)
     queries = query_unit.astype(jnp.bfloat16)
     keys_own = key_unit.astype(jnp.bfloat16)
-    keys_values = tree_gather(jnp.concatenate([keys_own, value_low], axis=1))
+    keys_values = group_gather(jnp.concatenate([keys_own, value_low], axis=1), "ctx")
     heads_low, scale = attend(queries, keys_values, *visible)
-    branch_one = line_scatter(contract_cols(heads_low, w_attn_out).astype(jnp.bfloat16))
+    branch_one = group_scatter(contract_cols(heads_low, w_attn_out).astype(jnp.bfloat16), "tp")
     kept = (
         hidden_group,
         visible,
@@ -419,15 +380,15 @@
     alpha_attn, alpha_mlp, scale_qk, scale_up, scale_gate = vectors
     tokens_wide = tokens_own.astype(jnp.float32)
     hidden_one = mix_rows(tokens_wide, branch_one, alpha_attn)
-    hidden_one_group = line_gather(hidden_one.astype(jnp.bfloat16))
+    hidden_one_group = group_gather(hidden_one.astype(jnp.bfloat16), "tp")
     up_raw = jnp.dot(hidden_one_group, w_up, preferred_element_type=jnp.float32)
     gate_raw = jnp.dot(hidden_one_group, w_gate, preferred_element_type=jnp.float32)
     mixed_low = middle(up_raw, gate_raw, scale_up, scale_gate).astype(jnp.bfloat16)
-    branch_two = line_scatter(contract_cols(mixed_low, w_down).astype(jnp.bfloat16))
+    branch_two = group_scatter(contract_cols(mixed_low, w_down).astype(jnp.bfloat16), "tp")
     output_wide, pull_out = jax.vjp(mix_rows, hidden_one, branch_two, alpha_mlp)
     upstream = cotangent_own.astype(jnp.float32)
     hidden_one_direct, branch_two_grad, grad_alpha_mlp = pull_out(upstream)
-    branch_two_group = line_gather(branch_two_grad.astype(jnp.bfloat16))
+    branch_two_group = group_gather(branch_two_grad.astype(jnp.bfloat16), "tp")
     mixed_grad = (
         jnp.dot(branch_two_group, w_down, preferred_element_type=jnp.float32)
         .astype(jnp.bfloat16)
@@ -437,8 +398,8 @@
     up_grad, gate_grad, grad_scale_up, grad_scale_gate = pull_mid(mixed_grad)
     up_low = up_grad.astype(jnp.bfloat16)
     gate_low = gate_grad.astype(jnp.bfloat16)
-    hidden_one_grad = hidden_one_direct + line_scatter(
-        (contract_cols(up_low, w_up) + contract_cols(gate_low, w_gate)).astype(jnp.bfloat16)
+    hidden_one_grad = hidden_one_direct + group_scatter(
+        (contract_cols(up_low, w_up) + contract_cols(gate_low, w_gate)).astype(jnp.bfloat16), "tp"
     )
     hidden_again, pull_in = jax.vjp(mix_rows, tokens_wide, branch_one, alpha_attn)
     tokens_direct, branch_one_grad, grad_alpha_attn = pull_in(hidden_one_grad)
@@ -460,14 +421,14 @@
         scale,
         heads_low,
     ) = kept
-    branch_one_group = line_gather(branch_one_grad.astype(jnp.bfloat16))
+    branch_one_group = group_gather(branch_one_grad.astype(jnp.bfloat16), "tp")
     heads_grad = jnp.dot(
         branch_one_group, w_attn_out, preferred_element_type=jnp.float32
     ).astype(jnp.bfloat16)
     query_grads, tree_grads = attend_grad(
         queries, heads_grad, heads_low, keys_values, *visible, scale
     )
-    key_own_grad, value_own_grad = jnp.split(tree_scatter(tree_grads), 2, axis=1)
+    key_own_grad, value_own_grad = jnp.split(group_scatter(tree_grads, "ctx"), 2, axis=1)
     unit_again, pull_qk = jax.vjp(query_key, query_raw, key_raw, scale_qk)
     query_raw_grad, key_raw_grad, grad_scale_qk = pull_qk((query_grads, key_own_grad))
     query_low = query_raw_grad.astype(jnp.bfloat16)
@@ -478,7 +439,7 @@
         + contract_cols(key_low, w_key)
         + contract_cols(value_grad_low, w_value)
     )
-    grad_tokens = tokens_direct + line_scatter(input_part.astype(jnp.bfloat16))
+    grad_tokens = tokens_direct + group_scatter(input_part.astype(jnp.bfloat16), "tp")
     factors = (hidden_group, query_low, key_low, value_grad_low, heads_low, branch_one_group)
     return grad_tokens, factors, grad_scale_qk
 

time: 1020 us -> 987 us (0.968)
  starting transfers between devices: 210 us -> 72.2 us
  waiting for transfers between devices: 349 us -> 456 us
  other arithmetic: 118 us -> 89.6 us
  local copies, waits for them, and re-layouts: 87.3 us -> 108 us
    ppermute x40 -> x88, waiting for transfers between devices: 83.1 us -> 454 us  [swap(): lax.ppermute(value, axis, [(place, place ^ bit) for place in range(size)])]
    ppermute x96 -> x0, waiting for transfers between devices: 265 us -> none  [the longest x8 58.6 us: line_gather(): left_two = lax.ppermute(left_one, 'tp', [(2, 1), (1, 0)])]
    ppermute x96 -> x0, starting transfers between devices: 175 us -> none  [the longest x8 37.7 us: line_scatter(): right = lax.ppermute(add_low(right, one), 'tp', [(0, 1), (1, 2), (2, 3)])]
    ppermute x40 -> x88, starting transfers between devices: 34.3 us -> 72 us  [swap(): lax.ppermute(value, axis, [(place, place ^ bit) for place in range(size)])]
    unnamed x28 -> x8, other arithmetic: 31 us -> 6.4 us
    unnamed x274 -> x270, local copies, waits for them, and re-layouts: 15.6 us -> 27.3 us
    concatenate x8 -> x4, other arithmetic: 26.4 us -> 22.6 us  [the longest x2 19.2 us: group_gather(): jnp.concatenate([own_block, beside, across, swap(across, axis, 1)], axis=0)]
  transfers between devices with their start and end apart: 140 -> 92, of which waited for: 67 -> 43; matrix products, arithmetic and copies ran while one was open for 30% -> 31% of each run, Pallas kernels for 10% -> 10%
where the time goes in v4:
time: 987 us; the launch traced here: 975 us
  waiting for transfers between devices  456 us (46%)
  matrix products  134 us (14%)
  local copies, waits for them, and re-layouts  108 us (11%)
  Pallas kernels  99 us (10%)
  other arithmetic  89.6 us (9%)
  starting transfers between devices  72.2 us (7%)
  between operations  16.6 us (2%)
    ppermute x88, waiting for transfers between devices, swap(): lax.ppermute(value, axis, [(place, place ^ bit) for place in range(size)])  454 us
    ppermute x88, starting transfers between devices, swap(): lax.ppermute(value, axis, [(place, place ^ bit) for place in range(size)])  72 us
    pallas_call x2, Pallas kernels, attend_grad(): pl.pallas_call(attend_grad_body, grid=(keys // KEY_TILE,), in_specs=[pl.B...  64.3 us
    pallas_call x2, Pallas kernels, attend(): pl.pallas_call(attend_body, grid=(keys // KEY_TILE,), in_specs=[pl.BlockS...  34.7 us
    dot_general x14, matrix products, contract_cols(): lax.dot_general(former, latter, (((1,), (1,)), ((), ())), preferred_eleme...  33.7 us
    dot_general x7, matrix products, contract_rows(): lax.dot_general(former, latter, (((0,), (0,)), ((), ())), preferred_eleme...  29.5 us
    unnamed x270, local copies, waits for them, and re-layouts  27.3 us
  transfers between devices with their start and end apart: 92, of which 43 were waited for; matrix products, arithmetic and copies ran while one was open for 31% of the time, Pallas kernels for 10%

profile of v4, /device:TPU:0, one launch (start us, length us, event | category | flops | bytes accessed | tf_op | source)
XLA Modules:
  0.0 975.0 jit_solution(16569627108891044211)
XLA Ops:
  25.4 11.4 %collective-permute-done.16 = bf16[160,1280]{1,0:T(8,128)(2,1)S(1)} collective-permute-done((bf16[160,1280]{1,0:T(8,128)(2,1)S(1)}, bf16[160,1280]{1,0:T(8,128)(2,1)S(1)}, u32[]{:S(2)}, u32[]{:S(2)}) %collective-permute-start.16) | collective-permute-done | bytes 409632 | tf_op jit(solution)/shard_map/ppermute | solution.py:57
  38.5 14.5 %collective-permute-done.1 = bf16[160,1280]{1,0:T(8,128)(2,1)} collective-permute-done((bf16[160,1280]{1,0:T(8,128)(2,1)}, bf16[160,1280]{1,0:T(8,128)(2,1)}, u32[]{:S(2)}, u32[]{:S(2)}) %collective-permute-start.1) | collective-permute-done | bytes 409632 | tf_op jit(solution)/shard_map/ppermute | solution.py:57
  53.6 9.6 collective-permute-done.17
  100.5 5.5 multiply_convert_fusion.6
  117.6 15.0 %collective-permute-done.19 = bf16[640,640]{1,0:T(8,128)(2,1)} collective-permute-done((bf16[640,640]{1,0:T(8,128)(2,1)}, bf16[640,640]{1,0:T(8,128)(2,1)}, u32[]{:S(2)}, u32[]{:S(2)}) %collective-permute-start.19) | collective-permute-done | bytes 819232 | tf_op jit(solution)/shard_map/ppermute | solution.py:57
  140.1 17.9 %collective-permute-done.4 = bf16[640,640]{1,0:T(8,128)(2,1)S(1)} collective-permute-done((bf16[640,640]{1,0:T(8,128)(2,1)}, bf16[640,640]{1,0:T(8,128)(2,1)S(1)}, u32[]{:S(2)}, u32[]{:S(2)}) %collective-permute-start.4) | collective-permute-done | bytes 819232 | tf_op jit(solution)/shard_map/ppermute | solution.py:57
  158.0 9.3 pad_maximum_fusion.1.tree_ref
  167.4 17.3 %attend.3 = (bf16[640,320]{1,0:T(8,128)(2,1)S(1)}, f32[8,640]{1,0:T(8,128)S(1)}) custom-call(bf16[640,320]{1,0:T(8,128)(2,1)S(1)} %get-tuple-element.238.query_ref, bf16[2560,640]{1,0:T(8,128)(2,1)S(1)} %pad_maximum_fusion.1.tree_ref, bf16[2560,128]{1,0:T(8,128)(2,1)S(1)} %get-tuple-element.222.hot_ref, bf16[3,128,640]{2,1,0:T(8,128)(2,1)S(1)} %get-tuple-element.216.side_ref), custom_call_target="tpu_custom_call" | custom-call | tf_op jit(solution)/shard_map/attend/pallas_call | solution.py:212
  188.0 9.9 %pad_maximum_fusion.tree_ref = bf16[2560,640]{1,0:T(8,128)(2,1)S(1)} fusion(bf16[640,640]{1,0:T(8,128)(2,1)S(1)} %collective-permute-done.5, bf16[640,640]{1,0:T(8,128)(2,1)S(1)} %collective-permute-done.4, bf16[640,640]{1,0:T(8,128)(2,1)S(1)} %collective-permute-done.3, bf16[640,320]{1,0:T(8,128)(2,1)S(1)} %copy-done.52, bf16[640,320]{1,0:T(8,128)(2,1)S(1)} %copy-done.49), kind=kLoop, calls=%fused_computation.19 | loop fusion | flops 16384000 | bytes 6553600 | tf_op jit(solution)/shard_map/concatenate | solution.py:84
  197.9 17.4 %attend.2 = (bf16[640,320]{1,0:T(8,128)(2,1)S(1)}, f32[8,640]{1,0:T(8,128)S(1)}) custom-call(bf16[640,320]{1,0:T(8,128)(2,1)S(1)} %get-tuple-element.240.query_ref, bf16[2560,640]{1,0:T(8,128)(2,1)S(1)} %pad_maximum_fusion.tree_ref, bf16[2560,128]{1,0:T(8,128)(2,1)S(1)} %get-tuple-element.223.hot_ref, bf16[3,128,640]{2,1,0:T(8,128)(2,1)S(1)} %get-tuple-element.217.side_ref), custom_call_target="tpu_custom_call" | custom-call | tf_op jit(solution)/shard_map/attend/pallas_call | solution.py:212
  222.0 23.5 %collective-permute-done.7 = bf16[160,1280]{1,0:T(8,128)(2,1)S(1)} collective-permute-done((bf16[160,1280]{1,0:T(8,128)(2,1)S(1)}, bf16[160,1280]{1,0:T(8,128)(2,1)S(1)}, u32[]{:S(2)}, u32[]{:S(2)}) %collective-permute-start.7) | collective-permute-done | bytes 409632 | tf_op jit(solution)/shard_map/ppermute | solution.py:57
  248.0 17.7 %collective-permute-done.8 = bf16[160,1280]{1,0:T(8,128)(2,1)S(1)} collective-permute-done((bf16[160,1280]{1,0:T(8,128)(2,1)S(1)}, bf16[160,1280]{1,0:T(8,128)(2,1)S(1)}, u32[]{:S(2)}, u32[]{:S(2)}) %collective-permute-start.8) | collective-permute-done | bytes 409632 | tf_op jit(solution)/shard_map/ppermute | solution.py:57
  271.3 17.0 %collective-permute-done.10 = bf16[160,1280]{1,0:T(8,128)(2,1)S(1)} collective-permute-done((bf16[160,1280]{1,0:T(8,128)(2,1)S(1)}, bf16[160,1280]{1,0:T(8,128)(2,1)S(1)}, u32[]{:S(2)}, u32[]{:S(2)}) %collective-permute-start.10) | collective-permute-done | bytes 409632 | tf_op jit(solution)/shard_map/ppermute | solution.py:57
  290.1 9.3 collective-permute-done.11
  305.0 16.7 %collective-permute-done.25 = bf16[160,1280]{1,0:T(8,128)(2,1)} collective-permute-done((bf16[160,1280]{1,0:T(8,128)(2,1)}, bf16[160,1280]{1,0:T(8,128)(2,1)}, u32[]{:S(2)}, u32[]{:S(2)}) %collective-permute-start.25) | collective-permute-done | bytes 409632 | tf_op jit(solution)/shard_map/ppermute | solution.py:57
  321.7 6.5 fusion.123
  333.3 5.4 fusion.121
  338.7 4.9 fusion.122
  345.3 6.4 multiply_convert_fusion.5
  351.8 4.9 convolution_convert_fusion.7
  363.3 19.0 %collective-permute-done.13 = bf16[160,1280]{1,0:T(8,128)(2,1)S(1)} collective-permute-done((bf16[160,1280]{1,0:T(8,128)(2,1)S(1)}, bf16[160,1280]{1,0:T(8,128)(2,1)S(1)}, u32[]{:S(2)}, u32[]{:S(2)}) %collective-permute-start.13) | collective-permute-done | bytes 409632 | tf_op jit(solution)/shard_map/ppermute | solution.py:57
  382.5 19.8 %collective-permute-done.28 = bf16[160,1280]{1,0:T(8,128)(2,1)S(1)} collective-permute-done((bf16[160,1280]{1,0:T(8,128)(2,1)S(1)}, bf16[160,1280]{1,0:T(8,128)(2,1)S(1)}, u32[]{:S(2)}, u32[]{:S(2)}) %collective-permute-start.28) | collective-permute-done | bytes 409632 | tf_op jit(solution)/shard_map/ppermute | solution.py:57
  404.6 16.1 %collective-permute-done.29 = bf16[160,1280]{1,0:T(8,128)(2,1)S(1)} collective-permute-done((bf16[160,1280]{1,0:T(8,128)(2,1)S(1)}, bf16[160,1280]{1,0:T(8,128)(2,1)S(1)}, u32[]{:S(2)}, u32[]{:S(2)}) %collective-permute-start.29) | collective-permute-done | bytes 409632 | tf_op jit(solution)/shard_map/ppermute | solution.py:57
  428.3 16.2 %collective-permute-done.31 = bf16[160,1280]{1,0:T(8,128)(2,1)S(1)} collective-permute-done((bf16[160,1280]{1,0:T(8,128)(2,1)S(1)}, bf16[160,1280]{1,0:T(8,128)(2,1)S(1)}, u32[]{:S(2)}, u32[]{:S(2)}) %collective-permute-start.31) | collective-permute-done | bytes 409632 | tf_op jit(solution)/shard_map/ppermute | solution.py:57
  444.7 11.1 %collective-permute-done.32 = bf16[160,1280]{1,0:T(8,128)(2,1)S(1)} collective-permute-done((bf16[160,1280]{1,0:T(8,128)(2,1)S(1)}, bf16[160,1280]{1,0:T(8,128)(2,1)S(1)}, u32[]{:S(2)}, u32[]{:S(2)}) %collective-permute-start.32) | collective-permute-done | bytes 409632 | tf_op jit(solution)/shard_map/ppermute | solution.py:57
  462.1 14.5 %collective-permute-done.46 = bf16[160,1280]{1,0:T(8,128)(2,1)S(1)} collective-permute-done((bf16[160,1280]{1,0:T(8,128)(2,1)S(1)}, bf16[160,1280]{1,0:T(8,128)(2,1)S(1)}, u32[]{:S(2)}, u32[]{:S(2)}) %collective-permute-start.46) | collective-permute-done | bytes 409632 | tf_op jit(solution)/shard_map/ppermute | solution.py:57
  476.6 11.3 %collective-permute-done.47 = bf16[160,1280]{1,0:T(8,128)(2,1)S(1)} collective-permute-done((bf16[160,1280]{1,0:T(8,128)(2,1)S(1)}, bf16[160,1280]{1,0:T(8,128)(2,1)S(1)}, u32[]{:S(2)}, u32[]{:S(2)}) %collective-permute-start.47) | collective-permute-done | bytes 409632 | tf_op jit(solution)/shard_map/ppermute | solution.py:57
  487.9 4.8 convolution_convert_fusion
  494.0 12.5 %multiply_reduce_fusion.2 = (f32[1280]{0:T(1024)S(1)}, f32[1280]{0:T(1024)S(1)}, f32[1280]{0:T(1024)S(1)}, f32[1280]{0:T(1024)S(1)}, f32[640,1280]{1,0:T(8,128)S...) fusion(f32[640,1280]{1,0:T(8,128)} %copy-done.123, ...), kind=kOutput, calls=%fused_computation.40 | convolution fusion | flops 2138926080 | bytes 29521920 | tf_op jit(solution)/shard_map/dot_general | solution.py:393
  507.2 6.6 convolution_convert_fusion.1
  513.8 6.6 convolution_convert_fusion.2
  541.8 8.5 collective-permute-done.49
  550.9 25.3 %collective-permute-done.34 = bf16[160,1280]{1,0:T(8,128)(2,1)S(1)} collective-permute-done((bf16[160,1280]{1,0:T(8,128)(2,1)S(1)}, bf16[160,1280]{1,0:T(8,128)(2,1)S(1)}, u32[]{:S(2)}, u32[]{:S(2)}) %collective-permute-start.34) | collective-permute-done | bytes 409632 | tf_op jit(solution)/shard_map/ppermute | solution.py:57
  576.7 19.4 %collective-permute-done.35 = bf16[160,1280]{1,0:T(8,128)(2,1)S(1)} collective-permute-done((bf16[160,1280]{1,0:T(8,128)(2,1)S(1)}, bf16[160,1280]{1,0:T(8,128)(2,1)S(1)}, u32[]{:S(2)}, u32[]{:S(2)}) %collective-permute-start.35) | collective-permute-done | bytes 409632 | tf_op jit(solution)/shard_map/ppermute | solution.py:57
  609.6 14.9 %collective-permute-done.83 = f32[2560]{0:T(1024)S(1)} collective-permute-done((f32[2560]{0:T(1024)S(1)}, f32[2560]{0:T(1024)S(1)}, u32[]{:S(2)}, u32[]{:S(2)}) %collective-permute-start.83) | collective-permute-done | bytes 10272 | tf_op jit(solution)/shard_map/ppermute | solution.py:57
  664.8 9.9 %collective-permute-done.51 = bf16[160,1280]{1,0:T(8,128)(2,1)S(1)} collective-permute-done((bf16[160,1280]{1,0:T(8,128)(2,1)}, bf16[160,1280]{1,0:T(8,128)(2,1)S(1)}, u32[]{:S(2)}, u32[]{:S(2)}) %collective-permute-start.51) | collective-permute-done | bytes 409632 | tf_op jit(solution)/shard_map/ppermute | solution.py:57
  696.4 32.2 %attend_grad.3 = (f32[640,320]{1,0:T(8,128)S(1)}, bf16[2560,640]{1,0:T(8,128)(2,1)}) custom-call(bf16[640,640]{1,0:T(8,128)(2,1)S(1)} %get-tuple-element.260.both_ref, bf16[640,320]{1,0:T(8,128)(2,1)S(1)} %copy-done.8, bf16[2560,640]{1,0:T(8,128)(2,1)} %copy-done.1, bf16[2560,128]{1,0:T(8,128)(2,1)S(1)} %get-tuple-element.222.hot_ref, ...), custom_call_target="tpu_custom_call" | custom-call | tf_op jit(solution)/shard_map/attend_grad/pallas_call | solution.py:297
  738.6 32.2 %attend_grad.2 = (f32[640,320]{1,0:T(8,128)S(1)}, bf16[2560,640]{1,0:T(8,128)(2,1)}) custom-call(bf16[640,640]{1,0:T(8,128)(2,1)S(1)} %copy-done.6, bf16[640,320]{1,0:T(8,128)(2,1)S(1)} %copy-done.11, bf16[2560,640]{1,0:T(8,128)(2,1)} %copy-done, bf16[2560,128]{1,0:T(8,128)(2,1)S(1)} %get-tuple-element.223.hot_ref, bf16[3,128,640]{2,1,0:T(8,128)(2,1)S(1)} %copy-done.3, ...), custom_call_target="tpu_custom_call" | custom-call | tf_op jit(solution)/shard_map/attend_grad/pallas_call | solution.py:297
  785.1 12.4 %collective-permute-done.56 = bf16[640,640]{1,0:T(8,128)(2,1)} collective-permute-done((bf16[640,640]{1,0:T(8,128)(2,1)}, bf16[640,640]{1,0:T(8,128)(2,1)}, u32[]{:S(2)}, u32[]{:S(2)}) %collective-permute-start.56) | collective-permute-done | bytes 819232 | tf_op jit(solution)/shard_map/ppermute | solution.py:57
  807.0 7.6 collective-permute-done.41
  831.4 6.6 multiply_reduce_fusion.4
  851.1 4.5 convolution_convert_fusion.12
  857.8 6.1 concatenate.136
  878.3 13.9 %collective-permute-done.43 = bf16[160,1280]{1,0:T(8,128)(2,1)S(1)} collective-permute-done((bf16[160,1280]{1,0:T(8,128)(2,1)S(1)}, bf16[160,1280]{1,0:T(8,128)(2,1)S(1)}, u32[]{:S(2)}, u32[]{:S(2)}) %collective-permute-start.43) | collective-permute-done | bytes 409632 | tf_op jit(solution)/shard_map/ppermute | solution.py:57
  892.7 16.1 %collective-permute-done.58 = bf16[160,1280]{1,0:T(8,128)(2,1)S(1)} collective-permute-done((bf16[160,1280]{1,0:T(8,128)(2,1)S(1)}, bf16[160,1280]{1,0:T(8,128)(2,1)S(1)}, u32[]{:S(2)}, u32[]{:S(2)}) %collective-permute-start.58) | collective-permute-done | bytes 409632 | tf_op jit(solution)/shard_map/ppermute | solution.py:57
  915.8 22.7 %collective-permute-done.44 = bf16[160,1280]{1,0:T(8,128)(2,1)S(1)} collective-permute-done((bf16[160,1280]{1,0:T(8,128)(2,1)S(1)}, bf16[160,1280]{1,0:T(8,128)(2,1)S(1)}, u32[]{:S(2)}, u32[]{:S(2)}) %collective-permute-start.44) | collective-permute-done | bytes 409632 | tf_op jit(solution)/shard_map/ppermute | solution.py:57
  938.5 8.7 collective-permute-done.59
  952.4 7.5 collective-permute-done.61
  (675 shorter events, 331.5 us)
Async XLA Ops:
  7.2 56.0 %all-gather.5.cloned.1.call-start = ((), (), s32[]{:S(2)}) async-start(), calls=%async_computation | async-start | bytes 3686400 | tf_op jit(solution)/shard_map/all_gather | solution.py:471
  9.4 312.3 %all-gather.9.cloned.1.call-start = ((), (), s32[]{:S(2)}) async-start(), calls=%async_computation.2 | async-start | bytes 3686400 | tf_op jit(solution)/shard_map/all_gather | solution.py:471
  10.1 328.5 %all-gather.7.cloned.1.call-start = ((), (), s32[]{:S(2)}) async-start(), calls=%async_computation.1 | async-start | bytes 3686400 | tf_op jit(solution)/shard_map/all_gather | solution.py:471
  10.9 340.9 %all-gather.11.cloned.1.call-start = ((), (), s32[]{:S(2)}) async-start(), calls=%async_computation.3 | async-start | bytes 3686400 | tf_op jit(solution)/shard_map/all_gather | solution.py:471
  12.8 24.0 %collective-permute-start.16 = (bf16[160,1280]{1,0:T(8,128)(2,1)S(1)}, bf16[160,1280]{1,0:T(8,128)(2,1)S(1)}, u32[]{:S(2)}, u32[]{:S(2)}) collective-permute-start(bf16[160,1280]{1,0:T(8,128)(2,1)S(1)} %get-tuple-element.210), channel_id=1, source_target_pairs={{0,2},{1,3},{2,0},{3,1},{4,6},{5,7},{6,4},{7,5},{8,10},{9,11},{10,... | collective-permute-start | bytes 1228808 | tf_op jit(solution)/shard_map/ppermute | solution.py:57
  16.9 36.7 %collective-permute-start.15 = (bf16[160,1280]{1,0:T(8,128)(2,1)S(1)}, bf16[160,1280]{1,0:T(8,128)(2,1)S(1)}, u32[]{:S(2)}, u32[]{:S(2)}) collective-permute-start(bf16[160,1280]{1,0:T(8,128)(2,1)S(1)} %get-tuple-element.210), channel_id=1, source_target_pairs={{0,1},{1,0},{2,3},{3,2},{4,5},{5,4},{6,7},{7,6},{8,9},{9,8},{10,11... | collective-permute-start | bytes 1228808 | tf_op jit(solution)/shard_map/ppermute | solution.py:57
  18.5 34.5 %collective-permute-start.1 = (bf16[160,1280]{1,0:T(8,128)(2,1)}, bf16[160,1280]{1,0:T(8,128)(2,1)}, u32[]{:S(2)}, u32[]{:S(2)}) collective-permute-start(bf16[160,1280]{1,0:T(8,128)(2,1)} %get-tuple-element.211), channel_id=1, source_target_pairs={{0,2},{1,3},{2,0},{3,1},{4,6},{5,7},{6,4},{7,5},{8,10},{9,11},{10,... | collective-permute-start | bytes 1228808 | tf_op jit(solution)/shard_map/ppermute | solution.py:57
  18.8 47.8 %collective-permute-start = (bf16[160,1280]{1,0:T(8,128)(2,1)}, bf16[160,1280]{1,0:T(8,128)(2,1)}, u32[]{:S(2)}, u32[]{:S(2)}) collective-permute-start(bf16[160,1280]{1,0:T(8,128)(2,1)} %get-tuple-element.211), channel_id=1, source_target_pairs={{0,1},{1,0},{2,3},{3,2},{4,5},{5,4},{6,7},{7,6},{8,9},{9,8},{10,11... | collective-permute-start | bytes 1228808 | tf_op jit(solution)/shard_map/ppermute | solution.py:57
  36.9 26.4 %collective-permute-start.17 = (bf16[160,1280]{1,0:T(8,128)(2,1)S(1)}, bf16[160,1280]{1,0:T(8,128)(2,1)S(1)}, u32[]{:S(2)}, u32[]{:S(2)}) collective-permute-start(bf16[160,1280]{1,0:T(8,128)(2,1)S(1)} %collective-permute-done.16), channel_id=1, source_target_pairs={{0,1},{1,0},{2,3},{3,2},{4,5},{5,4},{6,7},{7,6},{8,9},{9,8},{10,11... | collective-permute-start | bytes 1228808 | tf_op jit(solution)/shard_map/ppermute | solution.py:57
  107.1 25.5 %collective-permute-start.19 = (bf16[640,640]{1,0:T(8,128)(2,1)}, bf16[640,640]{1,0:T(8,128)(2,1)}, u32[]{:S(2)}, u32[]{:S(2)}) collective-permute-start(bf16[640,640]{1,0:T(8,128)(2,1)} %pad_maximum_fusion.7), channel_id=1, source_target_pairs={{0,8},{4,12},{8,0},{12,4},{1,9},{5,13},{9,1},{13,5},{2,10},{6,14},... | collective-permute-start | bytes 2457608 | tf_op jit(solution)/shard_map/ppermute | solution.py:57
  109.3 48.8 %collective-permute-start.18 = (bf16[640,640]{1,0:T(8,128)(2,1)}, bf16[640,640]{1,0:T(8,128)(2,1)}, u32[]{:S(2)}, u32[]{:S(2)}) collective-permute-start(bf16[640,640]{1,0:T(8,128)(2,1)} %pad_maximum_fusion.7), channel_id=1, source_target_pairs={{0,4},{4,0},{8,12},{12,8},{1,5},{5,1},{9,13},{13,9},{2,6},{6,2},{1... | collective-permute-start | bytes 2457608 | tf_op jit(solution)/shard_map/ppermute | solution.py:57
  117.0 41.1 %collective-permute-start.4 = (bf16[640,640]{1,0:T(8,128)(2,1)}, bf16[640,640]{1,0:T(8,128)(2,1)S(1)}, u32[]{:S(2)}, u32[]{:S(2)}) collective-permute-start(bf16[640,640]{1,0:T(8,128)(2,1)} %pad_maximum_fusion.6), channel_id=1, source_target_pairs={{0,8},{4,12},{8,0},{12,4},{1,9},{5,13},{9,1},{13,5},{2,10},{6,14},... | collective-permute-start | bytes 2457608 | tf_op jit(solution)/shard_map/ppermute | solution.py:57
  132.6 25.4 %collective-permute-start.20 = (bf16[640,640]{1,0:T(8,128)(2,1)}, bf16[640,640]{1,0:T(8,128)(2,1)S(1)}, u32[]{:S(2)}, u32[]{:S(2)}) collective-permute-start(bf16[640,640]{1,0:T(8,128)(2,1)} %collective-permute-done.19), channel_id=1, source_target_pairs={{0,4},{4,0},{8,12},{12,8},{1,5},{5,1},{9,13},{13,9},{2,6},{6,2},{1... | collective-permute-start | bytes 2457608 | tf_op jit(solution)/shard_map/ppermute | solution.py:57
  139.6 48.4 %collective-permute-start.3 = (bf16[640,640]{1,0:T(8,128)(2,1)}, bf16[640,640]{1,0:T(8,128)(2,1)S(1)}, u32[]{:S(2)}, u32[]{:S(2)}) collective-permute-start(bf16[640,640]{1,0:T(8,128)(2,1)} %pad_maximum_fusion.6), channel_id=1, source_target_pairs={{0,4},{4,0},{8,12},{12,8},{1,5},{5,1},{9,13},{13,9},{2,6},{6,2},{1... | collective-permute-start | bytes 2457608 | tf_op jit(solution)/shard_map/ppermute | solution.py:57
  158.0 30.0 %collective-permute-start.5 = (bf16[640,640]{1,0:T(8,128)(2,1)S(1)}, bf16[640,640]{1,0:T(8,128)(2,1)S(1)}, u32[]{:S(2)}, u32[]{:S(2)}) collective-permute-start(bf16[640,640]{1,0:T(8,128)(2,1)S(1)} %collective-permute-done.4), channel_id=1, source_target_pairs={{0,4},{4,0},{8,12},{12,8},{1,5},{5,1},{9,13},{13,9},{2,6},{6,2},{1... | collective-permute-start | bytes 2457608 | tf_op jit(solution)/shard_map/ppermute | solution.py:57
  185.9 61.8 %collective-permute-start.21 = (bf16[160,1280]{1,0:T(8,128)(2,1)S(1)}, bf16[160,1280]{1,0:T(8,128)(2,1)S(1)}, u32[]{:S(2)}, u32[]{:S(2)}) collective-permute-start(bf16[160,1280]{1,0:T(8,128)(2,1)S(1)} %get-tuple-element.196), channel_id=1, source_target_pairs={{0,1},{1,0},{2,3},{3,2},{4,5},{5,4},{6,7},{7,6},{8,9},{9,8},{10,11... | collective-permute-start | bytes 1228808 | tf_op jit(solution)/shard_map/ppermute | solution.py:57
  187.2 31.4 %collective-permute-start.22 = (bf16[160,1280]{1,0:T(8,128)(2,1)S(1)}, bf16[160,1280]{1,0:T(8,128)(2,1)}, u32[]{:S(2)}, u32[]{:S(2)}) collective-permute-start(bf16[160,1280]{1,0:T(8,128)(2,1)S(1)} %get-tuple-element.197), channel_id=1, source_target_pairs={{0,1},{1,0},{2,3},{3,2},{4,5},{5,4},{6,7},{7,6},{8,9},{9,8},{10,11... | collective-permute-start | bytes 1228808 | tf_op jit(solution)/shard_map/ppermute | solution.py:57
  216.6 31.4 %collective-permute-start.6 = (bf16[160,1280]{1,0:T(8,128)(2,1)S(1)}, bf16[160,1280]{1,0:T(8,128)(2,1)S(1)}, u32[]{:S(2)}, u32[]{:S(2)}) collective-permute-start(bf16[160,1280]{1,0:T(8,128)(2,1)S(1)} %get-tuple-element.198), channel_id=1, source_target_pairs={{0,1},{1,0},{2,3},{3,2},{4,5},{5,4},{6,7},{7,6},{8,9},{9,8},{10,11... | collective-permute-start | bytes 1228808 | tf_op jit(solution)/shard_map/ppermute | solution.py:57
  217.9 27.5 %collective-permute-start.7 = (bf16[160,1280]{1,0:T(8,128)(2,1)S(1)}, bf16[160,1280]{1,0:T(8,128)(2,1)S(1)}, u32[]{:S(2)}, u32[]{:S(2)}) collective-permute-start(bf16[160,1280]{1,0:T(8,128)(2,1)S(1)} %get-tuple-element.199), channel_id=1, source_target_pairs={{0,1},{1,0},{2,3},{3,2},{4,5},{5,4},{6,7},{7,6},{8,9},{9,8},{10,11... | collective-permute-start | bytes 1228808 | tf_op jit(solution)/shard_map/ppermute | solution.py:57
  219.8 27.9 %collective-permute-start.23 = (bf16[160,1280]{1,0:T(8,128)(2,1)S(1)}, bf16[160,1280]{1,0:T(8,128)(2,1)S(1)}, u32[]{:S(2)}, u32[]{:S(2)}) collective-permute-start(bf16[160,1280]{1,0:T(8,128)(2,1)S(1)} %add_convert_fusion.7), channel_id=1, source_target_pairs={{0,2},{1,3},{2,0},{3,1},{4,6},{5,7},{6,4},{7,5},{8,10},{9,11},{10,... | collective-permute-start | bytes 1228808 | tf_op jit(solution)/shard_map/ppermute | solution.py:57
  303.2 25.0 %collective-permute-start.24 = (bf16[160,1280]{1,0:T(8,128)(2,1)}, bf16[160,1280]{1,0:T(8,128)(2,1)}, u32[]{:S(2)}, u32[]{:S(2)}) collective-permute-start(bf16[160,1280]{1,0:T(8,128)(2,1)} %get-tuple-element.139), channel_id=1, source_target_pairs={{0,1},{1,0},{2,3},{3,2},{4,5},{5,4},{6,7},{7,6},{8,9},{9,8},{10,11... | collective-permute-start | bytes 1228808 | tf_op jit(solution)/shard_map/ppermute | solution.py:57
  356.7 47.6 %collective-permute-start.12 = (bf16[160,1280]{1,0:T(8,128)(2,1)S(1)}, bf16[160,1280]{1,0:T(8,128)(2,1)S(1)}, u32[]{:S(2)}, u32[]{:S(2)}) collective-permute-start(bf16[160,1280]{1,0:T(8,128)(2,1)S(1)} %get-tuple-element.192), channel_id=1, source_target_pairs={{0,1},{1,0},{2,3},{3,2},{4,5},{5,4},{6,7},{7,6},{8,9},{9,8},{10,11... | collective-permute-start | bytes 1228808 | tf_op jit(solution)/shard_map/ppermute | solution.py:57
  357.1 25.3 %collective-permute-start.13 = (bf16[160,1280]{1,0:T(8,128)(2,1)S(1)}, bf16[160,1280]{1,0:T(8,128)(2,1)S(1)}, u32[]{:S(2)}, u32[]{:S(2)}) collective-permute-start(bf16[160,1280]{1,0:T(8,128)(2,1)S(1)} %get-tuple-element.193), channel_id=1, source_target_pairs={{0,1},{1,0},{2,3},{3,2},{4,5},{5,4},{6,7},{7,6},{8,9},{9,8},{10,11... | collective-permute-start | bytes 1228808 | tf_op jit(solution)/shard_map/ppermute | solution.py:57
  361.2 43.3 %collective-permute-start.27 = (bf16[160,1280]{1,0:T(8,128)(2,1)S(1)}, bf16[160,1280]{1,0:T(8,128)(2,1)S(1)}, u32[]{:S(2)}, u32[]{:S(2)}) collective-permute-start(bf16[160,1280]{1,0:T(8,128)(2,1)S(1)} %get-tuple-element.194), channel_id=1, source_target_pairs={{0,1},{1,0},{2,3},{3,2},{4,5},{5,4},{6,7},{7,6},{8,9},{9,8},{10,11... | collective-permute-start | bytes 1228808 | tf_op jit(solution)/shard_map/ppermute | solution.py:57
  361.6 40.7 %collective-permute-start.28 = (bf16[160,1280]{1,0:T(8,128)(2,1)S(1)}, bf16[160,1280]{1,0:T(8,128)(2,1)S(1)}, u32[]{:S(2)}, u32[]{:S(2)}) collective-permute-start(bf16[160,1280]{1,0:T(8,128)(2,1)S(1)} %get-tuple-element.195), channel_id=1, source_target_pairs={{0,1},{1,0},{2,3},{3,2},{4,5},{5,4},{6,7},{7,6},{8,9},{9,8},{10,11... | collective-permute-start | bytes 1228808 | tf_op jit(solution)/shard_map/ppermute | solution.py:57
  382.4 21.8 %collective-permute-start.14 = (bf16[160,1280]{1,0:T(8,128)(2,1)S(1)}, bf16[160,1280]{1,0:T(8,128)(2,1)S(1)}, u32[]{:S(2)}, u32[]{:S(2)}) collective-permute-start(bf16[160,1280]{1,0:T(8,128)(2,1)S(1)} %add_convert_fusion.8), channel_id=1, source_target_pairs={{0,2},{1,3},{2,0},{3,1},{4,6},{5,7},{6,4},{7,5},{8,10},{9,11},{10,... | collective-permute-start | bytes 1228808 | tf_op jit(solution)/shard_map/ppermute | solution.py:57
  494.0 135.8 %collective-permute-start.75 = (bf16[2,2,160,1280]{3,2,1,0:T(8,128)(2,1)}, bf16[2,2,160,1280]{3,2,1,0:T(8,128)(2,1)S(1)}, u32[]{:S(2)}, u32[]{:S(2)}) collective-permute-start(bf16[2,2,160,1280]{3,2,1,0:T(8,128)(2,1)} %dynamic-slice_bitcast_fusion), channel_id=1, source_target_pairs={{0,4},{4,0},{8,12},{12,8},{1,5},{5,1},{9,13},{13,9},{2,6},{6,2},{1... | collective-permute-start | bytes 4915208 | tf_op jit(solution)/shard_map/ppermute | solution.py:57
  529.2 47.5 %collective-permute-start.48 = (bf16[160,1280]{1,0:T(8,128)(2,1)S(1)}, bf16[160,1280]{1,0:T(8,128)(2,1)S(1)}, u32[]{:S(2)}, u32[]{:S(2)}) collective-permute-start(bf16[160,1280]{1,0:T(8,128)(2,1)S(1)} %get-tuple-element.188), channel_id=1, source_target_pairs={{0,1},{1,0},{2,3},{3,2},{4,5},{5,4},{6,7},{7,6},{8,9},{9,8},{10,11... | collective-permute-start | bytes 1228808 | tf_op jit(solution)/shard_map/ppermute | solution.py:57
  539.6 37.1 %collective-permute-start.33 = (bf16[160,1280]{1,0:T(8,128)(2,1)S(1)}, bf16[160,1280]{1,0:T(8,128)(2,1)S(1)}, u32[]{:S(2)}, u32[]{:S(2)}) collective-permute-start(bf16[160,1280]{1,0:T(8,128)(2,1)S(1)} %get-tuple-element.190), channel_id=1, source_target_pairs={{0,1},{1,0},{2,3},{3,2},{4,5},{5,4},{6,7},{7,6},{8,9},{9,8},{10,11... | collective-permute-start | bytes 1228808 | tf_op jit(solution)/shard_map/ppermute | solution.py:57
  539.9 36.3 %collective-permute-start.34 = (bf16[160,1280]{1,0:T(8,128)(2,1)S(1)}, bf16[160,1280]{1,0:T(8,128)(2,1)S(1)}, u32[]{:S(2)}, u32[]{:S(2)}) collective-permute-start(bf16[160,1280]{1,0:T(8,128)(2,1)S(1)} %get-tuple-element.191), channel_id=1, source_target_pairs={{0,1},{1,0},{2,3},{3,2},{4,5},{5,4},{6,7},{7,6},{8,9},{9,8},{10,11... | collective-permute-start | bytes 1228808 | tf_op jit(solution)/shard_map/ppermute | solution.py:57
  550.4 26.3 %collective-permute-start.50 = (bf16[160,1280]{1,0:T(8,128)(2,1)S(1)}, bf16[160,1280]{1,0:T(8,128)(2,1)S(1)}, u32[]{:S(2)}, u32[]{:S(2)}) collective-permute-start(bf16[160,1280]{1,0:T(8,128)(2,1)S(1)} %add_convert_fusion.3), channel_id=1, source_target_pairs={{0,2},{1,3},{2,0},{3,1},{4,6},{5,7},{6,4},{7,5},{8,10},{9,11},{10,... | collective-permute-start | bytes 1228808 | tf_op jit(solution)/shard_map/ppermute | solution.py:57
  576.6 57.7 %collective-permute-start.70 = (bf16[2,2,160,1280]{3,2,1,0:T(8,128)(2,1)S(1)}, bf16[2,2,160,1280]{3,2,1,0:T(8,128)(2,1)S(1)}, u32[]{:S(2)}, u32[]{:S(2)}) collective-permute-start(bf16[2,2,160,1280]{3,2,1,0:T(8,128)(2,1)S(1)} %dynamic-slice_bitcast_fusion.1), channel_id=1, source_target_pairs={{0,4},{4,0},{8,12},{12,8},{1,5},{5,1},{9,13},{13,9},{2,6},{6,2},{1... | collective-permute-start | bytes 4915208 | tf_op jit(solution)/shard_map/ppermute | solution.py:57
  602.8 26.9 %collective-permute-start.37 = (bf16[160,1280]{1,0:T(8,128)(2,1)S(1)}, bf16[160,1280]{1,0:T(8,128)(2,1)S(1)}, u32[]{:S(2)}, u32[]{:S(2)}) collective-permute-start(bf16[160,1280]{1,0:T(8,128)(2,1)S(1)} %get-tuple-element.145), channel_id=1, source_target_pairs={{0,2},{1,3},{2,0},{3,1},{4,6},{5,7},{6,4},{7,5},{8,10},{9,11},{10,... | collective-permute-start | bytes 1228808 | tf_op jit(solution)/shard_map/ppermute | solution.py:57
  602.9 26.8 %collective-permute-start.36 = (bf16[160,1280]{1,0:T(8,128)(2,1)S(1)}, bf16[160,1280]{1,0:T(8,128)(2,1)S(1)}, u32[]{:S(2)}, u32[]{:S(2)}) collective-permute-start(bf16[160,1280]{1,0:T(8,128)(2,1)S(1)} %get-tuple-element.145), channel_id=1, source_target_pairs={{0,1},{1,0},{2,3},{3,2},{4,5},{5,4},{6,7},{7,6},{8,9},{9,8},{10,11... | collective-permute-start | bytes 1228808 | tf_op jit(solution)/shard_map/ppermute | solution.py:57
  633.8 22.9 %collective-permute-start.76 = (bf16[2,160,640]{2,1,0:T(8,128)(2,1)}, bf16[2,160,640]{2,1,0:T(8,128)(2,1)}, u32[]{:S(2)}, u32[]{:S(2)}) collective-permute-start(bf16[2,160,640]{2,1,0:T(8,128)(2,1)} %dynamic-slice_bitcast_fusion.5), channel_id=1, source_target_pairs={{0,8},{4,12},{8,0},{12,4},{1,9},{5,13},{9,1},{13,5},{2,10},{6,14},... | collective-permute-start | bytes 1228808 | tf_op jit(solution)/shard_map/ppermute | solution.py:57
  636.7 21.4 %collective-permute-start.71 = (bf16[2,160,640]{2,1,0:T(8,128)(2,1)}, bf16[2,160,640]{2,1,0:T(8,128)(2,1)}, u32[]{:S(2)}, u32[]{:S(2)}) collective-permute-start(bf16[2,160,640]{2,1,0:T(8,128)(2,1)} %dynamic-slice_bitcast_fusion.7), channel_id=1, source_target_pairs={{0,8},{4,12},{8,0},{12,4},{1,9},{5,13},{9,1},{13,5},{2,10},{6,14},... | collective-permute-start | bytes 1228808 | tf_op jit(solution)/shard_map/ppermute | solution.py:57
  653.2 23.4 %collective-permute-start.52 = (bf16[160,1280]{1,0:T(8,128)(2,1)}, bf16[160,1280]{1,0:T(8,128)(2,1)S(1)}, u32[]{:S(2)}, u32[]{:S(2)}) collective-permute-start(bf16[160,1280]{1,0:T(8,128)(2,1)} %get-tuple-element.143), channel_id=1, source_target_pairs={{0,2},{1,3},{2,0},{3,1},{4,6},{5,7},{6,4},{7,5},{8,10},{9,11},{10,... | collective-permute-start | bytes 1228808 | tf_op jit(solution)/shard_map/ppermute | solution.py:57
  678.0 232.0 %collective-permute-start.67 = (bf16[160,640]{1,0:T(8,128)(2,1)S(1)}, bf16[160,640]{1,0:T(8,128)(2,1)}, u32[]{:S(2)}, u32[]{:S(2)}) collective-permute-start(bf16[160,640]{1,0:T(8,128)(2,1)S(1)} %dynamic-slice_bitcast_fusion.17), channel_id=1, source_target_pairs={{0,16},{16,0},{1,17},{17,1},{2,18},{18,2},{3,19},{19,3},{4,20},{20... | collective-permute-start | bytes 614408 | tf_op jit(solution)/shard_map/ppermute | solution.py:57
  731.3 42.3 %collective-permute-start.55 = (bf16[640,640]{1,0:T(8,128)(2,1)}, bf16[640,640]{1,0:T(8,128)(2,1)}, u32[]{:S(2)}, u32[]{:S(2)}) collective-permute-start(bf16[640,640]{1,0:T(8,128)(2,1)} %get-tuple-element.171), channel_id=1, source_target_pairs={{0,4},{4,0},{8,12},{12,8},{1,5},{5,1},{9,13},{13,9},{2,6},{6,2},{1... | collective-permute-start | bytes 2457608 | tf_op jit(solution)/shard_map/ppermute | solution.py:57
  735.9 49.2 %collective-permute-start.54 = (bf16[640,640]{1,0:T(8,128)(2,1)}, bf16[640,640]{1,0:T(8,128)(2,1)}, u32[]{:S(2)}, u32[]{:S(2)}) collective-permute-start(bf16[640,640]{1,0:T(8,128)(2,1)} %get-tuple-element.170), channel_id=1, source_target_pairs={{0,4},{4,0},{8,12},{12,8},{1,5},{5,1},{9,13},{13,9},{2,6},{6,2},{1... | collective-permute-start | bytes 2457608 | tf_op jit(solution)/shard_map/ppermute | solution.py:57
  780.9 26.1 %collective-permute-start.39 = (bf16[640,640]{1,0:T(8,128)(2,1)}, bf16[640,640]{1,0:T(8,128)(2,1)}, u32[]{:S(2)}, u32[]{:S(2)}) collective-permute-start(bf16[640,640]{1,0:T(8,128)(2,1)} %get-tuple-element.168), channel_id=1, source_target_pairs={{0,4},{4,0},{8,12},{12,8},{1,5},{5,1},{9,13},{13,9},{2,6},{6,2},{1... | collective-permute-start | bytes 2457608 | tf_op jit(solution)/shard_map/ppermute | solution.py:57
  783.7 30.9 %collective-permute-start.41 = (bf16[640,640]{1,0:T(8,128)(2,1)}, bf16[640,640]{1,0:T(8,128)(2,1)}, u32[]{:S(2)}, u32[]{:S(2)}) collective-permute-start(bf16[640,640]{1,0:T(8,128)(2,1)} %add_convert_fusion.1), channel_id=1, source_target_pairs={{0,8},{4,12},{8,0},{12,4},{1,9},{5,13},{9,1},{13,5},{2,10},{6,14},... | collective-permute-start | bytes 2457608 | tf_op jit(solution)/shard_map/ppermute | solution.py:57
  838.0 38.8 %collective-permute-start.85 = (f32[320]{0:T(512)S(1)}, f32[320]{0:T(512)S(1)}, u32[]{:S(2)}, u32[]{:S(2)}) collective-permute-start(f32[320]{0:T(512)S(1)} %add_add_fusion.14), channel_id=1, source_target_pairs={{0,16},{16,0},{1,17},{17,1},{2,18},{18,2},{3,19},{19,3},{4,20},{20... | collective-permute-start | bytes 3848 | tf_op jit(solution)/shard_map/ppermute | solution.py:57
  865.7 82.1 %collective-permute-start.60 = (bf16[2,2,160,1280]{3,2,1,0:T(8,128)(2,1)S(1)}, bf16[2,2,160,1280]{3,2,1,0:T(8,128)(2,1)S(1)}, u32[]{:S(2)}, u32[]{:S(2)}) collective-permute-start(bf16[2,2,160,1280]{3,2,1,0:T(8,128)(2,1)S(1)} %dynamic-slice_bitcast_fusion.3), channel_id=1, source_target_pairs={{0,4},{4,0},{8,12},{12,8},{1,5},{5,1},{9,13},{13,9},{2,6},{6,2},{1... | collective-permute-start | bytes 4915208 | tf_op jit(solution)/shard_map/ppermute | solution.py:57
  871.1 44.8 %collective-permute-start.42 = (bf16[160,1280]{1,0:T(8,128)(2,1)S(1)}, bf16[160,1280]{1,0:T(8,128)(2,1)S(1)}, u32[]{:S(2)}, u32[]{:S(2)}) collective-permute-start(bf16[160,1280]{1,0:T(8,128)(2,1)S(1)} %get-tuple-element.184), channel_id=1, source_target_pairs={{0,1},{1,0},{2,3},{3,2},{4,5},{5,4},{6,7},{7,6},{8,9},{9,8},{10,11... | collective-permute-start | bytes 1228808 | tf_op jit(solution)/shard_map/ppermute | solution.py:57
  878.0 37.8 %collective-permute-start.57 = (bf16[160,1280]{1,0:T(8,128)(2,1)S(1)}, bf16[160,1280]{1,0:T(8,128)(2,1)S(1)}, u32[]{:S(2)}, u32[]{:S(2)}) collective-permute-start(bf16[160,1280]{1,0:T(8,128)(2,1)S(1)} %get-tuple-element.186), channel_id=1, source_target_pairs={{0,1},{1,0},{2,3},{3,2},{4,5},{5,4},{6,7},{7,6},{8,9},{9,8},{10,11... | collective-permute-start | bytes 1228808 | tf_op jit(solution)/shard_map/ppermute | solution.py:57
  910.0 28.5 %collective-permute-start.44 = (bf16[160,1280]{1,0:T(8,128)(2,1)S(1)}, bf16[160,1280]{1,0:T(8,128)(2,1)S(1)}, u32[]{:S(2)}, u32[]{:S(2)}) collective-permute-start(bf16[160,1280]{1,0:T(8,128)(2,1)S(1)} %add_convert_fusion.4), channel_id=1, source_target_pairs={{0,2},{1,3},{2,0},{3,1},{4,6},{5,7},{6,4},{7,5},{8,10},{9,11},{10,... | collective-permute-start | bytes 1228808 | tf_op jit(solution)/shard_map/ppermute | solution.py:57
  912.3 34.9 %collective-permute-start.59 = (bf16[160,1280]{1,0:T(8,128)(2,1)S(1)}, bf16[160,1280]{1,0:T(8,128)(2,1)S(1)}, u32[]{:S(2)}, u32[]{:S(2)}) collective-permute-start(bf16[160,1280]{1,0:T(8,128)(2,1)S(1)} %add_convert_fusion.2), channel_id=1, source_target_pairs={{0,2},{1,3},{2,0},{3,1},{4,6},{5,7},{6,4},{7,5},{8,10},{9,11},{10,... | collective-permute-start | bytes 1228808 | tf_op jit(solution)/shard_map/ppermute | solution.py:57
  (168 other events, 2635.9 us)
Sparse Core Ops, SparseCore 0:
  10.5 35.6 all-gather.4
  48.1 32.8 all-gather.8
  82.9 37.9 all-gather.6
  122.6 41.3 all-gather.10

commit v5 on v4

--- a/solution.py
+++ b/solution.py
@@ -15,8 +15,8 @@
 
 
 EPSILON = 1e-06
-MASKED = -1e30
 HIGHEST = lax.Precision.HIGHEST
+SPREAD = ("shard", "ctx")
 
 
 def unit_rows(values):
@@ -94,6 +94,101 @@
     beside = swap(beside, axis, 1)
     across = swap(add_low(across, far), axis, 2)
     return own.astype(jnp.float32) + beside.astype(jnp.float32) + across.astype(jnp.float32)
+
+
+def in_plane():
+    return (lax.axis_size("shard"), lax.axis_size("ctx"), lax.axis_size("tp")) == (2, 4, 4)
+
+
+def hop(value, bits):
+    return lax.ppermute(value, SPREAD, [(place, place ^ bits) for place in range(8)])
+
+
+def hidden_gather(own_block):
+    if not in_plane():
+        return group_gather(own_block, "tp")
+    return jnp.concatenate([own_block] + [hop(own_block, bits) for bits in (2, 4, 6)], axis=0)
+
+
+def hidden_scatter(partial_low):
+    if not in_plane():
+        return group_scatter(partial_low, "tp")
+    own, along, aside, across = jnp.split(partial_low, 4, axis=0)
+    total = own.astype(jnp.float32)
+    for value, bits in ((along, 2), (aside, 4), (across, 6)):
+        total = total + hop(value, bits).astype(jnp.float32)
+    return total
+
+
+def hidden_weights(w_up, w_gate, w_down):
+    if not in_plane():
+        return tuple(
+            lax.all_gather(matrix, SPREAD, axis=1, tiled=True)
+            for matrix in (w_up.T, w_gate.T, w_down)
+        )
+    rows, hidden = w_up.shape
+    part = hidden // 8
+    packed = jnp.stack(
+        [
+            w_up.reshape(rows, 8, part).transpose(1, 2, 0),
+            w_gate.reshape(rows, 8, part).transpose(1, 2, 0),
+            w_down.reshape(8, part, rows),
+        ],
+        axis=1,
+    )
+    packed = lax.all_to_all(packed, SPREAD, 0, 0)
+    matrices = packed.transpose(1, 2, 0, 3).reshape(3, part, 8 * rows)
+    out = []
+    for place in range(3):
+        own_core = group_gather(matrices[place], "tp")
+        out.append(jnp.concatenate([own_core, swap(own_core, "ctx", 1)], axis=0))
+    return tuple(out)
+
+
+def hidden_scales(*scales):
+    if not in_plane():
+        return scales
+    part = scales[0].shape[0] // 8
+    first = lax.axis_index(SPREAD) * part
+    own = jnp.stack([lax.dynamic_slice_in_dim(scale, first, part) for scale in scales])
+    line = group_gather(own[None], "tp")
+    both = jnp.concatenate([line, swap(line, "ctx", 1)], axis=0)
+    return tuple(both[:, place].reshape(-1) for place in range(len(scales)))
+
+
+def hidden_weight_grads(products):
+    if not in_plane():
+        return [
+            lax.psum_scatter(product, SPREAD, scatter_dimension=1, tiled=True).astype(jnp.float32)
+            for product in products
+        ]
+    sums = []
+    for product in products:
+        half = product.shape[0] // 2
+        line = add_low(product[:half], swap(product[half:], "ctx", 1))
+        sums.append(group_scatter(line, "tp").astype(jnp.bfloat16))
+    part, width = sums[0].shape
+    packed = jnp.stack([total.reshape(part, 8, width // 8).transpose(1, 0, 2) for total in sums], 1)
+    packed = lax.all_to_all(packed, SPREAD, 0, 0).astype(jnp.float32)
+    return [packed[:, place].reshape(8 * part, width // 8) for place in range(3)]
+
+
+def hidden_scale_grads(sums):
+    if not in_plane():
+        return butterfly(sums, SPREAD)
+    count, hidden = sums.shape
+    parts = sums.reshape(count, 2, 4, hidden // 8)
+    line = hidden_line_sum(parts[:, 0] + swap(parts[:, 1], "ctx", 1))
+    blank = jnp.zeros((count, 8, hidden // 8), jnp.float32)
+    place = lax.axis_index(SPREAD)
+    spread_out = lax.dynamic_update_slice_in_dim(blank, line[:, None], place, 1)
+    return butterfly(spread_out, SPREAD).reshape(count, hidden)
+
+
+def hidden_line_sum(parts):
+    own, beside, across, far = (parts[:, place] for place in range(4))
+    across = across + swap(far, "tp", 1)
+    return own + swap(beside, "tp", 1) + swap(across, "tp", 2)
 
 
 def owner_scatter(product_low):
@@ -380,26 +475,27 @@
     alpha_attn, alpha_mlp, scale_qk, scale_up, scale_gate = vectors
     tokens_wide = tokens_own.astype(jnp.float32)
     hidden_one = mix_rows(tokens_wide, branch_one, alpha_attn)
-    hidden_one_group = group_gather(hidden_one.astype(jnp.bfloat16), "tp")
-    up_raw = jnp.dot(hidden_one_group, w_up, preferred_element_type=jnp.float32)
-    gate_raw = jnp.dot(hidden_one_group, w_gate, preferred_element_type=jnp.float32)
+    hidden_one_group = hidden_gather(hidden_one.astype(jnp.bfloat16))
+    up_raw = contract_cols(hidden_one_group, w_up)
+    gate_raw = contract_cols(hidden_one_group, w_gate)
     mixed_low = middle(up_raw, gate_raw, scale_up, scale_gate).astype(jnp.bfloat16)
-    branch_two = group_scatter(contract_cols(mixed_low, w_down).astype(jnp.bfloat16), "tp")
+    branch_two = hidden_scatter(
+        jnp.dot(mixed_low, w_down, preferred_element_type=jnp.float32).astype(jnp.bfloat16)
+    )
     output_wide, pull_out = jax.vjp(mix_rows, hidden_one, branch_two, alpha_mlp)
     upstream = cotangent_own.astype(jnp.float32)
     hidden_one_direct, branch_two_grad, grad_alpha_mlp = pull_out(upstream)
-    branch_two_group = group_gather(branch_two_grad.astype(jnp.bfloat16), "tp")
-    mixed_grad = (
-        jnp.dot(branch_two_group, w_down, preferred_element_type=jnp.float32)
-        .astype(jnp.bfloat16)
-        .astype(jnp.float32)
-    )
+    branch_two_group = hidden_gather(branch_two_grad.astype(jnp.bfloat16))
+    mixed_grad = contract_cols(branch_two_group, w_down).astype(jnp.bfloat16).astype(jnp.float32)
     middle_value, pull_mid = jax.vjp(middle, up_raw, gate_raw, scale_up, scale_gate)
     up_grad, gate_grad, grad_scale_up, grad_scale_gate = pull_mid(mixed_grad)
     up_low = up_grad.astype(jnp.bfloat16)
     gate_low = gate_grad.astype(jnp.bfloat16)
-    hidden_one_grad = hidden_one_direct + group_scatter(
-        (contract_cols(up_low, w_up) + contract_cols(gate_low, w_gate)).astype(jnp.bfloat16), "tp"
+    hidden_one_grad = hidden_one_direct + hidden_scatter(
+        (
+            jnp.dot(up_low, w_up, preferred_element_type=jnp.float32)
+            + jnp.dot(gate_low, w_gate, preferred_element_type=jnp.float32)
+        ).astype(jnp.bfloat16)
     )
     hidden_again, pull_in = jax.vjp(mix_rows, tokens_wide, branch_one, alpha_attn)
     tokens_direct, branch_one_grad, grad_alpha_attn = pull_in(hidden_one_grad)
@@ -463,12 +559,10 @@
     cotangent,
 ):
     local_heads = w_query.shape[1]
-    local_hidden = w_up.shape[1]
-    vectors = (alpha_attn, alpha_mlp, scale_qk, scale_up, scale_gate)
-    spread = ("shard", "ctx")
+    vectors = (alpha_attn, alpha_mlp, scale_qk) + hidden_scales(scale_up, scale_gate)
 
     def spread_gather(own_block):
-        return lax.all_gather(own_block, spread, axis=0, tiled=True)
+        return lax.all_gather(own_block, SPREAD, axis=0, tiled=True)
 
     packed = spread_gather(jnp.concatenate([w_query, w_key, w_value, w_attn_out.T], axis=1))
     gathered = (
@@ -476,10 +570,7 @@
         packed[:, local_heads : 2 * local_heads],
         packed[:, 2 * local_heads : 3 * local_heads],
         packed[:, 3 * local_heads :],
-        spread_gather(w_up),
-        spread_gather(w_gate),
-        spread_gather(w_down.T),
-    )
+    ) + hidden_weights(w_up, w_gate, w_down)
     micros = range(tokens.shape[0])
     front = [
         forward_attention(gathered, vectors, tokens[m, 0], parents[m, 0], slot_segment[m, 0])
@@ -502,12 +593,16 @@
         stack(lambda m: back[m][1][place]) for place in range(6)
     )
 
-    def to_owner(former, latter):
-        return owner_scatter(contract_rows(former, latter).astype(jnp.bfloat16))
-
-    grad_d = to_owner(top_all, mixed_all).T
-    grad_u = to_owner(hidden_all, up_all)
-    grad_g = to_owner(hidden_all, gate_all)
+    grad_u, grad_g, grad_d = hidden_weight_grads(
+        [
+            contract_rows(former, latter).astype(jnp.bfloat16)
+            for former, latter in (
+                (up_all, hidden_all),
+                (gate_all, hidden_all),
+                (mixed_all, top_all),
+            )
+        ]
+    )
     attention_product = jnp.concatenate(
         [
             contract_rows(tokens_all, query_all),
@@ -523,10 +618,10 @@
     sum_attn, sum_mlp, sum_up, sum_gate = (
         sum(mid[m][4][place] for m in micros) for place in range(4)
     )
-    sum_qk = butterfly(sum(back[m][2] for m in micros), spread)
+    sum_qk = butterfly(sum(back[m][2] for m in micros), SPREAD)
     width = sum_attn.shape[0]
-    sums = butterfly(jnp.concatenate([sum_attn, sum_mlp, sum_up, sum_gate]), spread)
-    alphas = butterfly(sums[: 2 * width], ("tp",))
+    alphas = butterfly(jnp.concatenate([sum_attn, sum_mlp]), SPREAD + ("tp",))
+    sum_up, sum_gate = hidden_scale_grads(jnp.stack([sum_up, sum_gate]))
     return (
         jnp.stack([mid[m][0] for m in micros])[:, None],
         jnp.stack([back[m][0] for m in micros])[:, None],
@@ -534,14 +629,14 @@
         grad_k,
         grad_v,
         grad_o.T,
-        grad_u,
-        grad_g,
+        grad_u.T,
+        grad_g.T,
         grad_d,
         alphas[:width],
         alphas[width:],
         sum_qk,
-        sums[2 * width : 2 * width + local_hidden],
-        sums[2 * width + local_hidden :],
+        sum_up,
+        sum_gate,
     )
 
 

time: 987 us -> 1110 us (1.12)
  local copies, waits for them, and re-layouts: 108 us -> 170 us
  starting transfers between devices: 72.2 us -> 119 us
  other arithmetic: 89.6 us -> 116 us
    ppermute x88 -> x84, waiting for transfers between devices: 454 us -> 369 us  [swap(): lax.ppermute(value, axis, [(place, place ^ bit) for place in range(size)])]
    ppermute x0 -> x24, waiting for transfers between devices: none -> 85.7 us  [hop(): lax.ppermute(value, SPREAD, [(place, place ^ bits) for place in range(8)])]
    ppermute x0 -> x24, starting transfers between devices: none -> 29 us  [hop(): lax.ppermute(value, SPREAD, [(place, place ^ bits) for place in range(8)])]
    dot_general x6, matrix products: 39.2 us -> 18.2 us  [the longest x2 9.08 us: feed_forward(): jnp.dot(up_low, w_up, preferred_element_type=jnp.float32)]
    unnamed x270 -> x313, local copies, waits for them, and re-layouts: 27.3 us -> 43.7 us
    dot_general x14, matrix products: 33.7 us -> 49.6 us  [contract_cols(): lax.dot_general(former, latter, (((1,), (1,)), ((), ())), preferred_eleme...]
    slice x2 -> x8, local copies, waits for them, and re-layouts: 0.61 us -> 15.8 us  [the longest x4 8.43 us: hidden_weights(): own_core = group_gather(matrices[place], 'tp')]
    ppermute x88 -> x84, starting transfers between devices: 72 us -> 80.4 us  [swap(): lax.ppermute(value, axis, [(place, place ^ bit) for place in range(size)])]
  transfers between devices with their start and end apart: 92 -> 111, of which waited for: 43 -> 51; matrix products, arithmetic and copies ran while one was open for 31% -> 33% of each run, Pallas kernels for 10% -> 9%
where the time goes in v5:
time: 1110 us; the launch traced here: 1100 us
  waiting for transfers between devices  454 us (41%)
  local copies, waits for them, and re-layouts  170 us (15%)
  matrix products  130 us (12%)
  starting transfers between devices  119 us (11%)
  other arithmetic  116 us (10%)
  Pallas kernels  98.9 us (9%)
  between operations  16.7 us (2%)
    ppermute x84, waiting for transfers between devices, swap(): lax.ppermute(value, axis, [(place, place ^ bit) for place in range(size)])  369 us
    ppermute x24, waiting for transfers between devices, hop(): lax.ppermute(value, SPREAD, [(place, place ^ bits) for place in range(8)])  85.7 us
    ppermute x84, starting transfers between devices, swap(): lax.ppermute(value, axis, [(place, place ^ bit) for place in range(size)])  80.4 us
    pallas_call x2, Pallas kernels, attend_grad(): pl.pallas_call(attend_grad_body, grid=(keys // KEY_TILE,), in_specs=[pl.B...  64.4 us
    dot_general x14, matrix products, contract_cols(): lax.dot_general(former, latter, (((1,), (1,)), ((), ())), preferred_eleme...  49.6 us
    unnamed x313, local copies, waits for them, and re-layouts  43.7 us
    pallas_call x2, Pallas kernels, attend(): pl.pallas_call(attend_body, grid=(keys // KEY_TILE,), in_specs=[pl.BlockS...  34.5 us
    dot_general x7, matrix products, contract_rows(): lax.dot_general(former, latter, (((0,), (0,)), ((), ())), preferred_eleme...  31.2 us
  transfers between devices with their start and end apart: 111, of which 51 were waited for; matrix products, arithmetic and copies ran while one was open for 33% of the time, Pallas kernels for 9%

profile of v5, /device:TPU:0, one launch (start us, length us, event | category | flops | bytes accessed | tf_op | source)
XLA Modules:
  0.0 1104.3 jit_solution(8390174493653742890)
XLA Ops:
  40.1 18.1 %collective-permute-done.18 = f32[1,2,160]{2,1,0:T(2,128)S(1)} collective-permute-done((f32[1,2,160]{2,1,0:T(2,128)S(1)}, f32[1,2,160]{2,1,0:T(2,128)S(1)}, u32[]{:S(2)}, u32[]{:S(2)}) %collective-permute-start.18) | collective-permute-done | bytes 1312 | tf_op jit(solution)/shard_map/ppermute | solution.py:57
  65.6 15.8 %collective-permute-done.2 = bf16[160,1280]{1,0:T(8,128)(2,1)S(1)} collective-permute-done((bf16[160,1280]{1,0:T(8,128)(2,1)}, bf16[160,1280]{1,0:T(8,128)(2,1)S(1)}, u32[]{:S(2)}, u32[]{:S(2)}) %collective-permute-start.2) | collective-permute-done | bytes 409632 | tf_op jit(solution)/shard_map/ppermute | solution.py:57
  108.1 7.8 collective-permute-done.25
  118.0 15.6 %collective-permute-done.21 = bf16[160,1280]{1,0:T(8,128)(2,1)} collective-permute-done((bf16[160,1280]{1,0:T(8,128)(2,1)S(1)}, bf16[160,1280]{1,0:T(8,128)(2,1)}, u32[]{:S(2)}, u32[]{:S(2)}) %collective-permute-start.21) | collective-permute-done | bytes 409632 | tf_op jit(solution)/shard_map/ppermute | solution.py:57
  133.5 16.2 %collective-permute-done.13 = bf16[160,1280]{1,0:T(8,128)(2,1)} collective-permute-done((bf16[160,1280]{1,0:T(8,128)(2,1)S(1)}, bf16[160,1280]{1,0:T(8,128)(2,1)}, u32[]{:S(2)}, u32[]{:S(2)}) %collective-permute-start.13) | collective-permute-done | bytes 409632 | tf_op jit(solution)/shard_map/ppermute | solution.py:57
  161.5 6.2 collective-permute-done.22
  200.7 5.7 multiply_convert_fusion.6
  227.3 8.0 collective-permute-done.35
  241.9 10.4 collective-permute-done.4
  252.8 8.8 pad_maximum_fusion.1.tree_ref
  261.7 17.2 %attend.3 = (bf16[640,320]{1,0:T(8,128)(2,1)S(1)}, f32[8,640]{1,0:T(8,128)S(1)}) custom-call(bf16[640,320]{1,0:T(8,128)(2,1)S(1)} %get-tuple-element.272.query_ref, bf16[2560,640]{1,0:T(8,128)(2,1)S(1)} %pad_maximum_fusion.1.tree_ref, bf16[2560,128]{1,0:T(8,128)(2,1)S(1)} %get-tuple-element.254.hot_ref, bf16[3,128,640]{2,1,0:T(8,128)(2,1)S(1)} %get-tuple-element.248.side_ref), custom_call_target="tpu_custom_call" | custom-call | tf_op jit(solution)/shard_map/attend/pallas_call | solution.py:307
  283.0 8.6 pad_maximum_fusion.tree_ref
  291.7 17.2 %attend.2 = (bf16[640,320]{1,0:T(8,128)(2,1)S(1)}, f32[8,640]{1,0:T(8,128)S(1)}) custom-call(bf16[640,320]{1,0:T(8,128)(2,1)S(1)} %get-tuple-element.274.query_ref, bf16[2560,640]{1,0:T(8,128)(2,1)S(1)} %pad_maximum_fusion.tree_ref, bf16[2560,128]{1,0:T(8,128)(2,1)S(1)} %get-tuple-element.255.hot_ref, bf16[3,128,640]{2,1,0:T(8,128)(2,1)S(1)} %get-tuple-element.249.side_ref), custom_call_target="tpu_custom_call" | custom-call | tf_op jit(solution)/shard_map/attend/pallas_call | solution.py:307
  313.4 16.4 %collective-permute-done.7 = bf16[160,1280]{1,0:T(8,128)(2,1)S(1)} collective-permute-done((bf16[160,1280]{1,0:T(8,128)(2,1)S(1)}, bf16[160,1280]{1,0:T(8,128)(2,1)S(1)}, u32[]{:S(2)}, u32[]{:S(2)}) %collective-permute-start.7) | collective-permute-done | bytes 409632 | tf_op jit(solution)/shard_map/ppermute | solution.py:57
  334.5 23.7 %collective-permute-done.39 = bf16[160,1280]{1,0:T(8,128)(2,1)S(1)} collective-permute-done((bf16[160,1280]{1,0:T(8,128)(2,1)S(1)}, bf16[160,1280]{1,0:T(8,128)(2,1)S(1)}, u32[]{:S(2)}, u32[]{:S(2)}) %collective-permute-start.39) | collective-permute-done | bytes 409632 | tf_op jit(solution)/shard_map/ppermute | solution.py:57
  358.5 8.4 collective-permute-done.8
  374.5 6.1 collective-permute-done.9
  380.6 13.2 %collective-permute-done.10 = bf16[160,1280]{1,0:T(8,128)(2,1)S(1)} collective-permute-done((bf16[160,1280]{1,0:T(8,128)(2,1)S(1)}, bf16[160,1280]{1,0:T(8,128)(2,1)S(1)}, u32[]{:S(2)}, u32[]{:S(2)}) %collective-permute-start.10) | collective-permute-done | bytes 409632 | tf_op jit(solution)/shard_map/ppermute | solution.py:104
  401.6 6.0 fusion.115
  407.6 6.2 collective-permute-done.41
  417.8 10.3 multiply_convert_fusion.4
  444.9 8.3 collective-permute-done.45
  455.3 6.4 collective-permute-done.28
  461.7 8.2 collective-permute-done.30
  477.5 8.8 collective-permute-done.46
  486.3 8.7 collective-permute-done.47
  512.9 13.3 %multiply_reduce_fusion.2 = (f32[1280]{0:T(1024)S(1)}, f32[1280]{0:T(1024)S(1)}, f32[1280]{0:T(1024)S(1)}, f32[1280]{0:T(1024)S(1)}, f32[640,1280]{1,0:T(8,128)}...) fusion(f32[640,1280]{1,0:T(8,128)} %get-tuple-element.292, f32[640,1280]{1,0:T(8,128)} %fusion.112, ...), kind=kOutput, calls=%fused_computation.34 | convolution fusion | flops 2138926080 | bytes 29521920 | tf_op jit(solution)/shard_map/dot_general | solution.py:38
  535.0 6.1 convolution_convert_fusion.1
  541.1 6.1 convolution_convert_fusion.2
  570.3 10.3 collective-permute-done.105
  589.8 7.5 convolution_convert_fusion
  627.2 14.9 %collective-permute-done.96 = f32[2560]{0:T(1024)S(1)} collective-permute-done((f32[2560]{0:T(1024)S(1)}, f32[2560]{0:T(1024)S(1)}, u32[]{:S(2)}, u32[]{:S(2)}) %collective-permute-start.96) | collective-permute-done | bytes 10272 | tf_op jit(solution)/shard_map/ppermute | solution.py:57
  649.3 10.2 collective-permute-done.54
  695.0 34.2 %collective-permute-done.69 = bf16[160,1280]{1,0:T(8,128)(2,1)S(1)} collective-permute-done((bf16[160,1280]{1,0:T(8,128)(2,1)}, bf16[160,1280]{1,0:T(8,128)(2,1)S(1)}, u32[]{:S(2)}, u32[]{:S(2)}) %collective-permute-start.69) | collective-permute-done | bytes 409632 | tf_op jit(solution)/shard_map/ppermute | solution.py:57
  742.9 32.2 %attend_grad.2 = (f32[640,320]{1,0:T(8,128)S(1)}, bf16[2560,640]{1,0:T(8,128)(2,1)}) custom-call(bf16[640,640]{1,0:T(8,128)(2,1)S(1)} %get-tuple-element.293.both_ref, bf16[640,320]{1,0:T(8,128)(2,1)S(1)} %copy-done.10, bf16[2560,640]{1,0:T(8,128)(2,1)} %copy-done.1, bf16[2560,128]{1,0:T(8,128)(2,1)S(1)} %get-tuple-element.255.hot_ref, ...), custom_call_target="tpu_custom_call" | custom-call | tf_op jit(solution)/shard_map/attend_grad/pallas_call | solution.py:392
  781.1 32.2 %attend_grad.3 = (f32[640,320]{1,0:T(8,128)S(1)}, bf16[2560,640]{1,0:T(8,128)(2,1)}) custom-call(bf16[640,640]{1,0:T(8,128)(2,1)S(1)} %copy-done.4, bf16[640,320]{1,0:T(8,128)(2,1)S(1)} %copy-done.7, bf16[2560,640]{1,0:T(8,128)(2,1)} %copy-done, bf16[2560,128]{1,0:T(8,128)(2,1)S(1)} %get-tuple-element.254.hot_ref, ...), custom_call_target="tpu_custom_call" | custom-call | tf_op jit(solution)/shard_map/attend_grad/pallas_call | solution.py:392
  826.2 12.9 %collective-permute-done.83 = bf16[160,1280]{1,0:T(8,128)(2,1)S(1)} collective-permute-done((bf16[160,1280]{1,0:T(8,128)(2,1)S(1)}, bf16[160,1280]{1,0:T(8,128)(2,1)S(1)}, u32[]{:S(2)}, u32[]{:S(2)}) %collective-permute-start.83) | collective-permute-done | bytes 409632 | tf_op jit(solution)/shard_map/ppermute | solution.py:57
  839.9 10.1 collective-permute-done.92
  851.2 19.7 %collective-permute-done.88 = bf16[160,1280]{1,0:T(8,128)(2,1)S(1)} collective-permute-done((bf16[160,1280]{1,0:T(8,128)(2,1)S(1)}, bf16[160,1280]{1,0:T(8,128)(2,1)S(1)}, u32[]{:S(2)}, u32[]{:S(2)}) %collective-permute-start.88) | collective-permute-done | bytes 409632 | tf_op jit(solution)/shard_map/ppermute | solution.py:57
  875.1 5.1 collective-permute-start.72
  909.4 28.8 %collective-permute-done.57 = bf16[640,640]{1,0:T(8,128)(2,1)} collective-permute-done((bf16[640,640]{1,0:T(8,128)(2,1)}, bf16[640,640]{1,0:T(8,128)(2,1)}, u32[]{:S(2)}, u32[]{:S(2)}) %collective-permute-start.57) | collective-permute-done | bytes 819232 | tf_op jit(solution)/shard_map/ppermute | solution.py:57
  954.6 6.4 multiply_reduce_fusion.4
  982.0 6.0 concatenate.164
  1005.1 12.5 %collective-permute-done.59 = bf16[160,1280]{1,0:T(8,128)(2,1)S(1)} collective-permute-done((bf16[160,1280]{1,0:T(8,128)(2,1)S(1)}, bf16[160,1280]{1,0:T(8,128)(2,1)S(1)}, u32[]{:S(2)}, u32[]{:S(2)}) %collective-permute-start.59) | collective-permute-done | bytes 409632 | tf_op jit(solution)/shard_map/ppermute | solution.py:57
  1020.3 14.5 %collective-permute-done.74 = bf16[160,1280]{1,0:T(8,128)(2,1)S(1)} collective-permute-done((bf16[160,1280]{1,0:T(8,128)(2,1)S(1)}, bf16[160,1280]{1,0:T(8,128)(2,1)S(1)}, u32[]{:S(2)}, u32[]{:S(2)}) %collective-permute-start.74) | collective-permute-done | bytes 409632 | tf_op jit(solution)/shard_map/ppermute | solution.py:57
  1051.2 13.7 %collective-permute-done.60 = bf16[160,1280]{1,0:T(8,128)(2,1)S(1)} collective-permute-done((bf16[160,1280]{1,0:T(8,128)(2,1)}, bf16[160,1280]{1,0:T(8,128)(2,1)S(1)}, u32[]{:S(2)}, u32[]{:S(2)}) %collective-permute-start.60) | collective-permute-done | bytes 409632 | tf_op jit(solution)/shard_map/ppermute | solution.py:57
  1064.9 8.7 collective-permute-done.75
  1081.0 7.8 collective-permute-done.77
  (773 shorter events, 488.0 us)
Async XLA Ops:
  7.2 163.1 %all-gather.2.cloned.1.call-start = ((), (), s32[]{:S(2)}) async-start(), calls=%async_computation.2 | async-start | bytes 3686400 | tf_op jit(solution)/shard_map/all_gather | solution.py:565
  16.7 44.3 %collective-permute-start.32 = (bf16[160,1280]{1,0:T(8,128)(2,1)}, bf16[160,1280]{1,0:T(8,128)(2,1)}, u32[]{:S(2)}, u32[]{:S(2)}) collective-permute-start(bf16[160,1280]{1,0:T(8,128)(2,1)} %get-tuple-element.242), channel_id=1, source_target_pairs={{0,2},{1,3},{2,0},{3,1},{4,6},{5,7},{6,4},{7,5},{8,10},{9,11},{10,... | collective-permute-start | bytes 1228808 | tf_op jit(solution)/shard_map/ppermute | solution.py:57
  17.0 66.1 %collective-permute-start.31 = (bf16[160,1280]{1,0:T(8,128)(2,1)}, bf16[160,1280]{1,0:T(8,128)(2,1)}, u32[]{:S(2)}, u32[]{:S(2)}) collective-permute-start(bf16[160,1280]{1,0:T(8,128)(2,1)} %get-tuple-element.242), channel_id=1, source_target_pairs={{0,1},{1,0},{2,3},{3,2},{4,5},{5,4},{6,7},{7,6},{8,9},{9,8},{10,11... | collective-permute-start | bytes 1228808 | tf_op jit(solution)/shard_map/ppermute | solution.py:57
  21.7 66.5 %all-to-all-start = ((bf16[8,3,160,160]{3,2,1,0:T(8,128)(2,1)}), bf16[8,3,160,160]{3,2,1,0:T(8,128)(2,1)}, u32[]{:S(2)}, u32[]{:S(2)}) async-start(bf16[8,3,160,160]{3,2,1,0:T(8,128)(2,1)} %pad_maximum_fusion.2), calls=%async_computation | async-start | bytes 3932160 | tf_op jit(solution)/shard_map/all_to_all | solution.py:139
  26.2 34.8 %collective-permute-start.1 = (bf16[160,1280]{1,0:T(8,128)(2,1)}, bf16[160,1280]{1,0:T(8,128)(2,1)}, u32[]{:S(2)}, u32[]{:S(2)}) collective-permute-start(bf16[160,1280]{1,0:T(8,128)(2,1)} %get-tuple-element.243), channel_id=1, source_target_pairs={{0,2},{1,3},{2,0},{3,1},{4,6},{5,7},{6,4},{7,5},{8,10},{9,11},{10,... | collective-permute-start | bytes 1228808 | tf_op jit(solution)/shard_map/ppermute | solution.py:57
  98.9 34.6 %collective-permute-start.21 = (bf16[160,1280]{1,0:T(8,128)(2,1)S(1)}, bf16[160,1280]{1,0:T(8,128)(2,1)}, u32[]{:S(2)}, u32[]{:S(2)}) collective-permute-start(bf16[160,1280]{1,0:T(8,128)(2,1)S(1)} %squeeze.63), channel_id=1, source_target_pairs={{0,2},{1,3},{2,0},{3,1},{4,6},{5,7},{6,4},{7,5},{8,10},{9,11},{10,... | collective-permute-start | bytes 1228808 | tf_op jit(solution)/shard_map/ppermute | solution.py:57
  101.3 50.5 %collective-permute-start.20 = (bf16[160,1280]{1,0:T(8,128)(2,1)S(1)}, bf16[160,1280]{1,0:T(8,128)(2,1)}, u32[]{:S(2)}, u32[]{:S(2)}) collective-permute-start(bf16[160,1280]{1,0:T(8,128)(2,1)S(1)} %squeeze.63), channel_id=1, source_target_pairs={{0,1},{1,0},{2,3},{3,2},{4,5},{5,4},{6,7},{7,6},{8,9},{9,8},{10,11... | collective-permute-start | bytes 1228808 | tf_op jit(solution)/shard_map/ppermute | solution.py:57
  107.1 42.6 %collective-permute-start.13 = (bf16[160,1280]{1,0:T(8,128)(2,1)S(1)}, bf16[160,1280]{1,0:T(8,128)(2,1)}, u32[]{:S(2)}, u32[]{:S(2)}) collective-permute-start(bf16[160,1280]{1,0:T(8,128)(2,1)S(1)} %squeeze.62), channel_id=1, source_target_pairs={{0,2},{1,3},{2,0},{3,1},{4,6},{5,7},{6,4},{7,5},{8,10},{9,11},{10,... | collective-permute-start | bytes 1228808 | tf_op jit(solution)/shard_map/ppermute | solution.py:57
  115.9 38.3 %collective-permute-start.12 = (bf16[160,1280]{1,0:T(8,128)(2,1)S(1)}, bf16[160,1280]{1,0:T(8,128)(2,1)S(1)}, u32[]{:S(2)}, u32[]{:S(2)}) collective-permute-start(bf16[160,1280]{1,0:T(8,128)(2,1)S(1)} %squeeze.62), channel_id=1, source_target_pairs={{0,1},{1,0},{2,3},{3,2},{4,5},{5,4},{6,7},{7,6},{8,9},{9,8},{10,11... | collective-permute-start | bytes 1228808 | tf_op jit(solution)/shard_map/ppermute | solution.py:57
  115.9 43.0 %collective-permute-start.26 = (bf16[160,1280]{1,0:T(8,128)(2,1)}, bf16[160,1280]{1,0:T(8,128)(2,1)S(1)}, u32[]{:S(2)}, u32[]{:S(2)}) collective-permute-start(bf16[160,1280]{1,0:T(8,128)(2,1)} %collective-permute-done.25), channel_id=1, source_target_pairs={{0,1},{1,0},{2,3},{3,2},{4,5},{5,4},{6,7},{7,6},{8,9},{9,8},{10,11... | collective-permute-start | bytes 1228808 | tf_op jit(solution)/shard_map/ppermute | solution.py:57
  133.5 34.2 %collective-permute-start.22 = (bf16[160,1280]{1,0:T(8,128)(2,1)}, bf16[160,1280]{1,0:T(8,128)(2,1)S(1)}, u32[]{:S(2)}, u32[]{:S(2)}) collective-permute-start(bf16[160,1280]{1,0:T(8,128)(2,1)} %collective-permute-done.21), channel_id=1, source_target_pairs={{0,1},{1,0},{2,3},{3,2},{4,5},{5,4},{6,7},{7,6},{8,9},{9,8},{10,11... | collective-permute-start | bytes 1228808 | tf_op jit(solution)/shard_map/ppermute | solution.py:57
  149.7 77.2 %collective-permute-start.14 = (bf16[160,1280]{1,0:T(8,128)(2,1)}, bf16[160,1280]{1,0:T(8,128)(2,1)}, u32[]{:S(2)}, u32[]{:S(2)}) collective-permute-start(bf16[160,1280]{1,0:T(8,128)(2,1)} %collective-permute-done.13), channel_id=1, source_target_pairs={{0,1},{1,0},{2,3},{3,2},{4,5},{5,4},{6,7},{7,6},{8,9},{9,8},{10,11... | collective-permute-start | bytes 1228808 | tf_op jit(solution)/shard_map/ppermute | solution.py:57
  161.5 78.4 %collective-permute-start.27 = (bf16[640,1280]{1,0:T(8,128)(2,1)}, bf16[640,1280]{1,0:T(8,128)(2,1)}, u32[]{:S(2)}, u32[]{:S(2)}) collective-permute-start(bf16[640,1280]{1,0:T(8,128)(2,1)} %pad_maximum_fusion.8), channel_id=1, source_target_pairs={{0,4},{4,0},{8,12},{12,8},{1,5},{5,1},{9,13},{13,9},{2,6},{6,2},{1... | collective-permute-start | bytes 4915208 | tf_op jit(solution)/shard_map/ppermute | solution.py:57
  170.3 161.0 %collective-permute-start.23 = (bf16[640,1280]{1,0:T(8,128)(2,1)}, bf16[640,1280]{1,0:T(8,128)(2,1)}, u32[]{:S(2)}, u32[]{:S(2)}) collective-permute-start(bf16[640,1280]{1,0:T(8,128)(2,1)} %pad_maximum_fusion.7), channel_id=1, source_target_pairs={{0,4},{4,0},{8,12},{12,8},{1,5},{5,1},{9,13},{13,9},{2,6},{6,2},{1... | collective-permute-start | bytes 4915208 | tf_op jit(solution)/shard_map/ppermute | solution.py:57
  219.2 33.1 %collective-permute-start.34 = (bf16[640,640]{1,0:T(8,128)(2,1)}, bf16[640,640]{1,0:T(8,128)(2,1)}, u32[]{:S(2)}, u32[]{:S(2)}) collective-permute-start(bf16[640,640]{1,0:T(8,128)(2,1)} %pad_maximum_fusion.12), channel_id=1, source_target_pairs={{0,4},{4,0},{8,12},{12,8},{1,5},{5,1},{9,13},{13,9},{2,6},{6,2},{1... | collective-permute-start | bytes 2457608 | tf_op jit(solution)/shard_map/ppermute | solution.py:57
  239.9 130.1 %collective-permute-start.15 = (bf16[640,1280]{1,0:T(8,128)(2,1)}, bf16[640,1280]{1,0:T(8,128)(2,1)}, u32[]{:S(2)}, u32[]{:S(2)}) collective-permute-start(bf16[640,1280]{1,0:T(8,128)(2,1)} %pad_maximum_fusion.6), channel_id=1, source_target_pairs={{0,4},{4,0},{8,12},{12,8},{1,5},{5,1},{9,13},{13,9},{2,6},{6,2},{1... | collective-permute-start | bytes 4915208 | tf_op jit(solution)/shard_map/ppermute | solution.py:57
  252.3 30.7 %collective-permute-start.5 = (bf16[640,640]{1,0:T(8,128)(2,1)S(1)}, bf16[640,640]{1,0:T(8,128)(2,1)}, u32[]{:S(2)}, u32[]{:S(2)}) collective-permute-start(bf16[640,640]{1,0:T(8,128)(2,1)S(1)} %collective-permute-done.4), channel_id=1, source_target_pairs={{0,4},{4,0},{8,12},{12,8},{1,5},{5,1},{9,13},{13,9},{2,6},{6,2},{1... | collective-permute-start | bytes 2457608 | tf_op jit(solution)/shard_map/ppermute | solution.py:57
  281.0 53.5 %collective-permute-start.37 = (bf16[160,1280]{1,0:T(8,128)(2,1)S(1)}, bf16[160,1280]{1,0:T(8,128)(2,1)S(1)}, u32[]{:S(2)}, u32[]{:S(2)}) collective-permute-start(bf16[160,1280]{1,0:T(8,128)(2,1)S(1)} %get-tuple-element.225), channel_id=1, source_target_pairs={{0,1},{1,0},{2,3},{3,2},{4,5},{5,4},{6,7},{7,6},{8,9},{9,8},{10,11... | collective-permute-start | bytes 1228808 | tf_op jit(solution)/shard_map/ppermute | solution.py:57
  281.2 29.2 %collective-permute-start.38 = (bf16[160,1280]{1,0:T(8,128)(2,1)}, bf16[160,1280]{1,0:T(8,128)(2,1)}, u32[]{:S(2)}, u32[]{:S(2)}) collective-permute-start(bf16[160,1280]{1,0:T(8,128)(2,1)} %get-tuple-element.226), channel_id=1, source_target_pairs={{0,1},{1,0},{2,3},{3,2},{4,5},{5,4},{6,7},{7,6},{8,9},{9,8},{10,11... | collective-permute-start | bytes 1228808 | tf_op jit(solution)/shard_map/ppermute | solution.py:57
  310.2 48.3 %collective-permute-start.6 = (bf16[160,1280]{1,0:T(8,128)(2,1)S(1)}, bf16[160,1280]{1,0:T(8,128)(2,1)S(1)}, u32[]{:S(2)}, u32[]{:S(2)}) collective-permute-start(bf16[160,1280]{1,0:T(8,128)(2,1)S(1)} %get-tuple-element.230), channel_id=1, source_target_pairs={{0,1},{1,0},{2,3},{3,2},{4,5},{5,4},{6,7},{7,6},{8,9},{9,8},{10,11... | collective-permute-start | bytes 1228808 | tf_op jit(solution)/shard_map/ppermute | solution.py:57
  331.3 35.6 %collective-permute-start.8 = (bf16[160,1280]{1,0:T(8,128)(2,1)S(1)}, bf16[160,1280]{1,0:T(8,128)(2,1)S(1)}, u32[]{:S(2)}, u32[]{:S(2)}) collective-permute-start(bf16[160,1280]{1,0:T(8,128)(2,1)S(1)} %add_convert_fusion.14), channel_id=1, source_target_pairs={{0,2},{1,3},{2,0},{3,1},{4,6},{5,7},{6,4},{7,5},{8,10},{9,11},{10,... | collective-permute-start | bytes 1228808 | tf_op jit(solution)/shard_map/ppermute | solution.py:57
  438.8 31.1 %collective-permute-start.30 = (bf16[160,1280]{1,0:T(8,128)(2,1)S(1)}, bf16[160,1280]{1,0:T(8,128)(2,1)S(1)}, u32[]{:S(2)}, u32[]{:S(2)}) collective-permute-start(bf16[160,1280]{1,0:T(8,128)(2,1)S(1)} %get-tuple-element.228), channel_id=1, source_target_pairs={{0,24},{4,28},{8,16},{12,20},{16,8},{20,12},{24,0},{28,4},{1,25},{... | collective-permute-start | bytes 1228808 | tf_op jit(solution)/shard_map/ppermute | solution.py:104
  526.4 29.9 %collective-permute-start.101 = (f32[2,4,160]{2,0,1:T(2,128)S(1)}, f32[2,4,160]{2,0,1:T(2,128)S(1)}, u32[]{:S(2)}, u32[]{:S(2)}) collective-permute-start(f32[2,4,160]{2,0,1:T(2,128)S(1)} %fusion.128), channel_id=1, source_target_pairs={{0,4},{4,0},{8,12},{12,8},{1,5},{5,1},{9,13},{13,9},{2,6},{6,2},{1... | collective-permute-start | bytes 15368 | tf_op jit(solution)/shard_map/ppermute | solution.py:57
  557.7 30.6 %collective-permute-start.64 = (bf16[160,1280]{1,0:T(8,128)(2,1)}, bf16[160,1280]{1,0:T(8,128)(2,1)}, u32[]{:S(2)}, u32[]{:S(2)}) collective-permute-start(bf16[160,1280]{1,0:T(8,128)(2,1)} %get-tuple-element.216), channel_id=1, source_target_pairs={{0,8},{4,12},{8,0},{12,4},{16,24},{20,28},{24,16},{28,20},{1,9},{5... | collective-permute-start | bytes 1228808 | tf_op jit(solution)/shard_map/ppermute | solution.py:104
  558.3 45.4 %collective-permute-start.66 = (bf16[160,1280]{1,0:T(8,128)(2,1)}, bf16[160,1280]{1,0:T(8,128)(2,1)}, u32[]{:S(2)}, u32[]{:S(2)}) collective-permute-start(bf16[160,1280]{1,0:T(8,128)(2,1)} %get-tuple-element.217), channel_id=1, source_target_pairs={{0,24},{4,28},{8,16},{12,20},{16,8},{20,12},{24,0},{28,4},{1,25},{... | collective-permute-start | bytes 1228808 | tf_op jit(solution)/shard_map/ppermute | solution.py:104
  560.0 43.7 %collective-permute-start.65 = (bf16[160,1280]{1,0:T(8,128)(2,1)}, bf16[160,1280]{1,0:T(8,128)(2,1)}, u32[]{:S(2)}, u32[]{:S(2)}) collective-permute-start(bf16[160,1280]{1,0:T(8,128)(2,1)} %get-tuple-element.218), channel_id=1, source_target_pairs={{0,16},{4,20},{8,24},{12,28},{16,0},{20,4},{24,8},{28,12},{1,17},{... | collective-permute-start | bytes 1228808 | tf_op jit(solution)/shard_map/ppermute | solution.py:104
  564.8 39.5 %collective-permute-start.49 = (bf16[160,1280]{1,0:T(8,128)(2,1)}, bf16[160,1280]{1,0:T(8,128)(2,1)}, u32[]{:S(2)}, u32[]{:S(2)}) collective-permute-start(bf16[160,1280]{1,0:T(8,128)(2,1)} %get-tuple-element.219), channel_id=1, source_target_pairs={{0,8},{4,12},{8,0},{12,4},{16,24},{20,28},{24,16},{28,20},{1,9},{5... | collective-permute-start | bytes 1228808 | tf_op jit(solution)/shard_map/ppermute | solution.py:104
  603.7 68.7 %collective-permute-start.89 = (bf16[640,1280]{1,0:T(8,128)(2,1)}, bf16[640,1280]{1,0:T(8,128)(2,1)}, u32[]{:S(2)}, u32[]{:S(2)}) collective-permute-start(bf16[640,1280]{1,0:T(8,128)(2,1)} %slice.207), channel_id=1, source_target_pairs={{0,4},{4,0},{8,12},{12,8},{1,5},{5,1},{9,13},{13,9},{2,6},{6,2},{1... | collective-permute-start | bytes 4915208 | tf_op jit(solution)/shard_map/ppermute | solution.py:57
  603.7 73.3 %collective-permute-start.85 = (bf16[640,1280]{1,0:T(8,128)(2,1)}, bf16[640,1280]{1,0:T(8,128)(2,1)}, u32[]{:S(2)}, u32[]{:S(2)}) collective-permute-start(bf16[640,1280]{1,0:T(8,128)(2,1)} %slice.205), channel_id=1, source_target_pairs={{0,4},{4,0},{8,12},{12,8},{1,5},{5,1},{9,13},{13,9},{2,6},{6,2},{1... | collective-permute-start | bytes 4915208 | tf_op jit(solution)/shard_map/ppermute | solution.py:57
  647.6 42.5 %collective-permute-start.81 = (bf16[640,1280]{1,0:T(8,128)(2,1)}, bf16[640,1280]{1,0:T(8,128)(2,1)}, u32[]{:S(2)}, u32[]{:S(2)}) collective-permute-start(bf16[640,1280]{1,0:T(8,128)(2,1)} %slice.203), channel_id=1, source_target_pairs={{0,4},{4,0},{8,12},{12,8},{1,5},{5,1},{9,13},{13,9},{2,6},{6,2},{1... | collective-permute-start | bytes 4915208 | tf_op jit(solution)/shard_map/ppermute | solution.py:57
  675.9 163.3 %collective-permute-start.90 = (bf16[160,1280]{1,0:T(8,128)(2,1)}, bf16[160,1280]{1,0:T(8,128)(2,1)}, u32[]{:S(2)}, u32[]{:S(2)}) collective-permute-start(bf16[160,1280]{1,0:T(8,128)(2,1)} %get-tuple-element.208), channel_id=1, source_target_pairs={{0,1},{1,0},{2,3},{3,2},{4,5},{5,4},{6,7},{7,6},{8,9},{9,8},{10,11... | collective-permute-start | bytes 1228808 | tf_op jit(solution)/shard_map/ppermute | solution.py:57
  677.0 145.3 %collective-permute-start.91 = (bf16[160,1280]{1,0:T(8,128)(2,1)}, bf16[160,1280]{1,0:T(8,128)(2,1)}, u32[]{:S(2)}, u32[]{:S(2)}) collective-permute-start(bf16[160,1280]{1,0:T(8,128)(2,1)} %get-tuple-element.209), channel_id=1, source_target_pairs={{0,1},{1,0},{2,3},{3,2},{4,5},{5,4},{6,7},{7,6},{8,9},{9,8},{10,11... | collective-permute-start | bytes 1228808 | tf_op jit(solution)/shard_map/ppermute | solution.py:57
  686.0 165.2 %collective-permute-start.86 = (bf16[160,1280]{1,0:T(8,128)(2,1)}, bf16[160,1280]{1,0:T(8,128)(2,1)}, u32[]{:S(2)}, u32[]{:S(2)}) collective-permute-start(bf16[160,1280]{1,0:T(8,128)(2,1)} %get-tuple-element.206), channel_id=1, source_target_pairs={{0,1},{1,0},{2,3},{3,2},{4,5},{5,4},{6,7},{7,6},{8,9},{9,8},{10,11... | collective-permute-start | bytes 1228808 | tf_op jit(solution)/shard_map/ppermute | solution.py:57
  688.8 135.6 %collective-permute-start.87 = (bf16[160,1280]{1,0:T(8,128)(2,1)}, bf16[160,1280]{1,0:T(8,128)(2,1)}, u32[]{:S(2)}, u32[]{:S(2)}) collective-permute-start(bf16[160,1280]{1,0:T(8,128)(2,1)} %get-tuple-element.207), channel_id=1, source_target_pairs={{0,1},{1,0},{2,3},{3,2},{4,5},{5,4},{6,7},{7,6},{8,9},{9,8},{10,11... | collective-permute-start | bytes 1228808 | tf_op jit(solution)/shard_map/ppermute | solution.py:57
  690.2 39.0 %collective-permute-start.69 = (bf16[160,1280]{1,0:T(8,128)(2,1)}, bf16[160,1280]{1,0:T(8,128)(2,1)S(1)}, u32[]{:S(2)}, u32[]{:S(2)}) collective-permute-start(bf16[160,1280]{1,0:T(8,128)(2,1)} %collective-permute-done.68), channel_id=1, source_target_pairs={{0,1},{1,0},{2,3},{3,2},{4,5},{5,4},{6,7},{7,6},{8,9},{9,8},{10,11... | collective-permute-start | bytes 1228808 | tf_op jit(solution)/shard_map/ppermute | solution.py:57
  729.1 146.0 %collective-permute-start.82 = (bf16[160,1280]{1,0:T(8,128)(2,1)}, bf16[160,1280]{1,0:T(8,128)(2,1)}, u32[]{:S(2)}, u32[]{:S(2)}) collective-permute-start(bf16[160,1280]{1,0:T(8,128)(2,1)} %get-tuple-element.204), channel_id=1, source_target_pairs={{0,1},{1,0},{2,3},{3,2},{4,5},{5,4},{6,7},{7,6},{8,9},{9,8},{10,11... | collective-permute-start | bytes 1228808 | tf_op jit(solution)/shard_map/ppermute | solution.py:57
  839.1 61.8 %collective-permute-start.70 = (bf16[640,640]{1,0:T(8,128)(2,1)}, bf16[640,640]{1,0:T(8,128)(2,1)}, u32[]{:S(2)}, u32[]{:S(2)}) collective-permute-start(bf16[640,640]{1,0:T(8,128)(2,1)} %get-tuple-element.192), channel_id=1, source_target_pairs={{0,4},{4,0},{8,12},{12,8},{1,5},{5,1},{9,13},{13,9},{2,6},{6,2},{1... | collective-permute-start | bytes 2457608 | tf_op jit(solution)/shard_map/ppermute | solution.py:57
  839.3 33.6 %collective-permute-start.71 = (bf16[640,640]{1,0:T(8,128)(2,1)S(1)}, bf16[640,640]{1,0:T(8,128)(2,1)S(1)}, u32[]{:S(2)}, u32[]{:S(2)}) collective-permute-start(bf16[640,640]{1,0:T(8,128)(2,1)S(1)} %copy-done.85), channel_id=1, source_target_pairs={{0,4},{4,0},{8,12},{12,8},{1,5},{5,1},{9,13},{13,9},{2,6},{6,2},{1... | collective-permute-start | bytes 2457608 | tf_op jit(solution)/shard_map/ppermute | solution.py:57
  851.2 58.3 %collective-permute-start.55 = (bf16[640,640]{1,0:T(8,128)(2,1)}, bf16[640,640]{1,0:T(8,128)(2,1)}, u32[]{:S(2)}, u32[]{:S(2)}) collective-permute-start(bf16[640,640]{1,0:T(8,128)(2,1)} %get-tuple-element.190), channel_id=1, source_target_pairs={{0,4},{4,0},{8,12},{12,8},{1,5},{5,1},{9,13},{13,9},{2,6},{6,2},{1... | collective-permute-start | bytes 2457608 | tf_op jit(solution)/shard_map/ppermute | solution.py:57
  891.6 147.6 %all-to-all-start.1 = ((bf16[8,3,160,160]{3,2,1,0:T(8,128)(2,1)}), bf16[8,3,160,160]{3,2,1,0:T(8,128)(2,1)}, u32[]{:S(2)}, u32[]{:S(2)}) async-start(bf16[8,3,160,160]{3,2,1,0:T(8,128)(2,1)} %pad_maximum_fusion.3), calls=%async_computation.1 | async-start | bytes 3932160 | tf_op jit(solution)/shard_map/all_to_all | solution.py:172
  899.0 39.2 %collective-permute-start.57 = (bf16[640,640]{1,0:T(8,128)(2,1)}, bf16[640,640]{1,0:T(8,128)(2,1)}, u32[]{:S(2)}, u32[]{:S(2)}) collective-permute-start(bf16[640,640]{1,0:T(8,128)(2,1)} %add_convert_fusion.4), channel_id=1, source_target_pairs={{0,8},{4,12},{8,0},{12,4},{1,9},{5,13},{9,1},{13,5},{2,10},{6,14},... | collective-permute-start | bytes 2457608 | tf_op jit(solution)/shard_map/ppermute | solution.py:57
  961.0 41.0 %collective-permute-start.98 = (f32[320]{0:T(512)S(1)}, f32[320]{0:T(512)S(1)}, u32[]{:S(2)}, u32[]{:S(2)}) collective-permute-start(f32[320]{0:T(512)S(1)} %add_add_fusion.14), channel_id=1, source_target_pairs={{0,16},{16,0},{1,17},{17,1},{2,18},{18,2},{3,19},{19,3},{4,20},{20... | collective-permute-start | bytes 3848 | tf_op jit(solution)/shard_map/ppermute | solution.py:57
  990.9 84.2 %collective-permute-start.76 = (bf16[2,2,160,1280]{3,2,1,0:T(8,128)(2,1)}, bf16[2,2,160,1280]{3,2,1,0:T(8,128)(2,1)}, u32[]{:S(2)}, u32[]{:S(2)}) collective-permute-start(bf16[2,2,160,1280]{3,2,1,0:T(8,128)(2,1)} %dynamic-slice_bitcast_fusion), channel_id=1, source_target_pairs={{0,4},{4,0},{8,12},{12,8},{1,5},{5,1},{9,13},{13,9},{2,6},{6,2},{1... | collective-permute-start | bytes 4915208 | tf_op jit(solution)/shard_map/ppermute | solution.py:57
  996.4 54.8 %collective-permute-start.58 = (bf16[160,1280]{1,0:T(8,128)(2,1)}, bf16[160,1280]{1,0:T(8,128)(2,1)S(1)}, u32[]{:S(2)}, u32[]{:S(2)}) collective-permute-start(bf16[160,1280]{1,0:T(8,128)(2,1)} %get-tuple-element.212), channel_id=1, source_target_pairs={{0,1},{1,0},{2,3},{3,2},{4,5},{5,4},{6,7},{7,6},{8,9},{9,8},{10,11... | collective-permute-start | bytes 1228808 | tf_op jit(solution)/shard_map/ppermute | solution.py:57
  1003.1 48.1 %collective-permute-start.73 = (bf16[160,1280]{1,0:T(8,128)(2,1)}, bf16[160,1280]{1,0:T(8,128)(2,1)S(1)}, u32[]{:S(2)}, u32[]{:S(2)}) collective-permute-start(bf16[160,1280]{1,0:T(8,128)(2,1)} %get-tuple-element.214), channel_id=1, source_target_pairs={{0,1},{1,0},{2,3},{3,2},{4,5},{5,4},{6,7},{7,6},{8,9},{9,8},{10,11... | collective-permute-start | bytes 1228808 | tf_op jit(solution)/shard_map/ppermute | solution.py:57
  1003.3 31.5 %collective-permute-start.74 = (bf16[160,1280]{1,0:T(8,128)(2,1)S(1)}, bf16[160,1280]{1,0:T(8,128)(2,1)S(1)}, u32[]{:S(2)}, u32[]{:S(2)}) collective-permute-start(bf16[160,1280]{1,0:T(8,128)(2,1)S(1)} %get-tuple-element.215), channel_id=1, source_target_pairs={{0,1},{1,0},{2,3},{3,2},{4,5},{5,4},{6,7},{7,6},{8,9},{9,8},{10,11... | collective-permute-start | bytes 1228808 | tf_op jit(solution)/shard_map/ppermute | solution.py:57
  1034.8 30.0 %collective-permute-start.60 = (bf16[160,1280]{1,0:T(8,128)(2,1)}, bf16[160,1280]{1,0:T(8,128)(2,1)S(1)}, u32[]{:S(2)}, u32[]{:S(2)}) collective-permute-start(bf16[160,1280]{1,0:T(8,128)(2,1)} %add_convert_fusion.12), channel_id=1, source_target_pairs={{0,2},{1,3},{2,0},{3,1},{4,6},{5,7},{6,4},{7,5},{8,10},{9,11},{10,... | collective-permute-start | bytes 1228808 | tf_op jit(solution)/shard_map/ppermute | solution.py:57
  1038.6 35.0 %collective-permute-start.75 = (bf16[160,1280]{1,0:T(8,128)(2,1)}, bf16[160,1280]{1,0:T(8,128)(2,1)S(1)}, u32[]{:S(2)}, u32[]{:S(2)}) collective-permute-start(bf16[160,1280]{1,0:T(8,128)(2,1)} %add_convert_fusion.11), channel_id=1, source_target_pairs={{0,2},{1,3},{2,0},{3,1},{4,6},{5,7},{6,4},{7,5},{8,10},{9,11},{10,... | collective-permute-start | bytes 1228808 | tf_op jit(solution)/shard_map/ppermute | solution.py:57
  (199 other events, 3188.4 us)
Sparse Core Ops, SparseCore 0:
  19.4 46.7 all-gather.1

commit v6 on v5

--- a/solution.py
+++ b/solution.py
@@ -120,12 +120,9 @@
     return total
 
 
-def hidden_weights(w_up, w_gate, w_down):
+def hidden_shards(w_up, w_gate, w_down):
     if not in_plane():
-        return tuple(
-            lax.all_gather(matrix, SPREAD, axis=1, tiled=True)
-            for matrix in (w_up.T, w_gate.T, w_down)
-        )
+        return jnp.stack([w_up.T, w_gate.T, w_down])
     rows, hidden = w_up.shape
     part = hidden // 8
     packed = jnp.stack(
@@ -137,7 +134,14 @@
         axis=1,
     )
     packed = lax.all_to_all(packed, SPREAD, 0, 0)
-    matrices = packed.transpose(1, 2, 0, 3).reshape(3, part, 8 * rows)
+    return packed.transpose(1, 2, 0, 3).reshape(3, part, 8 * rows)
+
+
+def hidden_weights(matrices):
+    if not in_plane():
+        return tuple(
+            lax.all_gather(matrices[place], SPREAD, axis=1, tiled=True) for place in range(3)
+        )
     out = []
     for place in range(3):
         own_core = group_gather(matrices[place], "tp")
@@ -441,10 +445,9 @@
     return seen_factors(reachable, *row_labels(slots, group_size))
 
 
-def forward_attention(gathered, vectors, tokens_own, parents, slots):
-    w_query, w_key, w_value, w_attn_out = gathered[:4]
+def forward_attention(gathered, vectors, hidden_group, parents, slots):
+    w_query, w_key, w_value, w_attn_out = gathered
     alpha_attn, alpha_mlp, scale_qk, scale_up, scale_gate = vectors
-    hidden_group = group_gather(tokens_own, "tp")
     visible = visibility(parents, slots, hidden_group.shape[0])
     query_raw = jnp.dot(hidden_group, w_query, preferred_element_type=jnp.float32)
     key_raw = jnp.dot(hidden_group, w_key, preferred_element_type=jnp.float32)
@@ -471,7 +474,7 @@
 
 
 def feed_forward(gathered, vectors, tokens_own, branch_one, cotangent_own):
-    w_up, w_gate, w_down = gathered[4:]
+    w_up, w_gate, w_down = gathered
     alpha_attn, alpha_mlp, scale_qk, scale_up, scale_gate = vectors
     tokens_wide = tokens_own.astype(jnp.float32)
     hidden_one = mix_rows(tokens_wide, branch_one, alpha_attn)
@@ -504,8 +507,8 @@
     return output_wide.astype(jnp.bfloat16), tokens_direct, branch_one_grad, factors, sums
 
 
-def backward_attention(gathered, vectors, kept, branch_one_grad, tokens_direct):
-    w_query, w_key, w_value, w_attn_out = gathered[:4]
+def backward_attention(gathered, vectors, kept, branch_one_group, tokens_direct):
+    w_query, w_key, w_value, w_attn_out = gathered
     scale_qk = vectors[2]
     (
         hidden_group,
@@ -517,7 +520,6 @@
         scale,
         heads_low,
     ) = kept
-    branch_one_group = group_gather(branch_one_grad.astype(jnp.bfloat16), "tp")
     heads_grad = jnp.dot(
         branch_one_group, w_attn_out, preferred_element_type=jnp.float32
     ).astype(jnp.bfloat16)
@@ -570,18 +572,20 @@
         packed[:, local_heads : 2 * local_heads],
         packed[:, 2 * local_heads : 3 * local_heads],
         packed[:, 3 * local_heads :],
-    ) + hidden_weights(w_up, w_gate, w_down)
+    )
     micros = range(tokens.shape[0])
+    groups = [group_gather(tokens[m, 0], "tp") for m in micros]
+    shards, groups = lax.optimization_barrier((hidden_shards(w_up, w_gate, w_down), groups))
+    hidden_gathered = hidden_weights(shards)
     front = [
-        forward_attention(gathered, vectors, tokens[m, 0], parents[m, 0], slot_segment[m, 0])
+        forward_attention(gathered, vectors, groups[m], parents[m, 0], slot_segment[m, 0])
         for m in micros
     ]
     mid = [
-        feed_forward(gathered, vectors, tokens[m, 0], front[m][0], cotangent[m, 0]) for m in micros
+        feed_forward(hidden_gathered, vectors, tokens[m, 0], front[m][0], cotangent[m, 0])
+        for m in micros
     ]
-    back = [
-        backward_attention(gathered, vectors, front[m][1], mid[m][2], mid[m][1]) for m in micros
-    ]
+    tops = [group_gather(mid[m][2].astype(jnp.bfloat16), "tp") for m in micros]
 
     def stack(pick):
         return jnp.concatenate([pick(m) for m in micros], axis=0)
@@ -589,20 +593,23 @@
     mixed_all, top_all, hidden_all, up_all, gate_all = (
         stack(lambda m: mid[m][3][place]) for place in range(5)
     )
+    products = [
+        contract_rows(former, latter).astype(jnp.bfloat16)
+        for former, latter in (
+            (up_all, hidden_all),
+            (gate_all, hidden_all),
+            (mixed_all, top_all),
+        )
+    ]
+    products, tops[-1] = lax.optimization_barrier((products, tops[-1]))
+    back = [
+        backward_attention(gathered, vectors, front[m][1], tops[m], mid[m][1]) for m in micros
+    ]
     tokens_all, query_all, key_all, value_all, heads_all, branch_all = (
         stack(lambda m: back[m][1][place]) for place in range(6)
     )
 
-    grad_u, grad_g, grad_d = hidden_weight_grads(
-        [
-            contract_rows(former, latter).astype(jnp.bfloat16)
-            for former, latter in (
-                (up_all, hidden_all),
-                (gate_all, hidden_all),
-                (mixed_all, top_all),
-            )
-        ]
-    )
+    grad_u, grad_g, grad_d = hidden_weight_grads(products)
     attention_product = jnp.concatenate(
         [
             contract_rows(tokens_all, query_all),

time: 1110 us -> 1050 us (0.946)
  local copies, waits for them, and re-layouts: 170 us -> 141 us
  other arithmetic: 116 us -> 102 us
  matrix products: 130 us -> 117 us
    unnamed x313 -> x299, local copies, waits for them, and re-layouts: 43.7 us -> 31.3 us
    concatenate x6 -> x9, other arithmetic: 26 us -> 26.4 us  [group_gather(): jnp.concatenate([own_block, beside, across, swap(across, axis, 1)], axis=0)]
  transfers between devices with their start and end apart: 111 -> 111, of which waited for: 51 -> 57; matrix products, arithmetic and copies ran while one was open for 33% -> 29% of each run, Pallas kernels for 9% -> 6%
where the time goes in v6:
time: 1050 us; the launch traced here: 1040 us
  waiting for transfers between devices  452 us (43%)
  local copies, waits for them, and re-layouts  141 us (13%)
  matrix products  117 us (11%)
  starting transfers between devices  114 us (11%)
  other arithmetic  102 us (10%)
  Pallas kernels  99.6 us (9%)
  between operations  17.1 us (2%)
    ppermute x84, waiting for transfers between devices, swap(): lax.ppermute(value, axis, [(place, place ^ bit) for place in range(size)])  358 us
    ppermute x24, waiting for transfers between devices, hop(): lax.ppermute(value, SPREAD, [(place, place ^ bits) for place in range(8)])  93.9 us
    ppermute x84, starting transfers between devices, swap(): lax.ppermute(value, axis, [(place, place ^ bit) for place in range(size)])  74.8 us
    pallas_call x2, Pallas kernels, attend_grad(): pl.pallas_call(attend_grad_body, grid=(keys // KEY_TILE,), in_specs=[pl.B...  64.7 us
    dot_general x14, matrix products, contract_cols(): lax.dot_general(former, latter, (((1,), (1,)), ((), ())), preferred_eleme...  40.6 us
    pallas_call x2, Pallas kernels, attend(): pl.pallas_call(attend_body, grid=(keys // KEY_TILE,), in_specs=[pl.BlockS...  34.9 us
    dot_general x7, matrix products, contract_rows(): lax.dot_general(former, latter, (((0,), (0,)), ((), ())), preferred_eleme...  33.7 us
    unnamed x299, local copies, waits for them, and re-layouts  31.3 us
  transfers between devices with their start and end apart: 111, of which 57 were waited for; matrix products, arithmetic and copies ran while one was open for 29% of the time, Pallas kernels for 6%

profile of v6, /device:TPU:0, one launch (start us, length us, event | category | flops | bytes accessed | tf_op | source)
XLA Modules:
  0.0 1042.2 jit_solution(16191107306946142767)
XLA Ops:
  40.5 17.3 %collective-permute-done.21 = f32[1,2,160]{2,1,0:T(2,128)S(1)} collective-permute-done((f32[1,2,160]{2,1,0:T(2,128)S(1)}, f32[1,2,160]{2,1,0:T(2,128)S(1)}, u32[]{:S(2)}, u32[]{:S(2)}) %collective-permute-start.21) | collective-permute-done | bytes 1312 | tf_op jit(solution)/shard_map/ppermute | solution.py:57
  59.2 7.4 collective-permute-done.5
  92.4 14.9 %collective-permute-done.28 = bf16[160,1280]{1,0:T(8,128)(2,1)S(1)} collective-permute-done((bf16[160,1280]{1,0:T(8,128)(2,1)S(1)}, bf16[160,1280]{1,0:T(8,128)(2,1)S(1)}, u32[]{:S(2)}, u32[]{:S(2)}) %collective-permute-start.28) | collective-permute-done | bytes 409632 | tf_op jit(solution)/shard_map/ppermute | solution.py:57
  109.3 15.6 %collective-permute-done.24 = bf16[160,1280]{1,0:T(8,128)(2,1)S(1)} collective-permute-done((bf16[160,1280]{1,0:T(8,128)(2,1)S(1)}, bf16[160,1280]{1,0:T(8,128)(2,1)S(1)}, u32[]{:S(2)}, u32[]{:S(2)}) %collective-permute-start.24) | collective-permute-done | bytes 409632 | tf_op jit(solution)/shard_map/ppermute | solution.py:57
  124.9 15.8 %collective-permute-done.16 = bf16[160,1280]{1,0:T(8,128)(2,1)} collective-permute-done((bf16[160,1280]{1,0:T(8,128)(2,1)S(1)}, bf16[160,1280]{1,0:T(8,128)(2,1)}, u32[]{:S(2)}, u32[]{:S(2)}) %collective-permute-start.16) | collective-permute-done | bytes 409632 | tf_op jit(solution)/shard_map/ppermute | solution.py:57
  152.4 7.4 collective-permute-done.25
  204.4 5.9 multiply_convert_fusion.6
  229.1 10.0 collective-permute-done.35
  245.9 10.2 collective-permute-done.7
  256.6 8.8 pad_maximum_fusion.1.tree_ref
  265.5 17.2 %attend.3 = (bf16[640,320]{1,0:T(8,128)(2,1)S(1)}, f32[8,640]{1,0:T(8,128)S(1)}) custom-call(bf16[640,320]{1,0:T(8,128)(2,1)S(1)} %get-tuple-element.287.query_ref, bf16[2560,640]{1,0:T(8,128)(2,1)S(1)} %pad_maximum_fusion.1.tree_ref, bf16[2560,128]{1,0:T(8,128)(2,1)S(1)} %get-tuple-element.269.hot_ref, bf16[3,128,640]{2,1,0:T(8,128)(2,1)S(1)} %get-tuple-element.263.side_ref), custom_call_target="tpu_custom_call" | custom-call | tf_op jit(solution)/shard_map/attend/pallas_call | solution.py:311
  286.1 8.4 pad_maximum_fusion.tree_ref
  294.6 17.6 %attend.2 = (bf16[640,320]{1,0:T(8,128)(2,1)S(1)}, f32[8,640]{1,0:T(8,128)S(1)}) custom-call(bf16[640,320]{1,0:T(8,128)(2,1)S(1)} %copy-done.8, bf16[2560,640]{1,0:T(8,128)(2,1)S(1)} %pad_maximum_fusion.tree_ref, bf16[2560,128]{1,0:T(8,128)(2,1)S(1)} %copy-done.2, bf16[3,128,640]{2,1,0:T(8,128)(2,1)S(1)} %copy-done.10), custom_call_target="tpu_custom_call" | custom-call | tf_op jit(solution)/shard_map/attend/pallas_call | solution.py:311
  315.7 17.5 %collective-permute-done.10 = bf16[160,1280]{1,0:T(8,128)(2,1)S(1)} collective-permute-done((bf16[160,1280]{1,0:T(8,128)(2,1)S(1)}, bf16[160,1280]{1,0:T(8,128)(2,1)S(1)}, u32[]{:S(2)}, u32[]{:S(2)}) %collective-permute-start.10) | collective-permute-done | bytes 409632 | tf_op jit(solution)/shard_map/ppermute | solution.py:57
  337.8 23.8 %collective-permute-done.39 = bf16[160,1280]{1,0:T(8,128)(2,1)S(1)} collective-permute-done((bf16[160,1280]{1,0:T(8,128)(2,1)S(1)}, bf16[160,1280]{1,0:T(8,128)(2,1)S(1)}, u32[]{:S(2)}, u32[]{:S(2)}) %collective-permute-start.39) | collective-permute-done | bytes 409632 | tf_op jit(solution)/shard_map/ppermute | solution.py:57
  361.9 8.4 collective-permute-done.11
  377.3 6.7 collective-permute-done.12
  384.0 12.6 %collective-permute-done.13 = bf16[160,1280]{1,0:T(8,128)(2,1)S(1)} collective-permute-done((bf16[160,1280]{1,0:T(8,128)(2,1)S(1)}, bf16[160,1280]{1,0:T(8,128)(2,1)S(1)}, u32[]{:S(2)}, u32[]{:S(2)}) %collective-permute-start.13) | collective-permute-done | bytes 409632 | tf_op jit(solution)/shard_map/ppermute | solution.py:104
  410.2 5.9 collective-permute-done.41
  420.1 7.4 multiply_convert_fusion.4
  443.6 8.3 collective-permute-done.45
  454.2 5.8 collective-permute-done.31
  460.0 8.5 collective-permute-done.33
  476.0 8.8 collective-permute-done.46
  484.8 11.0 %collective-permute-done.47 = bf16[160,1280]{1,0:T(8,128)(2,1)S(1)} collective-permute-done((bf16[160,1280]{1,0:T(8,128)(2,1)S(1)}, bf16[160,1280]{1,0:T(8,128)(2,1)S(1)}, u32[]{:S(2)}, u32[]{:S(2)}) %collective-permute-start.47) | collective-permute-done | bytes 409632 | tf_op jit(solution)/shard_map/ppermute | solution.py:104
  510.6 12.4 %multiply_reduce_fusion.2 = (f32[1280]{0:T(1024)S(1)}, f32[1280]{0:T(1024)S(1)}, f32[1280]{0:T(1024)S(1)}, f32[1280]{0:T(1024)S(1)}, f32[640,1280]{1,0:T(8,128)}...) fusion(f32[640,1280]{1,0:T(8,128)} %get-tuple-element.307, f32[640,1280]{1,0:T(8,128)} %fusion.101, ...), kind=kOutput, calls=%fused_computation.34 | convolution fusion | flops 2138926080 | bytes 29521920 | tf_op jit(solution)/shard_map/dot_general | solution.py:38
  531.8 6.1 convolution_convert_fusion.1
  537.9 6.1 convolution_convert_fusion.2
  563.4 10.4 collective-permute-done.105
  583.2 9.1 convolution_convert_fusion
  593.7 7.6 collective-permute-done.50
  620.3 12.4 %collective-permute-done.96 = f32[2560]{0:T(1024)S(1)} collective-permute-done((f32[2560]{0:T(1024)S(1)}, f32[2560]{0:T(1024)S(1)}, u32[]{:S(2)}, u32[]{:S(2)}) %collective-permute-start.96) | collective-permute-done | bytes 10272 | tf_op jit(solution)/shard_map/ppermute | solution.py:57
  634.5 15.1 %collective-permute-done.97 = f32[2560]{0:T(1024)S(1)} collective-permute-done((f32[2560]{0:T(1024)S(1)}, f32[2560]{0:T(1024)S(1)}, u32[]{:S(2)}, u32[]{:S(2)}) %collective-permute-start.97) | collective-permute-done | bytes 10272 | tf_op jit(solution)/shard_map/ppermute | solution.py:57
  654.0 8.6 collective-permute-done.69
  676.5 32.2 %attend_grad.3 = (f32[640,320]{1,0:T(8,128)S(1)}, bf16[2560,640]{1,0:T(8,128)(2,1)}) custom-call(bf16[640,640]{1,0:T(8,128)(2,1)S(1)} %get-tuple-element.309.both_ref, bf16[640,320]{1,0:T(8,128)(2,1)S(1)} %copy-done.16, bf16[2560,640]{1,0:T(8,128)(2,1)} %copy-done.1, bf16[2560,128]{1,0:T(8,128)(2,1)S(1)} %copy-done.5, bf16[3,128,640]{2,1,0:T(8,128)(2,1)S(1)} %copy-done.13, ...), custom_call_target="tpu_custom_call" | custom-call | tf_op jit(solution)/shard_map/attend_grad/pallas_call | solution.py:396
  719.8 32.5 %attend_grad.2 = (f32[640,320]{1,0:T(8,128)S(1)}, bf16[2560,640]{1,0:T(8,128)(2,1)}) custom-call(bf16[640,640]{1,0:T(8,128)(2,1)S(1)} %copy-done.14, bf16[640,320]{1,0:T(8,128)(2,1)S(1)} %copy-done.19, bf16[2560,640]{1,0:T(8,128)(2,1)} %copy-done, bf16[2560,128]{1,0:T(8,128)(2,1)S(1)} %copy-done.3, bf16[3,128,640]{2,1,0:T(8,128)(2,1)S(1)} %copy-done.11, ...), custom_call_target="tpu_custom_call" | custom-call | tf_op jit(solution)/shard_map/attend_grad/pallas_call | solution.py:396
  772.4 6.3 collective-permute-done.72
  789.4 9.4 collective-permute-done.57
  834.3 5.8 concatenate.168
  868.4 16.3 %collective-permute-done.87 = bf16[160,1280]{1,0:T(8,128)(2,1)S(1)} collective-permute-done((bf16[160,1280]{1,0:T(8,128)(2,1)S(1)}, bf16[160,1280]{1,0:T(8,128)(2,1)S(1)}, u32[]{:S(2)}, u32[]{:S(2)}) %collective-permute-start.87) | collective-permute-done | bytes 409632 | tf_op jit(solution)/shard_map/ppermute | solution.py:57
  885.9 13.8 %collective-permute-done.83 = bf16[160,1280]{1,0:T(8,128)(2,1)S(1)} collective-permute-done((bf16[160,1280]{1,0:T(8,128)(2,1)S(1)}, bf16[160,1280]{1,0:T(8,128)(2,1)S(1)}, u32[]{:S(2)}, u32[]{:S(2)}) %collective-permute-start.83) | collective-permute-done | bytes 409632 | tf_op jit(solution)/shard_map/ppermute | solution.py:57
  901.0 8.3 collective-permute-done.59
  911.4 7.9 collective-permute-done.74
  921.7 12.8 %collective-permute-done.92 = bf16[160,1280]{1,0:T(8,128)(2,1)S(1)} collective-permute-done((bf16[160,1280]{1,0:T(8,128)(2,1)S(1)}, bf16[160,1280]{1,0:T(8,128)(2,1)S(1)}, u32[]{:S(2)}, u32[]{:S(2)}) %collective-permute-start.92) | collective-permute-done | bytes 409632 | tf_op jit(solution)/shard_map/ppermute | solution.py:57
  936.7 15.9 %collective-permute-done.88 = bf16[160,1280]{1,0:T(8,128)(2,1)S(1)} collective-permute-done((bf16[160,1280]{1,0:T(8,128)(2,1)S(1)}, bf16[160,1280]{1,0:T(8,128)(2,1)S(1)}, u32[]{:S(2)}, u32[]{:S(2)}) %collective-permute-start.88) | collective-permute-done | bytes 409632 | tf_op jit(solution)/shard_map/ppermute | solution.py:57
  955.8 24.7 %collective-permute-done.84 = bf16[160,1280]{1,0:T(8,128)(2,1)S(1)} collective-permute-done((bf16[160,1280]{1,0:T(8,128)(2,1)S(1)}, bf16[160,1280]{1,0:T(8,128)(2,1)S(1)}, u32[]{:S(2)}, u32[]{:S(2)}) %collective-permute-start.84) | collective-permute-done | bytes 409632 | tf_op jit(solution)/shard_map/ppermute | solution.py:57
  989.1 9.1 collective-permute-done.60
  998.2 8.7 collective-permute-done.75
  (758 shorter events, 452.7 us)
Async XLA Ops:
  7.2 154.1 %all-gather.2.cloned.1.call-start = ((), (), s32[]{:S(2)}) async-start(), calls=%async_computation.2 | async-start | bytes 3686400 | tf_op jit(solution)/shard_map/all_gather | solution.py:567
  8.9 27.9 %collective-permute-start.20 = (f32[1,2,160]{2,1,0:T(2,128)S(1)}, f32[1,2,160]{2,1,0:T(2,128)S(1)}, u32[]{:S(2)}, u32[]{:S(2)}) collective-permute-start(f32[1,2,160]{2,1,0:T(2,128)S(1)} %maximum_bitcast_fusion.2), channel_id=1, source_target_pairs={{0,2},{1,3},{2,0},{3,1},{4,6},{5,7},{6,4},{7,5},{8,10},{9,11},{10,... | collective-permute-start | bytes 3848 | tf_op jit(solution)/shard_map/ppermute | solution.py:57
  16.1 43.0 %collective-permute-start.3 = (bf16[160,1280]{1,0:T(8,128)(2,1)S(1)}, bf16[160,1280]{1,0:T(8,128)(2,1)}, u32[]{:S(2)}, u32[]{:S(2)}) collective-permute-start(bf16[160,1280]{1,0:T(8,128)(2,1)S(1)} %get-tuple-element.257), channel_id=1, source_target_pairs={{0,1},{1,0},{2,3},{3,2},{4,5},{5,4},{6,7},{7,6},{8,9},{9,8},{10,11... | collective-permute-start | bytes 1228808 | tf_op jit(solution)/shard_map/ppermute | solution.py:57
  21.9 54.0 %all-to-all-start = ((bf16[8,3,160,160]{3,2,1,0:T(8,128)(2,1)}), bf16[8,3,160,160]{3,2,1,0:T(8,128)(2,1)}, u32[]{:S(2)}, u32[]{:S(2)}) async-start(bf16[8,3,160,160]{3,2,1,0:T(8,128)(2,1)} %pad_maximum_fusion.2), calls=%async_computation | async-start | bytes 3932160 | tf_op jit(solution)/shard_map/all_to_all | solution.py:136
  26.2 31.6 %collective-permute-start.1 = (bf16[160,1280]{1,0:T(8,128)(2,1)S(1)}, bf16[160,1280]{1,0:T(8,128)(2,1)}, u32[]{:S(2)}, u32[]{:S(2)}) collective-permute-start(bf16[160,1280]{1,0:T(8,128)(2,1)S(1)} %get-tuple-element.258), channel_id=1, source_target_pairs={{0,2},{1,3},{2,0},{3,1},{4,6},{5,7},{6,4},{7,5},{8,10},{9,11},{10,... | collective-permute-start | bytes 1228808 | tf_op jit(solution)/shard_map/ppermute | solution.py:57
  36.8 32.2 %collective-permute-start = (bf16[160,1280]{1,0:T(8,128)(2,1)S(1)}, bf16[160,1280]{1,0:T(8,128)(2,1)S(1)}, u32[]{:S(2)}, u32[]{:S(2)}) collective-permute-start(bf16[160,1280]{1,0:T(8,128)(2,1)S(1)} %get-tuple-element.258), channel_id=1, source_target_pairs={{0,1},{1,0},{2,3},{3,2},{4,5},{5,4},{6,7},{7,6},{8,9},{9,8},{10,11... | collective-permute-start | bytes 1228808 | tf_op jit(solution)/shard_map/ppermute | solution.py:57
  87.0 37.9 %collective-permute-start.24 = (bf16[160,1280]{1,0:T(8,128)(2,1)S(1)}, bf16[160,1280]{1,0:T(8,128)(2,1)S(1)}, u32[]{:S(2)}, u32[]{:S(2)}) collective-permute-start(bf16[160,1280]{1,0:T(8,128)(2,1)S(1)} %get-tuple-element.242), channel_id=1, source_target_pairs={{0,2},{1,3},{2,0},{3,1},{4,6},{5,7},{6,4},{7,5},{8,10},{9,11},{10,... | collective-permute-start | bytes 1228808 | tf_op jit(solution)/shard_map/ppermute | solution.py:57
  89.0 51.8 %collective-permute-start.23 = (bf16[160,1280]{1,0:T(8,128)(2,1)S(1)}, bf16[160,1280]{1,0:T(8,128)(2,1)S(1)}, u32[]{:S(2)}, u32[]{:S(2)}) collective-permute-start(bf16[160,1280]{1,0:T(8,128)(2,1)S(1)} %get-tuple-element.242), channel_id=1, source_target_pairs={{0,1},{1,0},{2,3},{3,2},{4,5},{5,4},{6,7},{7,6},{8,9},{9,8},{10,11... | collective-permute-start | bytes 1228808 | tf_op jit(solution)/shard_map/ppermute | solution.py:57
  91.0 49.7 %collective-permute-start.16 = (bf16[160,1280]{1,0:T(8,128)(2,1)S(1)}, bf16[160,1280]{1,0:T(8,128)(2,1)}, u32[]{:S(2)}, u32[]{:S(2)}) collective-permute-start(bf16[160,1280]{1,0:T(8,128)(2,1)S(1)} %get-tuple-element.243), channel_id=1, source_target_pairs={{0,2},{1,3},{2,0},{3,1},{4,6},{5,7},{6,4},{7,5},{8,10},{9,11},{10,... | collective-permute-start | bytes 1228808 | tf_op jit(solution)/shard_map/ppermute | solution.py:57
  107.3 35.1 %collective-permute-start.15 = (bf16[160,1280]{1,0:T(8,128)(2,1)S(1)}, bf16[160,1280]{1,0:T(8,128)(2,1)S(1)}, u32[]{:S(2)}, u32[]{:S(2)}) collective-permute-start(bf16[160,1280]{1,0:T(8,128)(2,1)S(1)} %get-tuple-element.243), channel_id=1, source_target_pairs={{0,1},{1,0},{2,3},{3,2},{4,5},{5,4},{6,7},{7,6},{8,9},{9,8},{10,11... | collective-permute-start | bytes 1228808 | tf_op jit(solution)/shard_map/ppermute | solution.py:57
  107.3 43.8 %collective-permute-start.29 = (bf16[160,1280]{1,0:T(8,128)(2,1)S(1)}, bf16[160,1280]{1,0:T(8,128)(2,1)S(1)}, u32[]{:S(2)}, u32[]{:S(2)}) collective-permute-start(bf16[160,1280]{1,0:T(8,128)(2,1)S(1)} %collective-permute-done.28), channel_id=1, source_target_pairs={{0,1},{1,0},{2,3},{3,2},{4,5},{5,4},{6,7},{7,6},{8,9},{9,8},{10,11... | collective-permute-start | bytes 1228808 | tf_op jit(solution)/shard_map/ppermute | solution.py:57
  124.8 35.0 %collective-permute-start.25 = (bf16[160,1280]{1,0:T(8,128)(2,1)S(1)}, bf16[160,1280]{1,0:T(8,128)(2,1)S(1)}, u32[]{:S(2)}, u32[]{:S(2)}) collective-permute-start(bf16[160,1280]{1,0:T(8,128)(2,1)S(1)} %collective-permute-done.24), channel_id=1, source_target_pairs={{0,1},{1,0},{2,3},{3,2},{4,5},{5,4},{6,7},{7,6},{8,9},{9,8},{10,11... | collective-permute-start | bytes 1228808 | tf_op jit(solution)/shard_map/ppermute | solution.py:57
  140.7 88.0 %collective-permute-start.17 = (bf16[160,1280]{1,0:T(8,128)(2,1)}, bf16[160,1280]{1,0:T(8,128)(2,1)}, u32[]{:S(2)}, u32[]{:S(2)}) collective-permute-start(bf16[160,1280]{1,0:T(8,128)(2,1)} %collective-permute-done.16), channel_id=1, source_target_pairs={{0,1},{1,0},{2,3},{3,2},{4,5},{5,4},{6,7},{7,6},{8,9},{9,8},{10,11... | collective-permute-start | bytes 1228808 | tf_op jit(solution)/shard_map/ppermute | solution.py:57
  152.4 91.3 %collective-permute-start.30 = (bf16[640,1280]{1,0:T(8,128)(2,1)}, bf16[640,1280]{1,0:T(8,128)(2,1)}, u32[]{:S(2)}, u32[]{:S(2)}) collective-permute-start(bf16[640,1280]{1,0:T(8,128)(2,1)} %pad_maximum_fusion.9), channel_id=1, source_target_pairs={{0,4},{4,0},{8,12},{12,8},{1,5},{5,1},{9,13},{13,9},{2,6},{6,2},{1... | collective-permute-start | bytes 4915208 | tf_op jit(solution)/shard_map/ppermute | solution.py:57
  161.2 172.7 %collective-permute-start.26 = (bf16[640,1280]{1,0:T(8,128)(2,1)}, bf16[640,1280]{1,0:T(8,128)(2,1)}, u32[]{:S(2)}, u32[]{:S(2)}) collective-permute-start(bf16[640,1280]{1,0:T(8,128)(2,1)} %pad_maximum_fusion.8), channel_id=1, source_target_pairs={{0,4},{4,0},{8,12},{12,8},{1,5},{5,1},{9,13},{13,9},{2,6},{6,2},{1... | collective-permute-start | bytes 4915208 | tf_op jit(solution)/shard_map/ppermute | solution.py:57
  222.9 33.2 %collective-permute-start.34 = (bf16[640,640]{1,0:T(8,128)(2,1)}, bf16[640,640]{1,0:T(8,128)(2,1)}, u32[]{:S(2)}, u32[]{:S(2)}) collective-permute-start(bf16[640,640]{1,0:T(8,128)(2,1)} %pad_maximum_fusion.13), channel_id=1, source_target_pairs={{0,4},{4,0},{8,12},{12,8},{1,5},{5,1},{9,13},{13,9},{2,6},{6,2},{1... | collective-permute-start | bytes 2457608 | tf_op jit(solution)/shard_map/ppermute | solution.py:57
  243.8 129.5 %collective-permute-start.18 = (bf16[640,1280]{1,0:T(8,128)(2,1)}, bf16[640,1280]{1,0:T(8,128)(2,1)}, u32[]{:S(2)}, u32[]{:S(2)}) collective-permute-start(bf16[640,1280]{1,0:T(8,128)(2,1)} %pad_maximum_fusion.7), channel_id=1, source_target_pairs={{0,4},{4,0},{8,12},{12,8},{1,5},{5,1},{9,13},{13,9},{2,6},{6,2},{1... | collective-permute-start | bytes 4915208 | tf_op jit(solution)/shard_map/ppermute | solution.py:57
  256.1 28.1 %collective-permute-start.6 = (bf16[640,640]{1,0:T(8,128)(2,1)S(1)}, bf16[640,640]{1,0:T(8,128)(2,1)S(1)}, u32[]{:S(2)}, u32[]{:S(2)}) collective-permute-start(bf16[640,640]{1,0:T(8,128)(2,1)S(1)} %pad_maximum_fusion.12), channel_id=1, source_target_pairs={{0,4},{4,0},{8,12},{12,8},{1,5},{5,1},{9,13},{13,9},{2,6},{6,2},{1... | collective-permute-start | bytes 2457608 | tf_op jit(solution)/shard_map/ppermute | solution.py:57
  256.1 30.1 %collective-permute-start.8 = (bf16[640,640]{1,0:T(8,128)(2,1)S(1)}, bf16[640,640]{1,0:T(8,128)(2,1)}, u32[]{:S(2)}, u32[]{:S(2)}) collective-permute-start(bf16[640,640]{1,0:T(8,128)(2,1)S(1)} %collective-permute-done.7), channel_id=1, source_target_pairs={{0,4},{4,0},{8,12},{12,8},{1,5},{5,1},{9,13},{13,9},{2,6},{6,2},{1... | collective-permute-start | bytes 2457608 | tf_op jit(solution)/shard_map/ppermute | solution.py:57
  284.0 53.9 %collective-permute-start.37 = (bf16[160,1280]{1,0:T(8,128)(2,1)S(1)}, bf16[160,1280]{1,0:T(8,128)(2,1)S(1)}, u32[]{:S(2)}, u32[]{:S(2)}) collective-permute-start(bf16[160,1280]{1,0:T(8,128)(2,1)S(1)} %get-tuple-element.234), channel_id=1, source_target_pairs={{0,1},{1,0},{2,3},{3,2},{4,5},{5,4},{6,7},{7,6},{8,9},{9,8},{10,11... | collective-permute-start | bytes 1228808 | tf_op jit(solution)/shard_map/ppermute | solution.py:57
  284.2 29.5 %collective-permute-start.38 = (bf16[160,1280]{1,0:T(8,128)(2,1)S(1)}, bf16[160,1280]{1,0:T(8,128)(2,1)S(1)}, u32[]{:S(2)}, u32[]{:S(2)}) collective-permute-start(bf16[160,1280]{1,0:T(8,128)(2,1)S(1)} %get-tuple-element.235), channel_id=1, source_target_pairs={{0,1},{1,0},{2,3},{3,2},{4,5},{5,4},{6,7},{7,6},{8,9},{9,8},{10,11... | collective-permute-start | bytes 1228808 | tf_op jit(solution)/shard_map/ppermute | solution.py:57
  313.5 48.5 %collective-permute-start.9 = (bf16[160,1280]{1,0:T(8,128)(2,1)S(1)}, bf16[160,1280]{1,0:T(8,128)(2,1)S(1)}, u32[]{:S(2)}, u32[]{:S(2)}) collective-permute-start(bf16[160,1280]{1,0:T(8,128)(2,1)S(1)} %get-tuple-element.239), channel_id=1, source_target_pairs={{0,1},{1,0},{2,3},{3,2},{4,5},{5,4},{6,7},{7,6},{8,9},{9,8},{10,11... | collective-permute-start | bytes 1228808 | tf_op jit(solution)/shard_map/ppermute | solution.py:57
  333.1 28.5 %collective-permute-start.39 = (bf16[160,1280]{1,0:T(8,128)(2,1)S(1)}, bf16[160,1280]{1,0:T(8,128)(2,1)S(1)}, u32[]{:S(2)}, u32[]{:S(2)}) collective-permute-start(bf16[160,1280]{1,0:T(8,128)(2,1)S(1)} %add_convert_fusion.13), channel_id=1, source_target_pairs={{0,2},{1,3},{2,0},{3,1},{4,6},{5,7},{6,4},{7,5},{8,10},{9,11},{10,... | collective-permute-start | bytes 1228808 | tf_op jit(solution)/shard_map/ppermute | solution.py:57
  333.9 36.4 %collective-permute-start.11 = (bf16[160,1280]{1,0:T(8,128)(2,1)S(1)}, bf16[160,1280]{1,0:T(8,128)(2,1)S(1)}, u32[]{:S(2)}, u32[]{:S(2)}) collective-permute-start(bf16[160,1280]{1,0:T(8,128)(2,1)S(1)} %add_convert_fusion.14), channel_id=1, source_target_pairs={{0,2},{1,3},{2,0},{3,1},{4,6},{5,7},{6,4},{7,5},{8,10},{9,11},{10,... | collective-permute-start | bytes 1228808 | tf_op jit(solution)/shard_map/ppermute | solution.py:57
  437.1 31.3 %collective-permute-start.33 = (bf16[160,1280]{1,0:T(8,128)(2,1)S(1)}, bf16[160,1280]{1,0:T(8,128)(2,1)S(1)}, u32[]{:S(2)}, u32[]{:S(2)}) collective-permute-start(bf16[160,1280]{1,0:T(8,128)(2,1)S(1)} %get-tuple-element.237), channel_id=1, source_target_pairs={{0,24},{4,28},{8,16},{12,20},{16,8},{20,12},{24,0},{28,4},{1,25},{... | collective-permute-start | bytes 1228808 | tf_op jit(solution)/shard_map/ppermute | solution.py:104
  550.1 31.8 %collective-permute-start.64 = (bf16[160,1280]{1,0:T(8,128)(2,1)}, bf16[160,1280]{1,0:T(8,128)(2,1)}, u32[]{:S(2)}, u32[]{:S(2)}) collective-permute-start(bf16[160,1280]{1,0:T(8,128)(2,1)} %get-tuple-element.225), channel_id=1, source_target_pairs={{0,8},{4,12},{8,0},{12,4},{16,24},{20,28},{24,16},{28,20},{1,9},{5... | collective-permute-start | bytes 1228808 | tf_op jit(solution)/shard_map/ppermute | solution.py:104
  551.7 42.0 %collective-permute-start.66 = (bf16[160,1280]{1,0:T(8,128)(2,1)}, bf16[160,1280]{1,0:T(8,128)(2,1)}, u32[]{:S(2)}, u32[]{:S(2)}) collective-permute-start(bf16[160,1280]{1,0:T(8,128)(2,1)} %get-tuple-element.226), channel_id=1, source_target_pairs={{0,24},{4,28},{8,16},{12,20},{16,8},{20,12},{24,0},{28,4},{1,25},{... | collective-permute-start | bytes 1228808 | tf_op jit(solution)/shard_map/ppermute | solution.py:104
  553.1 40.6 %collective-permute-start.65 = (bf16[160,1280]{1,0:T(8,128)(2,1)}, bf16[160,1280]{1,0:T(8,128)(2,1)}, u32[]{:S(2)}, u32[]{:S(2)}) collective-permute-start(bf16[160,1280]{1,0:T(8,128)(2,1)} %get-tuple-element.227), channel_id=1, source_target_pairs={{0,16},{4,20},{8,24},{12,28},{16,0},{20,4},{24,8},{28,12},{1,17},{... | collective-permute-start | bytes 1228808 | tf_op jit(solution)/shard_map/ppermute | solution.py:104
  557.2 36.5 %collective-permute-start.49 = (bf16[160,1280]{1,0:T(8,128)(2,1)}, bf16[160,1280]{1,0:T(8,128)(2,1)}, u32[]{:S(2)}, u32[]{:S(2)}) collective-permute-start(bf16[160,1280]{1,0:T(8,128)(2,1)} %get-tuple-element.228), channel_id=1, source_target_pairs={{0,8},{4,12},{8,0},{12,4},{16,24},{20,28},{24,16},{28,20},{1,9},{5... | collective-permute-start | bytes 1228808 | tf_op jit(solution)/shard_map/ppermute | solution.py:104
  610.0 40.2 %collective-permute-start.68 = (bf16[160,1280]{1,0:T(8,128)(2,1)S(1)}, bf16[160,1280]{1,0:T(8,128)(2,1)S(1)}, u32[]{:S(2)}, u32[]{:S(2)}) collective-permute-start(bf16[160,1280]{1,0:T(8,128)(2,1)S(1)} %fusion.74), channel_id=1, source_target_pairs={{0,2},{1,3},{2,0},{3,1},{4,6},{5,7},{6,4},{7,5},{8,10},{9,11},{10,... | collective-permute-start | bytes 1228808 | tf_op jit(solution)/shard_map/ppermute | solution.py:57
  611.3 41.0 %collective-permute-start.67 = (bf16[160,1280]{1,0:T(8,128)(2,1)S(1)}, bf16[160,1280]{1,0:T(8,128)(2,1)S(1)}, u32[]{:S(2)}, u32[]{:S(2)}) collective-permute-start(bf16[160,1280]{1,0:T(8,128)(2,1)S(1)} %fusion.74), channel_id=1, source_target_pairs={{0,1},{1,0},{2,3},{3,2},{4,5},{5,4},{6,7},{7,6},{8,9},{9,8},{10,11... | collective-permute-start | bytes 1228808 | tf_op jit(solution)/shard_map/ppermute | solution.py:57
  617.3 34.3 %collective-permute-start.53 = (bf16[160,1280]{1,0:T(8,128)(2,1)S(1)}, bf16[160,1280]{1,0:T(8,128)(2,1)S(1)}, u32[]{:S(2)}, u32[]{:S(2)}) collective-permute-start(bf16[160,1280]{1,0:T(8,128)(2,1)S(1)} %get-tuple-element.167), channel_id=1, source_target_pairs={{0,2},{1,3},{2,0},{3,1},{4,6},{5,7},{6,4},{7,5},{8,10},{9,11},{10,... | collective-permute-start | bytes 1228808 | tf_op jit(solution)/shard_map/ppermute | solution.py:57
  619.1 33.1 %collective-permute-start.52 = (bf16[160,1280]{1,0:T(8,128)(2,1)S(1)}, bf16[160,1280]{1,0:T(8,128)(2,1)S(1)}, u32[]{:S(2)}, u32[]{:S(2)}) collective-permute-start(bf16[160,1280]{1,0:T(8,128)(2,1)S(1)} %get-tuple-element.167), channel_id=1, source_target_pairs={{0,1},{1,0},{2,3},{3,2},{4,5},{5,4},{6,7},{7,6},{8,9},{9,8},{10,11... | collective-permute-start | bytes 1228808 | tf_op jit(solution)/shard_map/ppermute | solution.py:57
  711.6 43.6 %collective-permute-start.71 = (bf16[640,640]{1,0:T(8,128)(2,1)}, bf16[640,640]{1,0:T(8,128)(2,1)}, u32[]{:S(2)}, u32[]{:S(2)}) collective-permute-start(bf16[640,640]{1,0:T(8,128)(2,1)} %get-tuple-element.205), channel_id=1, source_target_pairs={{0,4},{4,0},{8,12},{12,8},{1,5},{5,1},{9,13},{13,9},{2,6},{6,2},{1... | collective-permute-start | bytes 2457608 | tf_op jit(solution)/shard_map/ppermute | solution.py:57
  717.1 54.9 %collective-permute-start.70 = (bf16[640,640]{1,0:T(8,128)(2,1)}, bf16[640,640]{1,0:T(8,128)(2,1)}, u32[]{:S(2)}, u32[]{:S(2)}) collective-permute-start(bf16[640,640]{1,0:T(8,128)(2,1)} %get-tuple-element.204), channel_id=1, source_target_pairs={{0,4},{4,0},{8,12},{12,8},{1,5},{5,1},{9,13},{13,9},{2,6},{6,2},{1... | collective-permute-start | bytes 2457608 | tf_op jit(solution)/shard_map/ppermute | solution.py:57
  769.1 72.4 %collective-permute-start.89 = (bf16[640,1280]{1,0:T(8,128)(2,1)}, bf16[640,1280]{1,0:T(8,128)(2,1)}, u32[]{:S(2)}, u32[]{:S(2)}) collective-permute-start(bf16[640,1280]{1,0:T(8,128)(2,1)} %slice.176), channel_id=1, source_target_pairs={{0,4},{4,0},{8,12},{12,8},{1,5},{5,1},{9,13},{13,9},{2,6},{6,2},{1... | collective-permute-start | bytes 4915208 | tf_op jit(solution)/shard_map/ppermute | solution.py:57
  769.4 77.7 %collective-permute-start.85 = (bf16[640,1280]{1,0:T(8,128)(2,1)}, bf16[640,1280]{1,0:T(8,128)(2,1)}, u32[]{:S(2)}, u32[]{:S(2)}) collective-permute-start(bf16[640,1280]{1,0:T(8,128)(2,1)} %slice.174), channel_id=1, source_target_pairs={{0,4},{4,0},{8,12},{12,8},{1,5},{5,1},{9,13},{13,9},{2,6},{6,2},{1... | collective-permute-start | bytes 4915208 | tf_op jit(solution)/shard_map/ppermute | solution.py:57
  772.1 77.9 %collective-permute-start.81 = (bf16[640,1280]{1,0:T(8,128)(2,1)}, bf16[640,1280]{1,0:T(8,128)(2,1)}, u32[]{:S(2)}, u32[]{:S(2)}) collective-permute-start(bf16[640,1280]{1,0:T(8,128)(2,1)} %slice.172), channel_id=1, source_target_pairs={{0,4},{4,0},{8,12},{12,8},{1,5},{5,1},{9,13},{13,9},{2,6},{6,2},{1... | collective-permute-start | bytes 4915208 | tf_op jit(solution)/shard_map/ppermute | solution.py:57
  818.0 41.7 %collective-permute-start.98 = (f32[320]{0:T(512)S(1)}, f32[320]{0:T(512)S(1)}, u32[]{:S(2)}, u32[]{:S(2)}) collective-permute-start(f32[320]{0:T(512)S(1)} %add_add_fusion.14), channel_id=1, source_target_pairs={{0,16},{16,0},{1,17},{17,1},{2,18},{18,2},{3,19},{19,3},{4,20},{20... | collective-permute-start | bytes 3848 | tf_op jit(solution)/shard_map/ppermute | solution.py:57
  841.5 168.9 %collective-permute-start.76 = (bf16[2,2,160,1280]{3,2,1,0:T(8,128)(2,1)}, bf16[2,2,160,1280]{3,2,1,0:T(8,128)(2,1)}, u32[]{:S(2)}, u32[]{:S(2)}) collective-permute-start(bf16[2,2,160,1280]{3,2,1,0:T(8,128)(2,1)} %dynamic-slice_bitcast_fusion), channel_id=1, source_target_pairs={{0,4},{4,0},{8,12},{12,8},{1,5},{5,1},{9,13},{13,9},{2,6},{6,2},{1... | collective-permute-start | bytes 4915208 | tf_op jit(solution)/shard_map/ppermute | solution.py:57
  845.8 74.3 %collective-permute-start.90 = (bf16[160,1280]{1,0:T(8,128)(2,1)S(1)}, bf16[160,1280]{1,0:T(8,128)(2,1)S(1)}, u32[]{:S(2)}, u32[]{:S(2)}) collective-permute-start(bf16[160,1280]{1,0:T(8,128)(2,1)S(1)} %get-tuple-element.217), channel_id=1, source_target_pairs={{0,1},{1,0},{2,3},{3,2},{4,5},{5,4},{6,7},{7,6},{8,9},{9,8},{10,11... | collective-permute-start | bytes 1228808 | tf_op jit(solution)/shard_map/ppermute | solution.py:57
  850.1 84.6 %collective-permute-start.86 = (bf16[160,1280]{1,0:T(8,128)(2,1)S(1)}, bf16[160,1280]{1,0:T(8,128)(2,1)S(1)}, u32[]{:S(2)}, u32[]{:S(2)}) collective-permute-start(bf16[160,1280]{1,0:T(8,128)(2,1)S(1)} %get-tuple-element.215), channel_id=1, source_target_pairs={{0,1},{1,0},{2,3},{3,2},{4,5},{5,4},{6,7},{7,6},{8,9},{9,8},{10,11... | collective-permute-start | bytes 1228808 | tf_op jit(solution)/shard_map/ppermute | solution.py:57
  867.1 85.7 %collective-permute-start.82 = (bf16[160,1280]{1,0:T(8,128)(2,1)S(1)}, bf16[160,1280]{1,0:T(8,128)(2,1)S(1)}, u32[]{:S(2)}, u32[]{:S(2)}) collective-permute-start(bf16[160,1280]{1,0:T(8,128)(2,1)S(1)} %get-tuple-element.213), channel_id=1, source_target_pairs={{0,1},{1,0},{2,3},{3,2},{4,5},{5,4},{6,7},{7,6},{8,9},{9,8},{10,11... | collective-permute-start | bytes 1228808 | tf_op jit(solution)/shard_map/ppermute | solution.py:57
  920.1 69.0 %collective-permute-start.58 = (bf16[160,1280]{1,0:T(8,128)(2,1)}, bf16[160,1280]{1,0:T(8,128)(2,1)S(1)}, u32[]{:S(2)}, u32[]{:S(2)}) collective-permute-start(bf16[160,1280]{1,0:T(8,128)(2,1)} %get-tuple-element.221), channel_id=1, source_target_pairs={{0,1},{1,0},{2,3},{3,2},{4,5},{5,4},{6,7},{7,6},{8,9},{9,8},{10,11... | collective-permute-start | bytes 1228808 | tf_op jit(solution)/shard_map/ppermute | solution.py:57
  934.7 54.4 %collective-permute-start.73 = (bf16[160,1280]{1,0:T(8,128)(2,1)}, bf16[160,1280]{1,0:T(8,128)(2,1)}, u32[]{:S(2)}, u32[]{:S(2)}) collective-permute-start(bf16[160,1280]{1,0:T(8,128)(2,1)} %get-tuple-element.223), channel_id=1, source_target_pairs={{0,1},{1,0},{2,3},{3,2},{4,5},{5,4},{6,7},{7,6},{8,9},{9,8},{10,11... | collective-permute-start | bytes 1228808 | tf_op jit(solution)/shard_map/ppermute | solution.py:57
  952.6 27.9 %collective-permute-start.84 = (bf16[160,1280]{1,0:T(8,128)(2,1)S(1)}, bf16[160,1280]{1,0:T(8,128)(2,1)S(1)}, u32[]{:S(2)}, u32[]{:S(2)}) collective-permute-start(bf16[160,1280]{1,0:T(8,128)(2,1)S(1)} %add_convert_fusion.10), channel_id=1, source_target_pairs={{0,2},{1,3},{2,0},{3,1},{4,6},{5,7},{6,4},{7,5},{8,10},{9,11},{10,... | collective-permute-start | bytes 1228808 | tf_op jit(solution)/shard_map/ppermute | solution.py:57
  952.8 45.4 %collective-permute-start.60 = (bf16[160,1280]{1,0:T(8,128)(2,1)}, bf16[160,1280]{1,0:T(8,128)(2,1)}, u32[]{:S(2)}, u32[]{:S(2)}) collective-permute-start(bf16[160,1280]{1,0:T(8,128)(2,1)} %add_convert_fusion.12), channel_id=1, source_target_pairs={{0,2},{1,3},{2,0},{3,1},{4,6},{5,7},{6,4},{7,5},{8,10},{9,11},{10,... | collective-permute-start | bytes 1228808 | tf_op jit(solution)/shard_map/ppermute | solution.py:57
  985.5 30.8 %all-to-all-start.1 = ((bf16[8,3,160,160]{3,2,1,0:T(8,128)(2,1)}), bf16[8,3,160,160]{3,2,1,0:T(8,128)(2,1)S(1)}, u32[]{:S(2)}, u32[]{:S(2)}) async-start(bf16[8,3,160,160]{3,2,1,0:T(8,128)(2,1)} %pad_maximum_fusion.3), calls=%async_computation.1 | async-start | bytes 3932160 | tf_op jit(solution)/shard_map/all_to_all | solution.py:176
  (197 other events, 3106.2 us)
Sparse Core Ops, SparseCore 0:
  18.5 47.6 all-gather.1

commit v7 on v6

--- a/solution.py
+++ b/solution.py
@@ -144,7 +144,7 @@
         )
     out = []
     for place in range(3):
-        own_core = group_gather(matrices[place], "tp")
+        own_core = lax.all_gather(matrices[place], "tp", axis=0, tiled=True)
         out.append(jnp.concatenate([own_core, swap(own_core, "ctx", 1)], axis=0))
     return tuple(out)
 
@@ -155,7 +155,7 @@
     part = scales[0].shape[0] // 8
     first = lax.axis_index(SPREAD) * part
     own = jnp.stack([lax.dynamic_slice_in_dim(scale, first, part) for scale in scales])
-    line = group_gather(own[None], "tp")
+    line = lax.all_gather(own, "tp")
     both = jnp.concatenate([line, swap(line, "ctx", 1)], axis=0)
     return tuple(both[:, place].reshape(-1) for place in range(len(scales)))
 
@@ -170,7 +170,7 @@
     for product in products:
         half = product.shape[0] // 2
         line = add_low(product[:half], swap(product[half:], "ctx", 1))
-        sums.append(group_scatter(line, "tp").astype(jnp.bfloat16))
+        sums.append(lax.psum_scatter(line, "tp", scatter_dimension=0, tiled=True))
     part, width = sums[0].shape
     packed = jnp.stack([total.reshape(part, 8, width // 8).transpose(1, 0, 2) for total in sums], 1)
     packed = lax.all_to_all(packed, SPREAD, 0, 0).astype(jnp.float32)
@@ -182,17 +182,12 @@
         return butterfly(sums, SPREAD)
     count, hidden = sums.shape
     parts = sums.reshape(count, 2, 4, hidden // 8)
-    line = hidden_line_sum(parts[:, 0] + swap(parts[:, 1], "ctx", 1))
+    line = butterfly(parts[:, 0] + swap(parts[:, 1], "ctx", 1), ("tp",))
+    line = lax.dynamic_index_in_dim(line, lax.axis_index("tp"), 1, keepdims=False)
     blank = jnp.zeros((count, 8, hidden // 8), jnp.float32)
     place = lax.axis_index(SPREAD)
     spread_out = lax.dynamic_update_slice_in_dim(blank, line[:, None], place, 1)
     return butterfly(spread_out, SPREAD).reshape(count, hidden)
-
-
-def hidden_line_sum(parts):
-    own, beside, across, far = (parts[:, place] for place in range(4))
-    across = across + swap(far, "tp", 1)
-    return own + swap(beside, "tp", 1) + swap(across, "tp", 2)
 
 
 def owner_scatter(product_low):

time: 1050 us -> 995 us (0.948)
  waiting for transfers between devices: 452 us -> 361 us
  blocking collectives: 0 us -> 39.6 us
  starting transfers between devices: 114 us -> 94.1 us
  matrix products: 117 us -> 131 us
  other arithmetic: 102 us -> 113 us
    ppermute x84 -> x62, waiting for transfers between devices: 358 us -> 263 us  [swap(): lax.ppermute(value, axis, [(place, place ^ bit) for place in range(size)])]
    all_gather x0 -> x1, blocking collectives: none -> 39.6 us  [hidden_scales(): line = lax.all_gather(own, 'tp')]
    ppermute x84 -> x62, starting transfers between devices: 74.8 us -> 55.4 us  [swap(): lax.ppermute(value, axis, [(place, place ^ bit) for place in range(size)])]
    concatenate x9 -> x5, other arithmetic: 26.4 us -> 19.9 us  [group_gather(): jnp.concatenate([own_block, beside, across, swap(across, axis, 1)], axis=0)]
    convert_element_type x15 -> x12, other arithmetic: 17 us -> 21.7 us  [add_low(): (former.astype(jnp.float32) + latter.astype(jnp.float32)).astype(jnp.bflo...]
    unnamed x299 -> x240, local copies, waits for them, and re-layouts: 31.3 us -> 27.2 us
  transfers between devices with their start and end apart: 111 -> 95, of which waited for: 57 -> 38; matrix products, arithmetic and copies ran while one was open for 29% -> 34% of each run, Pallas kernels for 6% -> 10%
where the time goes in v7:
time: 995 us; the launch traced here: 987 us
  waiting for transfers between devices  361 us (36%)
  local copies, waits for them, and re-layouts  132 us (13%)
  matrix products  131 us (13%)
  other arithmetic  113 us (11%)
  Pallas kernels  99.6 us (10%)
  starting transfers between devices  94.1 us (9%)
  blocking collectives  39.6 us (4%)
  between operations  16.3 us (2%)
    ppermute x62, waiting for transfers between devices, swap(): lax.ppermute(value, axis, [(place, place ^ bit) for place in range(size)])  263 us
    ppermute x24, waiting for transfers between devices, hop(): lax.ppermute(value, SPREAD, [(place, place ^ bits) for place in range(8)])  97.7 us
    pallas_call x2, Pallas kernels, attend_grad(): pl.pallas_call(attend_grad_body, grid=(keys // KEY_TILE,), in_specs=[pl.B...  64.7 us
    ppermute x62, starting transfers between devices, swap(): lax.ppermute(value, axis, [(place, place ^ bit) for place in range(size)])  55.4 us
    dot_general x14, matrix products, contract_cols(): lax.dot_general(former, latter, (((1,), (1,)), ((), ())), preferred_eleme...  47.4 us
    all_gather x1, blocking collectives, hidden_scales(): line = lax.all_gather(own, 'tp')  39.6 us
    pallas_call x2, Pallas kernels, attend(): pl.pallas_call(attend_body, grid=(keys // KEY_TILE,), in_specs=[pl.BlockS...  34.9 us
    dot_general x7, matrix products, contract_rows(): lax.dot_general(former, latter, (((0,), (0,)), ((), ())), preferred_eleme...  32.6 us
  transfers between devices with their start and end apart: 95, of which 38 were waited for; matrix products, arithmetic and copies ran while one was open for 34% of the time, Pallas kernels for 10%

profile of v7, /device:TPU:0, one launch (start us, length us, event | category | flops | bytes accessed | tf_op | source)
XLA Modules:
  0.0 987.1 jit_solution(3362174808544298031)
XLA Ops:
  18.3 39.6 %all-gather.4 = f32[4,2,160]{2,1,0:T(2,128)S(1)} all-gather(f32[1,2,160]{2,1,0:T(2,128)S(1)} %maximum_bitcast_fusion.2), channel_id=3, replica_groups=mesh['shard'=2,'ctx'=4,'tp'=4] {'tp'}, dimensions={0}, use_global_device_ids=true | all-gather | bytes 6400 | tf_op jit(solution)/shard_map/all_gather | solution.py:158
  68.7 10.2 %collective-permute-done.5 = bf16[160,1280]{1,0:T(8,128)(2,1)S(1)} collective-permute-done((bf16[160,1280]{1,0:T(8,128)(2,1)}, bf16[160,1280]{1,0:T(8,128)(2,1)S(1)}, u32[]{:S(2)}, u32[]{:S(2)}) %collective-permute-start.5) | collective-permute-done | bytes 409632 | tf_op jit(solution)/shard_map/ppermute | solution.py:57
  81.3 5.9 collective-permute-done.2
  145.1 5.2 multiply_convert_fusion.6
  161.8 11.1 %collective-permute-done.23 = bf16[640,640]{1,0:T(8,128)(2,1)} collective-permute-done((bf16[640,640]{1,0:T(8,128)(2,1)}, bf16[640,640]{1,0:T(8,128)(2,1)}, u32[]{:S(2)}, u32[]{:S(2)}) %collective-permute-start.23) | collective-permute-done | bytes 819232 | tf_op jit(solution)/shard_map/ppermute | solution.py:57
  176.9 11.4 %collective-permute-done.7 = bf16[640,640]{1,0:T(8,128)(2,1)} collective-permute-done((bf16[640,640]{1,0:T(8,128)(2,1)}, bf16[640,640]{1,0:T(8,128)(2,1)}, u32[]{:S(2)}, u32[]{:S(2)}) %collective-permute-start.7) | collective-permute-done | bytes 819232 | tf_op jit(solution)/shard_map/ppermute | solution.py:57
  188.4 5.9 pad_maximum_fusion.4.tree_ref
  194.3 17.2 %attend.3 = (bf16[640,320]{1,0:T(8,128)(2,1)S(1)}, f32[8,640]{1,0:T(8,128)S(1)}) custom-call(bf16[640,320]{1,0:T(8,128)(2,1)S(1)} %get-tuple-element.278.query_ref, bf16[2560,640]{1,0:T(8,128)(2,1)S(1)} %pad_maximum_fusion.4.tree_ref, bf16[2560,128]{1,0:T(8,128)(2,1)S(1)} %get-tuple-element.262.hot_ref, bf16[3,128,640]{2,1,0:T(8,128)(2,1)S(1)} %get-tuple-element.252.side_ref), custom_call_target="tpu_custom_call" | custom-call | tf_op jit(solution)/shard_map/attend/pallas_call | solution.py:306
  215.9 9.2 pad_maximum_fusion.tree_ref
  225.2 17.7 %attend.2 = (bf16[640,320]{1,0:T(8,128)(2,1)S(1)}, f32[8,640]{1,0:T(8,128)S(1)}) custom-call(bf16[640,320]{1,0:T(8,128)(2,1)S(1)} %copy-done.8, bf16[2560,640]{1,0:T(8,128)(2,1)S(1)} %pad_maximum_fusion.tree_ref, bf16[2560,128]{1,0:T(8,128)(2,1)S(1)} %copy-done.2, bf16[3,128,640]{2,1,0:T(8,128)(2,1)S(1)} %copy-done.10), custom_call_target="tpu_custom_call" | custom-call | tf_op jit(solution)/shard_map/attend/pallas_call | solution.py:306
  249.2 24.7 %collective-permute-done.10 = bf16[160,1280]{1,0:T(8,128)(2,1)S(1)} collective-permute-done((bf16[160,1280]{1,0:T(8,128)(2,1)S(1)}, bf16[160,1280]{1,0:T(8,128)(2,1)S(1)}, u32[]{:S(2)}, u32[]{:S(2)}) %collective-permute-start.10) | collective-permute-done | bytes 409632 | tf_op jit(solution)/shard_map/ppermute | solution.py:57
  277.7 16.5 %collective-permute-done.11 = bf16[160,1280]{1,0:T(8,128)(2,1)} collective-permute-done((bf16[160,1280]{1,0:T(8,128)(2,1)}, bf16[160,1280]{1,0:T(8,128)(2,1)}, u32[]{:S(2)}, u32[]{:S(2)}) %collective-permute-start.11) | collective-permute-done | bytes 409632 | tf_op jit(solution)/shard_map/ppermute | solution.py:57
  303.7 6.9 collective-permute-done.12
  313.5 9.4 collective-permute-done.13
  338.8 4.4 collective-permute-done.29
  343.1 5.4 fusion.101
  348.6 7.3 multiply_convert_fusion.4
  372.1 8.3 collective-permute-done.33
  382.5 6.0 collective-permute-done.19
  388.5 8.6 collective-permute-done.21
  405.3 8.1 collective-permute-done.34
  413.5 13.6 %collective-permute-done.35 = bf16[160,1280]{1,0:T(8,128)(2,1)S(1)} collective-permute-done((bf16[160,1280]{1,0:T(8,128)(2,1)S(1)}, bf16[160,1280]{1,0:T(8,128)(2,1)S(1)}, u32[]{:S(2)}, u32[]{:S(2)}) %collective-permute-start.35) | collective-permute-done | bytes 409632 | tf_op jit(solution)/shard_map/ppermute | solution.py:104
  436.6 4.3 collective-permute-done.50
  443.8 11.0 %multiply_reduce_fusion.1 = (f32[1280]{0:T(1024)S(1)}, f32[1280]{0:T(1024)S(1)}, f32[640,1280]{1,0:T(8,128)}, bf16[640,1280]{1,0:T(8,128)(2,1)}, bf16[640,1280]{...) fusion(f32[640,1280]{1,0:T(8,128)S(1)} %fusion.103, f32[640,1280]{1,0:T(8,128)} %copy-done.105, ...), kind=kOutput, calls=%fused_computation.36 | convolution fusion | flops 2145479680 | bytes 29521920 | tf_op jit(solution)/shard_map/dot_general | solution.py:38
  459.0 6.5 convolution_convert_fusion.1
  465.5 6.2 convolution_convert_fusion.2
  490.5 4.9 fusion.16
  512.4 6.8 collective-permute-done.39
  519.2 7.7 collective-permute-done.38
  546.6 6.0 convolution_convert_fusion
  556.1 8.2 collective-permute-done.75
  564.2 4.3 collective-permute-start.76
  568.5 6.6 collective-permute-done.56
  578.7 8.7 collective-permute-done.57
  600.4 32.3 %attend_grad.3 = (f32[640,320]{1,0:T(8,128)S(1)}, bf16[2560,640]{1,0:T(8,128)(2,1)}) custom-call(bf16[640,640]{1,0:T(8,128)(2,1)S(1)} %get-tuple-element.300.both_ref, bf16[640,320]{1,0:T(8,128)(2,1)S(1)} %copy-done.16, bf16[2560,640]{1,0:T(8,128)(2,1)} %copy-done.1, bf16[2560,128]{1,0:T(8,128)(2,1)S(1)} %copy-done.5, bf16[3,128,640]{2,1,0:T(8,128)(2,1)S(1)} %copy-done.13, ...), custom_call_target="tpu_custom_call" | custom-call | tf_op jit(solution)/shard_map/attend_grad/pallas_call | solution.py:391
  643.8 32.5 %attend_grad.2 = (f32[640,320]{1,0:T(8,128)S(1)}, bf16[2560,640]{1,0:T(8,128)(2,1)}) custom-call(bf16[640,640]{1,0:T(8,128)(2,1)S(1)} %copy-done.14, bf16[640,320]{1,0:T(8,128)(2,1)S(1)} %copy-done.19, bf16[2560,640]{1,0:T(8,128)(2,1)} %copy-done, bf16[2560,128]{1,0:T(8,128)(2,1)S(1)} %copy-done.3, bf16[3,128,640]{2,1,0:T(8,128)(2,1)S(1)} %copy-done.11, ...), custom_call_target="tpu_custom_call" | custom-call | tf_op jit(solution)/shard_map/attend_grad/pallas_call | solution.py:391
  696.8 6.4 collective-permute-done.60
  714.2 9.3 collective-permute-done.45
  733.2 4.1 convolution_convert_fusion.10
  740.8 6.6 multiply_reduce_fusion.4
  753.4 4.5 convolution_convert_fusion.11
  766.9 5.7 concatenate.148
  801.0 26.7 %collective-permute-done.47 = bf16[160,1280]{1,0:T(8,128)(2,1)} collective-permute-done((bf16[160,1280]{1,0:T(8,128)(2,1)}, bf16[160,1280]{1,0:T(8,128)(2,1)}, u32[]{:S(2)}, u32[]{:S(2)}) %collective-permute-start.47) | collective-permute-done | bytes 409632 | tf_op jit(solution)/shard_map/ppermute | solution.py:57
  828.8 19.3 %collective-permute-done.62 = bf16[160,1280]{1,0:T(8,128)(2,1)S(1)} collective-permute-done((bf16[160,1280]{1,0:T(8,128)(2,1)}, bf16[160,1280]{1,0:T(8,128)(2,1)S(1)}, u32[]{:S(2)}, u32[]{:S(2)}) %collective-permute-start.62) | collective-permute-done | bytes 409632 | tf_op jit(solution)/shard_map/ppermute | solution.py:57
  857.0 44.6 %collective-permute-done.48 = bf16[160,1280]{1,0:T(8,128)(2,1)S(1)} collective-permute-done((bf16[160,1280]{1,0:T(8,128)(2,1)S(1)}, bf16[160,1280]{1,0:T(8,128)(2,1)S(1)}, u32[]{:S(2)}, u32[]{:S(2)}) %collective-permute-start.48) | collective-permute-done | bytes 409632 | tf_op jit(solution)/shard_map/ppermute | solution.py:57
  901.7 11.3 %collective-permute-done.63 = bf16[160,1280]{1,0:T(8,128)(2,1)S(1)} collective-permute-done((bf16[160,1280]{1,0:T(8,128)(2,1)S(1)}, bf16[160,1280]{1,0:T(8,128)(2,1)S(1)}, u32[]{:S(2)}, u32[]{:S(2)}) %collective-permute-start.63) | collective-permute-done | bytes 409632 | tf_op jit(solution)/shard_map/ppermute | solution.py:57
  921.2 6.9 collective-permute-done.65
  943.4 26.6 %collective-permute-done.68 = bf16[160,640]{1,0:T(8,128)(2,1)S(1)} collective-permute-done((bf16[160,640]{1,0:T(8,128)(2,1)S(1)}, bf16[160,640]{1,0:T(8,128)(2,1)S(1)}, u32[]{:S(2)}, u32[]{:S(2)}) %collective-permute-start.68) | collective-permute-done | bytes 204832 | tf_op jit(solution)/shard_map/ppermute | solution.py:57
  (657 shorter events, 400.4 us)
Async XLA Ops:
  7.2 95.0 %all-gather.10.cloned.1.call-start = ((), (), s32[]{:S(2)}) async-start(), calls=%async_computation.5 | async-start | bytes 3686400 | tf_op jit(solution)/shard_map/all_gather | solution.py:562
  10.5 55.8 %collective-permute-start.4 = (bf16[160,1280]{1,0:T(8,128)(2,1)S(1)}, bf16[160,1280]{1,0:T(8,128)(2,1)}, u32[]{:S(2)}, u32[]{:S(2)}) collective-permute-start(bf16[160,1280]{1,0:T(8,128)(2,1)S(1)} %get-tuple-element.246), channel_id=1, source_target_pairs={{0,2},{1,3},{2,0},{3,1},{4,6},{5,7},{6,4},{7,5},{8,10},{9,11},{10,... | collective-permute-start | bytes 1228808 | tf_op jit(solution)/shard_map/ppermute | solution.py:57
  14.7 54.1 %collective-permute-start.3 = (bf16[160,1280]{1,0:T(8,128)(2,1)S(1)}, bf16[160,1280]{1,0:T(8,128)(2,1)}, u32[]{:S(2)}, u32[]{:S(2)}) collective-permute-start(bf16[160,1280]{1,0:T(8,128)(2,1)S(1)} %get-tuple-element.246), channel_id=1, source_target_pairs={{0,1},{1,0},{2,3},{3,2},{4,5},{5,4},{6,7},{7,6},{8,9},{9,8},{10,11... | collective-permute-start | bytes 1228808 | tf_op jit(solution)/shard_map/ppermute | solution.py:57
  16.2 50.7 %collective-permute-start.1 = (bf16[160,1280]{1,0:T(8,128)(2,1)S(1)}, bf16[160,1280]{1,0:T(8,128)(2,1)S(1)}, u32[]{:S(2)}, u32[]{:S(2)}) collective-permute-start(bf16[160,1280]{1,0:T(8,128)(2,1)S(1)} %get-tuple-element.247), channel_id=1, source_target_pairs={{0,2},{1,3},{2,0},{3,1},{4,6},{5,7},{6,4},{7,5},{8,10},{9,11},{10,... | collective-permute-start | bytes 1228808 | tf_op jit(solution)/shard_map/ppermute | solution.py:57
  16.6 64.8 %collective-permute-start = (bf16[160,1280]{1,0:T(8,128)(2,1)S(1)}, bf16[160,1280]{1,0:T(8,128)(2,1)}, u32[]{:S(2)}, u32[]{:S(2)}) collective-permute-start(bf16[160,1280]{1,0:T(8,128)(2,1)S(1)} %get-tuple-element.247), channel_id=1, source_target_pairs={{0,1},{1,0},{2,3},{3,2},{4,5},{5,4},{6,7},{7,6},{8,9},{9,8},{10,11... | collective-permute-start | bytes 1228808 | tf_op jit(solution)/shard_map/ppermute | solution.py:57
  57.9 118.0 %collective-permute-start.16 = (f32[4,2,160]{2,1,0:T(2,128)S(1)}, f32[4,2,160]{2,1,0:T(2,128)S(1)}, u32[]{:S(2)}, u32[]{:S(2)}) collective-permute-start(f32[4,2,160]{2,1,0:T(2,128)S(1)} %all-gather.4), channel_id=1, source_target_pairs={{0,4},{4,0},{8,12},{12,8},{1,5},{5,1},{9,13},{13,9},{2,6},{6,2},{1... | collective-permute-start | bytes 15368 | tf_op jit(solution)/shard_map/ppermute | solution.py:57
  61.4 29.1 %all-to-all-start = ((bf16[8,3,160,160]{3,2,1,0:T(8,128)(2,1)}), bf16[8,3,160,160]{3,2,1,0:T(8,128)(2,1)S(1)}, u32[]{:S(2)}, u32[]{:S(2)}) async-start(bf16[8,3,160,160]{3,2,1,0:T(8,128)(2,1)} %pad_maximum_fusion.5), calls=%async_computation | async-start | bytes 3932160 | tf_op jit(solution)/shard_map/all_to_all | solution.py:136
  65.2 211.0 %all-gather.14.cloned.1.call-start = ((), (), s32[]{:S(2)}) async-start(), calls=%async_computation.10 | async-start | bytes 2048000 | tf_op jit(solution)/shard_map/all_gather | solution.py:147
  97.5 204.7 %all-gather.12.cloned.1.call-start = ((), (), s32[]{:S(2)}) async-start(), calls=%async_computation.9 | async-start | bytes 2048000 | tf_op jit(solution)/shard_map/all_gather | solution.py:147
  101.7 200.6 %all-gather.16.cloned.1.call-start = ((), (), s32[]{:S(2)}) async-start(), calls=%async_computation.11 | async-start | bytes 2048000 | tf_op jit(solution)/shard_map/all_gather | solution.py:147
  153.3 35.0 %collective-permute-start.22 = (bf16[640,640]{1,0:T(8,128)(2,1)}, bf16[640,640]{1,0:T(8,128)(2,1)}, u32[]{:S(2)}, u32[]{:S(2)}) collective-permute-start(bf16[640,640]{1,0:T(8,128)(2,1)} %pad_maximum_fusion.13), channel_id=1, source_target_pairs={{0,4},{4,0},{8,12},{12,8},{1,5},{5,1},{9,13},{13,9},{2,6},{6,2},{1... | collective-permute-start | bytes 2457608 | tf_op jit(solution)/shard_map/ppermute | solution.py:57
  160.6 27.8 %collective-permute-start.7 = (bf16[640,640]{1,0:T(8,128)(2,1)}, bf16[640,640]{1,0:T(8,128)(2,1)}, u32[]{:S(2)}, u32[]{:S(2)}) collective-permute-start(bf16[640,640]{1,0:T(8,128)(2,1)} %pad_maximum_fusion.12), channel_id=1, source_target_pairs={{0,8},{4,12},{8,0},{12,4},{1,9},{5,13},{9,1},{13,5},{2,10},{6,14},... | collective-permute-start | bytes 2457608 | tf_op jit(solution)/shard_map/ppermute | solution.py:57
  176.1 753.8 %reduce-scatter.8.cloned.1.call-start = ((), (), s32[]{:S(2)}) async-start(), calls=%async_computation.8 | async-start | bytes 2048000 | tf_op jit(solution)/shard_map/reduce_scatter | solution.py:173
  176.4 39.5 %collective-permute-start.6 = (bf16[640,640]{1,0:T(8,128)(2,1)}, bf16[640,640]{1,0:T(8,128)(2,1)S(1)}, u32[]{:S(2)}, u32[]{:S(2)}) collective-permute-start(bf16[640,640]{1,0:T(8,128)(2,1)} %pad_maximum_fusion.12), channel_id=1, source_target_pairs={{0,4},{4,0},{8,12},{12,8},{1,5},{5,1},{9,13},{13,9},{2,6},{6,2},{1... | collective-permute-start | bytes 2457608 | tf_op jit(solution)/shard_map/ppermute | solution.py:57
  188.4 27.5 %collective-permute-start.8 = (bf16[640,640]{1,0:T(8,128)(2,1)}, bf16[640,640]{1,0:T(8,128)(2,1)S(1)}, u32[]{:S(2)}, u32[]{:S(2)}) collective-permute-start(bf16[640,640]{1,0:T(8,128)(2,1)} %collective-permute-done.7), channel_id=1, source_target_pairs={{0,4},{4,0},{8,12},{12,8},{1,5},{5,1},{9,13},{13,9},{2,6},{6,2},{1... | collective-permute-start | bytes 2457608 | tf_op jit(solution)/shard_map/ppermute | solution.py:57
  213.8 62.3 %collective-permute-start.25 = (bf16[160,1280]{1,0:T(8,128)(2,1)}, bf16[160,1280]{1,0:T(8,128)(2,1)}, u32[]{:S(2)}, u32[]{:S(2)}) collective-permute-start(bf16[160,1280]{1,0:T(8,128)(2,1)} %get-tuple-element.226), channel_id=1, source_target_pairs={{0,1},{1,0},{2,3},{3,2},{4,5},{5,4},{6,7},{7,6},{8,9},{9,8},{10,11... | collective-permute-start | bytes 1228808 | tf_op jit(solution)/shard_map/ppermute | solution.py:57
  214.0 32.9 %collective-permute-start.26 = (bf16[160,1280]{1,0:T(8,128)(2,1)}, bf16[160,1280]{1,0:T(8,128)(2,1)}, u32[]{:S(2)}, u32[]{:S(2)}) collective-permute-start(bf16[160,1280]{1,0:T(8,128)(2,1)} %get-tuple-element.227), channel_id=1, source_target_pairs={{0,1},{1,0},{2,3},{3,2},{4,5},{5,4},{6,7},{7,6},{8,9},{9,8},{10,11... | collective-permute-start | bytes 1228808 | tf_op jit(solution)/shard_map/ppermute | solution.py:57
  244.8 32.9 %collective-permute-start.9 = (bf16[160,1280]{1,0:T(8,128)(2,1)}, bf16[160,1280]{1,0:T(8,128)(2,1)}, u32[]{:S(2)}, u32[]{:S(2)}) collective-permute-start(bf16[160,1280]{1,0:T(8,128)(2,1)} %get-tuple-element.231), channel_id=1, source_target_pairs={{0,1},{1,0},{2,3},{3,2},{4,5},{5,4},{6,7},{7,6},{8,9},{9,8},{10,11... | collective-permute-start | bytes 1228808 | tf_op jit(solution)/shard_map/ppermute | solution.py:57
  245.0 28.9 %collective-permute-start.10 = (bf16[160,1280]{1,0:T(8,128)(2,1)S(1)}, bf16[160,1280]{1,0:T(8,128)(2,1)S(1)}, u32[]{:S(2)}, u32[]{:S(2)}) collective-permute-start(bf16[160,1280]{1,0:T(8,128)(2,1)S(1)} %get-tuple-element.232), channel_id=1, source_target_pairs={{0,1},{1,0},{2,3},{3,2},{4,5},{5,4},{6,7},{7,6},{8,9},{9,8},{10,11... | collective-permute-start | bytes 1228808 | tf_op jit(solution)/shard_map/ppermute | solution.py:57
  276.1 50.8 %collective-permute-start.17 = (bf16[640,1280]{1,0:T(8,128)(2,1)}, bf16[640,1280]{1,0:T(8,128)(2,1)}, u32[]{:S(2)}, u32[]{:S(2)}) collective-permute-start(bf16[640,1280]{1,0:T(8,128)(2,1)} %bitcast.236), channel_id=1, source_target_pairs={{0,4},{4,0},{8,12},{12,8},{1,5},{5,1},{9,13},{13,9},{2,6},{6,2},{1... | collective-permute-start | bytes 4915208 | tf_op jit(solution)/shard_map/ppermute | solution.py:57
  302.2 30.5 %collective-permute-start.15 = (bf16[640,1280]{1,0:T(8,128)(2,1)}, bf16[640,1280]{1,0:T(8,128)(2,1)}, u32[]{:S(2)}, u32[]{:S(2)}) collective-permute-start(bf16[640,1280]{1,0:T(8,128)(2,1)} %bitcast.241), channel_id=1, source_target_pairs={{0,4},{4,0},{8,12},{12,8},{1,5},{5,1},{9,13},{13,9},{2,6},{6,2},{1... | collective-permute-start | bytes 4915208 | tf_op jit(solution)/shard_map/ppermute | solution.py:57
  302.2 53.6 %collective-permute-start.18 = (bf16[640,1280]{1,0:T(8,128)(2,1)}, bf16[640,1280]{1,0:T(8,128)(2,1)S(1)}, u32[]{:S(2)}, u32[]{:S(2)}) collective-permute-start(bf16[640,1280]{1,0:T(8,128)(2,1)} %bitcast.246), channel_id=1, source_target_pairs={{0,4},{4,0},{8,12},{12,8},{1,5},{5,1},{9,13},{13,9},{2,6},{6,2},{1... | collective-permute-start | bytes 4915208 | tf_op jit(solution)/shard_map/ppermute | solution.py:57
  366.0 31.1 %collective-permute-start.21 = (bf16[160,1280]{1,0:T(8,128)(2,1)S(1)}, bf16[160,1280]{1,0:T(8,128)(2,1)S(1)}, u32[]{:S(2)}, u32[]{:S(2)}) collective-permute-start(bf16[160,1280]{1,0:T(8,128)(2,1)S(1)} %get-tuple-element.229), channel_id=1, source_target_pairs={{0,24},{4,28},{8,16},{12,20},{16,8},{20,12},{24,0},{28,4},{1,25},{... | collective-permute-start | bytes 1228808 | tf_op jit(solution)/shard_map/ppermute | solution.py:104
  370.9 27.5 %collective-permute-start.20 = (bf16[160,1280]{1,0:T(8,128)(2,1)S(1)}, bf16[160,1280]{1,0:T(8,128)(2,1)S(1)}, u32[]{:S(2)}, u32[]{:S(2)}) collective-permute-start(bf16[160,1280]{1,0:T(8,128)(2,1)S(1)} %get-tuple-element.230), channel_id=1, source_target_pairs={{0,16},{4,20},{8,24},{12,28},{16,0},{20,4},{24,8},{28,12},{1,17},{... | collective-permute-start | bytes 1228808 | tf_op jit(solution)/shard_map/ppermute | solution.py:104
  455.1 28.9 %collective-permute-start.80 = (f32[2,4,160]{2,1,0:T(4,128)S(1)}, f32[2,4,160]{2,1,0:T(4,128)S(1)}, u32[]{:S(2)}, u32[]{:S(2)}) collective-permute-start(f32[2,4,160]{2,1,0:T(4,128)S(1)} %slice_bitcast_fusion.3), channel_id=1, source_target_pairs={{0,4},{4,0},{8,12},{12,8},{1,5},{5,1},{9,13},{13,9},{2,6},{6,2},{1... | collective-permute-start | bytes 15368 | tf_op jit(solution)/shard_map/ppermute | solution.py:57
  480.4 30.6 %collective-permute-start.54 = (bf16[160,1280]{1,0:T(8,128)(2,1)}, bf16[160,1280]{1,0:T(8,128)(2,1)}, u32[]{:S(2)}, u32[]{:S(2)}) collective-permute-start(bf16[160,1280]{1,0:T(8,128)(2,1)} %get-tuple-element.218), channel_id=1, source_target_pairs={{0,24},{4,28},{8,16},{12,20},{16,8},{20,12},{24,0},{28,4},{1,25},{... | collective-permute-start | bytes 1228808 | tf_op jit(solution)/shard_map/ppermute | solution.py:104
  482.5 29.9 %collective-permute-start.53 = (bf16[160,1280]{1,0:T(8,128)(2,1)}, bf16[160,1280]{1,0:T(8,128)(2,1)}, u32[]{:S(2)}, u32[]{:S(2)}) collective-permute-start(bf16[160,1280]{1,0:T(8,128)(2,1)} %get-tuple-element.219), channel_id=1, source_target_pairs={{0,16},{4,20},{8,24},{12,28},{16,0},{20,4},{24,8},{28,12},{1,17},{... | collective-permute-start | bytes 1228808 | tf_op jit(solution)/shard_map/ppermute | solution.py:104
  511.0 41.6 %collective-permute-start.85 = (f32[2,8,160]{2,1,0:T(8,128)S(1)}, f32[2,8,160]{2,1,0:T(8,128)S(1)}, u32[]{:S(2)}, u32[]{:S(2)}) collective-permute-start(f32[2,8,160]{2,1,0:T(8,128)S(1)} %add.649), channel_id=1, source_target_pairs={{0,8},{4,12},{8,0},{12,4},{1,9},{5,13},{9,1},{13,5},{2,10},{6,14},... | collective-permute-start | bytes 30728 | tf_op jit(solution)/shard_map/ppermute | solution.py:57
  536.5 38.6 %collective-permute-start.41 = (bf16[160,1280]{1,0:T(8,128)(2,1)S(1)}, bf16[160,1280]{1,0:T(8,128)(2,1)S(1)}, u32[]{:S(2)}, u32[]{:S(2)}) collective-permute-start(bf16[160,1280]{1,0:T(8,128)(2,1)S(1)} %get-tuple-element.165), channel_id=1, source_target_pairs={{0,2},{1,3},{2,0},{3,1},{4,6},{5,7},{6,4},{7,5},{8,10},{9,11},{10,... | collective-permute-start | bytes 1228808 | tf_op jit(solution)/shard_map/ppermute | solution.py:57
  536.5 40.6 %collective-permute-start.40 = (bf16[160,1280]{1,0:T(8,128)(2,1)S(1)}, bf16[160,1280]{1,0:T(8,128)(2,1)S(1)}, u32[]{:S(2)}, u32[]{:S(2)}) collective-permute-start(bf16[160,1280]{1,0:T(8,128)(2,1)S(1)} %get-tuple-element.165), channel_id=1, source_target_pairs={{0,1},{1,0},{2,3},{3,2},{4,5},{5,4},{6,7},{7,6},{8,9},{9,8},{10,11... | collective-permute-start | bytes 1228808 | tf_op jit(solution)/shard_map/ppermute | solution.py:57
  545.6 29.5 %collective-permute-start.56 = (bf16[160,1280]{1,0:T(8,128)(2,1)S(1)}, bf16[160,1280]{1,0:T(8,128)(2,1)S(1)}, u32[]{:S(2)}, u32[]{:S(2)}) collective-permute-start(bf16[160,1280]{1,0:T(8,128)(2,1)S(1)} %fusion.74), channel_id=1, source_target_pairs={{0,2},{1,3},{2,0},{3,1},{4,6},{5,7},{6,4},{7,5},{8,10},{9,11},{10,... | collective-permute-start | bytes 1228808 | tf_op jit(solution)/shard_map/ppermute | solution.py:57
  564.2 286.5 %collective-permute-start.76 = (f32[2560]{0:T(1024)S(1)}, f32[2560]{0:T(1024)S(1)}, u32[]{:S(2)}, u32[]{:S(2)}) collective-permute-start(f32[2560]{0:T(1024)S(1)} %add.633), channel_id=1, source_target_pairs={{0,2},{1,3},{2,0},{3,1},{4,6},{5,7},{6,4},{7,5},{8,10},{9,11},{10,... | collective-permute-start | bytes 30728 | tf_op jit(solution)/shard_map/ppermute | solution.py:57
  635.5 43.6 %collective-permute-start.59 = (bf16[640,640]{1,0:T(8,128)(2,1)}, bf16[640,640]{1,0:T(8,128)(2,1)}, u32[]{:S(2)}, u32[]{:S(2)}) collective-permute-start(bf16[640,640]{1,0:T(8,128)(2,1)} %get-tuple-element.203), channel_id=1, source_target_pairs={{0,4},{4,0},{8,12},{12,8},{1,5},{5,1},{9,13},{13,9},{2,6},{6,2},{1... | collective-permute-start | bytes 2457608 | tf_op jit(solution)/shard_map/ppermute | solution.py:57
  641.1 55.5 %collective-permute-start.58 = (bf16[640,640]{1,0:T(8,128)(2,1)}, bf16[640,640]{1,0:T(8,128)(2,1)}, u32[]{:S(2)}, u32[]{:S(2)}) collective-permute-start(bf16[640,640]{1,0:T(8,128)(2,1)} %get-tuple-element.202), channel_id=1, source_target_pairs={{0,4},{4,0},{8,12},{12,8},{1,5},{5,1},{9,13},{13,9},{2,6},{6,2},{1... | collective-permute-start | bytes 2457608 | tf_op jit(solution)/shard_map/ppermute | solution.py:57
  693.8 35.8 %collective-permute-start.71 = (bf16[640,1280]{1,0:T(8,128)(2,1)}, bf16[640,1280]{1,0:T(8,128)(2,1)}, u32[]{:S(2)}, u32[]{:S(2)}) collective-permute-start(bf16[640,1280]{1,0:T(8,128)(2,1)} %slice.164), channel_id=1, source_target_pairs={{0,4},{4,0},{8,12},{12,8},{1,5},{5,1},{9,13},{13,9},{2,6},{6,2},{1... | collective-permute-start | bytes 4915208 | tf_op jit(solution)/shard_map/ppermute | solution.py:57
  696.6 79.0 %collective-permute-start.70 = (bf16[640,1280]{1,0:T(8,128)(2,1)}, bf16[640,1280]{1,0:T(8,128)(2,1)}, u32[]{:S(2)}, u32[]{:S(2)}) collective-permute-start(bf16[640,1280]{1,0:T(8,128)(2,1)} %slice.162), channel_id=1, source_target_pairs={{0,4},{4,0},{8,12},{12,8},{1,5},{5,1},{9,13},{13,9},{2,6},{6,2},{1... | collective-permute-start | bytes 4915208 | tf_op jit(solution)/shard_map/ppermute | solution.py:57
  714.2 76.2 %collective-permute-start.69 = (bf16[640,1280]{1,0:T(8,128)(2,1)}, bf16[640,1280]{1,0:T(8,128)(2,1)}, u32[]{:S(2)}, u32[]{:S(2)}) collective-permute-start(bf16[640,1280]{1,0:T(8,128)(2,1)} %slice.160), channel_id=1, source_target_pairs={{0,4},{4,0},{8,12},{12,8},{1,5},{5,1},{9,13},{13,9},{2,6},{6,2},{1... | collective-permute-start | bytes 4915208 | tf_op jit(solution)/shard_map/ppermute | solution.py:57
  733.1 198.8 %reduce-scatter.6.cloned.1.call-start = ((), (), s32[]{:S(2)}) async-start(), calls=%async_computation.7 | async-start | bytes 2048000 | tf_op jit(solution)/shard_map/reduce_scatter | solution.py:173
  749.7 48.9 %collective-permute-start.77 = (f32[320]{0:T(512)S(1)}, f32[320]{0:T(512)S(1)}, u32[]{:S(2)}, u32[]{:S(2)}) collective-permute-start(f32[320]{0:T(512)S(1)} %add_add_fusion.14), channel_id=1, source_target_pairs={{0,16},{16,0},{1,17},{17,1},{2,18},{18,2},{3,19},{19,3},{4,20},{20... | collective-permute-start | bytes 3848 | tf_op jit(solution)/shard_map/ppermute | solution.py:57
  775.6 139.1 %collective-permute-start.64 = (bf16[2,2,160,1280]{3,2,1,0:T(8,128)(2,1)}, bf16[2,2,160,1280]{3,2,1,0:T(8,128)(2,1)}, u32[]{:S(2)}, u32[]{:S(2)}) collective-permute-start(bf16[2,2,160,1280]{3,2,1,0:T(8,128)(2,1)} %dynamic-slice_bitcast_fusion), channel_id=1, source_target_pairs={{0,4},{4,0},{8,12},{12,8},{1,5},{5,1},{9,13},{13,9},{2,6},{6,2},{1... | collective-permute-start | bytes 4915208 | tf_op jit(solution)/shard_map/ppermute | solution.py:57
  779.9 154.0 %reduce-scatter.4.cloned.1.call-start = ((), (), s32[]{:S(2)}) async-start(), calls=%async_computation.6 | async-start | bytes 2048000 | tf_op jit(solution)/shard_map/reduce_scatter | solution.py:173
  786.3 70.8 %collective-permute-start.46 = (bf16[160,1280]{1,0:T(8,128)(2,1)}, bf16[160,1280]{1,0:T(8,128)(2,1)}, u32[]{:S(2)}, u32[]{:S(2)}) collective-permute-start(bf16[160,1280]{1,0:T(8,128)(2,1)} %get-tuple-element.213), channel_id=1, source_target_pairs={{0,1},{1,0},{2,3},{3,2},{4,5},{5,4},{6,7},{7,6},{8,9},{9,8},{10,11... | collective-permute-start | bytes 1228808 | tf_op jit(solution)/shard_map/ppermute | solution.py:57
  790.4 37.3 %collective-permute-start.47 = (bf16[160,1280]{1,0:T(8,128)(2,1)}, bf16[160,1280]{1,0:T(8,128)(2,1)}, u32[]{:S(2)}, u32[]{:S(2)}) collective-permute-start(bf16[160,1280]{1,0:T(8,128)(2,1)} %get-tuple-element.214), channel_id=1, source_target_pairs={{0,1},{1,0},{2,3},{3,2},{4,5},{5,4},{6,7},{7,6},{8,9},{9,8},{10,11... | collective-permute-start | bytes 1228808 | tf_op jit(solution)/shard_map/ppermute | solution.py:57
  800.8 56.3 %collective-permute-start.61 = (bf16[160,1280]{1,0:T(8,128)(2,1)}, bf16[160,1280]{1,0:T(8,128)(2,1)S(1)}, u32[]{:S(2)}, u32[]{:S(2)}) collective-permute-start(bf16[160,1280]{1,0:T(8,128)(2,1)} %get-tuple-element.215), channel_id=1, source_target_pairs={{0,1},{1,0},{2,3},{3,2},{4,5},{5,4},{6,7},{7,6},{8,9},{9,8},{10,11... | collective-permute-start | bytes 1228808 | tf_op jit(solution)/shard_map/ppermute | solution.py:57
  850.7 50.9 %collective-permute-start.48 = (bf16[160,1280]{1,0:T(8,128)(2,1)S(1)}, bf16[160,1280]{1,0:T(8,128)(2,1)S(1)}, u32[]{:S(2)}, u32[]{:S(2)}) collective-permute-start(bf16[160,1280]{1,0:T(8,128)(2,1)S(1)} %add_convert_fusion.6), channel_id=1, source_target_pairs={{0,2},{1,3},{2,0},{3,1},{4,6},{5,7},{6,4},{7,5},{8,10},{9,11},{10,... | collective-permute-start | bytes 1228808 | tf_op jit(solution)/shard_map/ppermute | solution.py:57
  852.6 60.4 %collective-permute-start.63 = (bf16[160,1280]{1,0:T(8,128)(2,1)S(1)}, bf16[160,1280]{1,0:T(8,128)(2,1)S(1)}, u32[]{:S(2)}, u32[]{:S(2)}) collective-permute-start(bf16[160,1280]{1,0:T(8,128)(2,1)S(1)} %add_convert_fusion.5), channel_id=1, source_target_pairs={{0,2},{1,3},{2,0},{3,1},{4,6},{5,7},{6,4},{7,5},{8,10},{9,11},{10,... | collective-permute-start | bytes 1228808 | tf_op jit(solution)/shard_map/ppermute | solution.py:57
  937.7 33.9 %all-to-all-start.1 = ((bf16[8,3,160,160]{3,2,1,0:T(8,128)(2,1)}), bf16[8,3,160,160]{3,2,1,0:T(8,128)(2,1)S(1)}, u32[]{:S(2)}, u32[]{:S(2)}) async-start(bf16[8,3,160,160]{3,2,1,0:T(8,128)(2,1)} %pad_maximum_fusion.6), calls=%async_computation.4 | async-start | bytes 3932160 | tf_op jit(solution)/shard_map/all_to_all | solution.py:176
  941.4 28.6 %collective-permute-start.68 = (bf16[160,640]{1,0:T(8,128)(2,1)S(1)}, bf16[160,640]{1,0:T(8,128)(2,1)S(1)}, u32[]{:S(2)}, u32[]{:S(2)}) collective-permute-start(bf16[160,640]{1,0:T(8,128)(2,1)S(1)} %dynamic-slice_bitcast_fusion.3), channel_id=1, source_target_pairs={{0,8},{4,12},{8,0},{12,4},{1,9},{5,13},{9,1},{13,5},{2,10},{6,14},... | collective-permute-start | bytes 614408 | tf_op jit(solution)/shard_map/ppermute | solution.py:57
  (157 other events, 2131.6 us)
Sparse Core Ops, SparseCore 0:
  10.5 35.5 all-gather.9
  97.6 35.9 all-gather.13
  135.2 37.0 all-gather.11
  176.3 36.0 all-gather.15
  733.2 34.4 reduce-scatter.7
  780.0 59.7 reduce-scatter.5
  842.1 61.2 reduce-scatter.3

commit v8 on v7

v8 whole, which is shorter than its diff:
```python
import math

import jax
import jax.numpy as jnp
from jax import lax
from jax.experimental import pallas as pl
from jax.experimental.pallas import tpu as pltpu
from jax.sharding import PartitionSpec as P

D = 1280
HDIM = 64
SEG = 64
SEGS = 40
TREE_TOK = 2560


EPSILON = 1e-06
HIGHEST = lax.Precision.HIGHEST
SPREAD = ("shard", "ctx")


def unit_rows(values):
    return values * lax.rsqrt(jnp.sum(values * values, axis=-1, keepdims=True) + EPSILON)


def contract_rows(former, latter):
    return lax.dot_general(
        former, latter, (((0,), (0,)), ((), ())), preferred_element_type=jnp.float32
    )


def contract_cols(former, latter):
    return lax.dot_general(
        former, latter, (((1,), (1,)), ((), ())), preferred_element_type=jnp.float32
    )


def mix_rows(residual, branch, mixing):
    return unit_rows(residual + mixing * (unit_rows(branch) - residual))


def swap(value, axis, bit):
    size = lax.axis_size(axis)
    return lax.ppermute(value, axis, [(place, place ^ bit) for place in range(size)])


def add_low(former, latter):
    return (former.astype(jnp.float32) + latter.astype(jnp.float32)).astype(jnp.bfloat16)


def butterfly(value, axes):
    for axis in axes:
        bit = 1
        while bit < lax.axis_size(axis):
            value = value + swap(value, axis, bit)
            bit *= 2
    return value


def group_order(axis):
    size = lax.axis_size(axis)
    places = jnp.arange(size, dtype=jnp.int32)
    return places ^ lax.axis_index(axis) if size == 4 else places


def group_gather(own_block, axis):
    if lax.axis_size(axis) != 4:
        return [lax.all_gather(own_block, axis, axis=0, tiled=True)]
    across = swap(own_block, axis, 2)
    beside = swap(own_block, axis, 1)
    return [own_block, beside, across, swap(across, axis, 1)]


def group_scatter(pieces, axis):
    if lax.axis_size(axis) != 4:
        return [lax.psum_scatter(pieces[0], axis, scatter_dimension=0, tiled=True)]
    own, beside, across, far = pieces
    far = swap(far, axis, 1)
    beside = swap(beside, axis, 1)
    return [own, beside, swap(add_low(across, far), axis, 2)]


def total_wide(parts):
    return sum(part.astype(jnp.float32) for part in parts)


def in_plane():
    return (lax.axis_size("shard"), lax.axis_size("ctx"), lax.axis_size("tp")) == (2, 4, 4)


def hop(value, bits):
    return lax.ppermute(value, SPREAD, [(place, place ^ bits) for place in range(8)])


def hidden_gather(own_block):
    if not in_plane():
        return group_gather(own_block, "tp")
    return [own_block] + [hop(own_block, bits) for bits in (2, 4, 6)]


def hidden_scatter(pieces):
    if not in_plane():
        return group_scatter(pieces, "tp")
    return [pieces[0]] + [hop(piece, bits) for piece, bits in zip(pieces[1:], (2, 4, 6))]


def hidden_shards(w_up, w_gate, w_down):
    if not in_plane():
        return jnp.stack([w_up.T, w_gate.T, w_down])
    rows, hidden = w_up.shape
    part = hidden // 8
    packed = jnp.stack(
        [
            w_up.reshape(rows, 8, part).transpose(1, 2, 0),
            w_gate.reshape(rows, 8, part).transpose(1, 2, 0),
            w_down.reshape(8, part, rows),
        ],
        axis=1,
    )
    packed = lax.all_to_all(packed, SPREAD, 0, 0)
    return packed.transpose(1, 2, 0, 3).reshape(3, part, 8 * rows)


def hidden_weights(matrices):
    if not in_plane():
        return [
            [lax.all_gather(matrices[place], SPREAD, axis=1, tiled=True)] for place in range(3)
        ]
    lines = [lax.all_gather(matrices[place], "tp", axis=0, tiled=True) for place in range(3)]
    return [[line, swap(line, "ctx", 1)] for line in lines]


def hidden_scales(*scales):
    if not in_plane():
        return scales
    part = scales[0].shape[0] // 8
    first = lax.axis_index(SPREAD) * part
    own = jnp.stack([lax.dynamic_slice_in_dim(scale, first, part) for scale in scales])
    line = jnp.concatenate(group_gather(own[None], "tp"), axis=0)
    line = jnp.take(line, group_order("tp"), axis=0)
    both = jnp.concatenate([line, swap(line, "ctx", 1)], axis=0)
    return tuple(both[:, place].reshape(-1) for place in range(len(scales)))


def core_sums(products):
    if not in_plane():
        return products
    half = products[0].shape[0] // 2
    return [add_low(product[:half], swap(product[half:], "ctx", 1)) for product in products]


def hidden_weight_grads(lines):
    if not in_plane():
        return [
            lax.psum_scatter(line, SPREAD, scatter_dimension=1, tiled=True).astype(jnp.float32)
            for line in lines
        ]
    sums = [lax.psum_scatter(line, "tp", scatter_dimension=0, tiled=True) for line in lines]
    part, width = sums[0].shape
    packed = jnp.stack([total.reshape(part, 8, width // 8).transpose(1, 0, 2) for total in sums], 1)
    packed = lax.all_to_all(packed, SPREAD, 0, 0).astype(jnp.float32)
    return [packed[:, place].reshape(8 * part, width // 8) for place in range(3)]


def hidden_scale_grads(sums):
    if not in_plane():
        return butterfly(sums, SPREAD)
    count, hidden = sums.shape
    parts = sums.reshape(count, 2, 4, hidden // 8)
    line = butterfly(parts[:, 0] + swap(parts[:, 1], "ctx", 1), ("tp",))
    line = lax.dynamic_index_in_dim(line, lax.axis_index("tp"), 1, keepdims=False)
    blank = jnp.zeros((count, 8, hidden // 8), jnp.float32)
    place = lax.axis_index(SPREAD)
    spread_out = lax.dynamic_update_slice_in_dim(blank, line[:, None], place, 1)
    return butterfly(spread_out, SPREAD).reshape(count, hidden)


def owner_scatter(product_low):
    if lax.axis_size("ctx") != 4 or lax.axis_size("shard") != 2:
        return lax.psum_scatter(
            product_low, ("shard", "ctx"), scatter_dimension=0, tiled=True
        ).astype(jnp.float32)
    place = lax.axis_index("ctx")
    core, along = place % 2, place // 2
    plane = lax.axis_index("shard")
    rows, width = product_low.shape
    blocks = product_low.reshape(2, 2, 2, rows // 8, width)

    def pick(value, index, axis):
        return lax.dynamic_index_in_dim(value, index, axis, keepdims=False)

    blocks = add_low(pick(blocks, core, 2), swap(pick(blocks, 1 - core, 2), "ctx", 1))
    former, latter = blocks[..., : width // 2], blocks[..., width // 2 :]
    former_in = swap(pick(former, 1 - along, 1), "ctx", 2)
    latter_in = swap(pick(latter, 1 - plane, 0), "shard", 1)
    former = add_low(pick(former, along, 1), former_in)
    latter = add_low(pick(latter, plane, 0), latter_in)
    former_in = swap(pick(former, 1 - plane, 0), "shard", 1)
    latter_in = swap(pick(latter, 1 - along, 0), "ctx", 2)
    return jnp.concatenate(
        [
            pick(former, plane, 0).astype(jnp.float32) + former_in.astype(jnp.float32),
            pick(latter, along, 0).astype(jnp.float32) + latter_in.astype(jnp.float32),
        ],
        axis=1,
    )


def row_labels(slots, group_size):
    tree_rows = group_size * lax.axis_size("ctx")
    chunk = group_size // lax.axis_size("tp")
    within = (group_order("tp")[:, None] * chunk + jnp.arange(chunk, dtype=jnp.int32)).reshape(-1)
    keys = (group_order("ctx")[:, None] * group_size + within[None, :]).reshape(-1)
    onehot = (keys[:, None] // SEG == jnp.arange(tree_rows // SEG, dtype=jnp.int32)[None, :])
    segment = jnp.sum(jnp.where(onehot, slots[None, :], 0), axis=1)
    offset = keys % SEG
    if lax.axis_size("ctx") != 4:
        first = lax.axis_index("ctx") * group_size
    else:
        first = 0
    return (
        lax.dynamic_slice_in_dim(segment, first, group_size),
        lax.dynamic_slice_in_dim(offset, first, group_size),
        segment,
        offset,
    )


LOG2_SCALE = math.sqrt(HDIM) * math.log2(math.e)
LANES = 128
KEY_TILE = 256


def copies(sources, targets, sems):
    moves = [
        pltpu.make_async_copy(source, target, sems.at[place])
        for place, (source, target) in enumerate(zip(sources, targets))
    ]
    for move in moves:
        move.start()
    return moves


def row_blocks(ref, count):
    rows = ref.shape[0] // count
    return [ref.at[pl.ds(place * rows, rows)] for place in range(count)]


ANYWHERE = pl.BlockSpec(memory_space=pl.ANY)


def half_kept(value, unit, axis):
    place = lax.broadcasted_iota(jnp.int32, value.shape, axis)
    inside = (place >= HDIM) if unit % 2 else (place < HDIM)
    return jnp.where(inside, value, jnp.zeros_like(value))


def seen_tile(hot_ref, side_ref):
    hot = hot_ref[...]
    strict = jnp.dot(hot, side_ref[0], preferred_element_type=jnp.float32)
    same = jnp.dot(hot, side_ref[1], preferred_element_type=jnp.float32)
    before = jnp.dot(hot, side_ref[2], preferred_element_type=jnp.float32)
    return (strict + same * before).astype(jnp.bfloat16)


def pair_of(unit):
    return slice(unit // 2 * LANES, unit // 2 * LANES + LANES)


def attend_body(count, query_ref, *refs):
    pieces, refs = refs[:count], refs[count:]
    (hot_ref, side_ref, weight_ref, out_ref, scale_ref), refs = refs[:5], refs[5:]
    outs, (tree_ref, turned_ref, sum_ref, sems) = refs[:-4], refs[-4:]
    heads = query_ref.shape[1] // HDIM
    step = pl.program_id(0)

    @pl.when(step == 0)
    def prepare():
        moves = copies(pieces, row_blocks(tree_ref, count), sems)
        turned = query_ref[...].astype(jnp.float32).T.astype(jnp.bfloat16)
        blank = jnp.zeros((HDIM, turned.shape[1]), jnp.bfloat16)
        for head in range(heads):
            own = turned[head * HDIM : (head + 1) * HDIM]
            halves = [blank, own] if head % 2 else [own, blank]
            turned_ref[head] = jnp.concatenate(halves, axis=0)
        sum_ref[...] = jnp.zeros_like(sum_ref)
        for move in moves:
            move.wait()

    tree = tree_ref[pl.ds(step * KEY_TILE, KEY_TILE)]
    values_turned = tree[:, heads * HDIM :].astype(jnp.float32).T.astype(jnp.bfloat16)
    seen = seen_tile(hot_ref, side_ref)
    ones = jnp.ones((sum_ref.shape[1] - HDIM, tree.shape[0]), jnp.bfloat16)
    for head in range(heads):
        scores = jnp.dot(tree[:, pair_of(head)], turned_ref[head], preferred_element_type=jnp.float32)
        lifted = jnp.exp2(scores * LOG2_SCALE).astype(jnp.bfloat16) * seen
        own = jnp.concatenate([values_turned[head * HDIM : (head + 1) * HDIM], ones], axis=0)
        sum_ref[head] += jnp.dot(own, lifted, preferred_element_type=jnp.float32)

    @pl.when(step == pl.num_programs(0) - 1)
    def finish():
        parts = []
        for head in range(heads):
            inverse = 1.0 / sum_ref[head, HDIM : HDIM + 1]
            scale_ref[head : head + 1] = inverse
            parts.append(sum_ref[head, :HDIM] * inverse)
        low = jnp.concatenate(parts, axis=0).T.astype(jnp.bfloat16)
        out_ref[...] = low
        width = low.shape[1]
        rows = low.shape[0] // len(outs)
        for place, out in enumerate(outs):
            out[...] = contract_cols(
                low[place * rows : (place + 1) * rows], weight_ref[:, 3 * width :]
            ).astype(jnp.bfloat16)


def attend(query, pieces, hot, side, weight, count_out):
    rows, features = query.shape
    wide = weight.shape[0]
    count, width = len(pieces), pieces[0].shape[1]
    keys = pieces[0].shape[0] * count
    heads = features // HDIM
    whole = lambda step: (0, 0)
    return pl.pallas_call(
        lambda *refs: attend_body(count, *refs),
        grid=(keys // KEY_TILE,),
        in_specs=[pl.BlockSpec((rows, features), whole)]
        + [ANYWHERE] * count
        + [
            pl.BlockSpec((KEY_TILE, LANES), lambda step: (step, 0)),
            pl.BlockSpec((3, LANES, rows), lambda step: (0, 0, 0)),
            pl.BlockSpec(weight.shape, whole),
        ],
        out_specs=[
            pl.BlockSpec((rows, features), whole),
            pl.BlockSpec((8, rows), whole),
        ]
        + [pl.BlockSpec((rows // count_out, wide), whole)] * count_out,
        out_shape=[
            jax.ShapeDtypeStruct((rows, features), jnp.bfloat16),
            jax.ShapeDtypeStruct((8, rows), jnp.float32),
        ]
        + [jax.ShapeDtypeStruct((rows // count_out, wide), jnp.bfloat16)] * count_out,
        scratch_shapes=[
            pltpu.VMEM((keys, width), jnp.bfloat16),
            pltpu.VMEM((heads, LANES, rows), jnp.bfloat16),
            pltpu.VMEM((heads, HDIM + 16, rows), jnp.float32),
            pltpu.SemaphoreType.DMA((count,)),
        ],
        compiler_params=pltpu.CompilerParams(vmem_limit_bytes=48 << 20),
        name="attend",
    )(query, *pieces, hot, side, weight)


def attend_grad_body(count, tops, query_ref, heads_ref, *refs):
    pieces, refs = refs[:count], refs[count:]
    top_refs, refs = refs[:tops], refs[tops:]
    (hot_ref, side_ref, scale_ref, weight_ref, query_out), refs = refs[:5], refs[5:]
    outs, refs = refs[:count], refs[count:]
    group_out, tree_ref, tree_out, group, turned_ref, plain_ref, delta_ref, sum_ref = refs[:8]
    sems, top_sems, group_sem = refs[8:]
    heads = heads_ref.shape[1] // HDIM
    units = 2 * heads
    step = pl.program_id(0)

    @pl.when(step == 0)
    def prepare():
        moves = copies(pieces, row_blocks(tree_ref, count), sems)
        gathers = copies(top_refs, row_blocks(group, tops), top_sems)
        for gather in gathers:
            gather.wait()
        keep = pltpu.make_async_copy(group, group_out, group_sem)
        keep.start()
        features = query_ref.shape[1]
        upstream = jnp.dot(
            group[...], weight_ref[:, 3 * features :], preferred_element_type=jnp.float32
        )
        both = jnp.concatenate([query_ref[...], upstream.astype(jnp.bfloat16)], axis=1)
        turned = both.astype(jnp.float32).T
        kept = heads_ref[...].astype(jnp.float32).T
        blank = jnp.zeros((HDIM, turned.shape[1]), jnp.bfloat16)
        for unit in range(units):
            own = turned[unit * HDIM : (unit + 1) * HDIM].astype(jnp.bfloat16)
            halves = [blank, own] if unit % 2 else [own, blank]
            turned_ref[unit] = jnp.concatenate(halves, axis=0)
            plain_ref[unit] = half_kept(both[:, pair_of(unit)], unit, 1)
        for head in range(heads):
            rows = slice(head * HDIM, (head + 1) * HDIM)
            pulled = turned[(heads + head) * HDIM : (heads + head + 1) * HDIM]
            delta_ref[head : head + 1] = jnp.sum(kept[rows] * pulled, axis=0, keepdims=True)
        sum_ref[...] = jnp.zeros_like(sum_ref)
        for move in moves:
            move.wait()
        keep.wait()

    here = pl.ds(step * KEY_TILE, KEY_TILE)
    tree = tree_ref[here]
    keys_turned = tree[:, : heads * HDIM].astype(jnp.float32).T.astype(jnp.bfloat16)
    seen = seen_tile(hot_ref, side_ref)
    weights, slopes = [], []
    for head in range(heads):
        scores = jnp.dot(tree[:, pair_of(head)], turned_ref[head], preferred_element_type=jnp.float32)
        weight = jnp.exp2(scores * LOG2_SCALE) * scale_ref[head : head + 1]
        pull = jnp.dot(
            tree[:, pair_of(heads + head)], turned_ref[heads + head], preferred_element_type=jnp.float32
        )
        slope = (weight * (pull - delta_ref[head : head + 1])).astype(jnp.bfloat16) * seen
        rows = slice(head * HDIM, (head + 1) * HDIM)
        sum_ref[rows] += jnp.dot(keys_turned[rows], slope, preferred_element_type=jnp.float32)
        weights.append(weight.astype(jnp.bfloat16) * seen)
        slopes.append(slope)
    terms = slopes + weights
    score_scale = math.sqrt(HDIM)
    for pair in range(heads):
        total = 0.0
        for unit in (2 * pair, 2 * pair + 1):
            part = jnp.dot(terms[unit], plain_ref[unit], preferred_element_type=jnp.float32)
            total = total + (part * score_scale if unit < heads else part)
        tree_out[here, pair * LANES : (pair + 1) * LANES] = total.astype(jnp.bfloat16)

    @pl.when(step == pl.num_programs(0) - 1)
    def finish():
        moves = copies(row_blocks(tree_out, count), outs, sems)
        query_out[...] = sum_ref[...].T * score_scale
        for move in moves:
            move.wait()


def attend_grad(query, tops, outs, pieces, hot, side, scale, weight):
    rows, features = query.shape
    wide = weight.shape[0]
    count, width = len(pieces), pieces[0].shape[1]
    keys = pieces[0].shape[0] * count
    heads = features // HDIM
    whole = lambda step: (0, 0)
    return pl.pallas_call(
        lambda *refs: attend_grad_body(count, len(tops), *refs),
        grid=(keys // KEY_TILE,),
        in_specs=[pl.BlockSpec((rows, features), whole)] * 2
        + [ANYWHERE] * (count + len(tops))
        + [
            pl.BlockSpec((KEY_TILE, LANES), lambda step: (step, 0)),
            pl.BlockSpec((3, LANES, rows), lambda step: (0, 0, 0)),
            pl.BlockSpec((8, rows), whole),
            pl.BlockSpec(weight.shape, whole),
        ],
        out_specs=[pl.BlockSpec((rows, features), whole)] + [ANYWHERE] * (count + 1),
        out_shape=[jax.ShapeDtypeStruct((rows, features), jnp.float32)]
        + [jax.ShapeDtypeStruct(piece.shape, jnp.bfloat16) for piece in pieces]
        + [jax.ShapeDtypeStruct((rows, wide), jnp.bfloat16)],
        scratch_shapes=[
            pltpu.VMEM((keys, width), jnp.bfloat16),
            pltpu.VMEM((keys, width), jnp.bfloat16),
            pltpu.VMEM((rows, wide), jnp.bfloat16),
            pltpu.VMEM((2 * heads, LANES, rows), jnp.bfloat16),
            pltpu.VMEM((2 * heads, rows, LANES), jnp.bfloat16),
            pltpu.VMEM((8, rows), jnp.float32),
            pltpu.VMEM((features, rows), jnp.float32),
            pltpu.SemaphoreType.DMA((count,)),
            pltpu.SemaphoreType.DMA((len(tops),)),
            pltpu.SemaphoreType.DMA,
        ],
        compiler_params=pltpu.CompilerParams(vmem_limit_bytes=56 << 20),
        name="attend_grad",
    )(query, outs, *pieces, *tops, hot, side, scale, weight)


def seen_factors(reachable, seg_query, off_query, segment, offset):
    segs = reachable.shape[0]
    labels = jnp.arange(LANES, dtype=jnp.int32)
    key_mark = jnp.where(labels < HDIM, segment[:, None], offset[:, None] + HDIM)
    hot = (key_mark == labels[None, :]).astype(jnp.bfloat16)
    query_hot = (labels[:, None] == seg_query[None, :]).astype(jnp.float32)
    wide = jnp.zeros((LANES, LANES), jnp.float32).at[:segs, :segs].set(reachable.T - jnp.eye(segs, dtype=jnp.float32))
    strict = jnp.dot(wide, query_hot, preferred_element_type=jnp.float32)
    same = query_hot
    before = ((labels[:, None] >= HDIM) & (labels[:, None] - HDIM <= off_query[None, :])).astype(jnp.float32)
    return hot, jnp.stack([strict, same, before]).astype(jnp.bfloat16)


def head_marks(features):
    row = lax.broadcasted_iota(jnp.int32, (features, LANES), 0) // HDIM
    column = lax.broadcasted_iota(jnp.int32, (features, LANES), 1)
    return (row == column).astype(jnp.float32)


def over_heads(values, marks):
    sums = jnp.dot(values, marks, precision=HIGHEST, preferred_element_type=jnp.float32)
    return sums, lambda heads: lax.dot_general(
        heads, marks, (((1,), (1,)), ((), ())), precision=HIGHEST, preferred_element_type=jnp.float32
    )


def project_body(count, *refs):
    pieces, refs = refs[:count], refs[count:]
    weight_ref, scale_ref, query_out, tree_out, raw_out, group_out, group, sems, group_sem = refs
    both = raw_out.shape[1]
    features = both // 2
    step = pl.program_id(0)
    keep = pltpu.make_async_copy(group, group_out, group_sem)

    @pl.when(step == 0)
    def assemble():
        moves = copies(pieces, row_blocks(group, count), sems)
        for move in moves:
            move.wait()
        keep.start()

    @pl.when(step == pl.num_programs(0) - 1)
    def kept():
        keep.wait()

    tile = query_out.shape[0]
    product = jnp.dot(
        group[pl.ds(step * tile, tile)], weight_ref[:, : 3 * features], preferred_element_type=jnp.float32
    )
    raw = product[:, :both]
    sums, spread_heads = over_heads(raw * raw, head_marks(both))
    unit = raw * spread_heads(lax.rsqrt(sums + EPSILON))
    scaled = (unit * scale_ref[...]).astype(jnp.bfloat16)
    raw_out[...] = raw
    query_out[...] = scaled[:, :features]
    tree_out[...] = jnp.concatenate(
        [scaled[:, features:], product[:, both:].astype(jnp.bfloat16)], axis=1
    )


def project(pieces, weight, scale):
    count, width = len(pieces), pieces[0].shape[1]
    rows = pieces[0].shape[0] * count
    features = weight.shape[1] // 4
    tile = rows // 4
    whole = lambda step: (0, 0)
    block = lambda columns: pl.BlockSpec((tile, columns), lambda step: (step, 0))
    return pl.pallas_call(
        lambda *refs: project_body(count, *refs),
        grid=(4,),
        in_specs=[ANYWHERE] * count
        + [
            pl.BlockSpec(weight.shape, whole),
            pl.BlockSpec((1, 2 * features), whole),
        ],
        out_specs=[block(features), block(2 * features), block(2 * features), ANYWHERE],
        out_shape=[
            jax.ShapeDtypeStruct((rows, features), jnp.bfloat16),
            jax.ShapeDtypeStruct((rows, 2 * features), jnp.bfloat16),
            jax.ShapeDtypeStruct((rows, 2 * features), jnp.float32),
            jax.ShapeDtypeStruct((rows, width), jnp.bfloat16),
        ],
        scratch_shapes=[
            pltpu.VMEM((rows, width), jnp.bfloat16),
            pltpu.SemaphoreType.DMA((count,)),
            pltpu.SemaphoreType.DMA,
        ],
        compiler_params=pltpu.CompilerParams(vmem_limit_bytes=40 << 20),
        name="project",
    )(*pieces, weight, scale)


def project_grad_body(count, query_ref, *refs):
    tree_refs, refs = refs[:count], refs[count:]
    (raw_ref, weight_ref, scale_ref, low_out, scale_out), part_outs = refs[:5], refs[5:]
    step = pl.program_id(0)
    both = raw_ref.shape[1]
    features = both // 2
    tree = sum(ref[...].astype(jnp.float32) for ref in tree_refs)
    upstream = jnp.concatenate([query_ref[...], tree[:, :features]], axis=1)
    raw = raw_ref[...]
    marks = head_marks(both)
    sums, spread_heads = over_heads(raw * raw, marks)
    inverse = spread_heads(lax.rsqrt(sums + EPSILON))
    unit = raw * inverse
    scale_out[...] = jnp.sum(upstream * unit, axis=0, keepdims=True)[None]
    pulled = upstream * scale_ref[...]
    inner = spread_heads(over_heads(unit * pulled, marks)[0])
    grads = inverse * (pulled - unit * inner)
    low = jnp.concatenate([grads, tree[:, features:]], axis=1).astype(jnp.bfloat16)
    low_out[...] = low
    part = contract_cols(low, weight_ref[:, : 3 * features]).astype(jnp.bfloat16)
    for place, part_out in enumerate(part_outs):

        @pl.when((step == place) | (len(part_outs) == 1))
        def store():
            part_out[...] = part


def project_grad(query_grad, tree_parts, raw, weight, scale, count_out):
    rows, both = raw.shape
    width = weight.shape[0]
    features = both // 2
    tile = rows // 4
    whole = lambda step: (0, 0)
    block = lambda columns: pl.BlockSpec((tile, columns), lambda step: (step, 0))
    return pl.pallas_call(
        lambda *refs: project_grad_body(len(tree_parts), *refs),
        grid=(4,),
        in_specs=[block(features)]
        + [block(both) for part in tree_parts]
        + [block(both), pl.BlockSpec(weight.shape, whole), pl.BlockSpec((1, both), whole)],
        out_specs=[
            block(3 * features),
            pl.BlockSpec((1, 1, both), lambda step: (step, 0, 0)),
        ]
        + ([block(width)] if count_out == 1 else [pl.BlockSpec((tile, width), whole)] * 4),
        out_shape=[
            jax.ShapeDtypeStruct((rows, 3 * features), jnp.bfloat16),
            jax.ShapeDtypeStruct((4, 1, both), jnp.float32),
        ]
        + [jax.ShapeDtypeStruct((rows // count_out, width), jnp.bfloat16)] * count_out,
        compiler_params=pltpu.CompilerParams(vmem_limit_bytes=40 << 20),
        name="project_grad",
    )(query_grad, *tree_parts, raw, weight, scale)


def gated(up, gate, scale_up, scale_gate):
    raw = gate * (scale_gate * math.sqrt(D))
    curve = 1.0 / (1.0 + jnp.exp(-raw))
    return raw, curve, raw * curve, up * scale_up


def hidden_body(count, halves, *refs):
    pieces, refs = refs[:count], refs[count:]
    weights, refs = refs[: 3 * halves], refs[3 * halves :]
    scale_ref, refs = refs[0], refs[1:]
    outs, refs = refs[:count], refs[count:]
    group_out, up_out, gate_out, mixed_out, group, matrices, total, sems, out_sem = refs
    half = up_out.shape[1] // halves
    moves = copies(pieces, row_blocks(group, count), sems)
    loads = [
        pltpu.make_async_copy(weights[place], matrices.at[place], sems.at[count + place])
        for place in range(3 * halves)
    ]
    for load in loads:
        load.start()
    for move in moves:
        move.wait()
    keep = pltpu.make_async_copy(group, group_out, out_sem)
    keep.start()
    for place in range(halves):
        columns = slice(place * half, (place + 1) * half)
        for matrix in range(3):
            loads[matrix * halves + place].wait()
        tokens = group[...]
        up = contract_cols(tokens, matrices[place])
        gate = contract_cols(tokens, matrices[halves + place])
        up_out[:, columns] = up.astype(jnp.bfloat16)
        gate_out[:, columns] = gate.astype(jnp.bfloat16)
        raw, curve, silu, scaled = gated(up, gate, scale_ref[0:1, columns], scale_ref[1:2, columns])
        mixed = (scaled * silu).astype(jnp.bfloat16)
        mixed_out[:, columns] = mixed
        part = jnp.dot(mixed, matrices[2 * halves + place], preferred_element_type=jnp.float32)
        total[...] = part if place == 0 else total[...] + part
    rows = group.shape[0] // count
    for place in range(count):
        outs[place][...] = total[place * rows : (place + 1) * rows].astype(jnp.bfloat16)
    keep.wait()


def hidden_forward(pieces, weights, scales):
    count, halves = len(pieces), len(weights[0])
    rows, width = pieces[0].shape[0] * count, pieces[0].shape[1]
    half = weights[0][0].shape[0]
    hidden = half * halves
    low = lambda columns: jax.ShapeDtypeStruct((rows, columns), jnp.bfloat16)
    vmem = pl.BlockSpec(memory_space=pltpu.VMEM)
    return pl.pallas_call(
        lambda *refs: hidden_body(count, halves, *refs),
        in_specs=[ANYWHERE] * (count + 3 * halves) + [vmem],
        out_specs=[vmem] * count + [ANYWHERE] + [vmem] * 3,
        out_shape=[jax.ShapeDtypeStruct(piece.shape, jnp.bfloat16) for piece in pieces]
        + [low(width), low(hidden), low(hidden), low(hidden)],
        scratch_shapes=[
            pltpu.VMEM((rows, width), jnp.bfloat16),
            pltpu.VMEM((3 * halves, half, width), jnp.bfloat16),
            pltpu.VMEM((rows, width), jnp.float32),
            pltpu.SemaphoreType.DMA((count + 3 * halves,)),
            pltpu.SemaphoreType.DMA,
        ],
        compiler_params=pltpu.CompilerParams(vmem_limit_bytes=52 << 20),
        name="hidden",
    )(*pieces, *[matrix for parts in weights for matrix in parts], jnp.stack(scales))


def hidden_grad_body(count, halves, *refs):
    pieces, refs = refs[:count], refs[count:]
    weights, refs = refs[: 3 * halves], refs[3 * halves :]
    scale_ref, up_ref, gate_ref = refs[:3]
    outs, refs = refs[3 : 3 + count], refs[3 + count :]
    group_out, up_out, gate_out, scale_out, group, matrices, total, sems, out_sem = refs
    half = up_out.shape[1] // halves
    moves = copies(pieces, row_blocks(group, count), sems)
    loads = [
        pltpu.make_async_copy(weights[place], matrices.at[place], sems.at[count + place])
        for place in range(3 * halves)
    ]
    for load in loads:
        load.start()
    for move in moves:
        move.wait()
    keep = pltpu.make_async_copy(group, group_out, out_sem)
    keep.start()
    for place in range(halves):
        columns = slice(place * half, (place + 1) * half)
        for matrix in range(3):
            loads[matrix * halves + place].wait()
        pulled = contract_cols(group[...], matrices[2 * halves + place])
        pulled = pulled.astype(jnp.bfloat16).astype(jnp.float32)
        up = up_ref[:, columns].astype(jnp.float32)
        gate = gate_ref[:, columns].astype(jnp.float32)
        scale_up, scale_gate = scale_ref[0:1, columns], scale_ref[1:2, columns]
        raw, curve, silu, scaled = gated(up, gate, scale_up, scale_gate)
        curved = pulled * silu
        up_low = (curved * scale_up).astype(jnp.bfloat16)
        bent = pulled * scaled * (curve * (1.0 + raw * (1.0 - curve)))
        gate_low = (bent * (scale_gate * math.sqrt(D))).astype(jnp.bfloat16)
        scale_out[0:1, columns] = jnp.sum(curved * up, axis=0, keepdims=True)
        scale_out[1:2, columns] = jnp.sum(bent * gate, axis=0, keepdims=True) * math.sqrt(D)
        up_out[:, columns] = up_low
        gate_out[:, columns] = gate_low
        part = jnp.dot(up_low, matrices[place], preferred_element_type=jnp.float32)
        part = part + jnp.dot(gate_low, matrices[halves + place], preferred_element_type=jnp.float32)
        total[...] = part if place == 0 else total[...] + part
    rows = group.shape[0] // count
    for place in range(count):
        outs[place][...] = total[place * rows : (place + 1) * rows].astype(jnp.bfloat16)
    keep.wait()


def hidden_backward(pieces, weights, scales, up, gate):
    count, halves = len(pieces), len(weights[0])
    rows, width = pieces[0].shape[0] * count, pieces[0].shape[1]
    half = weights[0][0].shape[0]
    hidden = half * halves
    low = lambda columns: jax.ShapeDtypeStruct((rows, columns), jnp.bfloat16)
    vmem = pl.BlockSpec(memory_space=pltpu.VMEM)
    return pl.pallas_call(
        lambda *refs: hidden_grad_body(count, halves, *refs),
        in_specs=[ANYWHERE] * (count + 3 * halves) + [vmem] * 3,
        out_specs=[vmem] * count + [ANYWHERE] + [vmem] * 3,
        out_shape=[jax.ShapeDtypeStruct(piece.shape, jnp.bfloat16) for piece in pieces]
        + [low(width), low(hidden), low(hidden), jax.ShapeDtypeStruct((8, hidden), jnp.float32)],
        scratch_shapes=[
            pltpu.VMEM((rows, width), jnp.bfloat16),
            pltpu.VMEM((3 * halves, half, width), jnp.bfloat16),
            pltpu.VMEM((rows, width), jnp.float32),
            pltpu.SemaphoreType.DMA((count + 3 * halves,)),
            pltpu.SemaphoreType.DMA,
        ],
        compiler_params=pltpu.CompilerParams(vmem_limit_bytes=56 << 20),
        name="hidden_grad",
    )(*pieces, *[matrix for parts in weights for matrix in parts], jnp.stack(scales), up, gate)


def visibility(parents, slots, group_size):
    labels = jnp.arange(SEGS, dtype=jnp.int32)
    linked = (parents[:, None] == labels[None, :]).astype(jnp.float32)
    reachable = jnp.maximum(linked, jnp.eye(SEGS, dtype=jnp.float32))
    for doubling in range(SEGS.bit_length()):
        reachable = jnp.minimum(jnp.dot(reachable, reachable, precision=HIGHEST), 1.0)
    return seen_factors(reachable, *row_labels(slots, group_size))


def forward_attention(packed, scale_both, pieces, parents, slots):
    rows = pieces[0].shape[0] * len(pieces)
    seen = visibility(parents, slots, rows)
    queries, tree_own, raw, group = project(pieces, packed, scale_both)
    tree = group_gather(tree_own, "ctx")
    heads_low, inverse, *parts = attend(queries, tree, *seen, packed, len(pieces))
    return group_scatter(parts, "tp"), (group, seen, queries, tree, raw, heads_low, inverse)


def feed_forward(weights, scales, alphas, tokens_own, branch_parts, cotangent_own):
    alpha_attn, alpha_mlp = alphas
    tokens_wide = tokens_own.astype(jnp.float32)
    branch_one = total_wide(branch_parts)
    hidden_one, pull_in = jax.vjp(mix_rows, tokens_wide, branch_one, alpha_attn)
    pieces = hidden_gather(hidden_one.astype(jnp.bfloat16))
    count = len(pieces)
    outs = hidden_forward(pieces, weights, scales)
    hidden_group, up, gate, mixed = outs[count:]
    branch_two = total_wide(hidden_scatter(outs[:count]))
    output_wide, pull_out = jax.vjp(mix_rows, hidden_one, branch_two, alpha_mlp)
    upstream = cotangent_own.astype(jnp.float32)
    hidden_direct, branch_two_grad, grad_alpha_mlp = pull_out(upstream)
    pieces = hidden_gather(branch_two_grad.astype(jnp.bfloat16))
    outs = hidden_backward(pieces, weights, scales, up, gate)
    top_group, up_low, gate_low, scale_sums = outs[count:]
    hidden_grad = hidden_direct + total_wide(hidden_scatter(outs[:count]))
    tokens_direct, branch_one_grad, grad_alpha_attn = pull_in(hidden_grad)
    tops = group_gather(branch_one_grad.astype(jnp.bfloat16), "tp")
    factors = ((up_low, hidden_group), (gate_low, hidden_group), (mixed, top_group))
    sums = (jnp.concatenate([grad_alpha_attn, grad_alpha_mlp]), scale_sums[:2])
    return output_wide.astype(jnp.bfloat16), tokens_direct, tops, factors, sums


def backward_attention(packed, scale_both, kept, tops, tokens_direct):
    group, seen, queries, tree, raw, heads_low, inverse = kept
    query_grads, *rest = attend_grad(
        queries, tops, heads_low, tree, *seen, inverse, packed
    )
    tree_grads, top_group = rest[:-1], rest[-1]
    tree_parts = group_scatter(tree_grads, "ctx")
    low, scale_sums, *parts = project_grad(
        query_grads, tree_parts, raw, packed, scale_both, len(tops)
    )
    grad_tokens = tokens_direct + total_wide(group_scatter(parts, "tp"))
    features = queries.shape[1]
    scale_sum = jnp.sum(scale_sums, axis=(0, 1))
    return grad_tokens, ((group, low), (top_group, heads_low)), (
        scale_sum[:features] + scale_sum[features:]
    )


def joint_product(factors):
    formers, latters = zip(*factors)
    return contract_rows(jnp.concatenate(formers, axis=0), jnp.concatenate(latters, axis=0))


def per_device(
    tokens,
    parents,
    slot_segment,
    w_query,
    w_key,
    w_value,
    w_attn_out,
    w_up,
    w_gate,
    w_down,
    alpha_attn,
    alpha_mlp,
    scale_qk,
    scale_up,
    scale_gate,
    cotangent,
):
    width = tokens.shape[-1]
    micros = range(tokens.shape[0])
    groups = [group_gather(tokens[m, 0], "tp") for m in micros]
    packed = lax.all_gather(
        jnp.concatenate([w_query, w_key, w_value, w_attn_out.T], axis=1),
        SPREAD,
        axis=0,
        tiled=True,
    )
    shards, groups = lax.optimization_barrier((hidden_shards(w_up, w_gate, w_down), groups))
    weights = hidden_weights(shards)
    scales = hidden_scales(scale_up, scale_gate)
    scale_both = jnp.concatenate([scale_qk, scale_qk])[None]
    front = [
        forward_attention(packed, scale_both, groups[m], parents[m, 0], slot_segment[m, 0])
        for m in micros
    ]
    mid = [
        feed_forward(
            weights, scales, (alpha_attn, alpha_mlp), tokens[m, 0], front[m][0], cotangent[m, 0]
        )
        for m in micros
    ]
    lines = core_sums(
        [
            joint_product([mid[m][3][place] for m in micros]).astype(jnp.bfloat16)
            for place in range(3)
        ]
    )
    tops = [mid[m][2] for m in micros]
    lines, tops[-1] = lax.optimization_barrier((lines, tops[-1]))
    grad_u, grad_g, grad_d = hidden_weight_grads(lines)
    back = [
        backward_attention(packed, scale_both, front[m][1], tops[m], mid[m][1]) for m in micros
    ]
    grad_attention = owner_scatter(
        jnp.concatenate(
            [joint_product([back[m][1][place] for m in micros]) for place in range(2)], axis=1
        ).astype(jnp.bfloat16)
    )
    grad_q, grad_k, grad_v, grad_o = jnp.split(grad_attention, 4, axis=1)
    sum_qk = butterfly(sum(back[m][2] for m in micros), SPREAD)
    alphas = butterfly(sum(mid[m][4][0] for m in micros), SPREAD + ("tp",))
    sum_up, sum_gate = hidden_scale_grads(sum(mid[m][4][1] for m in micros))
    return (
        jnp.stack([mid[m][0] for m in micros])[:, None],
        jnp.stack([back[m][0] for m in micros])[:, None],
        grad_q,
        grad_k,
        grad_v,
        grad_o.T,
        grad_u.T,
        grad_g.T,
        grad_d,
        alphas[:width],
        alphas[width:],
        sum_qk,
        sum_up,
        sum_gate,
    )


def solution(mesh):
    return jax.shard_map(
        per_device,
        mesh=mesh,
        in_specs=(
            P(None, "shard", ("ctx", "tp"), None),
            P(None, "shard", None),
            P(None, "shard", None),
            P(("shard", "ctx"), "tp"),
            P(("shard", "ctx"), "tp"),
            P(("shard", "ctx"), "tp"),
            P("tp", ("shard", "ctx")),
            P(("shard", "ctx"), "tp"),
            P(("shard", "ctx"), "tp"),
            P("tp", ("shard", "ctx")),
            P(),
            P(),
            P("tp"),
            P("tp"),
            P("tp"),
            P(None, "shard", ("ctx", "tp"), None),
        ),
        out_specs=(
            P(None, "shard", ("ctx", "tp"), None),
            P(None, "shard", ("ctx", "tp"), None),
            P(("shard", "ctx"), "tp"),
            P(("shard", "ctx"), "tp"),
            P(("shard", "ctx"), "tp"),
            P("tp", ("shard", "ctx")),
            P(("shard", "ctx"), "tp"),
            P(("shard", "ctx"), "tp"),
            P("tp", ("shard", "ctx")),
            P(),
            P(),
            P("tp"),
            P("tp"),
            P("tp"),
        ),
        check_vma=False,
    )
```

time: 995 us -> 821 us (0.83)
  Pallas kernels: 99.6 us -> 243 us
  matrix products: 131 us -> 33.3 us
  waiting for transfers between devices: 361 us -> 287 us
  other arithmetic: 113 us -> 51.2 us
  local copies, waits for them, and re-layouts: 132 us -> 78.8 us
  blocking collectives: 39.6 us -> 0 us
    pallas_call x4 -> x12, Pallas kernels: 99.6 us -> 243 us  [the longest x2 77.5 us: attend_grad(): pl.pallas_call(lambda *refs: attend_grad_body(count, len(tops), *refs), g...]
    dot_general x28 -> x0, matrix products: 95.2 us -> none  [the longest x14 47.4 us: contract_cols(): lax.dot_general(former, latter, (((1,), (1,)), ((), ())), preferred_eleme...]
    ppermute x24, waiting for transfers between devices: 97.7 us -> 32.2 us  [hop(): lax.ppermute(value, SPREAD, [(place, place ^ bits) for place in range(8)])]
    all_gather x1 -> x0, blocking collectives: 39.6 us -> none  [hidden_scales(): line = lax.all_gather(own, 'tp')]
    concatenate x9 -> x2, other arithmetic: 24.7 us -> 0.08 us  [the longest x1 0.08 us: per_device(): scale_both = jnp.concatenate([scale_qk, scale_qk])[None]]
    mul x14 -> x0, local copies, waits for them, and re-layouts: 15.1 us -> none  [the longest x12 14.9 us: unit_rows(): values * lax.rsqrt(jnp.sum(values * values, axis=-1, keepdims=True) + EPS...]
    split x12 -> x0, local copies, waits for them, and re-layouts: 14.5 us -> none  [the longest x6 9.52 us: group_scatter(): own, beside, across, far = jnp.split(partial_low, 4, axis=0)]
    unnamed x240 -> x209, local copies, waits for them, and re-layouts: 27.2 us -> 37.9 us
  transfers between devices with their start and end apart: 95 -> 98, of which waited for: 38 -> 32; matrix products, arithmetic and copies ran while one was open for 34% -> 14% of each run, Pallas kernels for 10% -> 30%
where the time goes in v8:
time: 821 us; the launch traced here: 812 us
  waiting for transfers between devices  287 us (35%)
  Pallas kernels  243 us (30%)
  starting transfers between devices  104 us (13%)
  local copies, waits for them, and re-layouts  78.8 us (10%)
  other arithmetic  51.2 us (6%)
  matrix products  33.3 us (4%)
  between operations  15.9 us (2%)
    ppermute x65, waiting for transfers between devices, swap(): lax.ppermute(value, axis, [(place, place ^ bit) for place in range(size)])  254 us
    pallas_call x2, Pallas kernels, attend_grad(): pl.pallas_call(lambda *refs: attend_grad_body(count, len(tops), *refs), g...  77.5 us
    ppermute x65, starting transfers between devices, swap(): lax.ppermute(value, axis, [(place, place ^ bit) for place in range(size)])  64.2 us
    pallas_call x2, Pallas kernels, attend(): pl.pallas_call(lambda *refs: attend_body(count, *refs), grid=(keys // KEY...  46.6 us
    pallas_call x2, Pallas kernels, hidden_backward(): pl.pallas_call(lambda *refs: hidden_grad_body(count, halves, *refs), in_s...  39.1 us
    unnamed x209, local copies, waits for them, and re-layouts  37.9 us
    ppermute x24, waiting for transfers between devices, hop(): lax.ppermute(value, SPREAD, [(place, place ^ bits) for place in range(8)])  32.2 us
    pallas_call x2, Pallas kernels, hidden_forward(): pl.pallas_call(lambda *refs: hidden_body(count, halves, *refs), in_specs=...  31.7 us
  transfers between devices with their start and end apart: 98, of which 32 were waited for; matrix products, arithmetic and copies ran while one was open for 14% of the time, Pallas kernels for 30%

profile of v8, /device:TPU:0, one launch (start us, length us, event | category | flops | bytes accessed | tf_op | source)
XLA Modules:
  0.0 812.2 jit_solution(17533732893055422700)
XLA Ops:
  12.9 5.3 all-to-all-start
  18.3 3.3 collective-permute-start.1
  28.2 21.3 %collective-permute-done.1.refs_2_ = bf16[160,1280]{1,0:T(8,128)(2,1)S(1)} collective-permute-done((bf16[160,1280]{1,0:T(8,128)(2,1)S(1)}, bf16[160,1280]{1,0:T(8,128)(2,1)S(1)}, u32[]{:S(2)}, u32[]{:S(2)}) %collective-permute-start.1) | collective-permute-done | bytes 409632 | tf_op jit(solution)/shard_map/ppermute | solution.py:44
  49.9 8.1 collective-permute-done.4.refs_2_
  59.0 4.0 copy.70
  63.0 4.5 reshape.545
  67.5 8.4 %collective-permute-done.5.refs_3_ = bf16[160,1280]{1,0:T(8,128)(2,1)S(1)} collective-permute-done((bf16[160,1280]{1,0:T(8,128)(2,1)S(1)}, bf16[160,1280]{1,0:T(8,128)(2,1)S(1)}, u32[]{:S(2)}, u32[]{:S(2)}) %collective-permute-start.5) | collective-permute-done | bytes 409632 | tf_op jit(solution)/shard_map/ppermute | solution.py:44
  85.8 9.1 %project.3 = (bf16[640,320]{1,0:T(8,128)(2,1)S(1)}, bf16[640,640]{1,0:T(8,128)(2,1)}, f32[640,640]{1,0:T(8,128)S(1)}, bf16[640,1280]{1,0:T(8,128)(2,1)S(1)}) custom-call(bf16[160,1280]{1,0:T(8,128)(2,1)S(1)} %copy-done.16, bf16[160,1280]{1,0:T(8,128)(2,1)S(1)} %collective-permute-done.3.refs_1_, bf16[160,1280]{1,0:T(8,128)(2,1)S(1)} %collective-permute-done.4.refs_2_, ...), custom_call_target="tpu_custom_call" | custom-call | tf_op jit(solution)/shard_map/project/pallas_call | solution.py:535
  98.5 9.2 %project.2 = (bf16[640,320]{1,0:T(8,128)(2,1)S(1)}, bf16[640,640]{1,0:T(8,128)(2,1)}, f32[640,640]{1,0:T(8,128)S(1)}, bf16[640,1280]{1,0:T(8,128)(2,1)S(1)}) custom-call(bf16[160,1280]{1,0:T(8,128)(2,1)S(1)} %copy-done.14, bf16[160,1280]{1,0:T(8,128)(2,1)S(1)} %collective-permute-done.refs_1_, bf16[160,1280]{1,0:T(8,128)(2,1)S(1)} %collective-permute-done.1.refs_2_, ...), custom_call_target="tpu_custom_call" | custom-call | tf_op jit(solution)/shard_map/project/pallas_call | solution.py:535
  113.1 5.1 collective-permute-done.26.refs_3_.refs_4_
  119.8 15.0 %collective-permute-done.7.refs_3_.refs_4_ = bf16[640,640]{1,0:T(8,128)(2,1)} collective-permute-done((bf16[640,640]{1,0:T(8,128)(2,1)}, bf16[640,640]{1,0:T(8,128)(2,1)}, u32[]{:S(2)}, u32[]{:S(2)}) %collective-permute-start.7) | collective-permute-done | bytes 819232 | tf_op jit(solution)/shard_map/ppermute | solution.py:44
  140.4 23.0 %attend.3 = (bf16[640,320]{1,0:T(8,128)(2,1)S(1)}, f32[8,640]{1,0:T(8,128)S(1)}, bf16[160,1280]{1,0:T(8,128)(2,1)S(1)}, bf16[160,1280]{1,0:T(8,128)(2,1)S(1)}, b...) custom-call(bf16[640,320]{1,0:T(8,128)(2,1)S(1)} %copy-done.10, ...), custom_call_target="tpu_custom_call" | custom-call | tf_op jit(solution)/shard_map/attend/pallas_call | solution.py:324
  166.3 28.6 %collective-permute-done.20 = f32[1,2,160]{2,1,0:T(2,128)S(1)} collective-permute-done((f32[1,2,160]{2,1,0:T(2,128)S(1)}, f32[1,2,160]{2,1,0:T(2,128)S(1)}, u32[]{:S(2)}, u32[]{:S(2)}) %collective-permute-start.20) | collective-permute-done | bytes 1312 | tf_op jit(solution)/shard_map/ppermute | solution.py:44
  196.6 23.6 %attend.2 = (bf16[640,320]{1,0:T(8,128)(2,1)S(1)}, f32[8,640]{1,0:T(8,128)S(1)}, bf16[160,1280]{1,0:T(8,128)(2,1)S(1)}, bf16[160,1280]{1,0:T(8,128)(2,1)}, bf16[...) custom-call(bf16[640,320]{1,0:T(8,128)(2,1)S(1)} %copy-done.12, ...), custom_call_target="tpu_custom_call" | custom-call | tf_op jit(solution)/shard_map/attend/pallas_call | solution.py:324
  225.0 5.9 collective-permute-start.30
  230.9 14.7 %collective-permute-done.10 = bf16[160,1280]{1,0:T(8,128)(2,1)S(1)} collective-permute-done((bf16[160,1280]{1,0:T(8,128)(2,1)S(1)}, bf16[160,1280]{1,0:T(8,128)(2,1)S(1)}, u32[]{:S(2)}, u32[]{:S(2)}) %collective-permute-start.10) | collective-permute-done | bytes 409632 | tf_op jit(solution)/shard_map/ppermute | solution.py:44
  251.3 14.4 %collective-permute-done.11 = bf16[160,1280]{1,0:T(8,128)(2,1)S(1)} collective-permute-done((bf16[160,1280]{1,0:T(8,128)(2,1)S(1)}, bf16[160,1280]{1,0:T(8,128)(2,1)S(1)}, u32[]{:S(2)}, u32[]{:S(2)}) %collective-permute-start.11) | collective-permute-done | bytes 409632 | tf_op jit(solution)/shard_map/ppermute | solution.py:44
  277.0 3.3 collective-permute-done.12.refs_1_
  282.6 3.2 collective-permute-done.13.refs_2_
  285.9 15.7 %hidden.2 = (bf16[160,1280]{1,0:T(8,128)(2,1)S(1)}, bf16[160,1280]{1,0:T(8,128)(2,1)S(1)}, bf16[160,1280]{1,0:T(8,128)(2,1)S(1)}, bf16[160,1280]{1,0:T(8,128)(2,...) custom-call(bf16[160,1280]{1,0:T(8,128)(2,1)} %multiply_convert_fusi, ...), custom_call_target="tpu_custom_call" | custom-call | tf_op jit(solution)/shard_map/hidden/pallas_call | solution.py:666
  306.7 16.0 %hidden.3 = (bf16[160,1280]{1,0:T(8,128)(2,1)S(1)}, bf16[160,1280]{1,0:T(8,128)(2,1)S(1)}, bf16[160,1280]{1,0:T(8,128)(2,1)S(1)}, bf16[160,1280]{1,0:T(8,128)(2,...) custom-call(bf16[160,1280]{1,0:T(8,128)(2,1)} %copy-done.68, ...), custom_call_target="tpu_custom_call" | custom-call | tf_op jit(solution)/shard_map/hidden/pallas_call | solution.py:666
  326.6 6.0 collective-permute-done.36
  332.7 8.5 %collective-permute-done.35 = bf16[160,1280]{1,0:T(8,128)(2,1)S(1)} collective-permute-done((bf16[160,1280]{1,0:T(8,128)(2,1)S(1)}, bf16[160,1280]{1,0:T(8,128)(2,1)S(1)}, u32[]{:S(2)}, u32[]{:S(2)}) %collective-permute-start.35) | collective-permute-done | bytes 409632 | tf_op jit(solution)/shard_map/ppermute | solution.py:92
  351.0 7.1 collective-permute-done.52.refs_1_
  363.3 19.8 %hidden_grad.3 = (bf16[160,1280]{1,0:T(8,128)(2,1)}, bf16[160,1280]{1,0:T(8,128)(2,1)}, bf16[160,1280]{1,0:T(8,128)(2,1)}, bf16[160,1280]{1,0:T(8,128)(2,1)}, bf...) custom-call(bf16[160,1280]{1,0:T(8,128)(2,1)} %copy-done.63, ...), custom_call_target="tpu_custom_call" | custom-call | tf_op jit(solution)/shard_map/hidden_grad/pallas_call | solution.py:736
  387.6 19.4 %hidden_grad.2 = (bf16[160,1280]{1,0:T(8,128)(2,1)}, bf16[160,1280]{1,0:T(8,128)(2,1)}, bf16[160,1280]{1,0:T(8,128)(2,1)}, bf16[160,1280]{1,0:T(8,128)(2,1)}, bf...) custom-call(bf16[160,1280]{1,0:T(8,128)(2,1)} %copy-done.62, ...), custom_call_target="tpu_custom_call" | custom-call | tf_op jit(solution)/shard_map/hidden_grad/pallas_call | solution.py:736
  410.2 7.7 convolution_convert_fusion.2
  418.4 4.8 convolution_convert_fusion.1
  434.8 3.4 collective-permute-start.62
  438.2 4.8 convolution_convert_fusion
  445.9 4.7 collective-permute-start.61
  450.6 6.3 collective-permute-done.62.refs_8_
  462.2 3.6 add_convert_fusion
  465.8 8.5 %collective-permute-done.63.refs_9_ = bf16[160,1280]{1,0:T(8,128)(2,1)} collective-permute-done((bf16[160,1280]{1,0:T(8,128)(2,1)}, bf16[160,1280]{1,0:T(8,128)(2,1)}, u32[]{:S(2)}, u32[]{:S(2)}) %collective-permute-start.63) | collective-permute-done | bytes 409632 | tf_op jit(solution)/shard_map/ppermute | solution.py:44
  478.7 33.2 %collective-permute-done.44.refs_8_ = bf16[160,1280]{1,0:T(8,128)(2,1)S(1)} collective-permute-done((bf16[160,1280]{1,0:T(8,128)(2,1)S(1)}, bf16[160,1280]{1,0:T(8,128)(2,1)S(1)}, u32[]{:S(2)}, u32[]{:S(2)}) %collective-permute-start.44) | collective-permute-done | bytes 409632 | tf_op jit(solution)/shard_map/ppermute | solution.py:44
  511.9 19.1 %collective-permute-done.45.refs_9_ = bf16[160,1280]{1,0:T(8,128)(2,1)S(1)} collective-permute-done((bf16[160,1280]{1,0:T(8,128)(2,1)S(1)}, bf16[160,1280]{1,0:T(8,128)(2,1)S(1)}, u32[]{:S(2)}, u32[]{:S(2)}) %collective-permute-start.45) | collective-permute-done | bytes 409632 | tf_op jit(solution)/shard_map/ppermute | solution.py:44
  531.7 38.9 %attend_grad.2 = (f32[640,320]{1,0:T(8,128)}, bf16[640,640]{1,0:T(8,128)(2,1)}, bf16[640,640]{1,0:T(8,128)(2,1)}, bf16[640,640]{1,0:T(8,128)(2,1)}, bf16[640,640]{1,0:T(8,128)(2,1)}, /*index=5*/bf16[640,1280]{1,0:T(8,128)(2,1)}) custom-call(bf16[640,320]{1,0:T(8,128)(2,1)} %copy-done.11, bf16[640,320]{1,0:T(8,128)(2,1)} %copy-done.26, ...), custom_call_target="tpu_custom_call" | custom-call | tf_op jit(solution)/shard_map/attend_grad/pallas_call | solution.py:436
  572.2 38.6 %attend_grad.3 = (f32[640,320]{1,0:T(8,128)}, bf16[640,640]{1,0:T(8,128)(2,1)}, bf16[640,640]{1,0:T(8,128)(2,1)}, bf16[640,640]{1,0:T(8,128)(2,1)}, bf16[640,640]{1,0:T(8,128)(2,1)}, /*index=5*/bf16[640,1280]{1,0:T(8,128)(2,1)}) custom-call(bf16[640,320]{1,0:T(8,128)(2,1)} %copy-done.9, bf16[640,320]{1,0:T(8,128)(2,1)} %copy-done.25, ...), custom_call_target="tpu_custom_call" | custom-call | tf_op jit(solution)/shard_map/attend_grad/pallas_call | solution.py:436
  631.6 4.0 collective-permute-done.88
  642.6 14.8 %project_grad.2 = (bf16[640,960]{1,0:T(8,128)(2,1)S(1)}, f32[4,1,640]{2,1,0:T(1,128)S(1)}, bf16[160,1280]{1,0:T(8,128)(2,1)S(1)}, bf16[160,1280]{1,0:T(8,128)(2,...) custom-call(f32[640,320]{1,0:T(8,128)S(1)} %copy-done.22, bf16[640,640]{1,0:T(8,128)(2,1)S(1)} %copy-done.24, ...), custom_call_target="tpu_custom_call" | custom-call | tf_op jit(solution)/shard_map/project_grad/pallas_call | solution.py:594
  665.3 4.3 fusion.20
  681.7 14.7 %project_grad.3 = (bf16[640,960]{1,0:T(8,128)(2,1)S(1)}, f32[4,1,640]{2,1,0:T(1,128)S(1)}, bf16[160,1280]{1,0:T(8,128)(2,1)S(1)}, bf16[160,1280]{1,0:T(8,128)(2,...) custom-call(f32[640,320]{1,0:T(8,128)S(1)} %copy-done.21, bf16[640,640]{1,0:T(8,128)(2,1)S(1)} %copy-done.23, ...), custom_call_target="tpu_custom_call" | custom-call | tf_op jit(solution)/shard_map/project_grad/pallas_call | solution.py:594
  701.0 7.6 convolution_convert_fusion.3
  714.0 13.3 %collective-permute-done.68 = bf16[160,1280]{1,0:T(8,128)(2,1)S(1)} collective-permute-done((bf16[160,1280]{1,0:T(8,128)(2,1)}, bf16[160,1280]{1,0:T(8,128)(2,1)S(1)}, u32[]{:S(2)}, u32[]{:S(2)}) %collective-permute-start.68) | collective-permute-done | bytes 409632 | tf_op jit(solution)/shard_map/ppermute | solution.py:44
  733.0 9.5 %collective-permute-done.67 = bf16[160,1280]{1,0:T(8,128)(2,1)S(1)} collective-permute-done((bf16[160,1280]{1,0:T(8,128)(2,1)S(1)}, bf16[160,1280]{1,0:T(8,128)(2,1)S(1)}, u32[]{:S(2)}, u32[]{:S(2)}) %collective-permute-start.67) | collective-permute-done | bytes 409632 | tf_op jit(solution)/shard_map/ppermute | solution.py:44
  742.5 7.1 collective-permute-done.69
  763.9 3.6 all-to-all-start.1
  772.5 23.6 %collective-permute-done.72 = bf16[160,640]{1,0:T(8,128)(2,1)S(1)} collective-permute-done((bf16[160,640]{1,0:T(8,128)(2,1)S(1)}, bf16[160,640]{1,0:T(8,128)(2,1)S(1)}, u32[]{:S(2)}, u32[]{:S(2)}) %collective-permute-start.72) | collective-permute-done | bytes 204832 | tf_op jit(solution)/shard_map/ppermute | solution.py:44
  (532 shorter events, 217.9 us)
Async XLA Ops:
  7.2 75.7 %all-gather.8.cloned.1.call-start = ((), (), s32[]{:S(2)}) async-start(), calls=%async_computation.5 | async-start | bytes 3686400 | tf_op jit(solution)/shard_map/all_gather | solution.py:840
  12.9 46.1 %all-to-all-start = ((bf16[8,3,160,160]{3,2,1,0:T(8,128)(2,1)}), bf16[8,3,160,160]{3,2,1,0:T(8,128)(2,1)}, u32[]{:S(2)}, u32[]{:S(2)}) async-start(bf16[8,3,160,160]{3,2,1,0:T(8,128)(2,1)} %pad_maximum_fusion), calls=%async_computation | async-start | bytes 3932160 | tf_op jit(solution)/shard_map/all_to_all | solution.py:120
  18.2 228.5 %all-gather.10.cloned.1.call-start = ((), (), s32[]{:S(2)}) async-start(), calls=%async_computation.9 | async-start | bytes 2048000 | tf_op jit(solution)/shard_map/all_gather | solution.py:129
  18.3 31.2 %collective-permute-start.1 = (bf16[160,1280]{1,0:T(8,128)(2,1)S(1)}, bf16[160,1280]{1,0:T(8,128)(2,1)S(1)}, u32[]{:S(2)}, u32[]{:S(2)}) collective-permute-start(bf16[160,1280]{1,0:T(8,128)(2,1)S(1)} %get-tuple-element.130.refs_0_), channel_id=1, source_target_pairs={{0,2},{1,3},{2,0},{3,1},{4,6},{5,7},{6,4},{7,5},{8,10},{9,11},{10,... | collective-permute-start | bytes 1228808 | tf_op jit(solution)/shard_map/ppermute | solution.py:44
  21.6 36.4 %collective-permute-start.4 = (bf16[160,1280]{1,0:T(8,128)(2,1)S(1)}, bf16[160,1280]{1,0:T(8,128)(2,1)S(1)}, u32[]{:S(2)}, u32[]{:S(2)}) collective-permute-start(bf16[160,1280]{1,0:T(8,128)(2,1)S(1)} %get-tuple-element.145.refs_0_), channel_id=1, source_target_pairs={{0,2},{1,3},{2,0},{3,1},{4,6},{5,7},{6,4},{7,5},{8,10},{9,11},{10,... | collective-permute-start | bytes 1228808 | tf_op jit(solution)/shard_map/ppermute | solution.py:44
  21.7 45.8 %collective-permute-start = (bf16[160,1280]{1,0:T(8,128)(2,1)S(1)}, bf16[160,1280]{1,0:T(8,128)(2,1)S(1)}, u32[]{:S(2)}, u32[]{:S(2)}) collective-permute-start(bf16[160,1280]{1,0:T(8,128)(2,1)S(1)} %get-tuple-element.130.refs_0_), channel_id=1, source_target_pairs={{0,1},{1,0},{2,3},{3,2},{4,5},{5,4},{6,7},{7,6},{8,9},{9,8},{10,11... | collective-permute-start | bytes 1228808 | tf_op jit(solution)/shard_map/ppermute | solution.py:44
  23.5 43.9 %collective-permute-start.3 = (bf16[160,1280]{1,0:T(8,128)(2,1)S(1)}, bf16[160,1280]{1,0:T(8,128)(2,1)S(1)}, u32[]{:S(2)}, u32[]{:S(2)}) collective-permute-start(bf16[160,1280]{1,0:T(8,128)(2,1)S(1)} %get-tuple-element.145.refs_0_), channel_id=1, source_target_pairs={{0,1},{1,0},{2,3},{3,2},{4,5},{5,4},{6,7},{7,6},{8,9},{9,8},{10,11... | collective-permute-start | bytes 1228808 | tf_op jit(solution)/shard_map/ppermute | solution.py:44
  25.3 139.9 %collective-permute-start.19 = (f32[1,2,160]{2,1,0:T(2,128)S(1)}, f32[1,2,160]{2,1,0:T(2,128)S(1)}, u32[]{:S(2)}, u32[]{:S(2)}) collective-permute-start(f32[1,2,160]{2,1,0:T(2,128)S(1)} %maximum_bitcast_fusion.2), channel_id=1, source_target_pairs={{0,2},{1,3},{2,0},{3,1},{4,6},{5,7},{6,4},{7,5},{8,10},{9,11},{10,... | collective-permute-start | bytes 3848 | tf_op jit(solution)/shard_map/ppermute | solution.py:44
  78.2 168.9 %all-gather.12.cloned.1.call-start = ((), (), s32[]{:S(2)}) async-start(), calls=%async_computation.10 | async-start | bytes 2048000 | tf_op jit(solution)/shard_map/all_gather | solution.py:129
  80.9 169.8 %all-gather.14.cloned.1.call-start = ((), (), s32[]{:S(2)}) async-start(), calls=%async_computation.11 | async-start | bytes 2048000 | tf_op jit(solution)/shard_map/all_gather | solution.py:129
  119.0 637.3 %reduce-scatter.8.cloned.1.call-start = ((), (), s32[]{:S(2)}) async-start(), calls=%async_computation.8 | async-start | bytes 2048000 | tf_op jit(solution)/shard_map/reduce_scatter | solution.py:158
  119.3 76.3 %collective-permute-start.6 = (bf16[640,640]{1,0:T(8,128)(2,1)}, bf16[640,640]{1,0:T(8,128)(2,1)}, u32[]{:S(2)}, u32[]{:S(2)}) collective-permute-start(bf16[640,640]{1,0:T(8,128)(2,1)} %get-tuple-element.135.refs_1_.refs_2_), channel_id=1, source_target_pairs={{0,4},{4,0},{8,12},{12,8},{1,5},{5,1},{9,13},{13,9},{2,6},{6,2},{1... | collective-permute-start | bytes 2457608 | tf_op jit(solution)/shard_map/ppermute | solution.py:44
  134.8 60.8 %collective-permute-start.8 = (bf16[640,640]{1,0:T(8,128)(2,1)}, bf16[640,640]{1,0:T(8,128)(2,1)}, u32[]{:S(2)}, u32[]{:S(2)}) collective-permute-start(bf16[640,640]{1,0:T(8,128)(2,1)} %collective-permute-done.7.refs_3_.refs_4_), channel_id=1, source_target_pairs={{0,4},{4,0},{8,12},{12,8},{1,5},{5,1},{9,13},{13,9},{2,6},{6,2},{1... | collective-permute-start | bytes 2457608 | tf_op jit(solution)/shard_map/ppermute | solution.py:44
  137.1 29.2 %collective-permute-start.18 = (f32[1,2,160]{2,1,0:T(2,128)S(1)}, f32[1,2,160]{2,1,0:T(2,128)S(1)}, u32[]{:S(2)}, u32[]{:S(2)}) collective-permute-start(f32[1,2,160]{2,1,0:T(2,128)S(1)} %maximum_bitcast_fusion.2), channel_id=1, source_target_pairs={{0,1},{1,0},{2,3},{3,2},{4,5},{5,4},{6,7},{7,6},{8,9},{9,8},{10,11... | collective-permute-start | bytes 3848 | tf_op jit(solution)/shard_map/ppermute | solution.py:44
  164.2 58.9 %collective-permute-start.29 = (bf16[160,1280]{1,0:T(8,128)(2,1)}, bf16[160,1280]{1,0:T(8,128)(2,1)}, u32[]{:S(2)}, u32[]{:S(2)}) collective-permute-start(bf16[160,1280]{1,0:T(8,128)(2,1)} %get-tuple-element.154), channel_id=1, source_target_pairs={{0,1},{1,0},{2,3},{3,2},{4,5},{5,4},{6,7},{7,6},{8,9},{9,8},{10,11... | collective-permute-start | bytes 1228808 | tf_op jit(solution)/shard_map/ppermute | solution.py:44
  165.1 29.8 %collective-permute-start.20 = (f32[1,2,160]{2,1,0:T(2,128)S(1)}, f32[1,2,160]{2,1,0:T(2,128)S(1)}, u32[]{:S(2)}, u32[]{:S(2)}) collective-permute-start(f32[1,2,160]{2,1,0:T(2,128)S(1)} %collective-permute-done.19), channel_id=1, source_target_pairs={{0,1},{1,0},{2,3},{3,2},{4,5},{5,4},{6,7},{7,6},{8,9},{9,8},{10,11... | collective-permute-start | bytes 3848 | tf_op jit(solution)/shard_map/ppermute | solution.py:44
  195.5 51.2 %collective-permute-start.28 = (bf16[160,1280]{1,0:T(8,128)(2,1)S(1)}, bf16[160,1280]{1,0:T(8,128)(2,1)}, u32[]{:S(2)}, u32[]{:S(2)}) collective-permute-start(bf16[160,1280]{1,0:T(8,128)(2,1)S(1)} %get-tuple-element.152), channel_id=1, source_target_pairs={{0,1},{1,0},{2,3},{3,2},{4,5},{5,4},{6,7},{7,6},{8,9},{9,8},{10,11... | collective-permute-start | bytes 1228808 | tf_op jit(solution)/shard_map/ppermute | solution.py:44
  223.0 27.7 %collective-permute-start.9 = (bf16[160,1280]{1,0:T(8,128)(2,1)}, bf16[160,1280]{1,0:T(8,128)(2,1)S(1)}, u32[]{:S(2)}, u32[]{:S(2)}) collective-permute-start(bf16[160,1280]{1,0:T(8,128)(2,1)} %get-tuple-element.137), channel_id=1, source_target_pairs={{0,1},{1,0},{2,3},{3,2},{4,5},{5,4},{6,7},{7,6},{8,9},{9,8},{10,11... | collective-permute-start | bytes 1228808 | tf_op jit(solution)/shard_map/ppermute | solution.py:44
  246.7 26.3 %collective-permute-start.15 = (bf16[640,1280]{1,0:T(8,128)(2,1)}, bf16[640,1280]{1,0:T(8,128)(2,1)}, u32[]{:S(2)}, u32[]{:S(2)}) collective-permute-start(bf16[640,1280]{1,0:T(8,128)(2,1)} %bitcast.163), channel_id=1, source_target_pairs={{0,4},{4,0},{8,12},{12,8},{1,5},{5,1},{9,13},{13,9},{2,6},{6,2},{1... | collective-permute-start | bytes 4915208 | tf_op jit(solution)/shard_map/ppermute | solution.py:44
  273.3 31.0 %collective-permute-start.31 = (bf16[160,1280]{1,0:T(8,128)(2,1)S(1)}, bf16[160,1280]{1,0:T(8,128)(2,1)}, u32[]{:S(2)}, u32[]{:S(2)}) collective-permute-start(bf16[160,1280]{1,0:T(8,128)(2,1)S(1)} %multiply_convert_fusion.2.refs_0_), channel_id=1, source_target_pairs={{0,8},{4,12},{8,0},{12,4},{16,24},{20,28},{24,16},{28,20},{1,9},{5... | collective-permute-start | bytes 1228808 | tf_op jit(solution)/shard_map/ppermute | solution.py:92
  275.4 29.7 %collective-permute-start.32 = (bf16[160,1280]{1,0:T(8,128)(2,1)S(1)}, bf16[160,1280]{1,0:T(8,128)(2,1)S(1)}, u32[]{:S(2)}, u32[]{:S(2)}) collective-permute-start(bf16[160,1280]{1,0:T(8,128)(2,1)S(1)} %multiply_convert_fusion.2.refs_0_), channel_id=1, source_target_pairs={{0,16},{4,20},{8,24},{12,28},{16,0},{20,4},{24,8},{28,12},{1,17},{... | collective-permute-start | bytes 1228808 | tf_op jit(solution)/shard_map/ppermute | solution.py:92
  349.2 37.1 %collective-permute-start.37 = (bf16[160,1280]{1,0:T(8,128)(2,1)S(1)}, bf16[160,1280]{1,0:T(8,128)(2,1)S(1)}, u32[]{:S(2)}, u32[]{:S(2)}) collective-permute-start(bf16[160,1280]{1,0:T(8,128)(2,1)S(1)} %get-tuple-element.324.refs_0_), channel_id=1, source_target_pairs={{0,8},{4,12},{8,0},{12,4},{16,24},{20,28},{24,16},{28,20},{1,9},{5... | collective-permute-start | bytes 1228808 | tf_op jit(solution)/shard_map/ppermute | solution.py:92
  350.0 36.7 %collective-permute-start.38 = (bf16[160,1280]{1,0:T(8,128)(2,1)S(1)}, bf16[160,1280]{1,0:T(8,128)(2,1)S(1)}, u32[]{:S(2)}, u32[]{:S(2)}) collective-permute-start(bf16[160,1280]{1,0:T(8,128)(2,1)S(1)} %get-tuple-element.324.refs_0_), channel_id=1, source_target_pairs={{0,16},{4,20},{8,24},{12,28},{16,0},{20,4},{24,8},{28,12},{1,17},{... | collective-permute-start | bytes 1228808 | tf_op jit(solution)/shard_map/ppermute | solution.py:92
  358.0 28.7 %collective-permute-start.39 = (bf16[160,1280]{1,0:T(8,128)(2,1)S(1)}, bf16[160,1280]{1,0:T(8,128)(2,1)S(1)}, u32[]{:S(2)}, u32[]{:S(2)}) collective-permute-start(bf16[160,1280]{1,0:T(8,128)(2,1)S(1)} %get-tuple-element.324.refs_0_), channel_id=1, source_target_pairs={{0,24},{4,28},{8,16},{12,20},{16,8},{20,12},{24,0},{28,4},{1,25},{... | collective-permute-start | bytes 1228808 | tf_op jit(solution)/shard_map/ppermute | solution.py:92
  383.1 34.8 %collective-permute-start.57 = (bf16[160,1280]{1,0:T(8,128)(2,1)}, bf16[160,1280]{1,0:T(8,128)(2,1)S(1)}, u32[]{:S(2)}, u32[]{:S(2)}) collective-permute-start(bf16[160,1280]{1,0:T(8,128)(2,1)} %get-tuple-element.182), channel_id=1, source_target_pairs={{0,24},{4,28},{8,16},{12,20},{16,8},{20,12},{24,0},{28,4},{1,25},{... | collective-permute-start | bytes 1228808 | tf_op jit(solution)/shard_map/ppermute | solution.py:92
  385.0 40.4 %collective-permute-start.56 = (bf16[160,1280]{1,0:T(8,128)(2,1)}, bf16[160,1280]{1,0:T(8,128)(2,1)S(1)}, u32[]{:S(2)}, u32[]{:S(2)}) collective-permute-start(bf16[160,1280]{1,0:T(8,128)(2,1)} %get-tuple-element.181), channel_id=1, source_target_pairs={{0,16},{4,20},{8,24},{12,28},{16,0},{20,4},{24,8},{28,12},{1,17},{... | collective-permute-start | bytes 1228808 | tf_op jit(solution)/shard_map/ppermute | solution.py:92
  386.3 39.2 %collective-permute-start.55 = (bf16[160,1280]{1,0:T(8,128)(2,1)}, bf16[160,1280]{1,0:T(8,128)(2,1)}, u32[]{:S(2)}, u32[]{:S(2)}) collective-permute-start(bf16[160,1280]{1,0:T(8,128)(2,1)} %get-tuple-element.180), channel_id=1, source_target_pairs={{0,8},{4,12},{8,0},{12,4},{16,24},{20,28},{24,16},{28,20},{1,9},{5... | collective-permute-start | bytes 1228808 | tf_op jit(solution)/shard_map/ppermute | solution.py:92
  425.5 32.1 %collective-permute-start.58 = (bf16[640,1280]{1,0:T(8,128)(2,1)S(1)}, bf16[640,1280]{1,0:T(8,128)(2,1)S(1)}, u32[]{:S(2)}, u32[]{:S(2)}) collective-permute-start(bf16[640,1280]{1,0:T(8,128)(2,1)S(1)} %slice.185), channel_id=1, source_target_pairs={{0,4},{4,0},{8,12},{12,8},{1,5},{5,1},{9,13},{13,9},{2,6},{6,2},{1... | collective-permute-start | bytes 4915208 | tf_op jit(solution)/shard_map/ppermute | solution.py:44
  425.5 33.6 %collective-permute-start.59 = (bf16[640,1280]{1,0:T(8,128)(2,1)}, bf16[640,1280]{1,0:T(8,128)(2,1)}, u32[]{:S(2)}, u32[]{:S(2)}) collective-permute-start(bf16[640,1280]{1,0:T(8,128)(2,1)} %slice.187), channel_id=1, source_target_pairs={{0,4},{4,0},{8,12},{12,8},{1,5},{5,1},{9,13},{13,9},{2,6},{6,2},{1... | collective-permute-start | bytes 4915208 | tf_op jit(solution)/shard_map/ppermute | solution.py:44
  474.3 284.0 %reduce-scatter.6.cloned.1.call-start = ((), (), s32[]{:S(2)}) async-start(), calls=%async_computation.7 | async-start | bytes 2048000 | tf_op jit(solution)/shard_map/reduce_scatter | solution.py:158
  474.4 37.5 %collective-permute-start.44 = (bf16[160,1280]{1,0:T(8,128)(2,1)S(1)}, bf16[160,1280]{1,0:T(8,128)(2,1)S(1)}, u32[]{:S(2)}, u32[]{:S(2)}) collective-permute-start(bf16[160,1280]{1,0:T(8,128)(2,1)S(1)} %copy-done.69), channel_id=1, source_target_pairs={{0,2},{1,3},{2,0},{3,1},{4,6},{5,7},{6,4},{7,5},{8,10},{9,11},{10,... | collective-permute-start | bytes 1228808 | tf_op jit(solution)/shard_map/ppermute | solution.py:44
  476.1 284.2 %reduce-scatter.4.cloned.1.call-start = ((), (), s32[]{:S(2)}) async-start(), calls=%async_computation.6 | async-start | bytes 2048000 | tf_op jit(solution)/shard_map/reduce_scatter | solution.py:158
  476.1 35.7 %collective-permute-start.43 = (bf16[160,1280]{1,0:T(8,128)(2,1)S(1)}, bf16[160,1280]{1,0:T(8,128)(2,1)S(1)}, u32[]{:S(2)}, u32[]{:S(2)}) collective-permute-start(bf16[160,1280]{1,0:T(8,128)(2,1)S(1)} %copy-done.69), channel_id=1, source_target_pairs={{0,1},{1,0},{2,3},{3,2},{4,5},{5,4},{6,7},{7,6},{8,9},{9,8},{10,11... | collective-permute-start | bytes 1228808 | tf_op jit(solution)/shard_map/ppermute | solution.py:44
  570.6 40.6 %collective-permute-start.47 = (bf16[640,640]{1,0:T(8,128)(2,1)}, bf16[640,640]{1,0:T(8,128)(2,1)S(1)}, u32[]{:S(2)}, u32[]{:S(2)}) collective-permute-start(bf16[640,640]{1,0:T(8,128)(2,1)} %get-tuple-element.171), channel_id=1, source_target_pairs={{0,4},{4,0},{8,12},{12,8},{1,5},{5,1},{9,13},{13,9},{2,6},{6,2},{1... | collective-permute-start | bytes 2457608 | tf_op jit(solution)/shard_map/ppermute | solution.py:44
  571.6 44.6 %collective-permute-start.83 = (f32[2,4,160]{2,1,0:T(4,128)S(1)}, f32[2,4,160]{2,1,0:T(4,128)S(1)}, u32[]{:S(2)}, u32[]{:S(2)}) collective-permute-start(f32[2,4,160]{2,1,0:T(4,128)S(1)} %slice_bitcast_fusion.3), channel_id=1, source_target_pairs={{0,4},{4,0},{8,12},{12,8},{1,5},{5,1},{9,13},{13,9},{2,6},{6,2},{1... | collective-permute-start | bytes 15368 | tf_op jit(solution)/shard_map/ppermute | solution.py:44
  572.1 68.1 %collective-permute-start.46 = (bf16[640,640]{1,0:T(8,128)(2,1)}, bf16[640,640]{1,0:T(8,128)(2,1)}, u32[]{:S(2)}, u32[]{:S(2)}) collective-permute-start(bf16[640,640]{1,0:T(8,128)(2,1)} %get-tuple-element.169), channel_id=1, source_target_pairs={{0,4},{4,0},{8,12},{12,8},{1,5},{5,1},{9,13},{13,9},{2,6},{6,2},{1... | collective-permute-start | bytes 2457608 | tf_op jit(solution)/shard_map/ppermute | solution.py:44
  610.8 25.3 %collective-permute-start.65 = (bf16[640,640]{1,0:T(8,128)(2,1)}, bf16[640,640]{1,0:T(8,128)(2,1)}, u32[]{:S(2)}, u32[]{:S(2)}) collective-permute-start(bf16[640,640]{1,0:T(8,128)(2,1)} %get-tuple-element.203), channel_id=1, source_target_pairs={{0,4},{4,0},{8,12},{12,8},{1,5},{5,1},{9,13},{13,9},{2,6},{6,2},{1... | collective-permute-start | bytes 2457608 | tf_op jit(solution)/shard_map/ppermute | solution.py:44
  614.5 25.7 %collective-permute-start.48 = (bf16[640,640]{1,0:T(8,128)(2,1)}, bf16[640,640]{1,0:T(8,128)(2,1)}, u32[]{:S(2)}, u32[]{:S(2)}) collective-permute-start(bf16[640,640]{1,0:T(8,128)(2,1)} %add_convert_fusion.4), channel_id=1, source_target_pairs={{0,8},{4,12},{8,0},{12,4},{1,9},{5,13},{9,1},{13,5},{2,10},{6,14},... | collective-permute-start | bytes 2457608 | tf_op jit(solution)/shard_map/ppermute | solution.py:44
  635.7 28.1 %collective-permute-start.78 = (f32[2560]{0:T(1024)S(1)}, f32[2560]{0:T(1024)S(1)}, u32[]{:S(2)}, u32[]{:S(2)}) collective-permute-start(f32[2560]{0:T(1024)S(1)} %add.520), channel_id=1, source_target_pairs={{0,1},{1,0},{2,3},{3,2},{4,5},{5,4},{6,7},{7,6},{8,9},{9,8},{10,11... | collective-permute-start | bytes 30728 | tf_op jit(solution)/shard_map/ppermute | solution.py:44
  636.1 41.7 %collective-permute-start.64 = (bf16[640,640]{1,0:T(8,128)(2,1)}, bf16[640,640]{1,0:T(8,128)(2,1)}, u32[]{:S(2)}, u32[]{:S(2)}) collective-permute-start(bf16[640,640]{1,0:T(8,128)(2,1)} %get-tuple-element.201), channel_id=1, source_target_pairs={{0,4},{4,0},{8,12},{12,8},{1,5},{5,1},{9,13},{13,9},{2,6},{6,2},{1... | collective-permute-start | bytes 2457608 | tf_op jit(solution)/shard_map/ppermute | solution.py:44
  638.6 39.2 %collective-permute-start.66 = (bf16[640,640]{1,0:T(8,128)(2,1)}, bf16[640,640]{1,0:T(8,128)(2,1)}, u32[]{:S(2)}, u32[]{:S(2)}) collective-permute-start(bf16[640,640]{1,0:T(8,128)(2,1)} %add_convert_fusion.3), channel_id=1, source_target_pairs={{0,8},{4,12},{8,0},{12,4},{1,9},{5,13},{9,1},{13,5},{2,10},{6,14},... | collective-permute-start | bytes 2457608 | tf_op jit(solution)/shard_map/ppermute | solution.py:44
  663.7 64.1 %collective-permute-start.79 = (f32[2560]{0:T(1024)S(1)}, f32[2560]{0:T(1024)S(1)}, u32[]{:S(2)}, u32[]{:S(2)}) collective-permute-start(f32[2560]{0:T(1024)S(1)} %add.521), channel_id=1, source_target_pairs={{0,2},{1,3},{2,0},{3,1},{4,6},{5,7},{6,4},{7,5},{8,10},{9,11},{10,... | collective-permute-start | bytes 30728 | tf_op jit(solution)/shard_map/ppermute | solution.py:44
  671.9 61.2 %collective-permute-start.49 = (bf16[160,1280]{1,0:T(8,128)(2,1)}, bf16[160,1280]{1,0:T(8,128)(2,1)}, u32[]{:S(2)}, u32[]{:S(2)}) collective-permute-start(bf16[160,1280]{1,0:T(8,128)(2,1)} %copy-done.41), channel_id=1, source_target_pairs={{0,1},{1,0},{2,3},{3,2},{4,5},{5,4},{6,7},{7,6},{8,9},{9,8},{10,11... | collective-permute-start | bytes 1228808 | tf_op jit(solution)/shard_map/ppermute | solution.py:44
  675.9 57.2 %collective-permute-start.51 = (bf16[160,1280]{1,0:T(8,128)(2,1)}, bf16[160,1280]{1,0:T(8,128)(2,1)}, u32[]{:S(2)}, u32[]{:S(2)}) collective-permute-start(bf16[160,1280]{1,0:T(8,128)(2,1)} %add_convert_fusion.6), channel_id=1, source_target_pairs={{0,2},{1,3},{2,0},{3,1},{4,6},{5,7},{6,4},{7,5},{8,10},{9,11},{10,... | collective-permute-start | bytes 1228808 | tf_op jit(solution)/shard_map/ppermute | solution.py:44
  699.6 27.6 %collective-permute-start.68 = (bf16[160,1280]{1,0:T(8,128)(2,1)}, bf16[160,1280]{1,0:T(8,128)(2,1)S(1)}, u32[]{:S(2)}, u32[]{:S(2)}) collective-permute-start(bf16[160,1280]{1,0:T(8,128)(2,1)} %get-tuple-element.208), channel_id=1, source_target_pairs={{0,1},{1,0},{2,3},{3,2},{4,5},{5,4},{6,7},{7,6},{8,9},{9,8},{10,11... | collective-permute-start | bytes 1228808 | tf_op jit(solution)/shard_map/ppermute | solution.py:44
  713.5 37.9 %collective-permute-start.70 = (bf16[2,2,160,1280]{3,2,1,0:T(8,128)(2,1)S(1)}, bf16[2,2,160,1280]{3,2,1,0:T(8,128)(2,1)S(1)}, u32[]{:S(2)}, u32[]{:S(2)}) collective-permute-start(bf16[2,2,160,1280]{3,2,1,0:T(8,128)(2,1)S(1)} %fusion.27), channel_id=1, source_target_pairs={{0,4},{4,0},{8,12},{12,8},{1,5},{5,1},{9,13},{13,9},{2,6},{6,2},{1... | collective-permute-start | bytes 4915208 | tf_op jit(solution)/shard_map/ppermute | solution.py:44
  763.9 34.0 %all-to-all-start.1 = ((bf16[8,3,160,160]{3,2,1,0:T(8,128)(2,1)}), bf16[8,3,160,160]{3,2,1,0:T(8,128)(2,1)S(1)}, u32[]{:S(2)}, u32[]{:S(2)}) async-start(bf16[8,3,160,160]{3,2,1,0:T(8,128)(2,1)} %pad_maximum_fusion.1), calls=%async_computation.4 | async-start | bytes 3932160 | tf_op jit(solution)/shard_map/all_to_all | solution.py:161
  768.8 27.3 %collective-permute-start.72 = (bf16[160,640]{1,0:T(8,128)(2,1)S(1)}, bf16[160,640]{1,0:T(8,128)(2,1)S(1)}, u32[]{:S(2)}, u32[]{:S(2)}) collective-permute-start(bf16[160,640]{1,0:T(8,128)(2,1)S(1)} %dynamic-slice_bitcast_fusion.3), channel_id=1, source_target_pairs={{0,16},{16,0},{1,17},{17,1},{2,18},{18,2},{3,19},{19,3},{4,20},{20... | collective-permute-start | bytes 614408 | tf_op jit(solution)/shard_map/ppermute | solution.py:44
  (152 other events, 1976.5 us)
Sparse Core Ops, SparseCore 0:
  10.5 47.6 all-gather.7
  78.4 40.6 all-gather.9
  120.6 37.0 all-gather.11
  159.1 49.2 all-gather.13
  474.4 55.2 reduce-scatter.7
  532.0 37.4 reduce-scatter.5
  672.0 56.0 reduce-scatter.3

commit v9 on v8

--- a/solution.py
+++ b/solution.py
@@ -42,6 +42,12 @@
 def swap(value, axis, bit):
     size = lax.axis_size(axis)
     return lax.ppermute(value, axis, [(place, place ^ bit) for place in range(size)])
+
+
+def after(value, *others):
+    for other in others:
+        value = value + (other[(slice(0, 1),) * other.ndim].reshape(()) * 0).astype(value.dtype)
+    return value
 
 
 def add_low(former, latter):
@@ -74,10 +80,7 @@
 def group_scatter(pieces, axis):
     if lax.axis_size(axis) != 4:
         return [lax.psum_scatter(pieces[0], axis, scatter_dimension=0, tiled=True)]
-    own, beside, across, far = pieces
-    far = swap(far, axis, 1)
-    beside = swap(beside, axis, 1)
-    return [own, beside, swap(add_low(across, far), axis, 2)]
+    return [pieces[0]] + [swap(piece, axis, bits) for piece, bits in zip(pieces[1:], (1, 2, 3))]
 
 
 def total_wide(parts):
@@ -149,61 +152,49 @@
     return [add_low(product[:half], swap(product[half:], "ctx", 1)) for product in products]
 
 
-def hidden_weight_grads(lines):
+def hidden_line_sums(lines):
     if not in_plane():
-        return [
-            lax.psum_scatter(line, SPREAD, scatter_dimension=1, tiled=True).astype(jnp.float32)
-            for line in lines
-        ]
-    sums = [lax.psum_scatter(line, "tp", scatter_dimension=0, tiled=True) for line in lines]
+        return lines
+    return [lax.psum_scatter(line, "tp", scatter_dimension=0, tiled=True) for line in lines]
+
+
+def hidden_spread(sums):
+    if not in_plane():
+        return jnp.stack(
+            [lax.psum_scatter(total, SPREAD, scatter_dimension=1, tiled=True) for total in sums]
+        )
     part, width = sums[0].shape
     packed = jnp.stack([total.reshape(part, 8, width // 8).transpose(1, 0, 2) for total in sums], 1)
-    packed = lax.all_to_all(packed, SPREAD, 0, 0).astype(jnp.float32)
-    return [packed[:, place].reshape(8 * part, width // 8) for place in range(3)]
-
-
-def hidden_scale_grads(sums):
+    return lax.all_to_all(packed, SPREAD, 0, 0)
+
+
+def hidden_weight_grads(spread_sums):
+    wide = spread_sums.astype(jnp.float32)
     if not in_plane():
-        return butterfly(sums, SPREAD)
-    count, hidden = sums.shape
-    parts = sums.reshape(count, 2, 4, hidden // 8)
-    line = butterfly(parts[:, 0] + swap(parts[:, 1], "ctx", 1), ("tp",))
-    line = lax.dynamic_index_in_dim(line, lax.axis_index("tp"), 1, keepdims=False)
+        return [wide[place] for place in range(3)]
+    return [wide[:, place].reshape(-1, wide.shape[-1]) for place in range(3)]
+
+
+def vector_sums(alphas, hidden_sums):
+    count, hidden = hidden_sums.shape
+    if not in_plane():
+        return jnp.concatenate([butterfly(alphas, ("tp",)), hidden_sums.reshape(-1)])
+    parts = hidden_sums.reshape(count, 2, 4, hidden // 8)
+    line = (parts[:, 0] + swap(parts[:, 1], "ctx", 1)).reshape(-1)
+    width = alphas.shape[0]
+    both = butterfly(jnp.concatenate([alphas, line]), ("tp",))
+    line = both[width:].reshape(count, 4, hidden // 8)
+    line = lax.dynamic_index_in_dim(line, lax.axis_index("tp"), 1, keepdims=True)
     blank = jnp.zeros((count, 8, hidden // 8), jnp.float32)
-    place = lax.axis_index(SPREAD)
-    spread_out = lax.dynamic_update_slice_in_dim(blank, line[:, None], place, 1)
-    return butterfly(spread_out, SPREAD).reshape(count, hidden)
+    placed = lax.dynamic_update_slice_in_dim(blank, line, lax.axis_index(SPREAD), 1)
+    return jnp.concatenate([both[:width], placed.reshape(-1)])
 
 
 def owner_scatter(product_low):
-    if lax.axis_size("ctx") != 4 or lax.axis_size("shard") != 2:
-        return lax.psum_scatter(
-            product_low, ("shard", "ctx"), scatter_dimension=0, tiled=True
-        ).astype(jnp.float32)
-    place = lax.axis_index("ctx")
-    core, along = place % 2, place // 2
-    plane = lax.axis_index("shard")
+    count = lax.axis_size(SPREAD)
     rows, width = product_low.shape
-    blocks = product_low.reshape(2, 2, 2, rows // 8, width)
-
-    def pick(value, index, axis):
-        return lax.dynamic_index_in_dim(value, index, axis, keepdims=False)
-
-    blocks = add_low(pick(blocks, core, 2), swap(pick(blocks, 1 - core, 2), "ctx", 1))
-    former, latter = blocks[..., : width // 2], blocks[..., width // 2 :]
-    former_in = swap(pick(former, 1 - along, 1), "ctx", 2)
-    latter_in = swap(pick(latter, 1 - plane, 0), "shard", 1)
-    former = add_low(pick(former, along, 1), former_in)
-    latter = add_low(pick(latter, plane, 0), latter_in)
-    former_in = swap(pick(former, 1 - plane, 0), "shard", 1)
-    latter_in = swap(pick(latter, 1 - along, 0), "ctx", 2)
-    return jnp.concatenate(
-        [
-            pick(former, plane, 0).astype(jnp.float32) + former_in.astype(jnp.float32),
-            pick(latter, along, 0).astype(jnp.float32) + latter_in.astype(jnp.float32),
-        ],
-        axis=1,
-    )
+    blocks = lax.all_to_all(product_low.reshape(count, rows // count, width), SPREAD, 0, 0)
+    return jnp.sum(blocks.astype(jnp.float32), axis=0)
 
 
 def row_labels(slots, group_size):
@@ -244,6 +235,10 @@
 def row_blocks(ref, count):
     rows = ref.shape[0] // count
     return [ref.at[pl.ds(place * rows, rows)] for place in range(count)]
+
+
+def core_time(micros):
+    return pl.CostEstimate(flops=int(micros * 1.15e9), transcendentals=0, bytes_accessed=1 << 20)
 
 
 ANYWHERE = pl.BlockSpec(memory_space=pl.ANY)
@@ -348,6 +343,7 @@
             pltpu.SemaphoreType.DMA((count,)),
         ],
         compiler_params=pltpu.CompilerParams(vmem_limit_bytes=48 << 20),
+        cost_estimate=core_time(23),
         name="attend",
     )(query, *pieces, hot, side, weight)
 
@@ -461,6 +457,7 @@
             pltpu.SemaphoreType.DMA,
         ],
         compiler_params=pltpu.CompilerParams(vmem_limit_bytes=56 << 20),
+        cost_estimate=core_time(38),
         name="attend_grad",
     )(query, outs, *pieces, *tops, hot, side, scale, weight)
 
@@ -553,6 +550,7 @@
             pltpu.SemaphoreType.DMA,
         ],
         compiler_params=pltpu.CompilerParams(vmem_limit_bytes=40 << 20),
+        cost_estimate=core_time(9),
         name="project",
     )(*pieces, weight, scale)
 
@@ -608,6 +606,7 @@
         ]
         + [jax.ShapeDtypeStruct((rows // count_out, width), jnp.bfloat16)] * count_out,
         compiler_params=pltpu.CompilerParams(vmem_limit_bytes=40 << 20),
+        cost_estimate=core_time(14),
         name="project_grad",
     )(query_grad, *tree_parts, raw, weight, scale)
 
@@ -677,6 +676,7 @@
             pltpu.SemaphoreType.DMA,
         ],
         compiler_params=pltpu.CompilerParams(vmem_limit_bytes=52 << 20),
+        cost_estimate=core_time(16),
         name="hidden",
     )(*pieces, *[matrix for parts in weights for matrix in parts], jnp.stack(scales))
 
@@ -747,6 +747,7 @@
             pltpu.SemaphoreType.DMA,
         ],
         compiler_params=pltpu.CompilerParams(vmem_limit_bytes=56 << 20),
+        cost_estimate=core_time(19),
         name="hidden_grad",
     )(*pieces, *[matrix for parts in weights for matrix in parts], jnp.stack(scales), up, gate)
 
@@ -843,12 +844,14 @@
         axis=0,
         tiled=True,
     )
-    shards, groups = lax.optimization_barrier((hidden_shards(w_up, w_gate, w_down), groups))
-    weights = hidden_weights(shards)
     scales = hidden_scales(scale_up, scale_gate)
     scale_both = jnp.concatenate([scale_qk, scale_qk])[None]
+    first = groups[0][-1]
+    shards = hidden_shards(after(w_up, first), after(w_gate, first), after(w_down, first))
+    weights = hidden_weights(shards)
+    scale_early = after(scale_both, *scales)
     front = [
-        forward_attention(packed, scale_both, groups[m], parents[m, 0], slot_segment[m, 0])
+        forward_attention(packed, scale_early, groups[m], parents[m, 0], slot_segment[m, 0])
         for m in micros
     ]
     mid = [
@@ -863,21 +866,26 @@
             for place in range(3)
         ]
     )
-    tops = [mid[m][2] for m in micros]
-    lines, tops[-1] = lax.optimization_barrier((lines, tops[-1]))
-    grad_u, grad_g, grad_d = hidden_weight_grads(lines)
+    vectors = vector_sums(
+        sum(mid[m][4][0] for m in micros), sum(mid[m][4][1] for m in micros)
+    )
+    line_sums = hidden_line_sums(lines)
+    spread_sums = hidden_spread(line_sums)
+    waits = [after(scale_both, *line_sums), after(scale_both, spread_sums)]
     back = [
-        backward_attention(packed, scale_both, front[m][1], tops[m], mid[m][1]) for m in micros
+        backward_attention(packed, waits[min(m, 1)], front[m][1], mid[m][2], mid[m][1])
+        for m in micros
     ]
+    grad_u, grad_g, grad_d = hidden_weight_grads(spread_sums)
     grad_attention = owner_scatter(
         jnp.concatenate(
             [joint_product([back[m][1][place] for m in micros]) for place in range(2)], axis=1
         ).astype(jnp.bfloat16)
     )
     grad_q, grad_k, grad_v, grad_o = jnp.split(grad_attention, 4, axis=1)
-    sum_qk = butterfly(sum(back[m][2] for m in micros), SPREAD)
-    alphas = butterfly(sum(mid[m][4][0] for m in micros), SPREAD + ("tp",))
-    sum_up, sum_gate = hidden_scale_grads(sum(mid[m][4][1] for m in micros))
+    sums = butterfly(jnp.concatenate([vectors, sum(back[m][2] for m in micros)]), SPREAD)
+    sum_alphas, sum_hidden, sum_qk = jnp.split(sums, [2 * width, sums.shape[0] - scale_qk.shape[0]])
+    sum_up, sum_gate = jnp.split(sum_hidden, 2)
     return (
         jnp.stack([mid[m][0] for m in micros])[:, None],
         jnp.stack([back[m][0] for m in micros])[:, None],
@@ -888,8 +896,8 @@
         grad_u.T,
         grad_g.T,
         grad_d,
-        alphas[:width],
-        alphas[width:],
+        sum_alphas[:width],
+        sum_alphas[width:],
         sum_qk,
         sum_up,
         sum_gate,

time: 821 us -> 877 us (1.068)
  starting transfers between devices: 104 us -> 121 us
  local copies, waits for them, and re-layouts: 78.8 us -> 94.8 us
  waiting for transfers between devices: 287 us -> 303 us
    ppermute x65 -> x52, waiting for transfers between devices: 254 us -> 223 us  [swap(): lax.ppermute(value, axis, [(place, place ^ bit) for place in range(size)])]
    all_to_all x1, waiting for transfers between devices: 0.01 us -> 24.2 us  [hidden_shards(): packed = lax.all_to_all(packed, SPREAD, 0, 0)]
    ppermute x24, waiting for transfers between devices: 32.2 us -> 56.1 us  [hop(): lax.ppermute(value, SPREAD, [(place, place ^ bits) for place in range(8)])]
    convert_element_type x12 -> x3, other arithmetic: 19.1 us -> 8.18 us  [add_low(): (former.astype(jnp.float32) + latter.astype(jnp.float32)).astype(jnp.bflo...]
    ppermute x65 -> x52, starting transfers between devices: 64.2 us -> 74.8 us  [swap(): lax.ppermute(value, axis, [(place, place ^ bit) for place in range(size)])]
    unnamed x209 -> x188, local copies, waits for them, and re-layouts: 37.9 us -> 37.4 us
  transfers between devices with their start and end apart: 98 -> 86, of which waited for: 32 -> 32; matrix products, arithmetic and copies ran while one was open for 14% -> 13% of each run, Pallas kernels for 30% -> 24%
where the time goes in v9:
time: 877 us; the launch traced here: 863 us
  waiting for transfers between devices  303 us (35%)
  Pallas kernels  239 us (27%)
  starting transfers between devices  121 us (14%)
  local copies, waits for them, and re-layouts  94.8 us (11%)
  other arithmetic  52.8 us (6%)
  matrix products  32 us (4%)
  between operations  20.4 us (2%)
    ppermute x52, waiting for transfers between devices, swap(): lax.ppermute(value, axis, [(place, place ^ bit) for place in range(size)])  223 us
    pallas_call x2, Pallas kernels, attend_grad(): pl.pallas_call(lambda *refs: attend_grad_body(count, len(tops), *refs), g...  77.1 us
    ppermute x52, starting transfers between devices, swap(): lax.ppermute(value, axis, [(place, place ^ bit) for place in range(size)])  74.8 us
    ppermute x24, waiting for transfers between devices, hop(): lax.ppermute(value, SPREAD, [(place, place ^ bits) for place in range(8)])  56.1 us
    pallas_call x2, Pallas kernels, attend(): pl.pallas_call(lambda *refs: attend_body(count, *refs), grid=(keys // KEY...  45.8 us
    pallas_call x2, Pallas kernels, hidden_backward(): pl.pallas_call(lambda *refs: hidden_grad_body(count, halves, *refs), in_s...  39.3 us
    unnamed x188, local copies, waits for them, and re-layouts  37.4 us
    ppermute x24, starting transfers between devices, hop(): lax.ppermute(value, SPREAD, [(place, place ^ bits) for place in range(8)])  31.7 us
  transfers between devices with their start and end apart: 86, of which 32 were waited for; matrix products, arithmetic and copies ran while one was open for 13% of the time, Pallas kernels for 24%

profile of v9, /device:TPU:0, one launch (start us, length us, event | category | flops | bytes accessed | tf_op | source)
XLA Modules:
  0.0 863.0 jit_solution(4696091081118447682)
XLA Ops:
  10.9 4.1 collective-permute-start.4
  22.7 17.1 %collective-permute-done.1.refs_2_ = bf16[160,1280]{1,0:T(8,128)(2,1)S(1)} collective-permute-done((bf16[160,1280]{1,0:T(8,128)(2,1)S(1)}, bf16[160,1280]{1,0:T(8,128)(2,1)S(1)}, u32[]{:S(2)}, u32[]{:S(2)}) %collective-permute-start.1) | collective-permute-done | bytes 409632 | tf_op jit(solution)/shard_map/ppermute | solution.py:44
  40.0 19.6 %collective-permute-done.2.refs_3_ = bf16[160,1280]{1,0:T(8,128)(2,1)S(1)} collective-permute-done((bf16[160,1280]{1,0:T(8,128)(2,1)S(1)}, bf16[160,1280]{1,0:T(8,128)(2,1)S(1)}, u32[]{:S(2)}, u32[]{:S(2)}) %collective-permute-start.2) | collective-permute-done | bytes 409632 | tf_op jit(solution)/shard_map/ppermute | solution.py:44
  69.5 4.3 all-to-all-start
  74.9 24.2 %all-to-all-done = bf16[8,3,160,160]{3,2,1,0:T(8,128)(2,1)} async-done(((bf16[8,3,160,160]{3,2,1,0:T(8,128)(2,1)}), bf16[8,3,160,160]{3,2,1,0:T(8,128)(2,1)}, u32[]{:S(2)}, u32[]{:S(2)}) %all-to-all-start) | async-done | bytes 1228832 | tf_op jit(solution)/shard_map/all_to_all | solution.py:123
  126.7 8.4 project.2
  138.1 9.6 %collective-permute-done.24.refs_3_ = bf16[160,1280]{1,0:T(8,128)(2,1)} collective-permute-done((bf16[160,1280]{1,0:T(8,128)(2,1)S(1)}, bf16[160,1280]{1,0:T(8,128)(2,1)}, u32[]{:S(2)}, u32[]{:S(2)}) %collective-permute-start.24) | collective-permute-done | bytes 409632 | tf_op jit(solution)/shard_map/ppermute | solution.py:44
  147.7 9.8 %project.3 = (bf16[640,320]{1,0:T(8,128)(2,1)S(1)}, bf16[640,640]{1,0:T(8,128)(2,1)}, f32[640,640]{1,0:T(8,128)S(1)}, bf16[640,1280]{1,0:T(8,128)(2,1)S(1)}) custom-call(bf16[160,1280]{1,0:T(8,128)(2,1)S(1)} %get-tuple-element.304.refs_0_, bf16[160,1280]{1,0:T(8,128)(2,1)} %collective-permute-done.22.refs_1_, ...), custom_call_target="tpu_custom_call" | custom-call | flops 10350000128 | bytes 1048576 | tf_op jit(solution)/shard_map/project/pallas_call | solution.py:532
  169.6 11.7 %collective-permute-done.26.refs_3_.refs_4_ = bf16[640,640]{1,0:T(8,128)(2,1)} collective-permute-done((bf16[640,640]{1,0:T(8,128)(2,1)}, bf16[640,640]{1,0:T(8,128)(2,1)}, u32[]{:S(2)}, u32[]{:S(2)}) %collective-permute-start.26) | collective-permute-done | bytes 819232 | tf_op jit(solution)/shard_map/ppermute | solution.py:44
  182.3 23.2 %attend.2 = (bf16[640,320]{1,0:T(8,128)(2,1)S(1)}, f32[8,640]{1,0:T(8,128)S(1)}, bf16[160,1280]{1,0:T(8,128)(2,1)S(1)}, bf16[160,1280]{1,0:T(8,128)(2,1)S(1)}, b...) custom-call(bf16[640,320]{1,0:T(8,128)(2,1)S(1)} %copy-done.33, ...), custom_call_target="tpu_custom_call" | custom-call | flops 26449999872 | bytes 1048576 | tf_op jit(solution)/shard_map/attend/pallas_call | solution.py:319
  212.3 22.6 %attend.3 = (bf16[640,320]{1,0:T(8,128)(2,1)S(1)}, f32[8,640]{1,0:T(8,128)S(1)}, bf16[160,1280]{1,0:T(8,128)(2,1)S(1)}, bf16[160,1280]{1,0:T(8,128)(2,1)S(1)}, b...) custom-call(bf16[640,320]{1,0:T(8,128)(2,1)S(1)} %copy-done.35, ...), custom_call_target="tpu_custom_call" | custom-call | flops 26449999872 | bytes 1048576 | tf_op jit(solution)/shard_map/attend/pallas_call | solution.py:319
  239.9 4.4 collective-permute-done.10
  244.3 11.2 %collective-permute-start.30 = (bf16[160,1280]{1,0:T(8,128)(2,1)S(1)}, bf16[160,1280]{1,0:T(8,128)(2,1)}, u32[]{:S(2)}, u32[]{:S(2)}) collective-permute-start(bf16[160,1280]{1,0:T(8,128)(2,1)S(1)} %get-tuple-element.129), channel_id=1, source_target_pairs={{0,3},{1,2},{2,1},{3,0},{4,7},{5,6},{6,5},{7,4},{8,11},{9,10},{10,... | collective-permute-start | bytes 1228808 | tf_op jit(solution)/shard_map/ppermute | solution.py:44
  262.0 27.5 %collective-permute-done.29 = bf16[160,1280]{1,0:T(8,128)(2,1)S(1)} collective-permute-done((bf16[160,1280]{1,0:T(8,128)(2,1)S(1)}, bf16[160,1280]{1,0:T(8,128)(2,1)S(1)}, u32[]{:S(2)}, u32[]{:S(2)}) %collective-permute-start.29) | collective-permute-done | bytes 409632 | tf_op jit(solution)/shard_map/ppermute | solution.py:44
  299.5 5.6 collective-permute-done.13.refs_1_
  307.6 7.9 collective-permute-done.14.refs_2_
  316.9 15.7 %hidden.2 = (bf16[160,1280]{1,0:T(8,128)(2,1)S(1)}, bf16[160,1280]{1,0:T(8,128)(2,1)S(1)}, bf16[160,1280]{1,0:T(8,128)(2,1)S(1)}, bf16[160,1280]{1,0:T(8,128)(2,...) custom-call(bf16[160,1280]{1,0:T(8,128)(2,1)} %copy-done.61, ...), custom_call_target="tpu_custom_call" | custom-call | flops 18400000000 | bytes 1048576 | tf_op jit(solution)/shard_map/hidden/pallas_call | solution.py:665
  337.7 15.9 %hidden.3 = (bf16[160,1280]{1,0:T(8,128)(2,1)S(1)}, bf16[160,1280]{1,0:T(8,128)(2,1)S(1)}, bf16[160,1280]{1,0:T(8,128)(2,1)S(1)}, bf16[160,1280]{1,0:T(8,128)(2,...) custom-call(bf16[160,1280]{1,0:T(8,128)(2,1)} %copy-done.60, ...), custom_call_target="tpu_custom_call" | custom-call | flops 18400000000 | bytes 1048576 | tf_op jit(solution)/shard_map/hidden/pallas_call | solution.py:665
  357.5 7.7 collective-permute-done.34
  365.2 5.6 collective-permute-done.35
  382.5 4.3 collective-permute-done.37.refs_1_
  388.9 7.2 collective-permute-done.38.refs_2_
  396.9 19.8 %hidden_grad.2 = (bf16[160,1280]{1,0:T(8,128)(2,1)}, bf16[160,1280]{1,0:T(8,128)(2,1)}, bf16[160,1280]{1,0:T(8,128)(2,1)}, bf16[160,1280]{1,0:T(8,128)(2,1)}, bf...) custom-call(bf16[160,1280]{1,0:T(8,128)(2,1)} %copy-done.63, ...), custom_call_target="tpu_custom_call" | custom-call | flops 21849999360 | bytes 1048576 | tf_op jit(solution)/shard_map/hidden_grad/pallas_call | solution.py:736
  417.8 19.5 %hidden_grad.3 = (bf16[160,1280]{1,0:T(8,128)(2,1)}, bf16[160,1280]{1,0:T(8,128)(2,1)}, bf16[160,1280]{1,0:T(8,128)(2,1)}, bf16[160,1280]{1,0:T(8,128)(2,1)}, bf...) custom-call(bf16[160,1280]{1,0:T(8,128)(2,1)} %copy-done.62, ...), custom_call_target="tpu_custom_call" | custom-call | flops 21849999360 | bytes 1048576 | tf_op jit(solution)/shard_map/hidden_grad/pallas_call | solution.py:736
  437.3 6.6 convolution_convert_fusion.2
  449.4 7.4 convolution_convert_fusion.1
  465.9 7.4 convolution_convert_fusion
  482.9 7.2 collective-permute-done.58
  490.1 7.9 collective-permute-done.59
  500.0 4.5 multiply_reduce_fusion.5
  506.8 9.4 %collective-permute-start.62 = (bf16[160,1280]{1,0:T(8,128)(2,1)S(1)}, bf16[160,1280]{1,0:T(8,128)(2,1)S(1)}, u32[]{:S(2)}, u32[]{:S(2)}) collective-permute-start(bf16[160,1280]{1,0:T(8,128)(2,1)S(1)} %get-tuple-element.320.refs_6_), channel_id=1, source_target_pairs={{0,2},{1,3},{2,0},{3,1},{4,6},{5,7},{6,4},{7,5},{8,10},{9,11},{10,... | collective-permute-start | bytes 1228808 | tf_op jit(solution)/shard_map/ppermute | solution.py:44
  520.7 35.0 %collective-permute-done.62.refs_8_ = bf16[160,1280]{1,0:T(8,128)(2,1)S(1)} collective-permute-done((bf16[160,1280]{1,0:T(8,128)(2,1)S(1)}, bf16[160,1280]{1,0:T(8,128)(2,1)S(1)}, u32[]{:S(2)}, u32[]{:S(2)}) %collective-permute-start.62) | collective-permute-done | bytes 409632 | tf_op jit(solution)/shard_map/ppermute | solution.py:44
  555.7 8.8 %collective-permute-done.44.refs_8_ = bf16[160,1280]{1,0:T(8,128)(2,1)} collective-permute-done((bf16[160,1280]{1,0:T(8,128)(2,1)}, bf16[160,1280]{1,0:T(8,128)(2,1)}, u32[]{:S(2)}, u32[]{:S(2)}) %collective-permute-start.44) | collective-permute-done | bytes 409632 | tf_op jit(solution)/shard_map/ppermute | solution.py:44
  568.1 5.1 collective-permute-done.63.refs_9_
  574.0 38.5 %attend_grad.3 = (f32[640,320]{1,0:T(8,128)}, bf16[640,640]{1,0:T(8,128)(2,1)}, bf16[640,640]{1,0:T(8,128)(2,1)}, bf16[640,640]{1,0:T(8,128)(2,1)}, bf16[640,640]{1,0:T(8,128)(2,1)}, /*index=5*/bf16[640,1280]{1,0:T(8,128)(2,1)}) custom-call(bf16[640,320]{1,0:T(8,128)(2,1)} %copy-done.34, bf16[640,320]{1,0:T(8,128)(2,1)} %copy-done.22, ...), custom_call_target="tpu_custom_call" | custom-call | flops 43699998720 | bytes 1048576 | tf_op jit(solution)/shard_map/attend_grad/pallas_call | solution.py:432
  624.9 4.5 all-to-all-start.1
  629.5 38.6 %attend_grad.2 = (f32[640,320]{1,0:T(8,128)}, bf16[640,640]{1,0:T(8,128)(2,1)}, bf16[640,640]{1,0:T(8,128)(2,1)}, bf16[640,640]{1,0:T(8,128)(2,1)}, bf16[640,640]{1,0:T(8,128)(2,1)}, /*index=5*/bf16[640,1280]{1,0:T(8,128)(2,1)}) custom-call(bf16[640,320]{1,0:T(8,128)(2,1)} %copy-done.32, bf16[640,320]{1,0:T(8,128)(2,1)} %copy-done.20, ...), custom_call_target="tpu_custom_call" | custom-call | flops 43699998720 | bytes 1048576 | tf_op jit(solution)/shard_map/attend_grad/pallas_call | solution.py:432
  687.6 12.9 %project_grad.3 = (bf16[640,960]{1,0:T(8,128)(2,1)S(1)}, f32[4,1,640]{2,1,0:T(1,128)S(1)}, bf16[160,1280]{1,0:T(8,128)(2,1)S(1)}, bf16[160,1280]{1,0:T(8,128)(2,...) custom-call(f32[640,320]{1,0:T(8,128)S(1)} %copy-done.36, bf16[640,640]{1,0:T(8,128)(2,1)S(1)} %copy-done.38, ...), custom_call_target="tpu_custom_call" | custom-call | flops 16099999744 | bytes 1048576 | tf_op jit(solution)/shard_map/project_grad/pallas_call | solution.py:592
  702.8 4.0 collective-permute-done.48.refs_4_
  706.8 14.1 %project_grad.2 = (bf16[640,960]{1,0:T(8,128)(2,1)S(1)}, f32[4,1,640]{2,1,0:T(1,128)S(1)}, bf16[160,1280]{1,0:T(8,128)(2,1)S(1)}, bf16[160,1280]{1,0:T(8,128)(2,...) custom-call(f32[640,320]{1,0:T(8,128)S(1)} %copy-done.37, bf16[640,640]{1,0:T(8,128)(2,1)S(1)} %copy-done.39, ...), custom_call_target="tpu_custom_call" | custom-call | flops 16099999744 | bytes 1048576 | tf_op jit(solution)/shard_map/project_grad/pallas_call | solution.py:592
  721.0 5.2 convolution_convert_fusion.3
  726.2 4.5 copy.76
  730.7 4.5 pad_maximum_fusion
  735.2 4.6 all-to-all-start.2
  751.2 18.7 %collective-permute-done.73 = f32[5440]{0:T(1024)S(1)} collective-permute-done((f32[5440]{0:T(1024)S(1)}, f32[5440]{0:T(1024)S(1)}, u32[]{:S(2)}, u32[]{:S(2)}) %collective-permute-start.73) | collective-permute-done | bytes 21792 | tf_op jit(solution)/shard_map/ppermute | solution.py:44
  771.1 10.2 %collective-permute-start.75 = (f32[5440]{0:T(1024)S(1)}, f32[5440]{0:T(1024)S(1)}, u32[]{:S(2)}, u32[]{:S(2)}) collective-permute-start(f32[5440]{0:T(1024)S(1)} %add.527), channel_id=1, source_target_pairs={{0,8},{4,12},{8,0},{12,4},{1,9},{5,13},{9,1},{13,5},{2,10},{6,14},... | collective-permute-start | bytes 65288 | tf_op jit(solution)/shard_map/ppermute | solution.py:44
  804.1 10.3 %collective-permute-done.68 = bf16[160,1280]{1,0:T(8,128)(2,1)} collective-permute-done((bf16[160,1280]{1,0:T(8,128)(2,1)S(1)}, bf16[160,1280]{1,0:T(8,128)(2,1)}, u32[]{:S(2)}, u32[]{:S(2)}) %collective-permute-start.68) | collective-permute-done | bytes 409632 | tf_op jit(solution)/shard_map/ppermute | solution.py:44
  814.5 33.9 %collective-permute-done.56 = bf16[160,1280]{1,0:T(8,128)(2,1)} collective-permute-done((bf16[160,1280]{1,0:T(8,128)(2,1)S(1)}, bf16[160,1280]{1,0:T(8,128)(2,1)}, u32[]{:S(2)}, u32[]{:S(2)}) %collective-permute-start.56) | collective-permute-done | bytes 409632 | tf_op jit(solution)/shard_map/ppermute | solution.py:44
  (487 shorter events, 231.9 us)
Async XLA Ops:
  7.2 115.6 %all-gather.5.cloned.1.call-start = ((), (), s32[]{:S(2)}) async-start(), calls=%async_computation.6 | async-start | bytes 3686400 | tf_op jit(solution)/shard_map/all_gather | solution.py:841
  10.9 95.7 %collective-permute-start.4 = (f32[1,2,160]{2,1,0:T(2,128)S(1)}, f32[1,2,160]{2,1,0:T(2,128)S(1)}, u32[]{:S(2)}, u32[]{:S(2)}) collective-permute-start(f32[1,2,160]{2,1,0:T(2,128)S(1)} %maximum_bitcast_fusion.2), channel_id=1, source_target_pairs={{0,2},{1,3},{2,0},{3,1},{4,6},{5,7},{6,4},{7,5},{8,10},{9,11},{10,... | collective-permute-start | bytes 3848 | tf_op jit(solution)/shard_map/ppermute | solution.py:44
  15.0 93.6 %collective-permute-start.3 = (f32[1,2,160]{2,1,0:T(2,128)S(1)}, f32[1,2,160]{2,1,0:T(2,128)S(1)}, u32[]{:S(2)}, u32[]{:S(2)}) collective-permute-start(f32[1,2,160]{2,1,0:T(2,128)S(1)} %maximum_bitcast_fusion.2), channel_id=1, source_target_pairs={{0,1},{1,0},{2,3},{3,2},{4,5},{5,4},{6,7},{7,6},{8,9},{9,8},{10,11... | collective-permute-start | bytes 3848 | tf_op jit(solution)/shard_map/ppermute | solution.py:44
  18.1 103.9 %collective-permute-start = (bf16[160,1280]{1,0:T(8,128)(2,1)S(1)}, bf16[160,1280]{1,0:T(8,128)(2,1)S(1)}, u32[]{:S(2)}, u32[]{:S(2)}) collective-permute-start(bf16[160,1280]{1,0:T(8,128)(2,1)S(1)} %get-tuple-element.305.refs_0_), channel_id=1, source_target_pairs={{0,1},{1,0},{2,3},{3,2},{4,5},{5,4},{6,7},{7,6},{8,9},{9,8},{10,11... | collective-permute-start | bytes 1228808 | tf_op jit(solution)/shard_map/ppermute | solution.py:44
  18.3 96.6 %collective-permute-start.23 = (bf16[160,1280]{1,0:T(8,128)(2,1)S(1)}, bf16[160,1280]{1,0:T(8,128)(2,1)S(1)}, u32[]{:S(2)}, u32[]{:S(2)}) collective-permute-start(bf16[160,1280]{1,0:T(8,128)(2,1)S(1)} %get-tuple-element.304.refs_0_), channel_id=1, source_target_pairs={{0,2},{1,3},{2,0},{3,1},{4,6},{5,7},{6,4},{7,5},{8,10},{9,11},{10,... | collective-permute-start | bytes 1228808 | tf_op jit(solution)/shard_map/ppermute | solution.py:44
  59.6 78.5 %collective-permute-start.22 = (bf16[160,1280]{1,0:T(8,128)(2,1)S(1)}, bf16[160,1280]{1,0:T(8,128)(2,1)}, u32[]{:S(2)}, u32[]{:S(2)}) collective-permute-start(bf16[160,1280]{1,0:T(8,128)(2,1)S(1)} %get-tuple-element.304.refs_0_), channel_id=1, source_target_pairs={{0,1},{1,0},{2,3},{3,2},{4,5},{5,4},{6,7},{7,6},{8,9},{9,8},{10,11... | collective-permute-start | bytes 1228808 | tf_op jit(solution)/shard_map/ppermute | solution.py:44
  69.5 29.6 %all-to-all-start = ((bf16[8,3,160,160]{3,2,1,0:T(8,128)(2,1)}), bf16[8,3,160,160]{3,2,1,0:T(8,128)(2,1)}, u32[]{:S(2)}, u32[]{:S(2)}) async-start(bf16[8,3,160,160]{3,2,1,0:T(8,128)(2,1)} %pad_maximum_fusion.1), calls=%async_computation | async-start | bytes 3932160 | tf_op jit(solution)/shard_map/all_to_all | solution.py:123
  73.9 181.7 %all-gather.7.cloned.1.call-start = ((), (), s32[]{:S(2)}) async-start(), calls=%async_computation.7 | async-start | bytes 2048000 | tf_op jit(solution)/shard_map/all_gather | solution.py:132
  103.7 152.0 %all-gather.9.cloned.1.call-start = ((), (), s32[]{:S(2)}) async-start(), calls=%async_computation.8 | async-start | bytes 2048000 | tf_op jit(solution)/shard_map/all_gather | solution.py:132
  114.9 32.8 %collective-permute-start.24 = (bf16[160,1280]{1,0:T(8,128)(2,1)S(1)}, bf16[160,1280]{1,0:T(8,128)(2,1)}, u32[]{:S(2)}, u32[]{:S(2)}) collective-permute-start(bf16[160,1280]{1,0:T(8,128)(2,1)S(1)} %collective-permute-done.23.refs_2_), channel_id=1, source_target_pairs={{0,1},{1,0},{2,3},{3,2},{4,5},{5,4},{6,7},{7,6},{8,9},{9,8},{10,11... | collective-permute-start | bytes 1228808 | tf_op jit(solution)/shard_map/ppermute | solution.py:44
  121.8 136.8 %all-gather.11.cloned.1.call-start = ((), (), s32[]{:S(2)}) async-start(), calls=%async_computation.9 | async-start | bytes 2048000 | tf_op jit(solution)/shard_map/all_gather | solution.py:132
  138.1 43.1 %collective-permute-start.7 = (bf16[640,640]{1,0:T(8,128)(2,1)S(1)}, bf16[640,640]{1,0:T(8,128)(2,1)}, u32[]{:S(2)}, u32[]{:S(2)}) collective-permute-start(bf16[640,640]{1,0:T(8,128)(2,1)S(1)} %get-tuple-element.115.refs_1_.refs_2_), channel_id=1, source_target_pairs={{0,4},{4,0},{8,12},{12,8},{1,5},{5,1},{9,13},{13,9},{2,6},{6,2},{1... | collective-permute-start | bytes 2457608 | tf_op jit(solution)/shard_map/ppermute | solution.py:44
  169.0 445.4 %reduce-scatter.4.cloned.1.call-start = ((), (), s32[]{:S(2)}) async-start(), calls=%async_computation.10 | async-start | bytes 2048000 | tf_op jit(solution)/shard_map/reduce_scatter | solution.py:158
  169.0 42.3 %collective-permute-start.25 = (bf16[640,640]{1,0:T(8,128)(2,1)}, bf16[640,640]{1,0:T(8,128)(2,1)S(1)}, u32[]{:S(2)}, u32[]{:S(2)}) collective-permute-start(bf16[640,640]{1,0:T(8,128)(2,1)} %get-tuple-element.125.refs_1_.refs_2_), channel_id=1, source_target_pairs={{0,4},{4,0},{8,12},{12,8},{1,5},{5,1},{9,13},{13,9},{2,6},{6,2},{1... | collective-permute-start | bytes 2457608 | tf_op jit(solution)/shard_map/ppermute | solution.py:44
  181.3 30.1 %collective-permute-start.27 = (bf16[640,640]{1,0:T(8,128)(2,1)}, bf16[640,640]{1,0:T(8,128)(2,1)S(1)}, u32[]{:S(2)}, u32[]{:S(2)}) collective-permute-start(bf16[640,640]{1,0:T(8,128)(2,1)} %collective-permute-done.26.refs_3_.refs_4_), channel_id=1, source_target_pairs={{0,4},{4,0},{8,12},{12,8},{1,5},{5,1},{9,13},{13,9},{2,6},{6,2},{1... | collective-permute-start | bytes 2457608 | tf_op jit(solution)/shard_map/ppermute | solution.py:44
  207.0 37.3 %collective-permute-start.10 = (bf16[160,1280]{1,0:T(8,128)(2,1)S(1)}, bf16[160,1280]{1,0:T(8,128)(2,1)S(1)}, u32[]{:S(2)}, u32[]{:S(2)}) collective-permute-start(bf16[160,1280]{1,0:T(8,128)(2,1)S(1)} %get-tuple-element.117), channel_id=1, source_target_pairs={{0,1},{1,0},{2,3},{3,2},{4,5},{5,4},{6,7},{7,6},{8,9},{9,8},{10,11... | collective-permute-start | bytes 1228808 | tf_op jit(solution)/shard_map/ppermute | solution.py:44
  207.0 48.6 %collective-permute-start.11 = (bf16[160,1280]{1,0:T(8,128)(2,1)}, bf16[160,1280]{1,0:T(8,128)(2,1)}, u32[]{:S(2)}, u32[]{:S(2)}) collective-permute-start(bf16[160,1280]{1,0:T(8,128)(2,1)} %get-tuple-element.118), channel_id=1, source_target_pairs={{0,2},{1,3},{2,0},{3,1},{4,6},{5,7},{6,4},{7,5},{8,10},{9,11},{10,... | collective-permute-start | bytes 1228808 | tf_op jit(solution)/shard_map/ppermute | solution.py:44
  210.6 45.1 %collective-permute-start.12 = (bf16[160,1280]{1,0:T(8,128)(2,1)}, bf16[160,1280]{1,0:T(8,128)(2,1)}, u32[]{:S(2)}, u32[]{:S(2)}) collective-permute-start(bf16[160,1280]{1,0:T(8,128)(2,1)} %get-tuple-element.119), channel_id=1, source_target_pairs={{0,3},{1,2},{2,1},{3,0},{4,7},{5,6},{6,5},{7,4},{8,11},{9,10},{10,... | collective-permute-start | bytes 1228808 | tf_op jit(solution)/shard_map/ppermute | solution.py:44
  236.3 53.2 %collective-permute-start.29 = (bf16[160,1280]{1,0:T(8,128)(2,1)S(1)}, bf16[160,1280]{1,0:T(8,128)(2,1)S(1)}, u32[]{:S(2)}, u32[]{:S(2)}) collective-permute-start(bf16[160,1280]{1,0:T(8,128)(2,1)S(1)} %get-tuple-element.128), channel_id=1, source_target_pairs={{0,2},{1,3},{2,0},{3,1},{4,6},{5,7},{6,4},{7,5},{8,10},{9,11},{10,... | collective-permute-start | bytes 1228808 | tf_op jit(solution)/shard_map/ppermute | solution.py:44
  244.3 45.1 %collective-permute-start.30 = (bf16[160,1280]{1,0:T(8,128)(2,1)S(1)}, bf16[160,1280]{1,0:T(8,128)(2,1)}, u32[]{:S(2)}, u32[]{:S(2)}) collective-permute-start(bf16[160,1280]{1,0:T(8,128)(2,1)S(1)} %get-tuple-element.129), channel_id=1, source_target_pairs={{0,3},{1,2},{2,1},{3,0},{4,7},{5,6},{6,5},{7,4},{8,11},{9,10},{10,... | collective-permute-start | bytes 1228808 | tf_op jit(solution)/shard_map/ppermute | solution.py:44
  255.6 40.2 %collective-permute-start.16 = (bf16[640,1280]{1,0:T(8,128)(2,1)}, bf16[640,1280]{1,0:T(8,128)(2,1)}, u32[]{:S(2)}, u32[]{:S(2)}) collective-permute-start(bf16[640,1280]{1,0:T(8,128)(2,1)} %all-gather.7.cloned.1.call-done.refs_4_), channel_id=1, source_target_pairs={{0,4},{4,0},{8,12},{12,8},{1,5},{5,1},{9,13},{13,9},{2,6},{6,2},{1... | collective-permute-start | bytes 4915208 | tf_op jit(solution)/shard_map/ppermute | solution.py:44
  255.7 40.7 %collective-permute-start.17 = (bf16[640,1280]{1,0:T(8,128)(2,1)}, bf16[640,1280]{1,0:T(8,128)(2,1)}, u32[]{:S(2)}, u32[]{:S(2)}) collective-permute-start(bf16[640,1280]{1,0:T(8,128)(2,1)} %all-gather.9.cloned.1.call-done.refs_6_), channel_id=1, source_target_pairs={{0,4},{4,0},{8,12},{12,8},{1,5},{5,1},{9,13},{13,9},{2,6},{6,2},{1... | collective-permute-start | bytes 4915208 | tf_op jit(solution)/shard_map/ppermute | solution.py:44
  261.9 36.0 %collective-permute-start.18 = (bf16[640,1280]{1,0:T(8,128)(2,1)}, bf16[640,1280]{1,0:T(8,128)(2,1)S(1)}, u32[]{:S(2)}, u32[]{:S(2)}) collective-permute-start(bf16[640,1280]{1,0:T(8,128)(2,1)} %all-gather.11.cloned.1.call-done.refs_8_), channel_id=1, source_target_pairs={{0,4},{4,0},{8,12},{12,8},{1,5},{5,1},{9,13},{13,9},{2,6},{6,2},{1... | collective-permute-start | bytes 4915208 | tf_op jit(solution)/shard_map/ppermute | solution.py:44
  296.4 38.3 %collective-permute-start.31 = (bf16[160,1280]{1,0:T(8,128)(2,1)S(1)}, bf16[160,1280]{1,0:T(8,128)(2,1)S(1)}, u32[]{:S(2)}, u32[]{:S(2)}) collective-permute-start(bf16[160,1280]{1,0:T(8,128)(2,1)S(1)} %multiply_convert_fusion.2.refs_0_), channel_id=1, source_target_pairs={{0,8},{4,12},{8,0},{12,4},{16,24},{20,28},{24,16},{28,20},{1,9},{5... | collective-permute-start | bytes 1228808 | tf_op jit(solution)/shard_map/ppermute | solution.py:95
  298.0 38.2 %collective-permute-start.32 = (bf16[160,1280]{1,0:T(8,128)(2,1)S(1)}, bf16[160,1280]{1,0:T(8,128)(2,1)S(1)}, u32[]{:S(2)}, u32[]{:S(2)}) collective-permute-start(bf16[160,1280]{1,0:T(8,128)(2,1)S(1)} %multiply_convert_fusion.2.refs_0_), channel_id=1, source_target_pairs={{0,16},{4,20},{8,24},{12,28},{16,0},{20,4},{24,8},{28,12},{1,17},{... | collective-permute-start | bytes 1228808 | tf_op jit(solution)/shard_map/ppermute | solution.py:95
  305.1 31.1 %collective-permute-start.33 = (bf16[160,1280]{1,0:T(8,128)(2,1)S(1)}, bf16[160,1280]{1,0:T(8,128)(2,1)S(1)}, u32[]{:S(2)}, u32[]{:S(2)}) collective-permute-start(bf16[160,1280]{1,0:T(8,128)(2,1)S(1)} %multiply_convert_fusion.2.refs_0_), channel_id=1, source_target_pairs={{0,24},{4,28},{8,16},{12,20},{16,8},{20,12},{24,0},{28,4},{1,25},{... | collective-permute-start | bytes 1228808 | tf_op jit(solution)/shard_map/ppermute | solution.py:95
  379.9 36.8 %collective-permute-start.49 = (bf16[160,1280]{1,0:T(8,128)(2,1)S(1)}, bf16[160,1280]{1,0:T(8,128)(2,1)S(1)}, u32[]{:S(2)}, u32[]{:S(2)}) collective-permute-start(bf16[160,1280]{1,0:T(8,128)(2,1)S(1)} %get-tuple-element.294.refs_0_), channel_id=1, source_target_pairs={{0,8},{4,12},{8,0},{12,4},{16,24},{20,28},{24,16},{28,20},{1,9},{5... | collective-permute-start | bytes 1228808 | tf_op jit(solution)/shard_map/ppermute | solution.py:95
  380.5 36.2 %collective-permute-start.50 = (bf16[160,1280]{1,0:T(8,128)(2,1)S(1)}, bf16[160,1280]{1,0:T(8,128)(2,1)S(1)}, u32[]{:S(2)}, u32[]{:S(2)}) collective-permute-start(bf16[160,1280]{1,0:T(8,128)(2,1)S(1)} %get-tuple-element.294.refs_0_), channel_id=1, source_target_pairs={{0,16},{4,20},{8,24},{12,28},{16,0},{20,4},{24,8},{28,12},{1,17},{... | collective-permute-start | bytes 1228808 | tf_op jit(solution)/shard_map/ppermute | solution.py:95
  386.8 29.9 %collective-permute-start.51 = (bf16[160,1280]{1,0:T(8,128)(2,1)S(1)}, bf16[160,1280]{1,0:T(8,128)(2,1)S(1)}, u32[]{:S(2)}, u32[]{:S(2)}) collective-permute-start(bf16[160,1280]{1,0:T(8,128)(2,1)S(1)} %get-tuple-element.294.refs_0_), channel_id=1, source_target_pairs={{0,24},{4,28},{8,16},{12,20},{16,8},{20,12},{24,0},{28,4},{1,25},{... | collective-permute-start | bytes 1228808 | tf_op jit(solution)/shard_map/ppermute | solution.py:95
  449.3 167.9 %reduce-scatter.6.cloned.1.call-start = ((), (), s32[]{:S(2)}) async-start(), calls=%async_computation.11 | async-start | bytes 2048000 | tf_op jit(solution)/shard_map/reduce_scatter | solution.py:158
  481.5 138.5 %reduce-scatter.8.cloned.1.call-start = ((), (), s32[]{:S(2)}) async-start(), calls=%async_computation.12 | async-start | bytes 2048000 | tf_op jit(solution)/shard_map/reduce_scatter | solution.py:158
  482.0 82.6 %collective-permute-start.54 = (bf16[640,1280]{1,0:T(8,128)(2,1)}, bf16[640,1280]{1,0:T(8,128)(2,1)}, u32[]{:S(2)}, u32[]{:S(2)}) collective-permute-start(bf16[640,1280]{1,0:T(8,128)(2,1)} %slice.243), channel_id=1, source_target_pairs={{0,4},{4,0},{8,12},{12,8},{1,5},{5,1},{9,13},{13,9},{2,6},{6,2},{1... | collective-permute-start | bytes 4915208 | tf_op jit(solution)/shard_map/ppermute | solution.py:44
  506.8 48.9 %collective-permute-start.62 = (bf16[160,1280]{1,0:T(8,128)(2,1)S(1)}, bf16[160,1280]{1,0:T(8,128)(2,1)S(1)}, u32[]{:S(2)}, u32[]{:S(2)}) collective-permute-start(bf16[160,1280]{1,0:T(8,128)(2,1)S(1)} %get-tuple-element.320.refs_6_), channel_id=1, source_target_pairs={{0,2},{1,3},{2,0},{3,1},{4,6},{5,7},{6,4},{7,5},{8,10},{9,11},{10,... | collective-permute-start | bytes 1228808 | tf_op jit(solution)/shard_map/ppermute | solution.py:44
  516.2 48.3 %collective-permute-start.44 = (bf16[160,1280]{1,0:T(8,128)(2,1)}, bf16[160,1280]{1,0:T(8,128)(2,1)}, u32[]{:S(2)}, u32[]{:S(2)}) collective-permute-start(bf16[160,1280]{1,0:T(8,128)(2,1)} %get-tuple-element.319.refs_6_), channel_id=1, source_target_pairs={{0,2},{1,3},{2,0},{3,1},{4,6},{5,7},{6,4},{7,5},{8,10},{9,11},{10,... | collective-permute-start | bytes 1228808 | tf_op jit(solution)/shard_map/ppermute | solution.py:44
  517.5 50.5 %collective-permute-start.61 = (bf16[160,1280]{1,0:T(8,128)(2,1)S(1)}, bf16[160,1280]{1,0:T(8,128)(2,1)S(1)}, u32[]{:S(2)}, u32[]{:S(2)}) collective-permute-start(bf16[160,1280]{1,0:T(8,128)(2,1)S(1)} %get-tuple-element.320.refs_6_), channel_id=1, source_target_pairs={{0,1},{1,0},{2,3},{3,2},{4,5},{5,4},{6,7},{7,6},{8,9},{9,8},{10,11... | collective-permute-start | bytes 1228808 | tf_op jit(solution)/shard_map/ppermute | solution.py:44
  520.6 108.9 %collective-permute-start.43 = (bf16[160,1280]{1,0:T(8,128)(2,1)}, bf16[160,1280]{1,0:T(8,128)(2,1)}, u32[]{:S(2)}, u32[]{:S(2)}) collective-permute-start(bf16[160,1280]{1,0:T(8,128)(2,1)} %get-tuple-element.319.refs_6_), channel_id=1, source_target_pairs={{0,1},{1,0},{2,3},{3,2},{4,5},{5,4},{6,7},{7,6},{8,9},{9,8},{10,11... | collective-permute-start | bytes 1228808 | tf_op jit(solution)/shard_map/ppermute | solution.py:44
  564.6 64.9 %collective-permute-start.45 = (bf16[160,1280]{1,0:T(8,128)(2,1)}, bf16[160,1280]{1,0:T(8,128)(2,1)}, u32[]{:S(2)}, u32[]{:S(2)}) collective-permute-start(bf16[160,1280]{1,0:T(8,128)(2,1)} %collective-permute-done.44.refs_8_), channel_id=1, source_target_pairs={{0,1},{1,0},{2,3},{3,2},{4,5},{5,4},{6,7},{7,6},{8,9},{9,8},{10,11... | collective-permute-start | bytes 1228808 | tf_op jit(solution)/shard_map/ppermute | solution.py:44
  612.5 69.4 %collective-permute-start.64 = (bf16[640,640]{1,0:T(8,128)(2,1)}, bf16[640,640]{1,0:T(8,128)(2,1)S(1)}, u32[]{:S(2)}, u32[]{:S(2)}) collective-permute-start(bf16[640,640]{1,0:T(8,128)(2,1)} %get-tuple-element.172), channel_id=1, source_target_pairs={{0,4},{4,0},{8,12},{12,8},{1,5},{5,1},{9,13},{13,9},{2,6},{6,2},{1... | collective-permute-start | bytes 2457608 | tf_op jit(solution)/shard_map/ppermute | solution.py:44
  612.6 69.4 %collective-permute-start.65 = (bf16[640,640]{1,0:T(8,128)(2,1)}, bf16[640,640]{1,0:T(8,128)(2,1)S(1)}, u32[]{:S(2)}, u32[]{:S(2)}) collective-permute-start(bf16[640,640]{1,0:T(8,128)(2,1)} %get-tuple-element.173), channel_id=1, source_target_pairs={{0,8},{4,12},{8,0},{12,4},{1,9},{5,13},{9,1},{13,5},{2,10},{6,14},... | collective-permute-start | bytes 2457608 | tf_op jit(solution)/shard_map/ppermute | solution.py:44
  614.1 67.8 %collective-permute-start.66 = (bf16[640,640]{1,0:T(8,128)(2,1)}, bf16[640,640]{1,0:T(8,128)(2,1)S(1)}, u32[]{:S(2)}, u32[]{:S(2)}) collective-permute-start(bf16[640,640]{1,0:T(8,128)(2,1)} %get-tuple-element.174), channel_id=1, source_target_pairs={{0,12},{4,8},{8,4},{12,0},{1,13},{5,9},{9,5},{13,1},{2,14},{6,10},... | collective-permute-start | bytes 2457608 | tf_op jit(solution)/shard_map/ppermute | solution.py:44
  624.9 55.0 %all-to-all-start.1 = ((bf16[8,3,160,160]{3,2,1,0:T(8,128)(2,1)}), bf16[8,3,160,160]{3,2,1,0:T(8,128)(2,1)}, u32[]{:S(2)}, u32[]{:S(2)}) async-start(bf16[8,3,160,160]{3,2,1,0:T(8,128)(2,1)} %pad_maximum_fusion.2), calls=%async_computation.4 | async-start | bytes 3932160 | tf_op jit(solution)/shard_map/all_to_all | solution.py:168
  668.1 34.7 %collective-permute-start.46 = (bf16[640,640]{1,0:T(8,128)(2,1)}, bf16[640,640]{1,0:T(8,128)(2,1)}, u32[]{:S(2)}, u32[]{:S(2)}) collective-permute-start(bf16[640,640]{1,0:T(8,128)(2,1)} %get-tuple-element.144), channel_id=1, source_target_pairs={{0,4},{4,0},{8,12},{12,8},{1,5},{5,1},{9,13},{13,9},{2,6},{6,2},{1... | collective-permute-start | bytes 2457608 | tf_op jit(solution)/shard_map/ppermute | solution.py:44
  668.6 34.2 %collective-permute-start.47 = (bf16[640,640]{1,0:T(8,128)(2,1)}, bf16[640,640]{1,0:T(8,128)(2,1)}, u32[]{:S(2)}, u32[]{:S(2)}) collective-permute-start(bf16[640,640]{1,0:T(8,128)(2,1)} %get-tuple-element.145), channel_id=1, source_target_pairs={{0,8},{4,12},{8,0},{12,4},{1,9},{5,13},{9,1},{13,5},{2,10},{6,14},... | collective-permute-start | bytes 2457608 | tf_op jit(solution)/shard_map/ppermute | solution.py:44
  735.2 117.1 %all-to-all-start.2 = ((bf16[8,160,1280]{2,1,0:T(8,128)(2,1)}), bf16[8,160,1280]{2,1,0:T(8,128)(2,1)}, u32[]{:S(2)}, u32[]{:S(2)}) async-start(bf16[8,160,1280]{2,1,0:T(8,128)(2,1)} %pad_maximum_fusion), calls=%async_computation.5 | async-start | bytes 6553600 | tf_op jit(solution)/shard_map/all_to_all | solution.py:196
  750.8 39.1 %collective-permute-start.67 = (bf16[160,1280]{1,0:T(8,128)(2,1)S(1)}, bf16[160,1280]{1,0:T(8,128)(2,1)S(1)}, u32[]{:S(2)}, u32[]{:S(2)}) collective-permute-start(bf16[160,1280]{1,0:T(8,128)(2,1)S(1)} %copy-done.19), channel_id=1, source_target_pairs={{0,1},{1,0},{2,3},{3,2},{4,5},{5,4},{6,7},{7,6},{8,9},{9,8},{10,11... | collective-permute-start | bytes 1228808 | tf_op jit(solution)/shard_map/ppermute | solution.py:44
  783.4 31.0 %collective-permute-start.68 = (bf16[160,1280]{1,0:T(8,128)(2,1)S(1)}, bf16[160,1280]{1,0:T(8,128)(2,1)}, u32[]{:S(2)}, u32[]{:S(2)}) collective-permute-start(bf16[160,1280]{1,0:T(8,128)(2,1)S(1)} %copy-done.17), channel_id=1, source_target_pairs={{0,2},{1,3},{2,0},{3,1},{4,6},{5,7},{6,4},{7,5},{8,10},{9,11},{10,... | collective-permute-start | bytes 1228808 | tf_op jit(solution)/shard_map/ppermute | solution.py:44
  786.9 61.5 %collective-permute-start.56 = (bf16[160,1280]{1,0:T(8,128)(2,1)S(1)}, bf16[160,1280]{1,0:T(8,128)(2,1)}, u32[]{:S(2)}, u32[]{:S(2)}) collective-permute-start(bf16[160,1280]{1,0:T(8,128)(2,1)S(1)} %get-tuple-element.162), channel_id=1, source_target_pairs={{0,2},{1,3},{2,0},{3,1},{4,6},{5,7},{6,4},{7,5},{8,10},{9,11},{10,... | collective-permute-start | bytes 1228808 | tf_op jit(solution)/shard_map/ppermute | solution.py:44
  790.7 57.7 %collective-permute-start.57 = (bf16[160,1280]{1,0:T(8,128)(2,1)S(1)}, bf16[160,1280]{1,0:T(8,128)(2,1)}, u32[]{:S(2)}, u32[]{:S(2)}) collective-permute-start(bf16[160,1280]{1,0:T(8,128)(2,1)S(1)} %get-tuple-element.163), channel_id=1, source_target_pairs={{0,3},{1,2},{2,1},{3,0},{4,7},{5,6},{6,5},{7,4},{8,11},{9,10},{10,... | collective-permute-start | bytes 1228808 | tf_op jit(solution)/shard_map/ppermute | solution.py:44
  (131 other events, 2091.7 us)
Sparse Core Ops, SparseCore 0:
  10.5 35.6 all-gather.4
  103.8 46.2 all-gather.6
  151.7 38.1 all-gather.8
  191.3 52.1 all-gather.10
  449.4 43.2 reduce-scatter.3
  495.0 45.1 reduce-scatter.5
  568.2 41.0 reduce-scatter.7

commit v10 on v9

--- a/solution.py
+++ b/solution.py
@@ -69,18 +69,26 @@
     return places ^ lax.axis_index(axis) if size == 4 else places
 
 
-def group_gather(own_block, axis):
+def group_gather(own_block, axis, gates=None):
     if lax.axis_size(axis) != 4:
         return [lax.all_gather(own_block, axis, axis=0, tiled=True)]
     across = swap(own_block, axis, 2)
     beside = swap(own_block, axis, 1)
-    return [own_block, beside, across, swap(across, axis, 1)]
-
-
-def group_scatter(pieces, axis):
+    source = across if gates is None else after(across, beside, *gates)
+    return [own_block, beside, across, swap(source, axis, 1)]
+
+
+def group_scatter(pieces, axis, hops=2):
     if lax.axis_size(axis) != 4:
-        return [lax.psum_scatter(pieces[0], axis, scatter_dimension=0, tiled=True)]
-    return [pieces[0]] + [swap(piece, axis, bits) for piece, bits in zip(pieces[1:], (1, 2, 3))]
+        parts = [lax.psum_scatter(pieces[0], axis, scatter_dimension=0, tiled=True)]
+        return parts, parts[0]
+    own, beside, across, far = pieces
+    if hops == 1:
+        parts = [swap(piece, axis, bits) for piece, bits in zip(pieces[1:], (1, 2, 3))]
+        return [own] + parts, parts[0]
+    far = swap(far, axis, 1)
+    across = swap(add_low(across, far), axis, 2)
+    return [own, swap(after(beside, far), axis, 1), across], far
 
 
 def total_wide(parts):
@@ -103,11 +111,11 @@
 
 def hidden_scatter(pieces):
     if not in_plane():
-        return group_scatter(pieces, "tp")
+        return group_scatter(pieces, "tp")[0]
     return [pieces[0]] + [hop(piece, bits) for piece, bits in zip(pieces[1:], (2, 4, 6))]
 
 
-def hidden_shards(w_up, w_gate, w_down):
+def hidden_blocks(w_up, w_gate, w_down):
     if not in_plane():
         return jnp.stack([w_up.T, w_gate.T, w_down])
     rows, hidden = w_up.shape
@@ -120,17 +128,21 @@
         ],
         axis=1,
     )
-    packed = lax.all_to_all(packed, SPREAD, 0, 0)
-    return packed.transpose(1, 2, 0, 3).reshape(3, part, 8 * rows)
-
-
-def hidden_weights(matrices):
-    if not in_plane():
-        return [
-            [lax.all_gather(matrices[place], SPREAD, axis=1, tiled=True)] for place in range(3)
-        ]
-    lines = [lax.all_gather(matrices[place], "tp", axis=0, tiled=True) for place in range(3)]
-    return [[line, swap(line, "ctx", 1)] for line in lines]
+    return lax.all_to_all(packed, SPREAD, 0, 0)
+
+
+def hidden_shards(blocks):
+    if not in_plane():
+        return blocks
+    rows = blocks.shape[2]
+    return blocks.transpose(1, 2, 0, 3).reshape(3, rows, -1)
+
+
+def hidden_weights(shards):
+    if not in_plane():
+        return [lax.all_gather(shards, SPREAD, axis=2, tiled=True)[None]]
+    line = lax.all_gather(shards, "tp", axis=0)
+    return [line, swap(line, "ctx", 1)]
 
 
 def hidden_scales(*scales):
@@ -191,10 +203,24 @@
 
 
 def owner_scatter(product_low):
-    count = lax.axis_size(SPREAD)
+    if not in_plane():
+        total = lax.psum_scatter(product_low, SPREAD, scatter_dimension=0, tiled=True)
+        return total.astype(jnp.float32)
+    place = lax.axis_index("ctx")
+    core, along, plane = place % 2, place // 2, lax.axis_index("shard")
     rows, width = product_low.shape
-    blocks = lax.all_to_all(product_low.reshape(count, rows // count, width), SPREAD, 0, 0)
-    return jnp.sum(blocks.astype(jnp.float32), axis=0)
+    blocks = product_low.reshape(4, 2, rows // 8, width)
+
+    def of_core(which):
+        return lax.dynamic_index_in_dim(blocks, which, 1, keepdims=False)
+
+    blocks = add_low(of_core(core), swap(of_core(1 - core), "ctx", 1))
+    chip = plane * 2 + along
+
+    def of_chip(bits):
+        return lax.dynamic_index_in_dim(blocks, chip ^ bits, 0, keepdims=False)
+
+    return total_wide([of_chip(0)] + [hop(of_chip(bits), 2 * bits) for bits in (1, 2, 3)])
 
 
 def row_labels(slots, group_size):
@@ -235,10 +261,6 @@
 def row_blocks(ref, count):
     rows = ref.shape[0] // count
     return [ref.at[pl.ds(place * rows, rows)] for place in range(count)]
-
-
-def core_time(micros):
-    return pl.CostEstimate(flops=int(micros * 1.15e9), transcendentals=0, bytes_accessed=1 << 20)
 
 
 ANYWHERE = pl.BlockSpec(memory_space=pl.ANY)
@@ -343,7 +365,6 @@
             pltpu.SemaphoreType.DMA((count,)),
         ],
         compiler_params=pltpu.CompilerParams(vmem_limit_bytes=48 << 20),
-        cost_estimate=core_time(23),
         name="attend",
     )(query, *pieces, hot, side, weight)
 
@@ -457,7 +478,6 @@
             pltpu.SemaphoreType.DMA,
         ],
         compiler_params=pltpu.CompilerParams(vmem_limit_bytes=56 << 20),
-        cost_estimate=core_time(38),
         name="attend_grad",
     )(query, outs, *pieces, *tops, hot, side, scale, weight)
 
@@ -550,7 +570,6 @@
             pltpu.SemaphoreType.DMA,
         ],
         compiler_params=pltpu.CompilerParams(vmem_limit_bytes=40 << 20),
-        cost_estimate=core_time(9),
         name="project",
     )(*pieces, weight, scale)
 
@@ -606,7 +625,6 @@
         ]
         + [jax.ShapeDtypeStruct((rows // count_out, width), jnp.bfloat16)] * count_out,
         compiler_params=pltpu.CompilerParams(vmem_limit_bytes=40 << 20),
-        cost_estimate=core_time(14),
         name="project_grad",
     )(query_grad, *tree_parts, raw, weight, scale)
 
@@ -619,14 +637,16 @@
 
 def hidden_body(count, halves, *refs):
     pieces, refs = refs[:count], refs[count:]
-    weights, refs = refs[: 3 * halves], refs[3 * halves :]
+    weights, refs = refs[:halves], refs[halves:]
     scale_ref, refs = refs[0], refs[1:]
     outs, refs = refs[:count], refs[count:]
     group_out, up_out, gate_out, mixed_out, group, matrices, total, sems, out_sem = refs
     half = up_out.shape[1] // halves
     moves = copies(pieces, row_blocks(group, count), sems)
     loads = [
-        pltpu.make_async_copy(weights[place], matrices.at[place], sems.at[count + place])
+        pltpu.make_async_copy(
+            weights[place % halves].at[:, place // halves], matrices.at[place], sems.at[count + place]
+        )
         for place in range(3 * halves)
     ]
     for load in loads:
@@ -640,14 +660,16 @@
         for matrix in range(3):
             loads[matrix * halves + place].wait()
         tokens = group[...]
-        up = contract_cols(tokens, matrices[place])
-        gate = contract_cols(tokens, matrices[halves + place])
+        up = contract_cols(tokens, matrices[place].reshape(half, -1))
+        gate = contract_cols(tokens, matrices[halves + place].reshape(half, -1))
         up_out[:, columns] = up.astype(jnp.bfloat16)
         gate_out[:, columns] = gate.astype(jnp.bfloat16)
         raw, curve, silu, scaled = gated(up, gate, scale_ref[0:1, columns], scale_ref[1:2, columns])
         mixed = (scaled * silu).astype(jnp.bfloat16)
         mixed_out[:, columns] = mixed
-        part = jnp.dot(mixed, matrices[2 * halves + place], preferred_element_type=jnp.float32)
+        part = jnp.dot(
+            mixed, matrices[2 * halves + place].reshape(half, -1), preferred_element_type=jnp.float32
+        )
         total[...] = part if place == 0 else total[...] + part
     rows = group.shape[0] // count
     for place in range(count):
@@ -656,41 +678,42 @@
 
 
 def hidden_forward(pieces, weights, scales):
-    count, halves = len(pieces), len(weights[0])
+    count, halves = len(pieces), len(weights)
     rows, width = pieces[0].shape[0] * count, pieces[0].shape[1]
-    half = weights[0][0].shape[0]
+    half = weights[0].shape[0] * weights[0].shape[2]
     hidden = half * halves
     low = lambda columns: jax.ShapeDtypeStruct((rows, columns), jnp.bfloat16)
     vmem = pl.BlockSpec(memory_space=pltpu.VMEM)
     return pl.pallas_call(
         lambda *refs: hidden_body(count, halves, *refs),
-        in_specs=[ANYWHERE] * (count + 3 * halves) + [vmem],
+        in_specs=[ANYWHERE] * (count + halves) + [vmem],
         out_specs=[vmem] * count + [ANYWHERE] + [vmem] * 3,
         out_shape=[jax.ShapeDtypeStruct(piece.shape, jnp.bfloat16) for piece in pieces]
         + [low(width), low(hidden), low(hidden), low(hidden)],
         scratch_shapes=[
             pltpu.VMEM((rows, width), jnp.bfloat16),
-            pltpu.VMEM((3 * halves, half, width), jnp.bfloat16),
+            pltpu.VMEM((3 * halves, weights[0].shape[0]) + weights[0].shape[2:], jnp.bfloat16),
             pltpu.VMEM((rows, width), jnp.float32),
             pltpu.SemaphoreType.DMA((count + 3 * halves,)),
             pltpu.SemaphoreType.DMA,
         ],
         compiler_params=pltpu.CompilerParams(vmem_limit_bytes=52 << 20),
-        cost_estimate=core_time(16),
         name="hidden",
-    )(*pieces, *[matrix for parts in weights for matrix in parts], jnp.stack(scales))
+    )(*pieces, *weights, jnp.stack(scales))
 
 
 def hidden_grad_body(count, halves, *refs):
     pieces, refs = refs[:count], refs[count:]
-    weights, refs = refs[: 3 * halves], refs[3 * halves :]
+    weights, refs = refs[:halves], refs[halves:]
     scale_ref, up_ref, gate_ref = refs[:3]
     outs, refs = refs[3 : 3 + count], refs[3 + count :]
     group_out, up_out, gate_out, scale_out, group, matrices, total, sems, out_sem = refs
     half = up_out.shape[1] // halves
     moves = copies(pieces, row_blocks(group, count), sems)
     loads = [
-        pltpu.make_async_copy(weights[place], matrices.at[place], sems.at[count + place])
+        pltpu.make_async_copy(
+            weights[place % halves].at[:, place // halves], matrices.at[place], sems.at[count + place]
+        )
         for place in range(3 * halves)
     ]
     for load in loads:
@@ -703,7 +726,7 @@
         columns = slice(place * half, (place + 1) * half)
         for matrix in range(3):
             loads[matrix * halves + place].wait()
-        pulled = contract_cols(group[...], matrices[2 * halves + place])
+        pulled = contract_cols(group[...], matrices[2 * halves + place].reshape(half, -1))
         pulled = pulled.astype(jnp.bfloat16).astype(jnp.float32)
         up = up_ref[:, columns].astype(jnp.float32)
         gate = gate_ref[:, columns].astype(jnp.float32)
@@ -717,8 +740,12 @@
         scale_out[1:2, columns] = jnp.sum(bent * gate, axis=0, keepdims=True) * math.sqrt(D)
         up_out[:, columns] = up_low
         gate_out[:, columns] = gate_low
-        part = jnp.dot(up_low, matrices[place], preferred_element_type=jnp.float32)
-        part = part + jnp.dot(gate_low, matrices[halves + place], preferred_element_type=jnp.float32)
+        part = jnp.dot(
+            up_low, matrices[place].reshape(half, -1), preferred_element_type=jnp.float32
+        )
+        part = part + jnp.dot(
+            gate_low, matrices[halves + place].reshape(half, -1), preferred_element_type=jnp.float32
+        )
         total[...] = part if place == 0 else total[...] + part
     rows = group.shape[0] // count
     for place in range(count):
@@ -727,29 +754,28 @@
 
 
 def hidden_backward(pieces, weights, scales, up, gate):
-    count, halves = len(pieces), len(weights[0])
+    count, halves = len(pieces), len(weights)
     rows, width = pieces[0].shape[0] * count, pieces[0].shape[1]
-    half = weights[0][0].shape[0]
+    half = weights[0].shape[0] * weights[0].shape[2]
     hidden = half * halves
     low = lambda columns: jax.ShapeDtypeStruct((rows, columns), jnp.bfloat16)
     vmem = pl.BlockSpec(memory_space=pltpu.VMEM)
     return pl.pallas_call(
         lambda *refs: hidden_grad_body(count, halves, *refs),
-        in_specs=[ANYWHERE] * (count + 3 * halves) + [vmem] * 3,
+        in_specs=[ANYWHERE] * (count + halves) + [vmem] * 3,
         out_specs=[vmem] * count + [ANYWHERE] + [vmem] * 3,
         out_shape=[jax.ShapeDtypeStruct(piece.shape, jnp.bfloat16) for piece in pieces]
         + [low(width), low(hidden), low(hidden), jax.ShapeDtypeStruct((8, hidden), jnp.float32)],
         scratch_shapes=[
             pltpu.VMEM((rows, width), jnp.bfloat16),
-            pltpu.VMEM((3 * halves, half, width), jnp.bfloat16),
+            pltpu.VMEM((3 * halves, weights[0].shape[0]) + weights[0].shape[2:], jnp.bfloat16),
             pltpu.VMEM((rows, width), jnp.float32),
             pltpu.SemaphoreType.DMA((count + 3 * halves,)),
             pltpu.SemaphoreType.DMA,
         ],
         compiler_params=pltpu.CompilerParams(vmem_limit_bytes=56 << 20),
-        cost_estimate=core_time(19),
         name="hidden_grad",
-    )(*pieces, *[matrix for parts in weights for matrix in parts], jnp.stack(scales), up, gate)
+    )(*pieces, *weights, jnp.stack(scales), up, gate)
 
 
 def visibility(parents, slots, group_size):
@@ -761,55 +787,63 @@
     return seen_factors(reachable, *row_labels(slots, group_size))
 
 
-def forward_attention(packed, scale_both, pieces, parents, slots):
+def prepare_attention(packed, scale_both, pieces, parents, slots):
     rows = pieces[0].shape[0] * len(pieces)
-    seen = visibility(parents, slots, rows)
     queries, tree_own, raw, group = project(pieces, packed, scale_both)
-    tree = group_gather(tree_own, "ctx")
-    heads_low, inverse, *parts = attend(queries, tree, *seen, packed, len(pieces))
-    return group_scatter(parts, "tp"), (group, seen, queries, tree, raw, heads_low, inverse)
-
-
-def feed_forward(weights, scales, alphas, tokens_own, branch_parts, cotangent_own):
-    alpha_attn, alpha_mlp = alphas
+    return visibility(parents, slots, rows), queries, group_gather(tree_own, "ctx"), raw, group
+
+
+def forward_attention(packed, prepared, count):
+    seen, queries, tree, raw, group = prepared
+    heads_low, inverse, *parts = attend(queries, tree, *seen, packed, count)
+    return group_scatter(parts, "tp")[0], (group, seen, queries, tree, raw, heads_low, inverse)
+
+
+def first_mix(tokens_own, branch_parts, alpha_attn, gates):
     tokens_wide = tokens_own.astype(jnp.float32)
-    branch_one = total_wide(branch_parts)
-    hidden_one, pull_in = jax.vjp(mix_rows, tokens_wide, branch_one, alpha_attn)
-    pieces = hidden_gather(hidden_one.astype(jnp.bfloat16))
-    count = len(pieces)
-    outs = hidden_forward(pieces, weights, scales)
-    hidden_group, up, gate, mixed = outs[count:]
-    branch_two = total_wide(hidden_scatter(outs[:count]))
-    output_wide, pull_out = jax.vjp(mix_rows, hidden_one, branch_two, alpha_mlp)
-    upstream = cotangent_own.astype(jnp.float32)
-    hidden_direct, branch_two_grad, grad_alpha_mlp = pull_out(upstream)
-    pieces = hidden_gather(branch_two_grad.astype(jnp.bfloat16))
-    outs = hidden_backward(pieces, weights, scales, up, gate)
-    top_group, up_low, gate_low, scale_sums = outs[count:]
-    hidden_grad = hidden_direct + total_wide(hidden_scatter(outs[:count]))
-    tokens_direct, branch_one_grad, grad_alpha_attn = pull_in(hidden_grad)
-    tops = group_gather(branch_one_grad.astype(jnp.bfloat16), "tp")
-    factors = ((up_low, hidden_group), (gate_low, hidden_group), (mixed, top_group))
-    sums = (jnp.concatenate([grad_alpha_attn, grad_alpha_mlp]), scale_sums[:2])
-    return output_wide.astype(jnp.bfloat16), tokens_direct, tops, factors, sums
-
-
-def backward_attention(packed, scale_both, kept, tops, tokens_direct):
+    hidden_one, pull_in = jax.vjp(
+        mix_rows, tokens_wide, total_wide(branch_parts), after(alpha_attn, *gates)
+    )
+    hidden_low = hidden_one.astype(jnp.bfloat16)
+    return (hidden_one, pull_in), hidden_low, hidden_gather(hidden_low)
+
+
+def second_mix(hidden_one, branch_parts, alpha_mlp, cotangent_own, gates):
+    output_wide, pull_out = jax.vjp(
+        mix_rows, hidden_one, total_wide(branch_parts), after(alpha_mlp, *gates)
+    )
+    hidden_direct, branch_grad, grad_alpha_mlp = pull_out(cotangent_own.astype(jnp.float32))
+    branch_low = branch_grad.astype(jnp.bfloat16)
+    kept = (output_wide.astype(jnp.bfloat16), hidden_direct, grad_alpha_mlp)
+    return kept, branch_low, hidden_gather(branch_low)
+
+
+def third_mix(pull_in, hidden_parts, hidden_direct, gates):
+    hidden_grad = total_wide(hidden_parts) + after(hidden_direct, *gates)
+    tokens_direct, branch_grad, grad_alpha_attn = pull_in(hidden_grad)
+    return tokens_direct, branch_grad.astype(jnp.bfloat16), grad_alpha_attn
+
+
+def backward_attention(packed, kept, tops, hops):
     group, seen, queries, tree, raw, heads_low, inverse = kept
-    query_grads, *rest = attend_grad(
-        queries, tops, heads_low, tree, *seen, inverse, packed
-    )
-    tree_grads, top_group = rest[:-1], rest[-1]
-    tree_parts = group_scatter(tree_grads, "ctx")
+    query_grads, *rest = attend_grad(queries, tops, heads_low, tree, *seen, inverse, packed)
+    tree_parts, first = group_scatter(rest[:-1], "ctx", hops)
+    return query_grads, tree_parts, (rest[-1], heads_low)
+
+
+def backward_projection(packed, scale_both, kept, attended, tokens_direct, hops):
+    group, raw = kept[0], kept[4]
+    query_grads, tree_parts, heads_factors = attended
+    count = lax.axis_size("tp") if lax.axis_size("tp") == 4 else 1
     low, scale_sums, *parts = project_grad(
-        query_grads, tree_parts, raw, packed, scale_both, len(tops)
-    )
-    grad_tokens = tokens_direct + total_wide(group_scatter(parts, "tp"))
-    features = queries.shape[1]
+        query_grads, tree_parts, raw, packed, scale_both, count
+    )
+    own_parts, first = group_scatter(parts, "tp", hops)
+    grad_tokens = tokens_direct + total_wide(own_parts)
+    features = scale_both.shape[1] // 2
     scale_sum = jnp.sum(scale_sums, axis=(0, 1))
-    return grad_tokens, ((group, low), (top_group, heads_low)), (
-        scale_sum[:features] + scale_sum[features:]
-    )
+    scale_sum = scale_sum[:features] + scale_sum[features:]
+    return grad_tokens, ((group, low), heads_factors), scale_sum, first
 
 
 def joint_product(factors):
@@ -837,7 +871,8 @@
 ):
     width = tokens.shape[-1]
     micros = range(tokens.shape[0])
-    groups = [group_gather(tokens[m, 0], "tp") for m in micros]
+    last = tokens.shape[0] - 1
+    groups = [group_gather(tokens[0, 0], "tp")]
     packed = lax.all_gather(
         jnp.concatenate([w_query, w_key, w_value, w_attn_out.T], axis=1),
         SPREAD,
@@ -846,48 +881,99 @@
     )
     scales = hidden_scales(scale_up, scale_gate)
     scale_both = jnp.concatenate([scale_qk, scale_qk])[None]
-    first = groups[0][-1]
-    shards = hidden_shards(after(w_up, first), after(w_gate, first), after(w_down, first))
+    blocks = hidden_blocks(w_up, w_gate, w_down)
+    prepared = []
+    gates = scales
+    for m in micros:
+        early = after(scale_both, *gates)
+        prepared.append(
+            prepare_attention(packed, early, groups[m], parents[m, 0], slot_segment[m, 0])
+        )
+        if m == last:
+            break
+        ahead = groups[m][len(groups[m]) // 2]
+        groups.append(group_gather(after(tokens[m + 1, 0], ahead), "tp", prepared[m][1:2]))
+        if m == 0:
+            shards = hidden_shards(after(blocks, groups[1][-1]))
+        tree = prepared[m][2]
+        gates = (tree[len(tree) // 2], shards)
+    if last == 0:
+        shards = hidden_shards(blocks)
     weights = hidden_weights(shards)
-    scale_early = after(scale_both, *scales)
-    front = [
-        forward_attention(packed, scale_early, groups[m], parents[m, 0], slot_segment[m, 0])
-        for m in micros
+    front = [forward_attention(packed, prepared[m], len(groups[m])) for m in micros]
+    gates = ()
+    opened, forwards, mixed, backwards, closed, tops = [], [], [], [], [], []
+    for m in micros:
+        kept, mark, pieces = first_mix(tokens[m, 0], front[m][0], alpha_attn, gates)
+        gates = (mark,)
+        count = len(pieces)
+        outs = hidden_forward(pieces, weights, scales)
+        opened.append(kept)
+        forwards.append((hidden_scatter(outs[:count]), outs[count:]))
+    for m in micros:
+        kept, mark, pieces = second_mix(
+            opened[m][0], forwards[m][0], alpha_mlp, cotangent[m, 0], gates
+        )
+        gates = (mark,)
+        up, gate = forwards[m][1][1:3]
+        outs = hidden_backward(pieces, weights, scales, up, gate)
+        mixed.append(kept)
+        backwards.append((hidden_scatter(outs[:count]), outs[count:]))
+    joined = []
+    for m in micros:
+        hidden_group, hidden_mixed = forwards[m][1][0], forwards[m][1][3]
+        top_group, up_low, gate_low = backwards[m][1][:3]
+        joined.append(((up_low, hidden_group), (gate_low, hidden_group), (hidden_mixed, top_group)))
+    products = [
+        joint_product([joined[m][place] for m in micros]).astype(jnp.bfloat16)
+        for place in range(3)
     ]
-    mid = [
-        feed_forward(
-            weights, scales, (alpha_attn, alpha_mlp), tokens[m, 0], front[m][0], cotangent[m, 0]
-        )
-        for m in micros
-    ]
-    lines = core_sums(
-        [
-            joint_product([mid[m][3][place] for m in micros]).astype(jnp.bfloat16)
-            for place in range(3)
-        ]
-    )
+    for m in micros:
+        closed.append(
+            third_mix(
+                opened[m][1],
+                backwards[m][0],
+                mixed[m][1],
+                gates,
+            )
+        )
+        gates = (closed[-1][1],)
+        tops.append(group_gather(closed[-1][1], "tp", products if m == last else ()))
+    lines = core_sums(products)
+    line_sums = hidden_line_sums([after(line, *[top[-1] for top in tops]) for line in lines])
+    spread_sums = hidden_spread(line_sums)
+    attended = [backward_attention(packed, front[m][1], tops[m], 1) for m in micros]
     vectors = vector_sums(
-        sum(mid[m][4][0] for m in micros), sum(mid[m][4][1] for m in micros)
-    )
-    line_sums = hidden_line_sums(lines)
-    spread_sums = hidden_spread(line_sums)
-    waits = [after(scale_both, *line_sums), after(scale_both, spread_sums)]
-    back = [
-        backward_attention(packed, waits[min(m, 1)], front[m][1], mid[m][2], mid[m][1])
-        for m in micros
-    ]
+        after(
+            sum(jnp.concatenate([closed[m][2], mixed[m][2]]) for m in micros), attended[-1][0]
+        ),
+        sum(backwards[m][1][3][:2] for m in micros),
+    )
+    gates = ()
+    back = []
+    for m in micros:
+        back.append(
+            backward_projection(
+                packed,
+                after(scale_both, *gates),
+                front[m][1],
+                attended[m],
+                closed[m][0],
+                1 if m == last else 2,
+            )
+        )
+        gates = (back[-1][3], spread_sums, vectors)
+    product = jnp.concatenate(
+        [joint_product([back[m][1][place] for m in micros]) for place in range(2)], axis=1
+    )
+    grad_attention = owner_scatter(product.astype(jnp.bfloat16))
+    grad_q, grad_k, grad_v, grad_o = jnp.split(grad_attention, 4, axis=1)
     grad_u, grad_g, grad_d = hidden_weight_grads(spread_sums)
-    grad_attention = owner_scatter(
-        jnp.concatenate(
-            [joint_product([back[m][1][place] for m in micros]) for place in range(2)], axis=1
-        ).astype(jnp.bfloat16)
-    )
-    grad_q, grad_k, grad_v, grad_o = jnp.split(grad_attention, 4, axis=1)
     sums = butterfly(jnp.concatenate([vectors, sum(back[m][2] for m in micros)]), SPREAD)
     sum_alphas, sum_hidden, sum_qk = jnp.split(sums, [2 * width, sums.shape[0] - scale_qk.shape[0]])
     sum_up, sum_gate = jnp.split(sum_hidden, 2)
     return (
-        jnp.stack([mid[m][0] for m in micros])[:, None],
+        jnp.stack([mixed[m][0] for m in micros])[:, None],
         jnp.stack([back[m][0] for m in micros])[:, None],
         grad_q,
         grad_k,

time: 877 us -> 765 us (0.87)
  waiting for transfers between devices: 303 us -> 206 us
  starting transfers between devices: 121 us -> 86 us
  between operations: 20.4 us -> 33.1 us
  other arithmetic: 52.8 us -> 62.1 us
    ppermute x52 -> x51, waiting for transfers between devices: 223 us -> 156 us  [swap(): lax.ppermute(value, axis, [(place, place ^ bit) for place in range(size)])]
    ppermute x52 -> x51, starting transfers between devices: 74.8 us -> 40 us  [swap(): lax.ppermute(value, axis, [(place, place ^ bit) for place in range(size)])]
    all_to_all x2 -> x1, waiting for transfers between devices: 24.2 us -> 0.01 us  [hidden_blocks(): return lax.all_to_all(packed, SPREAD, 0, 0)]
    ppermute x24 -> x27, waiting for transfers between devices: 56.1 us -> 32.5 us  [hop(): lax.ppermute(value, SPREAD, [(place, place ^ bits) for place in range(8)])]
    all_to_all x1, waiting for transfers between devices: 0.01 us -> 17.1 us  [hidden_spread(): return lax.all_to_all(packed, SPREAD, 0, 0)]
    slice x7 -> x26, local copies, waits for them, and re-layouts: 6.45 us -> 19 us  [after(): other[(slice(0, 1),) * other.ndim].reshape(()) * 0]
    ppermute x24 -> x27, starting transfers between devices: 31.7 us -> 36.4 us  [hop(): lax.ppermute(value, SPREAD, [(place, place ^ bits) for place in range(8)])]
    unnamed x188 -> x253, local copies, waits for them, and re-layouts: 37.4 us -> 34.5 us
  transfers between devices with their start and end apart: 86 -> 85, of which waited for: 32 -> 30; matrix products, arithmetic and copies ran while one was open for 13% -> 18% of each run, Pallas kernels for 24% -> 29%
where the time goes in v10:
time: 765 us; the launch traced here: 757 us
  Pallas kernels  242 us (32%)
  waiting for transfers between devices  206 us (27%)
  local copies, waits for them, and re-layouts  99.2 us (13%)
  starting transfers between devices  86 us (11%)
  other arithmetic  62.1 us (8%)
  between operations  33.1 us (4%)
  matrix products  29.3 us (4%)
    ppermute x51, waiting for transfers between devices, swap(): lax.ppermute(value, axis, [(place, place ^ bit) for place in range(size)])  156 us
    pallas_call x2, Pallas kernels, attend_grad(): pl.pallas_call(lambda *refs: attend_grad_body(count, len(tops), *refs), g...  77.4 us
    pallas_call x2, Pallas kernels, attend(): pl.pallas_call(lambda *refs: attend_body(count, *refs), grid=(keys // KEY...  45.2 us
    ppermute x51, starting transfers between devices, swap(): lax.ppermute(value, axis, [(place, place ^ bit) for place in range(size)])  40 us
    pallas_call x2, Pallas kernels, hidden_backward(): pl.pallas_call(lambda *refs: hidden_grad_body(count, halves, *refs), in_s...  39.4 us
    ppermute x27, starting transfers between devices, hop(): lax.ppermute(value, SPREAD, [(place, place ^ bits) for place in range(8)])  36.4 us
    unnamed x253, local copies, waits for them, and re-layouts  34.5 us
    ppermute x27, waiting for transfers between devices, hop(): lax.ppermute(value, SPREAD, [(place, place ^ bits) for place in range(8)])  32.5 us
  transfers between devices with their start and end apart: 85, of which 30 were waited for; matrix products, arithmetic and copies ran while one was open for 18% of the time, Pallas kernels for 29%

profile of v10, /device:TPU:0, one launch (start us, length us, event | category | flops | bytes accessed | tf_op | source)
XLA Modules:
  0.0 757.3 jit_solution(3518130071625926563)
XLA Ops:
  10.9 4.1 collective-permute-start.4
  23.7 4.5 all-to-all-start
  30.2 7.8 %collective-permute-done.1.refs_2_ = bf16[160,1280]{1,0:T(8,128)(2,1)S(1)} collective-permute-done((bf16[160,1280]{1,0:T(8,128)(2,1)S(1)}, bf16[160,1280]{1,0:T(8,128)(2,1)S(1)}, u32[]{:S(2)}, u32[]{:S(2)}) %collective-permute-start.1) | collective-permute-done | bytes 409632 | tf_op jit(solution)/shard_map/ppermute | solution.py:44
  45.7 13.5 %collective-permute-done.13.refs_1_ = bf16[160,1280]{1,0:T(8,128)(2,1)S(1)} collective-permute-done((bf16[160,1280]{1,0:T(8,128)(2,1)S(1)}, bf16[160,1280]{1,0:T(8,128)(2,1)S(1)}, u32[]{:S(2)}, u32[]{:S(2)}) %collective-permute-start.13) | collective-permute-done | bytes 409632 | tf_op jit(solution)/shard_map/ppermute | solution.py:44
  60.5 7.7 %collective-permute-done.2.refs_3_ = bf16[160,1280]{1,0:T(8,128)(2,1)S(1)} collective-permute-done((bf16[160,1280]{1,0:T(8,128)(2,1)S(1)}, bf16[160,1280]{1,0:T(8,128)(2,1)S(1)}, u32[]{:S(2)}, u32[]{:S(2)}) %collective-permute-start.2) | collective-permute-done | bytes 409632 | tf_op jit(solution)/shard_map/ppermute | solution.py:44
  70.1 9.1 %project.2 = (bf16[640,320]{1,0:T(8,128)(2,1)S(1)}, bf16[640,640]{1,0:T(8,128)(2,1)}, f32[640,640]{1,0:T(8,128)S(1)}, bf16[640,1280]{1,0:T(8,128)(2,1)S(1)}) custom-call(bf16[160,1280]{1,0:T(8,128)(2,1)S(1)} %slice_bitcast_fusion.refs_0_, bf16[160,1280]{1,0:T(8,128)(2,1)S(1)} %collective-permute-done.refs_1_, ...), custom_call_target="tpu_custom_call" | custom-call | tf_op jit(solution)/shard_map/project/pallas_call | solution.py:552
  83.0 10.2 %collective-permute-done.15.refs_3_ = bf16[160,1280]{1,0:T(8,128)(2,1)S(1)} collective-permute-done((bf16[160,1280]{1,0:T(8,128)(2,1)S(1)}, bf16[160,1280]{1,0:T(8,128)(2,1)S(1)}, u32[]{:S(2)}, u32[]{:S(2)}) %collective-permute-start.15) | collective-permute-done | bytes 409632 | tf_op jit(solution)/shard_map/ppermute | solution.py:44
  98.0 3.0 all_gather_reshape.3
  107.0 3.1 fusion.36
  110.1 14.0 %collective-permute-done.8.refs_3_.refs_4_ = bf16[640,640]{1,0:T(8,128)(2,1)} collective-permute-done((bf16[640,640]{1,0:T(8,128)(2,1)}, bf16[640,640]{1,0:T(8,128)(2,1)}, u32[]{:S(2)}, u32[]{:S(2)}) %collective-permute-start.8) | collective-permute-done | bytes 819232 | tf_op jit(solution)/shard_map/ppermute | solution.py:44
  124.9 4.5 reshape.760
  137.1 9.1 %project.3 = (bf16[640,320]{1,0:T(8,128)(2,1)S(1)}, bf16[640,640]{1,0:T(8,128)(2,1)}, f32[640,640]{1,0:T(8,128)S(1)}, bf16[640,1280]{1,0:T(8,128)(2,1)S(1)}) custom-call(bf16[160,1280]{1,0:T(8,128)(2,1)S(1)} %copy-done.15, bf16[160,1280]{1,0:T(8,128)(2,1)S(1)} %copy-done.29, bf16[160,1280]{1,0:T(8,128)(2,1)S(1)} %copy-done.13, ...), custom_call_target="tpu_custom_call" | custom-call | tf_op jit(solution)/shard_map/project/pallas_call | solution.py:552
  148.4 22.5 %attend.2 = (bf16[640,320]{1,0:T(8,128)(2,1)S(1)}, f32[8,640]{1,0:T(8,128)S(1)}, bf16[160,1280]{1,0:T(8,128)(2,1)S(1)}, bf16[160,1280]{1,0:T(8,128)(2,1)S(1)}, b...) custom-call(bf16[640,320]{1,0:T(8,128)(2,1)S(1)} %copy-done.9, ...), custom_call_target="tpu_custom_call" | custom-call | tf_op jit(solution)/shard_map/attend/pallas_call | solution.py:341
  174.0 24.4 %collective-permute-done.10 = bf16[160,1280]{1,0:T(8,128)(2,1)S(1)} collective-permute-done((bf16[160,1280]{1,0:T(8,128)(2,1)S(1)}, bf16[160,1280]{1,0:T(8,128)(2,1)S(1)}, u32[]{:S(2)}, u32[]{:S(2)}) %collective-permute-start.10) | collective-permute-done | bytes 409632 | tf_op jit(solution)/shard_map/ppermute | solution.py:44
  204.6 22.6 %attend.3 = (bf16[640,320]{1,0:T(8,128)(2,1)S(1)}, f32[8,640]{1,0:T(8,128)S(1)}, bf16[160,1280]{1,0:T(8,128)(2,1)S(1)}, bf16[160,1280]{1,0:T(8,128)(2,1)S(1)}, b...) custom-call(bf16[640,320]{1,0:T(8,128)(2,1)S(1)} %copy-done.11, ...), custom_call_target="tpu_custom_call" | custom-call | tf_op jit(solution)/shard_map/attend/pallas_call | solution.py:341
  230.3 8.6 %collective-permute-done.19 = bf16[160,1280]{1,0:T(8,128)(2,1)S(1)} collective-permute-done((bf16[160,1280]{1,0:T(8,128)(2,1)S(1)}, bf16[160,1280]{1,0:T(8,128)(2,1)S(1)}, u32[]{:S(2)}, u32[]{:S(2)}) %collective-permute-start.19) | collective-permute-done | bytes 409632 | tf_op jit(solution)/shard_map/ppermute | solution.py:44
  248.1 10.7 %collective-permute-done.20 = bf16[160,1280]{1,0:T(8,128)(2,1)S(1)} collective-permute-done((bf16[160,1280]{1,0:T(8,128)(2,1)}, bf16[160,1280]{1,0:T(8,128)(2,1)S(1)}, u32[]{:S(2)}, u32[]{:S(2)}) %collective-permute-start.20) | collective-permute-done | bytes 409632 | tf_op jit(solution)/shard_map/ppermute | solution.py:44
  268.4 3.8 collective-permute-done.24.refs_3_
  272.2 16.0 %hidden.2 = (bf16[160,1280]{1,0:T(8,128)(2,1)S(1)}, bf16[160,1280]{1,0:T(8,128)(2,1)}, bf16[160,1280]{1,0:T(8,128)(2,1)}, bf16[160,1280]{1,0:T(8,128)(2,1)S(1)},...) custom-call(bf16[160,1280]{1,0:T(8,128)(2,1)} %copy-done.95, ...), custom_call_target="tpu_custom_call" | custom-call | tf_op jit(solution)/shard_map/hidden/pallas_call | solution.py:687
  293.8 15.9 %hidden.3 = (bf16[160,1280]{1,0:T(8,128)(2,1)S(1)}, bf16[160,1280]{1,0:T(8,128)(2,1)S(1)}, bf16[160,1280]{1,0:T(8,128)(2,1)S(1)}, bf16[160,1280]{1,0:T(8,128)(2,...) custom-call(bf16[160,1280]{1,0:T(8,128)(2,1)} %copy-done.94, ...), custom_call_target="tpu_custom_call" | custom-call | tf_op jit(solution)/shard_map/hidden/pallas_call | solution.py:687
  324.7 7.9 %collective-permute-done.33 = bf16[160,1280]{1,0:T(8,128)(2,1)} collective-permute-done((bf16[160,1280]{1,0:T(8,128)(2,1)S(1)}, bf16[160,1280]{1,0:T(8,128)(2,1)}, u32[]{:S(2)}, u32[]{:S(2)}) %collective-permute-start.33) | collective-permute-done | bytes 409632 | tf_op jit(solution)/shard_map/ppermute | solution.py:103
  346.1 3.9 collective-permute-done.36.refs_2_
  350.0 19.9 %hidden_grad.2 = (bf16[160,1280]{1,0:T(8,128)(2,1)}, bf16[160,1280]{1,0:T(8,128)(2,1)}, bf16[160,1280]{1,0:T(8,128)(2,1)}, bf16[160,1280]{1,0:T(8,128)(2,1)}, bf...) custom-call(bf16[160,1280]{1,0:T(8,128)(2,1)} %fusion.47.refs_0_, ...), custom_call_target="tpu_custom_call" | custom-call | tf_op jit(solution)/shard_map/hidden_grad/pallas_call | solution.py:763
  369.9 19.5 %hidden_grad.3 = (bf16[160,1280]{1,0:T(8,128)(2,1)}, bf16[160,1280]{1,0:T(8,128)(2,1)}, bf16[160,1280]{1,0:T(8,128)(2,1)}, bf16[160,1280]{1,0:T(8,128)(2,1)}, bf...) custom-call(bf16[160,1280]{1,0:T(8,128)(2,1)} %fusion.48.refs_0_, ...), custom_call_target="tpu_custom_call" | custom-call | tf_op jit(solution)/shard_map/hidden_grad/pallas_call | solution.py:763
  389.5 6.7 convolution_convert_fusion.2
  402.2 4.8 convolution_convert_fusion.1
  408.8 4.8 convolution_convert_fusion
  428.7 8.2 %collective-permute-done.55 = bf16[160,1280]{1,0:T(8,128)(2,1)} collective-permute-done((bf16[160,1280]{1,0:T(8,128)(2,1)}, bf16[160,1280]{1,0:T(8,128)(2,1)}, u32[]{:S(2)}, u32[]{:S(2)}) %collective-permute-start.55) | collective-permute-done | bytes 409632 | tf_op jit(solution)/shard_map/ppermute | solution.py:103
  444.9 5.1 collective-permute-done.42.refs_8_
  450.0 11.9 %collective-permute-done.56.refs_7_ = bf16[160,1280]{1,0:T(8,128)(2,1)S(1)} collective-permute-done((bf16[160,1280]{1,0:T(8,128)(2,1)S(1)}, bf16[160,1280]{1,0:T(8,128)(2,1)S(1)}, u32[]{:S(2)}, u32[]{:S(2)}) %collective-permute-start.56) | collective-permute-done | bytes 409632 | tf_op jit(solution)/shard_map/ppermute | solution.py:44
  466.0 8.1 %collective-permute-done.43.refs_9_ = bf16[160,1280]{1,0:T(8,128)(2,1)S(1)} collective-permute-done((bf16[160,1280]{1,0:T(8,128)(2,1)S(1)}, bf16[160,1280]{1,0:T(8,128)(2,1)S(1)}, u32[]{:S(2)}, u32[]{:S(2)}) %collective-permute-start.43) | collective-permute-done | bytes 409632 | tf_op jit(solution)/shard_map/ppermute | solution.py:44
  475.3 6.6 collective-permute-done.58.refs_9_
  483.1 3.4 fusion.31
  486.8 3.5 collective-permute-done.63
  493.3 3.3 collective-permute-done.64
  499.3 38.7 %attend_grad.2 = (f32[640,320]{1,0:T(8,128)}, bf16[640,640]{1,0:T(8,128)(2,1)}, bf16[640,640]{1,0:T(8,128)(2,1)}, bf16[640,640]{1,0:T(8,128)(2,1)}, bf16[640,640]{1,0:T(8,128)(2,1)}, /*index=5*/bf16[640,1280]{1,0:T(8,128)(2,1)}) custom-call(bf16[640,320]{1,0:T(8,128)(2,1)} %copy-done.8, bf16[640,320]{1,0:T(8,128)(2,1)} %copy-done.24, ...), custom_call_target="tpu_custom_call" | custom-call | tf_op jit(solution)/shard_map/attend_grad/pallas_call | solution.py:453
  541.4 38.7 %attend_grad.3 = (f32[640,320]{1,0:T(8,128)}, bf16[640,640]{1,0:T(8,128)(2,1)}, bf16[640,640]{1,0:T(8,128)(2,1)}, bf16[640,640]{1,0:T(8,128)(2,1)}, bf16[640,640]{1,0:T(8,128)(2,1)}, /*index=5*/bf16[640,1280]{1,0:T(8,128)(2,1)}) custom-call(bf16[640,320]{1,0:T(8,128)(2,1)} %copy-done.10, bf16[640,320]{1,0:T(8,128)(2,1)} %copy-done.26, ...), custom_call_target="tpu_custom_call" | custom-call | tf_op jit(solution)/shard_map/attend_grad/pallas_call | solution.py:453
  582.5 3.9 collective-permute-done.66
  592.9 15.4 %project_grad.2 = (bf16[640,960]{1,0:T(8,128)(2,1)S(1)}, f32[4,1,640]{2,1,0:T(1,128)S(1)}, bf16[160,1280]{1,0:T(8,128)(2,1)S(1)}, bf16[160,1280]{1,0:T(8,128)(2,...) custom-call(f32[640,320]{1,0:T(8,128)S(1)} %copy-done.21, bf16[640,640]{1,0:T(8,128)(2,1)S(1)} %copy-done.23, ...), custom_call_target="tpu_custom_call" | custom-call | tf_op jit(solution)/shard_map/project_grad/pallas_call | solution.py:611
  635.4 4.3 all-to-all-start.1
  647.9 17.1 %all-to-all-done.1 = bf16[8,3,160,160]{3,2,1,0:T(8,128)(2,1)} async-done(((bf16[8,3,160,160]{3,2,1,0:T(8,128)(2,1)}), bf16[8,3,160,160]{3,2,1,0:T(8,128)(2,1)}, u32[]{:S(2)}, u32[]{:S(2)}) %all-to-all-start.1) | async-done | bytes 1228832 | tf_op jit(solution)/shard_map/all_to_all | solution.py:180
  670.7 14.2 %project_grad.3 = (bf16[640,960]{1,0:T(8,128)(2,1)S(1)}, f32[4,1,640]{2,1,0:T(1,128)S(1)}, bf16[160,1280]{1,0:T(8,128)(2,1)S(1)}, bf16[160,1280]{1,0:T(8,128)(2,...) custom-call(f32[640,320]{1,0:T(8,128)S(1)} %copy-done.20, bf16[640,640]{1,0:T(8,128)(2,1)S(1)} %copy-done.22, ...), custom_call_target="tpu_custom_call" | custom-call | tf_op jit(solution)/shard_map/project_grad/pallas_call | solution.py:611
  689.1 7.6 convolution_convert_fusion.3
  696.6 3.0 copy.91
  699.7 3.0 fusion.27
  714.1 3.5 fusion.79
  732.1 8.2 %collective-permute-done.69 = bf16[160,1280]{1,0:T(8,128)(2,1)} collective-permute-done((bf16[160,1280]{1,0:T(8,128)(2,1)S(1)}, bf16[160,1280]{1,0:T(8,128)(2,1)}, u32[]{:S(2)}, u32[]{:S(2)}) %collective-permute-start.69) | collective-permute-done | bytes 409632 | tf_op jit(solution)/shard_map/ppermute | solution.py:44
  743.2 6.2 collective-permute-done.73
  (585 shorter events, 227.7 us)
Async XLA Ops:
  7.2 61.0 %all-gather.3.cloned.1.call-start = ((), (), s32[]{:S(2)}) async-start(), calls=%async_computation.5 | async-start | bytes 3686400 | tf_op jit(solution)/shard_map/all_gather | solution.py:876
  15.0 25.2 %collective-permute-start.3 = (f32[1,2,160]{2,1,0:T(2,128)S(1)}, f32[1,2,160]{2,1,0:T(2,128)S(1)}, u32[]{:S(2)}, u32[]{:S(2)}) collective-permute-start(f32[1,2,160]{2,1,0:T(2,128)S(1)} %maximum_bitcast_fusion.2), channel_id=1, source_target_pairs={{0,1},{1,0},{2,3},{3,2},{4,5},{5,4},{6,7},{7,6},{8,9},{9,8},{10,11... | collective-permute-start | bytes 3848 | tf_op jit(solution)/shard_map/ppermute | solution.py:44
  18.0 42.4 %collective-permute-start = (bf16[160,1280]{1,0:T(8,128)(2,1)S(1)}, bf16[160,1280]{1,0:T(8,128)(2,1)S(1)}, u32[]{:S(2)}, u32[]{:S(2)}) collective-permute-start(bf16[160,1280]{1,0:T(8,128)(2,1)S(1)} %slice_bitcast_fusion.refs_0_), channel_id=1, source_target_pairs={{0,1},{1,0},{2,3},{3,2},{4,5},{5,4},{6,7},{7,6},{8,9},{9,8},{10,11... | collective-permute-start | bytes 1228808 | tf_op jit(solution)/shard_map/ppermute | solution.py:44
  23.7 71.4 %all-to-all-start = ((bf16[8,3,160,160]{3,2,1,0:T(8,128)(2,1)}), bf16[8,3,160,160]{3,2,1,0:T(8,128)(2,1)}, u32[]{:S(2)}, u32[]{:S(2)}) async-start(bf16[8,3,160,160]{3,2,1,0:T(8,128)(2,1)} %pad_maximum_fusion), calls=%async_computation | async-start | bytes 3932160 | tf_op jit(solution)/shard_map/all_to_all | solution.py:131
  28.2 172.2 %all-gather.5.cloned.1.call-start = ((), (), s32[]{:S(2)}) async-start(), calls=%async_computation.6 | async-start | bytes 6144000 | tf_op jit(solution)/shard_map/all_gather | solution.py:144
  39.3 43.2 %collective-permute-start.14 = (bf16[160,1280]{1,0:T(8,128)(2,1)S(1)}, bf16[160,1280]{1,0:T(8,128)(2,1)S(1)}, u32[]{:S(2)}, u32[]{:S(2)}) collective-permute-start(bf16[160,1280]{1,0:T(8,128)(2,1)S(1)} %add_bitcast_fusion.3.refs_0_), channel_id=1, source_target_pairs={{0,2},{1,3},{2,0},{3,1},{4,6},{5,7},{6,4},{7,5},{8,10},{9,11},{10,... | collective-permute-start | bytes 1228808 | tf_op jit(solution)/shard_map/ppermute | solution.py:44
  40.2 27.9 %collective-permute-start.2 = (bf16[160,1280]{1,0:T(8,128)(2,1)S(1)}, bf16[160,1280]{1,0:T(8,128)(2,1)S(1)}, u32[]{:S(2)}, u32[]{:S(2)}) collective-permute-start(bf16[160,1280]{1,0:T(8,128)(2,1)S(1)} %collective-permute-done.1.refs_2_), channel_id=1, source_target_pairs={{0,1},{1,0},{2,3},{3,2},{4,5},{5,4},{6,7},{7,6},{8,9},{9,8},{10,11... | collective-permute-start | bytes 1228808 | tf_op jit(solution)/shard_map/ppermute | solution.py:44
  101.0 518.2 %reduce-scatter.4.cloned.1.call-start = ((), (), s32[]{:S(2)}) async-start(), calls=%async_computation.7 | async-start | bytes 2048000 | tf_op jit(solution)/shard_map/reduce_scatter | solution.py:170
  110.1 38.1 %collective-permute-start.7 = (bf16[640,640]{1,0:T(8,128)(2,1)}, bf16[640,640]{1,0:T(8,128)(2,1)}, u32[]{:S(2)}, u32[]{:S(2)}) collective-permute-start(bf16[640,640]{1,0:T(8,128)(2,1)} %get-tuple-element.115.refs_1_.refs_2_), channel_id=1, source_target_pairs={{0,4},{4,0},{8,12},{12,8},{1,5},{5,1},{9,13},{13,9},{2,6},{6,2},{1... | collective-permute-start | bytes 2457608 | tf_op jit(solution)/shard_map/ppermute | solution.py:44
  124.2 24.1 %collective-permute-start.9 = (bf16[640,640]{1,0:T(8,128)(2,1)}, bf16[640,640]{1,0:T(8,128)(2,1)}, u32[]{:S(2)}, u32[]{:S(2)}) collective-permute-start(bf16[640,640]{1,0:T(8,128)(2,1)} %collective-permute-done.8.refs_3_.refs_4_), channel_id=1, source_target_pairs={{0,4},{4,0},{8,12},{12,8},{1,5},{5,1},{9,13},{13,9},{2,6},{6,2},{1... | collective-permute-start | bytes 2457608 | tf_op jit(solution)/shard_map/ppermute | solution.py:44
  146.3 27.2 %collective-permute-start.17 = (bf16[640,640]{1,0:T(8,128)(2,1)}, bf16[640,640]{1,0:T(8,128)(2,1)}, u32[]{:S(2)}, u32[]{:S(2)}) collective-permute-start(bf16[640,640]{1,0:T(8,128)(2,1)} %get-tuple-element.121.refs_1_.refs_2_), channel_id=1, source_target_pairs={{0,8},{4,12},{8,0},{12,4},{1,9},{5,13},{9,1},{13,5},{2,10},{6,14},... | collective-permute-start | bytes 2457608 | tf_op jit(solution)/shard_map/ppermute | solution.py:44
  172.5 25.9 %collective-permute-start.10 = (bf16[160,1280]{1,0:T(8,128)(2,1)S(1)}, bf16[160,1280]{1,0:T(8,128)(2,1)S(1)}, u32[]{:S(2)}, u32[]{:S(2)}) collective-permute-start(bf16[160,1280]{1,0:T(8,128)(2,1)S(1)} %get-tuple-element.118), channel_id=1, source_target_pairs={{0,1},{1,0},{2,3},{3,2},{4,5},{5,4},{6,7},{7,6},{8,9},{9,8},{10,11... | collective-permute-start | bytes 1228808 | tf_op jit(solution)/shard_map/ppermute | solution.py:44
  173.5 31.0 %collective-permute-start.16 = (bf16[640,640]{1,0:T(8,128)(2,1)}, bf16[640,640]{1,0:T(8,128)(2,1)S(1)}, u32[]{:S(2)}, u32[]{:S(2)}) collective-permute-start(bf16[640,640]{1,0:T(8,128)(2,1)} %get-tuple-element.121.refs_1_.refs_2_), channel_id=1, source_target_pairs={{0,4},{4,0},{8,12},{12,8},{1,5},{5,1},{9,13},{13,9},{2,6},{6,2},{1... | collective-permute-start | bytes 2457608 | tf_op jit(solution)/shard_map/ppermute | solution.py:44
  173.6 31.0 %collective-permute-start.18 = (bf16[640,640]{1,0:T(8,128)(2,1)}, bf16[640,640]{1,0:T(8,128)(2,1)}, u32[]{:S(2)}, u32[]{:S(2)}) collective-permute-start(bf16[640,640]{1,0:T(8,128)(2,1)} %collective-permute-done.17.refs_3_.refs_4_), channel_id=1, source_target_pairs={{0,4},{4,0},{8,12},{12,8},{1,5},{5,1},{9,13},{13,9},{2,6},{6,2},{1... | collective-permute-start | bytes 2457608 | tf_op jit(solution)/shard_map/ppermute | solution.py:44
  200.4 27.0 %collective-permute-start.11 = (bf16[160,1280]{1,0:T(8,128)(2,1)}, bf16[160,1280]{1,0:T(8,128)(2,1)}, u32[]{:S(2)}, u32[]{:S(2)}) collective-permute-start(bf16[160,1280]{1,0:T(8,128)(2,1)} %broadcast_add_fusion.3), channel_id=1, source_target_pairs={{0,1},{1,0},{2,3},{3,2},{4,5},{5,4},{6,7},{7,6},{8,9},{9,8},{10,11... | collective-permute-start | bytes 1228808 | tf_op jit(solution)/shard_map/ppermute | solution.py:44
  200.4 71.8 %collective-permute-start.25 = (bf16[4,3,160,1280]{3,2,1,0:T(8,128)(2,1)}, bf16[4,3,160,1280]{3,2,1,0:T(8,128)(2,1)}, u32[]{:S(2)}, u32[]{:S(2)}) collective-permute-start(bf16[4,3,160,1280]{3,2,1,0:T(8,128)(2,1)} %all-gather.5.cloned.1.call-done.refs_4_), channel_id=1, source_target_pairs={{0,4},{4,0},{8,12},{12,8},{1,5},{5,1},{9,13},{13,9},{2,6},{6,2},{1... | collective-permute-start | bytes 14745608 | tf_op jit(solution)/shard_map/ppermute | solution.py:44
  201.6 25.8 %collective-permute-start.12 = (bf16[160,1280]{1,0:T(8,128)(2,1)S(1)}, bf16[160,1280]{1,0:T(8,128)(2,1)S(1)}, u32[]{:S(2)}, u32[]{:S(2)}) collective-permute-start(bf16[160,1280]{1,0:T(8,128)(2,1)S(1)} %add_convert_fusion.5), channel_id=1, source_target_pairs={{0,2},{1,3},{2,0},{3,1},{4,6},{5,7},{6,4},{7,5},{8,10},{9,11},{10,... | collective-permute-start | bytes 1228808 | tf_op jit(solution)/shard_map/ppermute | solution.py:44
  264.5 26.7 %collective-permute-start.29 = (bf16[160,1280]{1,0:T(8,128)(2,1)S(1)}, bf16[160,1280]{1,0:T(8,128)(2,1)}, u32[]{:S(2)}, u32[]{:S(2)}) collective-permute-start(bf16[160,1280]{1,0:T(8,128)(2,1)S(1)} %multiply_convert_fusion.2.refs_0_), channel_id=1, source_target_pairs={{0,8},{4,12},{8,0},{12,4},{16,24},{20,28},{24,16},{28,20},{1,9},{5... | collective-permute-start | bytes 1228808 | tf_op jit(solution)/shard_map/ppermute | solution.py:103
  266.3 26.7 %collective-permute-start.30 = (bf16[160,1280]{1,0:T(8,128)(2,1)S(1)}, bf16[160,1280]{1,0:T(8,128)(2,1)S(1)}, u32[]{:S(2)}, u32[]{:S(2)}) collective-permute-start(bf16[160,1280]{1,0:T(8,128)(2,1)S(1)} %multiply_convert_fusion.2.refs_0_), channel_id=1, source_target_pairs={{0,16},{4,20},{8,24},{12,28},{16,0},{20,4},{24,8},{28,12},{1,17},{... | collective-permute-start | bytes 1228808 | tf_op jit(solution)/shard_map/ppermute | solution.py:103
  267.8 25.9 %collective-permute-start.31 = (bf16[160,1280]{1,0:T(8,128)(2,1)S(1)}, bf16[160,1280]{1,0:T(8,128)(2,1)}, u32[]{:S(2)}, u32[]{:S(2)}) collective-permute-start(bf16[160,1280]{1,0:T(8,128)(2,1)S(1)} %multiply_convert_fusion.2.refs_0_), channel_id=1, source_target_pairs={{0,24},{4,28},{8,16},{12,20},{16,8},{20,12},{24,0},{28,4},{1,25},{... | collective-permute-start | bytes 1228808 | tf_op jit(solution)/shard_map/ppermute | solution.py:103
  288.2 24.5 %collective-permute-start.26 = (bf16[160,1280]{1,0:T(8,128)(2,1)}, bf16[160,1280]{1,0:T(8,128)(2,1)}, u32[]{:S(2)}, u32[]{:S(2)}) collective-permute-start(bf16[160,1280]{1,0:T(8,128)(2,1)} %get-tuple-element.127), channel_id=1, source_target_pairs={{0,8},{4,12},{8,0},{12,4},{16,24},{20,28},{24,16},{28,20},{1,9},{5... | collective-permute-start | bytes 1228808 | tf_op jit(solution)/shard_map/ppermute | solution.py:103
  289.8 23.5 %collective-permute-start.27 = (bf16[160,1280]{1,0:T(8,128)(2,1)}, bf16[160,1280]{1,0:T(8,128)(2,1)}, u32[]{:S(2)}, u32[]{:S(2)}) collective-permute-start(bf16[160,1280]{1,0:T(8,128)(2,1)} %get-tuple-element.128), channel_id=1, source_target_pairs={{0,16},{4,20},{8,24},{12,28},{16,0},{20,4},{24,8},{28,12},{1,17},{... | collective-permute-start | bytes 1228808 | tf_op jit(solution)/shard_map/ppermute | solution.py:103
  317.0 22.9 %collective-permute-start.35 = (bf16[160,1280]{1,0:T(8,128)(2,1)}, bf16[160,1280]{1,0:T(8,128)(2,1)}, u32[]{:S(2)}, u32[]{:S(2)}) collective-permute-start(bf16[160,1280]{1,0:T(8,128)(2,1)} %fusion.47.refs_0_), channel_id=1, source_target_pairs={{0,8},{4,12},{8,0},{12,4},{16,24},{20,28},{24,16},{28,20},{1,9},{5... | collective-permute-start | bytes 1228808 | tf_op jit(solution)/shard_map/ppermute | solution.py:103
  318.4 31.5 %collective-permute-start.36 = (bf16[160,1280]{1,0:T(8,128)(2,1)}, bf16[160,1280]{1,0:T(8,128)(2,1)}, u32[]{:S(2)}, u32[]{:S(2)}) collective-permute-start(bf16[160,1280]{1,0:T(8,128)(2,1)} %fusion.47.refs_0_), channel_id=1, source_target_pairs={{0,16},{4,20},{8,24},{12,28},{16,0},{20,4},{24,8},{28,12},{1,17},{... | collective-permute-start | bytes 1228808 | tf_op jit(solution)/shard_map/ppermute | solution.py:103
  322.3 27.7 %collective-permute-start.37 = (bf16[160,1280]{1,0:T(8,128)(2,1)}, bf16[160,1280]{1,0:T(8,128)(2,1)}, u32[]{:S(2)}, u32[]{:S(2)}) collective-permute-start(bf16[160,1280]{1,0:T(8,128)(2,1)} %fusion.47.refs_0_), channel_id=1, source_target_pairs={{0,24},{4,28},{8,16},{12,20},{16,8},{20,12},{24,0},{28,4},{1,25},{... | collective-permute-start | bytes 1228808 | tf_op jit(solution)/shard_map/ppermute | solution.py:103
  337.7 32.2 %collective-permute-start.50 = (bf16[160,1280]{1,0:T(8,128)(2,1)}, bf16[160,1280]{1,0:T(8,128)(2,1)}, u32[]{:S(2)}, u32[]{:S(2)}) collective-permute-start(bf16[160,1280]{1,0:T(8,128)(2,1)} %fusion.48.refs_0_), channel_id=1, source_target_pairs={{0,8},{4,12},{8,0},{12,4},{16,24},{20,28},{24,16},{28,20},{1,9},{5... | collective-permute-start | bytes 1228808 | tf_op jit(solution)/shard_map/ppermute | solution.py:103
  338.7 31.2 %collective-permute-start.51 = (bf16[160,1280]{1,0:T(8,128)(2,1)}, bf16[160,1280]{1,0:T(8,128)(2,1)}, u32[]{:S(2)}, u32[]{:S(2)}) collective-permute-start(bf16[160,1280]{1,0:T(8,128)(2,1)} %fusion.48.refs_0_), channel_id=1, source_target_pairs={{0,16},{4,20},{8,24},{12,28},{16,0},{20,4},{24,8},{28,12},{1,17},{... | collective-permute-start | bytes 1228808 | tf_op jit(solution)/shard_map/ppermute | solution.py:103
  339.9 30.0 %collective-permute-start.52 = (bf16[160,1280]{1,0:T(8,128)(2,1)}, bf16[160,1280]{1,0:T(8,128)(2,1)}, u32[]{:S(2)}, u32[]{:S(2)}) collective-permute-start(bf16[160,1280]{1,0:T(8,128)(2,1)} %fusion.48.refs_0_), channel_id=1, source_target_pairs={{0,24},{4,28},{8,16},{12,20},{16,8},{20,12},{24,0},{28,4},{1,25},{... | collective-permute-start | bytes 1228808 | tf_op jit(solution)/shard_map/ppermute | solution.py:103
  401.5 81.5 %collective-permute-start.62 = (bf16[640,1280]{1,0:T(8,128)(2,1)}, bf16[640,1280]{1,0:T(8,128)(2,1)}, u32[]{:S(2)}, u32[]{:S(2)}) collective-permute-start(bf16[640,1280]{1,0:T(8,128)(2,1)} %slice.316), channel_id=1, source_target_pairs={{0,4},{4,0},{8,12},{12,8},{1,5},{5,1},{9,13},{13,9},{2,6},{6,2},{1... | collective-permute-start | bytes 4915208 | tf_op jit(solution)/shard_map/ppermute | solution.py:44
  427.5 22.4 %collective-permute-start.42 = (bf16[160,1280]{1,0:T(8,128)(2,1)}, bf16[160,1280]{1,0:T(8,128)(2,1)S(1)}, u32[]{:S(2)}, u32[]{:S(2)}) collective-permute-start(bf16[160,1280]{1,0:T(8,128)(2,1)} %fusion.49.refs_6_), channel_id=1, source_target_pairs={{0,2},{1,3},{2,0},{3,1},{4,6},{5,7},{6,4},{7,5},{8,10},{9,11},{10,... | collective-permute-start | bytes 1228808 | tf_op jit(solution)/shard_map/ppermute | solution.py:44
  440.8 25.1 %collective-permute-start.57 = (bf16[160,1280]{1,0:T(8,128)(2,1)S(1)}, bf16[160,1280]{1,0:T(8,128)(2,1)S(1)}, u32[]{:S(2)}, u32[]{:S(2)}) collective-permute-start(bf16[160,1280]{1,0:T(8,128)(2,1)S(1)} %fusion.50.refs_6_), channel_id=1, source_target_pairs={{0,2},{1,3},{2,0},{3,1},{4,6},{5,7},{6,4},{7,5},{8,10},{9,11},{10,... | collective-permute-start | bytes 1228808 | tf_op jit(solution)/shard_map/ppermute | solution.py:44
  449.9 24.1 %collective-permute-start.43 = (bf16[160,1280]{1,0:T(8,128)(2,1)S(1)}, bf16[160,1280]{1,0:T(8,128)(2,1)S(1)}, u32[]{:S(2)}, u32[]{:S(2)}) collective-permute-start(bf16[160,1280]{1,0:T(8,128)(2,1)S(1)} %broadcast_add_fusion.1), channel_id=1, source_target_pairs={{0,1},{1,0},{2,3},{3,2},{4,5},{5,4},{6,7},{7,6},{8,9},{9,8},{10,11... | collective-permute-start | bytes 1228808 | tf_op jit(solution)/shard_map/ppermute | solution.py:44
  486.6 137.3 %reduce-scatter.6.cloned.1.call-start = ((), (), s32[]{:S(2)}) async-start(), calls=%async_computation.8 | async-start | bytes 2048000 | tf_op jit(solution)/shard_map/reduce_scatter | solution.py:170
  492.1 136.5 %reduce-scatter.8.cloned.1.call-start = ((), (), s32[]{:S(2)}) async-start(), calls=%async_computation.9 | async-start | bytes 2048000 | tf_op jit(solution)/shard_map/reduce_scatter | solution.py:170
  538.1 49.4 %collective-permute-start.44 = (bf16[640,640]{1,0:T(8,128)(2,1)}, bf16[640,640]{1,0:T(8,128)(2,1)}, u32[]{:S(2)}, u32[]{:S(2)}) collective-permute-start(bf16[640,640]{1,0:T(8,128)(2,1)} %get-tuple-element.144), channel_id=1, source_target_pairs={{0,4},{4,0},{8,12},{12,8},{1,5},{5,1},{9,13},{13,9},{2,6},{6,2},{1... | collective-permute-start | bytes 2457608 | tf_op jit(solution)/shard_map/ppermute | solution.py:44
  538.3 49.8 %collective-permute-start.45 = (bf16[640,640]{1,0:T(8,128)(2,1)}, bf16[640,640]{1,0:T(8,128)(2,1)}, u32[]{:S(2)}, u32[]{:S(2)}) collective-permute-start(bf16[640,640]{1,0:T(8,128)(2,1)} %get-tuple-element.145), channel_id=1, source_target_pairs={{0,8},{4,12},{8,0},{12,4},{1,9},{5,13},{9,1},{13,5},{2,10},{6,14},... | collective-permute-start | bytes 2457608 | tf_op jit(solution)/shard_map/ppermute | solution.py:44
  538.6 50.5 %collective-permute-start.46 = (bf16[640,640]{1,0:T(8,128)(2,1)}, bf16[640,640]{1,0:T(8,128)(2,1)}, u32[]{:S(2)}, u32[]{:S(2)}) collective-permute-start(bf16[640,640]{1,0:T(8,128)(2,1)} %get-tuple-element.146), channel_id=1, source_target_pairs={{0,12},{4,8},{8,4},{12,0},{1,13},{5,9},{9,5},{13,1},{2,14},{6,10},... | collective-permute-start | bytes 2457608 | tf_op jit(solution)/shard_map/ppermute | solution.py:44
  582.1 84.8 %collective-permute-start.59 = (bf16[640,640]{1,0:T(8,128)(2,1)}, bf16[640,640]{1,0:T(8,128)(2,1)}, u32[]{:S(2)}, u32[]{:S(2)}) collective-permute-start(bf16[640,640]{1,0:T(8,128)(2,1)} %get-tuple-element.172), channel_id=1, source_target_pairs={{0,4},{4,0},{8,12},{12,8},{1,5},{5,1},{9,13},{13,9},{2,6},{6,2},{1... | collective-permute-start | bytes 2457608 | tf_op jit(solution)/shard_map/ppermute | solution.py:44
  586.4 80.5 %collective-permute-start.60 = (bf16[640,640]{1,0:T(8,128)(2,1)}, bf16[640,640]{1,0:T(8,128)(2,1)}, u32[]{:S(2)}, u32[]{:S(2)}) collective-permute-start(bf16[640,640]{1,0:T(8,128)(2,1)} %get-tuple-element.173), channel_id=1, source_target_pairs={{0,8},{4,12},{8,0},{12,4},{1,9},{5,13},{9,1},{13,5},{2,10},{6,14},... | collective-permute-start | bytes 2457608 | tf_op jit(solution)/shard_map/ppermute | solution.py:44
  587.4 79.5 %collective-permute-start.61 = (bf16[640,640]{1,0:T(8,128)(2,1)}, bf16[640,640]{1,0:T(8,128)(2,1)}, u32[]{:S(2)}, u32[]{:S(2)}) collective-permute-start(bf16[640,640]{1,0:T(8,128)(2,1)} %get-tuple-element.174), channel_id=1, source_target_pairs={{0,12},{4,8},{8,4},{12,0},{1,13},{5,9},{9,5},{13,1},{2,14},{6,10},... | collective-permute-start | bytes 2457608 | tf_op jit(solution)/shard_map/ppermute | solution.py:44
  588.1 29.8 %collective-permute-start.67 = (f32[3840]{0:T(1024)S(1)}, f32[3840]{0:T(1024)S(1)}, u32[]{:S(2)}, u32[]{:S(2)}) collective-permute-start(f32[3840]{0:T(1024)S(1)} %fusion.104), channel_id=1, source_target_pairs={{0,2},{1,3},{2,0},{3,1},{4,6},{5,7},{6,4},{7,5},{8,10},{9,11},{10,... | collective-permute-start | bytes 46088 | tf_op jit(solution)/shard_map/ppermute | solution.py:44
  611.8 28.2 %collective-permute-start.47 = (bf16[160,1280]{1,0:T(8,128)(2,1)}, bf16[160,1280]{1,0:T(8,128)(2,1)}, u32[]{:S(2)}, u32[]{:S(2)}) collective-permute-start(bf16[160,1280]{1,0:T(8,128)(2,1)} %get-tuple-element.150), channel_id=1, source_target_pairs={{0,1},{1,0},{2,3},{3,2},{4,5},{5,4},{6,7},{7,6},{8,9},{9,8},{10,11... | collective-permute-start | bytes 1228808 | tf_op jit(solution)/shard_map/ppermute | solution.py:44
  635.4 29.6 %all-to-all-start.1 = ((bf16[8,3,160,160]{3,2,1,0:T(8,128)(2,1)}), bf16[8,3,160,160]{3,2,1,0:T(8,128)(2,1)}, u32[]{:S(2)}, u32[]{:S(2)}) async-start(bf16[8,3,160,160]{3,2,1,0:T(8,128)(2,1)} %pad_maximum_fusion.1), calls=%async_computation.4 | async-start | bytes 3932160 | tf_op jit(solution)/shard_map/all_to_all | solution.py:180
  643.6 63.1 %collective-permute-start.48 = (bf16[160,1280]{1,0:T(8,128)(2,1)}, bf16[160,1280]{1,0:T(8,128)(2,1)}, u32[]{:S(2)}, u32[]{:S(2)}) collective-permute-start(bf16[160,1280]{1,0:T(8,128)(2,1)} %broadcast_add_fusion), channel_id=1, source_target_pairs={{0,1},{1,0},{2,3},{3,2},{4,5},{5,4},{6,7},{7,6},{8,9},{9,8},{10,11... | collective-permute-start | bytes 1228808 | tf_op jit(solution)/shard_map/ppermute | solution.py:44
  646.0 60.8 %collective-permute-start.49 = (bf16[160,1280]{1,0:T(8,128)(2,1)}, bf16[160,1280]{1,0:T(8,128)(2,1)}, u32[]{:S(2)}, u32[]{:S(2)}) collective-permute-start(bf16[160,1280]{1,0:T(8,128)(2,1)} %add_convert_fusion.3), channel_id=1, source_target_pairs={{0,2},{1,3},{2,0},{3,1},{4,6},{5,7},{6,4},{7,5},{8,10},{9,11},{10,... | collective-permute-start | bytes 1228808 | tf_op jit(solution)/shard_map/ppermute | solution.py:44
  702.7 23.4 %collective-permute-start.71 = (bf16[4,160,1280]{2,1,0:T(8,128)(2,1)}, bf16[4,160,1280]{2,1,0:T(8,128)(2,1)}, u32[]{:S(2)}, u32[]{:S(2)}) collective-permute-start(bf16[4,160,1280]{2,1,0:T(8,128)(2,1)} %fusion.27), channel_id=1, source_target_pairs={{0,4},{4,0},{8,12},{12,8},{1,5},{5,1},{9,13},{13,9},{2,6},{6,2},{1... | collective-permute-start | bytes 4915208 | tf_op jit(solution)/shard_map/ppermute | solution.py:44
  709.4 30.9 %collective-permute-start.69 = (bf16[160,1280]{1,0:T(8,128)(2,1)S(1)}, bf16[160,1280]{1,0:T(8,128)(2,1)}, u32[]{:S(2)}, u32[]{:S(2)}) collective-permute-start(bf16[160,1280]{1,0:T(8,128)(2,1)S(1)} %copy-done.49), channel_id=1, source_target_pairs={{0,2},{1,3},{2,0},{3,1},{4,6},{5,7},{6,4},{7,5},{8,10},{9,11},{10,... | collective-permute-start | bytes 1228808 | tf_op jit(solution)/shard_map/ppermute | solution.py:44
  711.3 29.0 %collective-permute-start.70 = (bf16[160,1280]{1,0:T(8,128)(2,1)S(1)}, bf16[160,1280]{1,0:T(8,128)(2,1)}, u32[]{:S(2)}, u32[]{:S(2)}) collective-permute-start(bf16[160,1280]{1,0:T(8,128)(2,1)S(1)} %copy-done.47), channel_id=1, source_target_pairs={{0,3},{1,2},{2,1},{3,0},{4,7},{5,6},{6,5},{7,4},{8,11},{9,10},{10,... | collective-permute-start | bytes 1228808 | tf_op jit(solution)/shard_map/ppermute | solution.py:44
  (161 other events, 1826.8 us)
Sparse Core Ops, SparseCore 0:
  10.5 47.0 all-gather.2
  101.1 95.7 all-gather.4
  486.7 35.7 reduce-scatter.3
  524.7 35.3 reduce-scatter.5
  562.2 36.0 reduce-scatter.7

commit v11 on v10

--- a/solution.py
+++ b/solution.py
@@ -170,13 +170,16 @@
     return [lax.psum_scatter(line, "tp", scatter_dimension=0, tiled=True) for line in lines]
 
 
-def hidden_spread(sums):
-    if not in_plane():
-        return jnp.stack(
-            [lax.psum_scatter(total, SPREAD, scatter_dimension=1, tiled=True) for total in sums]
-        )
+def hidden_pack(sums):
+    if not in_plane():
+        return jnp.stack(sums)
     part, width = sums[0].shape
-    packed = jnp.stack([total.reshape(part, 8, width // 8).transpose(1, 0, 2) for total in sums], 1)
+    return jnp.stack([total.reshape(part, 8, width // 8).transpose(1, 0, 2) for total in sums], 1)
+
+
+def hidden_spread(packed):
+    if not in_plane():
+        return lax.psum_scatter(packed, SPREAD, scatter_dimension=2, tiled=True)
     return lax.all_to_all(packed, SPREAD, 0, 0)
 
 
@@ -245,7 +248,8 @@
 
 LOG2_SCALE = math.sqrt(HDIM) * math.log2(math.e)
 LANES = 128
-KEY_TILE = 256
+KEY_TILE = 1280
+GRAD_TILE = 640
 
 
 def copies(sources, targets, sems):
@@ -410,7 +414,7 @@
             move.wait()
         keep.wait()
 
-    here = pl.ds(step * KEY_TILE, KEY_TILE)
+    here = pl.ds(step * GRAD_TILE, GRAD_TILE)
     tree = tree_ref[here]
     keys_turned = tree[:, : heads * HDIM].astype(jnp.float32).T.astype(jnp.bfloat16)
     seen = seen_tile(hot_ref, side_ref)
@@ -452,11 +456,11 @@
     whole = lambda step: (0, 0)
     return pl.pallas_call(
         lambda *refs: attend_grad_body(count, len(tops), *refs),
-        grid=(keys // KEY_TILE,),
+        grid=(keys // GRAD_TILE,),
         in_specs=[pl.BlockSpec((rows, features), whole)] * 2
         + [ANYWHERE] * (count + len(tops))
         + [
-            pl.BlockSpec((KEY_TILE, LANES), lambda step: (step, 0)),
+            pl.BlockSpec((GRAD_TILE, LANES), lambda step: (step, 0)),
             pl.BlockSpec((3, LANES, rows), lambda step: (0, 0, 0)),
             pl.BlockSpec((8, rows), whole),
             pl.BlockSpec(weight.shape, whole),
@@ -498,14 +502,20 @@
 def head_marks(features):
     row = lax.broadcasted_iota(jnp.int32, (features, LANES), 0) // HDIM
     column = lax.broadcasted_iota(jnp.int32, (features, LANES), 1)
-    return (row == column).astype(jnp.float32)
+    return (row == column).astype(jnp.float32).astype(jnp.bfloat16)
+
+
+def wide_dot(values, marks, axis):
+    high = values.astype(jnp.bfloat16)
+    rest = (values - high.astype(jnp.float32)).astype(jnp.bfloat16)
+    dims = (((1,), (axis,)), ((), ()))
+    return lax.dot_general(
+        high, marks, dims, preferred_element_type=jnp.float32
+    ) + lax.dot_general(rest, marks, dims, preferred_element_type=jnp.float32)
 
 
 def over_heads(values, marks):
-    sums = jnp.dot(values, marks, precision=HIGHEST, preferred_element_type=jnp.float32)
-    return sums, lambda heads: lax.dot_general(
-        heads, marks, (((1,), (1,)), ((), ())), precision=HIGHEST, preferred_element_type=jnp.float32
-    )
+    return wide_dot(values, marks, 0), lambda heads: wide_dot(heads, marks, 1)
 
 
 def project_body(count, *refs):
@@ -941,7 +951,8 @@
         tops.append(group_gather(closed[-1][1], "tp", products if m == last else ()))
     lines = core_sums(products)
     line_sums = hidden_line_sums([after(line, *[top[-1] for top in tops]) for line in lines])
-    spread_sums = hidden_spread(line_sums)
+    packed_sums = hidden_pack(line_sums)
+    spread_sums = hidden_spread(packed_sums)
     attended = [backward_attention(packed, front[m][1], tops[m], 1) for m in micros]
     vectors = vector_sums(
         after(
@@ -962,7 +973,7 @@
                 1 if m == last else 2,
             )
         )
-        gates = (back[-1][3], spread_sums, vectors)
+        gates = (back[-1][3], packed_sums, vectors)
     product = jnp.concatenate(
         [joint_product([back[m][1][place] for m in micros]) for place in range(2)], axis=1
     )

time: 765 us -> 723 us (0.945)
  Pallas kernels: 242 us -> 205 us
  waiting for transfers between devices: 206 us -> 194 us
    pallas_call x2, Pallas kernels: 45.2 us -> 32.2 us  [attend(): pl.pallas_call(lambda *refs: attend_body(count, *refs), grid=(keys // KEY...]
    all_to_all x1, waiting for transfers between devices: 17.1 us -> 5.38 us  [hidden_spread(): return lax.all_to_all(packed, SPREAD, 0, 0)]
    pallas_call x2, Pallas kernels: 29.6 us -> 18.5 us  [project_grad(): pl.pallas_call(lambda *refs: project_grad_body(len(tree_parts), *refs), g...]
    pallas_call x2, Pallas kernels: 77.4 us -> 69.7 us  [attend_grad(): pl.pallas_call(lambda *refs: attend_grad_body(count, len(tops), *refs), g...]
    unnamed x253 -> x245, local copies, waits for them, and re-layouts: 34.5 us -> 34.4 us
  transfers between devices with their start and end apart: 85 -> 85, of which waited for: 30 -> 32; matrix products, arithmetic and copies ran while one was open for 18% -> 20% of each run, Pallas kernels for 29% -> 26%
where the time goes in v11:
time: 723 us; the launch traced here: 716 us
  Pallas kernels  205 us (28%)
  waiting for transfers between devices  194 us (27%)
  local copies, waits for them, and re-layouts  98.4 us (14%)
  starting transfers between devices  85.4 us (12%)
  other arithmetic  68.5 us (9%)
  between operations  33.2 us (5%)
  matrix products  31.8 us (4%)
    ppermute x51, waiting for transfers between devices, swap(): lax.ppermute(value, axis, [(place, place ^ bit) for place in range(size)])  156 us
    pallas_call x2, Pallas kernels, attend_grad(): pl.pallas_call(lambda *refs: attend_grad_body(count, len(tops), *refs), g...  69.7 us
    pallas_call x2, Pallas kernels, hidden_backward(): pl.pallas_call(lambda *refs: hidden_grad_body(count, halves, *refs), in_s...  39.2 us
    ppermute x51, starting transfers between devices, swap(): lax.ppermute(value, axis, [(place, place ^ bit) for place in range(size)])  38.9 us
    ppermute x27, starting transfers between devices, hop(): lax.ppermute(value, SPREAD, [(place, place ^ bits) for place in range(8)])  36.6 us
    unnamed x245, local copies, waits for them, and re-layouts  34.4 us
    ppermute x27, waiting for transfers between devices, hop(): lax.ppermute(value, SPREAD, [(place, place ^ bits) for place in range(8)])  32.6 us
    pallas_call x2, Pallas kernels, attend(): pl.pallas_call(lambda *refs: attend_body(count, *refs), grid=(keys // KEY...  32.2 us
  transfers between devices with their start and end apart: 85, of which 32 were waited for; matrix products, arithmetic and copies ran while one was open for 20% of the time, Pallas kernels for 26%

profile of v11, /device:TPU:0, one launch (start us, length us, event | category | flops | bytes accessed | tf_op | source)
XLA Modules:
  0.0 715.6 jit_solution(15237466339241841482)
XLA Ops:
  10.9 4.1 collective-permute-start.4
  23.7 4.5 all-to-all-start
  30.1 7.8 %collective-permute-done.1.refs_2_ = bf16[160,1280]{1,0:T(8,128)(2,1)S(1)} collective-permute-done((bf16[160,1280]{1,0:T(8,128)(2,1)S(1)}, bf16[160,1280]{1,0:T(8,128)(2,1)S(1)}, u32[]{:S(2)}, u32[]{:S(2)}) %collective-permute-start.1) | collective-permute-done | bytes 409632 | tf_op jit(solution)/shard_map/ppermute | solution.py:44
  45.7 13.5 %collective-permute-done.13.refs_1_ = bf16[160,1280]{1,0:T(8,128)(2,1)S(1)} collective-permute-done((bf16[160,1280]{1,0:T(8,128)(2,1)S(1)}, bf16[160,1280]{1,0:T(8,128)(2,1)S(1)}, u32[]{:S(2)}, u32[]{:S(2)}) %collective-permute-start.13) | collective-permute-done | bytes 409632 | tf_op jit(solution)/shard_map/ppermute | solution.py:44
  60.5 7.7 %collective-permute-done.2.refs_3_ = bf16[160,1280]{1,0:T(8,128)(2,1)S(1)} collective-permute-done((bf16[160,1280]{1,0:T(8,128)(2,1)S(1)}, bf16[160,1280]{1,0:T(8,128)(2,1)S(1)}, u32[]{:S(2)}, u32[]{:S(2)}) %collective-permute-start.2) | collective-permute-done | bytes 409632 | tf_op jit(solution)/shard_map/ppermute | solution.py:44
  70.1 6.4 project.2
  81.4 10.2 %collective-permute-done.15.refs_3_ = bf16[160,1280]{1,0:T(8,128)(2,1)S(1)} collective-permute-done((bf16[160,1280]{1,0:T(8,128)(2,1)S(1)}, bf16[160,1280]{1,0:T(8,128)(2,1)S(1)}, u32[]{:S(2)}, u32[]{:S(2)}) %collective-permute-start.15) | collective-permute-done | bytes 409632 | tf_op jit(solution)/shard_map/ppermute | solution.py:44
  96.4 3.0 all_gather_reshape.3
  105.4 3.2 fusion.36
  108.6 14.0 %collective-permute-done.8.refs_3_.refs_4_ = bf16[640,640]{1,0:T(8,128)(2,1)} collective-permute-done((bf16[640,640]{1,0:T(8,128)(2,1)}, bf16[640,640]{1,0:T(8,128)(2,1)}, u32[]{:S(2)}, u32[]{:S(2)}) %collective-permute-start.8) | collective-permute-done | bytes 819232 | tf_op jit(solution)/shard_map/ppermute | solution.py:44
  123.3 4.5 reshape.760
  135.6 6.4 project.3
  145.3 16.1 %attend.2 = (bf16[640,320]{1,0:T(8,128)(2,1)S(1)}, f32[8,640]{1,0:T(8,128)S(1)}, bf16[160,1280]{1,0:T(8,128)(2,1)S(1)}, bf16[160,1280]{1,0:T(8,128)(2,1)S(1)}, b...) custom-call(bf16[640,320]{1,0:T(8,128)(2,1)S(1)} %copy-done.9, ...), custom_call_target="tpu_custom_call" | custom-call | tf_op jit(solution)/shard_map/attend/pallas_call | solution.py:345
  164.4 31.8 %collective-permute-done.10 = bf16[160,1280]{1,0:T(8,128)(2,1)S(1)} collective-permute-done((bf16[160,1280]{1,0:T(8,128)(2,1)S(1)}, bf16[160,1280]{1,0:T(8,128)(2,1)S(1)}, u32[]{:S(2)}, u32[]{:S(2)}) %collective-permute-start.10) | collective-permute-done | bytes 409632 | tf_op jit(solution)/shard_map/ppermute | solution.py:44
  201.3 16.1 %attend.3 = (bf16[640,320]{1,0:T(8,128)(2,1)S(1)}, f32[8,640]{1,0:T(8,128)S(1)}, bf16[160,1280]{1,0:T(8,128)(2,1)S(1)}, bf16[160,1280]{1,0:T(8,128)(2,1)S(1)}, b...) custom-call(bf16[640,320]{1,0:T(8,128)(2,1)S(1)} %copy-done.11, ...), custom_call_target="tpu_custom_call" | custom-call | tf_op jit(solution)/shard_map/attend/pallas_call | solution.py:345
  223.9 5.9 collective-permute-done.19
  241.3 9.1 %collective-permute-done.20 = bf16[160,1280]{1,0:T(8,128)(2,1)S(1)} collective-permute-done((bf16[160,1280]{1,0:T(8,128)(2,1)}, bf16[160,1280]{1,0:T(8,128)(2,1)S(1)}, u32[]{:S(2)}, u32[]{:S(2)}) %collective-permute-start.20) | collective-permute-done | bytes 409632 | tf_op jit(solution)/shard_map/ppermute | solution.py:44
  264.0 16.0 %hidden.2 = (bf16[160,1280]{1,0:T(8,128)(2,1)S(1)}, bf16[160,1280]{1,0:T(8,128)(2,1)}, bf16[160,1280]{1,0:T(8,128)(2,1)}, bf16[160,1280]{1,0:T(8,128)(2,1)S(1)},...) custom-call(bf16[160,1280]{1,0:T(8,128)(2,1)} %multiply_convert_fusi, ...), custom_call_target="tpu_custom_call" | custom-call | tf_op jit(solution)/shard_map/hidden/pallas_call | solution.py:697
  285.5 16.1 %hidden.3 = (bf16[160,1280]{1,0:T(8,128)(2,1)S(1)}, bf16[160,1280]{1,0:T(8,128)(2,1)S(1)}, bf16[160,1280]{1,0:T(8,128)(2,1)S(1)}, bf16[160,1280]{1,0:T(8,128)(2,...) custom-call(bf16[160,1280]{1,0:T(8,128)(2,1)} %copy-done.92, ...), custom_call_target="tpu_custom_call" | custom-call | tf_op jit(solution)/shard_map/hidden/pallas_call | solution.py:697
  316.6 6.3 collective-permute-done.33
  341.7 19.6 %hidden_grad.2 = (bf16[160,1280]{1,0:T(8,128)(2,1)}, bf16[160,1280]{1,0:T(8,128)(2,1)}, bf16[160,1280]{1,0:T(8,128)(2,1)}, bf16[160,1280]{1,0:T(8,128)(2,1)}, bf...) custom-call(bf16[160,1280]{1,0:T(8,128)(2,1)} %fusion.47.refs_0_, ...), custom_call_target="tpu_custom_call" | custom-call | tf_op jit(solution)/shard_map/hidden_grad/pallas_call | solution.py:773
  361.4 19.5 %hidden_grad.3 = (bf16[160,1280]{1,0:T(8,128)(2,1)}, bf16[160,1280]{1,0:T(8,128)(2,1)}, bf16[160,1280]{1,0:T(8,128)(2,1)}, bf16[160,1280]{1,0:T(8,128)(2,1)}, bf...) custom-call(bf16[160,1280]{1,0:T(8,128)(2,1)} %fusion.48.refs_0_, ...), custom_call_target="tpu_custom_call" | custom-call | tf_op jit(solution)/shard_map/hidden_grad/pallas_call | solution.py:773
  381.0 6.7 convolution_convert_fusion.2
  393.8 4.8 convolution_convert_fusion.1
  400.3 5.1 convolution_convert_fusion
  419.5 7.8 %collective-permute-done.54 = bf16[160,1280]{1,0:T(8,128)(2,1)} collective-permute-done((bf16[160,1280]{1,0:T(8,128)(2,1)}, bf16[160,1280]{1,0:T(8,128)(2,1)}, u32[]{:S(2)}, u32[]{:S(2)}) %collective-permute-start.54) | collective-permute-done | bytes 409632 | tf_op jit(solution)/shard_map/ppermute | solution.py:103
  438.1 3.4 collective-permute-done.42.refs_8_
  441.6 14.0 %collective-permute-done.56.refs_7_ = bf16[160,1280]{1,0:T(8,128)(2,1)S(1)} collective-permute-done((bf16[160,1280]{1,0:T(8,128)(2,1)S(1)}, bf16[160,1280]{1,0:T(8,128)(2,1)S(1)}, u32[]{:S(2)}, u32[]{:S(2)}) %collective-permute-start.56) | collective-permute-done | bytes 409632 | tf_op jit(solution)/shard_map/ppermute | solution.py:44
  457.7 8.6 %collective-permute-done.43.refs_9_ = bf16[160,1280]{1,0:T(8,128)(2,1)S(1)} collective-permute-done((bf16[160,1280]{1,0:T(8,128)(2,1)S(1)}, bf16[160,1280]{1,0:T(8,128)(2,1)S(1)}, u32[]{:S(2)}, u32[]{:S(2)}) %collective-permute-start.43) | collective-permute-done | bytes 409632 | tf_op jit(solution)/shard_map/ppermute | solution.py:44
  467.5 7.5 %collective-permute-done.58.refs_9_ = bf16[160,1280]{1,0:T(8,128)(2,1)S(1)} collective-permute-done((bf16[160,1280]{1,0:T(8,128)(2,1)S(1)}, bf16[160,1280]{1,0:T(8,128)(2,1)S(1)}, u32[]{:S(2)}, u32[]{:S(2)}) %collective-permute-start.58) | collective-permute-done | bytes 409632 | tf_op jit(solution)/shard_map/ppermute | solution.py:44
  476.3 3.4 fusion.31
  480.0 3.5 collective-permute-done.73
  488.9 34.7 %attend_grad.2 = (f32[640,320]{1,0:T(8,128)}, bf16[640,640]{1,0:T(8,128)(2,1)}, bf16[640,640]{1,0:T(8,128)(2,1)}, bf16[640,640]{1,0:T(8,128)(2,1)}, bf16[640,640]{1,0:T(8,128)(2,1)}, /*index=5*/bf16[640,1280]{1,0:T(8,128)(2,1)}) custom-call(bf16[640,320]{1,0:T(8,128)(2,1)} %copy-done.8, bf16[640,320]{1,0:T(8,128)(2,1)} %copy-done.24, ...), custom_call_target="tpu_custom_call" | custom-call | tf_op jit(solution)/shard_map/attend_grad/pallas_call | solution.py:457
  525.7 35.1 %attend_grad.3 = (f32[640,320]{1,0:T(8,128)}, bf16[640,640]{1,0:T(8,128)(2,1)}, bf16[640,640]{1,0:T(8,128)(2,1)}, bf16[640,640]{1,0:T(8,128)(2,1)}, bf16[640,640]{1,0:T(8,128)(2,1)}, /*index=5*/bf16[640,1280]{1,0:T(8,128)(2,1)}) custom-call(bf16[640,320]{1,0:T(8,128)(2,1)} %copy-done.10, bf16[640,320]{1,0:T(8,128)(2,1)} %copy-done.25, ...), custom_call_target="tpu_custom_call" | custom-call | tf_op jit(solution)/shard_map/attend_grad/pallas_call | solution.py:457
  568.6 9.7 %project_grad.2 = (bf16[640,960]{1,0:T(8,128)(2,1)S(1)}, f32[4,1,640]{2,1,0:T(1,128)S(1)}, bf16[160,1280]{1,0:T(8,128)(2,1)S(1)}, bf16[160,1280]{1,0:T(8,128)(2,...) custom-call(f32[640,320]{1,0:T(8,128)S(1)} %copy-done.21, bf16[640,640]{1,0:T(8,128)(2,1)S(1)} %copy-done.23, ...), custom_call_target="tpu_custom_call" | custom-call | tf_op jit(solution)/shard_map/project_grad/pallas_call | solution.py:621
  583.4 3.2 fusion.35
  586.7 4.3 fusion.20
  613.5 8.8 %project_grad.3 = (bf16[640,960]{1,0:T(8,128)(2,1)S(1)}, f32[4,1,640]{2,1,0:T(1,128)S(1)}, bf16[160,1280]{1,0:T(8,128)(2,1)S(1)}, bf16[160,1280]{1,0:T(8,128)(2,...) custom-call(f32[640,320]{1,0:T(8,128)S(1)} %copy-done.20, bf16[640,640]{1,0:T(8,128)(2,1)S(1)} %copy-done.22, ...), custom_call_target="tpu_custom_call" | custom-call | tf_op jit(solution)/shard_map/project_grad/pallas_call | solution.py:621
  628.3 7.6 %convolution_convert_fusion.3 = bf16[1280,960]{0,1:T(8,128)(2,1)} fusion(bf16[640,1280]{1,0:T(8,128)(2,1)} %copy-done.41, bf16[640,1280]{1,0:T(8,128)(2,1)} %copy-done.40, bf16[640,960]{1,0:T(8,128)(2,1)} %copy-done.43, bf16[640,960]{1,0:T(8,128)(2,1)} %copy-done.42), kind=kOutput, calls=%fused_computation.6 | convolution fusion | flops 3158425600 | bytes 8192000 | tf_op jit(solution)/shard_map/dot_general | solution.py:27
  635.9 4.6 copy.89
  640.5 2.9 fusion.27
  644.7 3.2 collective-permute-start.68
  655.8 3.0 pad_maximum_fusion.1
  658.8 4.7 all-to-all-start.1
  664.7 9.8 %collective-permute-done.67 = bf16[160,1280]{1,0:T(8,128)(2,1)} collective-permute-done((bf16[160,1280]{1,0:T(8,128)(2,1)S(1)}, bf16[160,1280]{1,0:T(8,128)(2,1)}, u32[]{:S(2)}, u32[]{:S(2)}) %collective-permute-start.67) | collective-permute-done | bytes 409632 | tf_op jit(solution)/shard_map/ppermute | solution.py:44
  683.9 5.4 all-to-all-done.1
  689.2 3.5 fusion.79
  699.1 7.2 %collective-permute-done.72 = bf16[160,1280]{1,0:T(8,128)(2,1)} collective-permute-done((bf16[160,1280]{1,0:T(8,128)(2,1)S(1)}, bf16[160,1280]{1,0:T(8,128)(2,1)}, u32[]{:S(2)}, u32[]{:S(2)}) %collective-permute-start.72) | collective-permute-done | bytes 409632 | tf_op jit(solution)/shard_map/ppermute | solution.py:103
  (577 shorter events, 228.5 us)
Async XLA Ops:
  7.2 61.0 %all-gather.3.cloned.1.call-start = ((), (), s32[]{:S(2)}) async-start(), calls=%async_computation.5 | async-start | bytes 3686400 | tf_op jit(solution)/shard_map/all_gather | solution.py:886
  15.0 25.2 %collective-permute-start.3 = (f32[1,2,160]{2,1,0:T(2,128)S(1)}, f32[1,2,160]{2,1,0:T(2,128)S(1)}, u32[]{:S(2)}, u32[]{:S(2)}) collective-permute-start(f32[1,2,160]{2,1,0:T(2,128)S(1)} %maximum_bitcast_fusion.2), channel_id=1, source_target_pairs={{0,1},{1,0},{2,3},{3,2},{4,5},{5,4},{6,7},{7,6},{8,9},{9,8},{10,11... | collective-permute-start | bytes 3848 | tf_op jit(solution)/shard_map/ppermute | solution.py:44
  18.0 42.4 %collective-permute-start = (bf16[160,1280]{1,0:T(8,128)(2,1)S(1)}, bf16[160,1280]{1,0:T(8,128)(2,1)S(1)}, u32[]{:S(2)}, u32[]{:S(2)}) collective-permute-start(bf16[160,1280]{1,0:T(8,128)(2,1)S(1)} %slice_bitcast_fusion.refs_0_), channel_id=1, source_target_pairs={{0,1},{1,0},{2,3},{3,2},{4,5},{5,4},{6,7},{7,6},{8,9},{9,8},{10,11... | collective-permute-start | bytes 1228808 | tf_op jit(solution)/shard_map/ppermute | solution.py:44
  23.7 69.9 %all-to-all-start = ((bf16[8,3,160,160]{3,2,1,0:T(8,128)(2,1)}), bf16[8,3,160,160]{3,2,1,0:T(8,128)(2,1)}, u32[]{:S(2)}, u32[]{:S(2)}) async-start(bf16[8,3,160,160]{3,2,1,0:T(8,128)(2,1)} %pad_maximum_fusion), calls=%async_computation | async-start | bytes 3932160 | tf_op jit(solution)/shard_map/all_to_all | solution.py:131
  28.1 170.0 %all-gather.5.cloned.1.call-start = ((), (), s32[]{:S(2)}) async-start(), calls=%async_computation.6 | async-start | bytes 6144000 | tf_op jit(solution)/shard_map/all_gather | solution.py:144
  39.3 41.7 %collective-permute-start.14 = (bf16[160,1280]{1,0:T(8,128)(2,1)S(1)}, bf16[160,1280]{1,0:T(8,128)(2,1)S(1)}, u32[]{:S(2)}, u32[]{:S(2)}) collective-permute-start(bf16[160,1280]{1,0:T(8,128)(2,1)S(1)} %add_bitcast_fusion.3.refs_0_), channel_id=1, source_target_pairs={{0,2},{1,3},{2,0},{3,1},{4,6},{5,7},{6,4},{7,5},{8,10},{9,11},{10,... | collective-permute-start | bytes 1228808 | tf_op jit(solution)/shard_map/ppermute | solution.py:44
  40.2 27.9 %collective-permute-start.2 = (bf16[160,1280]{1,0:T(8,128)(2,1)S(1)}, bf16[160,1280]{1,0:T(8,128)(2,1)S(1)}, u32[]{:S(2)}, u32[]{:S(2)}) collective-permute-start(bf16[160,1280]{1,0:T(8,128)(2,1)S(1)} %collective-permute-done.1.refs_2_), channel_id=1, source_target_pairs={{0,1},{1,0},{2,3},{3,2},{4,5},{5,4},{6,7},{7,6},{8,9},{9,8},{10,11... | collective-permute-start | bytes 1228808 | tf_op jit(solution)/shard_map/ppermute | solution.py:44
  99.4 504.3 %reduce-scatter.4.cloned.1.call-start = ((), (), s32[]{:S(2)}) async-start(), calls=%async_computation.7 | async-start | bytes 2048000 | tf_op jit(solution)/shard_map/reduce_scatter | solution.py:170
  108.6 36.6 %collective-permute-start.7 = (bf16[640,640]{1,0:T(8,128)(2,1)}, bf16[640,640]{1,0:T(8,128)(2,1)}, u32[]{:S(2)}, u32[]{:S(2)}) collective-permute-start(bf16[640,640]{1,0:T(8,128)(2,1)} %get-tuple-element.115.refs_1_.refs_2_), channel_id=1, source_target_pairs={{0,4},{4,0},{8,12},{12,8},{1,5},{5,1},{9,13},{13,9},{2,6},{6,2},{1... | collective-permute-start | bytes 2457608 | tf_op jit(solution)/shard_map/ppermute | solution.py:44
  122.6 22.6 %collective-permute-start.9 = (bf16[640,640]{1,0:T(8,128)(2,1)}, bf16[640,640]{1,0:T(8,128)(2,1)}, u32[]{:S(2)}, u32[]{:S(2)}) collective-permute-start(bf16[640,640]{1,0:T(8,128)(2,1)} %collective-permute-done.8.refs_3_.refs_4_), channel_id=1, source_target_pairs={{0,4},{4,0},{8,12},{12,8},{1,5},{5,1},{9,13},{13,9},{2,6},{6,2},{1... | collective-permute-start | bytes 2457608 | tf_op jit(solution)/shard_map/ppermute | solution.py:44
  162.9 33.3 %collective-permute-start.10 = (bf16[160,1280]{1,0:T(8,128)(2,1)S(1)}, bf16[160,1280]{1,0:T(8,128)(2,1)S(1)}, u32[]{:S(2)}, u32[]{:S(2)}) collective-permute-start(bf16[160,1280]{1,0:T(8,128)(2,1)S(1)} %get-tuple-element.118), channel_id=1, source_target_pairs={{0,1},{1,0},{2,3},{3,2},{4,5},{5,4},{6,7},{7,6},{8,9},{9,8},{10,11... | collective-permute-start | bytes 1228808 | tf_op jit(solution)/shard_map/ppermute | solution.py:44
  163.9 37.3 %collective-permute-start.16 = (bf16[640,640]{1,0:T(8,128)(2,1)}, bf16[640,640]{1,0:T(8,128)(2,1)S(1)}, u32[]{:S(2)}, u32[]{:S(2)}) collective-permute-start(bf16[640,640]{1,0:T(8,128)(2,1)} %get-tuple-element.121.refs_1_.refs_2_), channel_id=1, source_target_pairs={{0,4},{4,0},{8,12},{12,8},{1,5},{5,1},{9,13},{13,9},{2,6},{6,2},{1... | collective-permute-start | bytes 2457608 | tf_op jit(solution)/shard_map/ppermute | solution.py:44
  164.3 36.9 %collective-permute-start.18 = (bf16[640,640]{1,0:T(8,128)(2,1)}, bf16[640,640]{1,0:T(8,128)(2,1)}, u32[]{:S(2)}, u32[]{:S(2)}) collective-permute-start(bf16[640,640]{1,0:T(8,128)(2,1)} %collective-permute-done.17.refs_3_.refs_4_), channel_id=1, source_target_pairs={{0,4},{4,0},{8,12},{12,8},{1,5},{5,1},{9,13},{13,9},{2,6},{6,2},{1... | collective-permute-start | bytes 2457608 | tf_op jit(solution)/shard_map/ppermute | solution.py:44
  198.2 65.8 %collective-permute-start.25 = (bf16[4,3,160,1280]{3,2,1,0:T(8,128)(2,1)}, bf16[4,3,160,1280]{3,2,1,0:T(8,128)(2,1)}, u32[]{:S(2)}, u32[]{:S(2)}) collective-permute-start(bf16[4,3,160,1280]{3,2,1,0:T(8,128)(2,1)} %all-gather.5.cloned.1.call-done.refs_4_), channel_id=1, source_target_pairs={{0,4},{4,0},{8,12},{12,8},{1,5},{5,1},{9,13},{13,9},{2,6},{6,2},{1... | collective-permute-start | bytes 14745608 | tf_op jit(solution)/shard_map/ppermute | solution.py:44
  236.5 22.9 %collective-permute-start.22 = (bf16[160,1280]{1,0:T(8,128)(2,1)}, bf16[160,1280]{1,0:T(8,128)(2,1)}, u32[]{:S(2)}, u32[]{:S(2)}) collective-permute-start(bf16[160,1280]{1,0:T(8,128)(2,1)} %multiply_convert_fusion.3.refs_0_), channel_id=1, source_target_pairs={{0,8},{4,12},{8,0},{12,4},{16,24},{20,28},{24,16},{28,20},{1,9},{5... | collective-permute-start | bytes 1228808 | tf_op jit(solution)/shard_map/ppermute | solution.py:103
  237.9 23.0 %collective-permute-start.23 = (bf16[160,1280]{1,0:T(8,128)(2,1)}, bf16[160,1280]{1,0:T(8,128)(2,1)}, u32[]{:S(2)}, u32[]{:S(2)}) collective-permute-start(bf16[160,1280]{1,0:T(8,128)(2,1)} %multiply_convert_fusion.3.refs_0_), channel_id=1, source_target_pairs={{0,16},{4,20},{8,24},{12,28},{16,0},{20,4},{24,8},{28,12},{1,17},{... | collective-permute-start | bytes 1228808 | tf_op jit(solution)/shard_map/ppermute | solution.py:103
  257.7 25.3 %collective-permute-start.29 = (bf16[160,1280]{1,0:T(8,128)(2,1)S(1)}, bf16[160,1280]{1,0:T(8,128)(2,1)S(1)}, u32[]{:S(2)}, u32[]{:S(2)}) collective-permute-start(bf16[160,1280]{1,0:T(8,128)(2,1)S(1)} %multiply_convert_fusion.2.refs_0_), channel_id=1, source_target_pairs={{0,8},{4,12},{8,0},{12,4},{16,24},{20,28},{24,16},{28,20},{1,9},{5... | collective-permute-start | bytes 1228808 | tf_op jit(solution)/shard_map/ppermute | solution.py:103
  259.4 25.3 %collective-permute-start.30 = (bf16[160,1280]{1,0:T(8,128)(2,1)S(1)}, bf16[160,1280]{1,0:T(8,128)(2,1)S(1)}, u32[]{:S(2)}, u32[]{:S(2)}) collective-permute-start(bf16[160,1280]{1,0:T(8,128)(2,1)S(1)} %multiply_convert_fusion.2.refs_0_), channel_id=1, source_target_pairs={{0,16},{4,20},{8,24},{12,28},{16,0},{20,4},{24,8},{28,12},{1,17},{... | collective-permute-start | bytes 1228808 | tf_op jit(solution)/shard_map/ppermute | solution.py:103
  260.9 24.6 %collective-permute-start.31 = (bf16[160,1280]{1,0:T(8,128)(2,1)S(1)}, bf16[160,1280]{1,0:T(8,128)(2,1)}, u32[]{:S(2)}, u32[]{:S(2)}) collective-permute-start(bf16[160,1280]{1,0:T(8,128)(2,1)S(1)} %multiply_convert_fusion.2.refs_0_), channel_id=1, source_target_pairs={{0,24},{4,28},{8,16},{12,20},{16,8},{20,12},{24,0},{28,4},{1,25},{... | collective-permute-start | bytes 1228808 | tf_op jit(solution)/shard_map/ppermute | solution.py:103
  280.0 24.7 %collective-permute-start.26 = (bf16[160,1280]{1,0:T(8,128)(2,1)}, bf16[160,1280]{1,0:T(8,128)(2,1)}, u32[]{:S(2)}, u32[]{:S(2)}) collective-permute-start(bf16[160,1280]{1,0:T(8,128)(2,1)} %get-tuple-element.127), channel_id=1, source_target_pairs={{0,8},{4,12},{8,0},{12,4},{16,24},{20,28},{24,16},{28,20},{1,9},{5... | collective-permute-start | bytes 1228808 | tf_op jit(solution)/shard_map/ppermute | solution.py:103
  281.4 23.8 %collective-permute-start.27 = (bf16[160,1280]{1,0:T(8,128)(2,1)}, bf16[160,1280]{1,0:T(8,128)(2,1)}, u32[]{:S(2)}, u32[]{:S(2)}) collective-permute-start(bf16[160,1280]{1,0:T(8,128)(2,1)} %get-tuple-element.128), channel_id=1, source_target_pairs={{0,16},{4,20},{8,24},{12,28},{16,0},{20,4},{24,8},{28,12},{1,17},{... | collective-permute-start | bytes 1228808 | tf_op jit(solution)/shard_map/ppermute | solution.py:103
  308.9 22.9 %collective-permute-start.35 = (bf16[160,1280]{1,0:T(8,128)(2,1)}, bf16[160,1280]{1,0:T(8,128)(2,1)}, u32[]{:S(2)}, u32[]{:S(2)}) collective-permute-start(bf16[160,1280]{1,0:T(8,128)(2,1)} %fusion.47.refs_0_), channel_id=1, source_target_pairs={{0,8},{4,12},{8,0},{12,4},{16,24},{20,28},{24,16},{28,20},{1,9},{5... | collective-permute-start | bytes 1228808 | tf_op jit(solution)/shard_map/ppermute | solution.py:103
  310.3 30.2 %collective-permute-start.36 = (bf16[160,1280]{1,0:T(8,128)(2,1)}, bf16[160,1280]{1,0:T(8,128)(2,1)}, u32[]{:S(2)}, u32[]{:S(2)}) collective-permute-start(bf16[160,1280]{1,0:T(8,128)(2,1)} %fusion.47.refs_0_), channel_id=1, source_target_pairs={{0,16},{4,20},{8,24},{12,28},{16,0},{20,4},{24,8},{28,12},{1,17},{... | collective-permute-start | bytes 1228808 | tf_op jit(solution)/shard_map/ppermute | solution.py:103
  314.3 27.5 %collective-permute-start.37 = (bf16[160,1280]{1,0:T(8,128)(2,1)}, bf16[160,1280]{1,0:T(8,128)(2,1)}, u32[]{:S(2)}, u32[]{:S(2)}) collective-permute-start(bf16[160,1280]{1,0:T(8,128)(2,1)} %fusion.47.refs_0_), channel_id=1, source_target_pairs={{0,24},{4,28},{8,16},{12,20},{16,8},{20,12},{24,0},{28,4},{1,25},{... | collective-permute-start | bytes 1228808 | tf_op jit(solution)/shard_map/ppermute | solution.py:103
  329.3 32.1 %collective-permute-start.50 = (bf16[160,1280]{1,0:T(8,128)(2,1)}, bf16[160,1280]{1,0:T(8,128)(2,1)}, u32[]{:S(2)}, u32[]{:S(2)}) collective-permute-start(bf16[160,1280]{1,0:T(8,128)(2,1)} %fusion.48.refs_0_), channel_id=1, source_target_pairs={{0,8},{4,12},{8,0},{12,4},{16,24},{20,28},{24,16},{28,20},{1,9},{5... | collective-permute-start | bytes 1228808 | tf_op jit(solution)/shard_map/ppermute | solution.py:103
  330.6 30.8 %collective-permute-start.51 = (bf16[160,1280]{1,0:T(8,128)(2,1)}, bf16[160,1280]{1,0:T(8,128)(2,1)}, u32[]{:S(2)}, u32[]{:S(2)}) collective-permute-start(bf16[160,1280]{1,0:T(8,128)(2,1)} %fusion.48.refs_0_), channel_id=1, source_target_pairs={{0,16},{4,20},{8,24},{12,28},{16,0},{20,4},{24,8},{28,12},{1,17},{... | collective-permute-start | bytes 1228808 | tf_op jit(solution)/shard_map/ppermute | solution.py:103
  331.9 29.5 %collective-permute-start.52 = (bf16[160,1280]{1,0:T(8,128)(2,1)}, bf16[160,1280]{1,0:T(8,128)(2,1)}, u32[]{:S(2)}, u32[]{:S(2)}) collective-permute-start(bf16[160,1280]{1,0:T(8,128)(2,1)} %fusion.48.refs_0_), channel_id=1, source_target_pairs={{0,24},{4,28},{8,16},{12,20},{16,8},{20,12},{24,0},{28,4},{1,25},{... | collective-permute-start | bytes 1228808 | tf_op jit(solution)/shard_map/ppermute | solution.py:103
  393.0 83.1 %collective-permute-start.62 = (bf16[640,1280]{1,0:T(8,128)(2,1)}, bf16[640,1280]{1,0:T(8,128)(2,1)}, u32[]{:S(2)}, u32[]{:S(2)}) collective-permute-start(bf16[640,1280]{1,0:T(8,128)(2,1)} %slice.316), channel_id=1, source_target_pairs={{0,4},{4,0},{8,12},{12,8},{1,5},{5,1},{9,13},{13,9},{2,6},{6,2},{1... | collective-permute-start | bytes 4915208 | tf_op jit(solution)/shard_map/ppermute | solution.py:44
  435.0 22.6 %collective-permute-start.57 = (bf16[160,1280]{1,0:T(8,128)(2,1)S(1)}, bf16[160,1280]{1,0:T(8,128)(2,1)S(1)}, u32[]{:S(2)}, u32[]{:S(2)}) collective-permute-start(bf16[160,1280]{1,0:T(8,128)(2,1)S(1)} %fusion.50.refs_6_), channel_id=1, source_target_pairs={{0,2},{1,3},{2,0},{3,1},{4,6},{5,7},{6,4},{7,5},{8,10},{9,11},{10,... | collective-permute-start | bytes 1228808 | tf_op jit(solution)/shard_map/ppermute | solution.py:44
  441.5 24.8 %collective-permute-start.43 = (bf16[160,1280]{1,0:T(8,128)(2,1)S(1)}, bf16[160,1280]{1,0:T(8,128)(2,1)S(1)}, u32[]{:S(2)}, u32[]{:S(2)}) collective-permute-start(bf16[160,1280]{1,0:T(8,128)(2,1)S(1)} %broadcast_add_fusion.1), channel_id=1, source_target_pairs={{0,1},{1,0},{2,3},{3,2},{4,5},{5,4},{6,7},{7,6},{8,9},{9,8},{10,11... | collective-permute-start | bytes 1228808 | tf_op jit(solution)/shard_map/ppermute | solution.py:44
  479.7 170.5 %reduce-scatter.6.cloned.1.call-start = ((), (), s32[]{:S(2)}) async-start(), calls=%async_computation.8 | async-start | bytes 2048000 | tf_op jit(solution)/shard_map/reduce_scatter | solution.py:170
  485.2 167.8 %reduce-scatter.8.cloned.1.call-start = ((), (), s32[]{:S(2)}) async-start(), calls=%async_computation.9 | async-start | bytes 2048000 | tf_op jit(solution)/shard_map/reduce_scatter | solution.py:170
  487.4 93.5 %collective-permute-start.74 = (bf16[640,1280]{1,0:T(8,128)(2,1)}, bf16[640,1280]{1,0:T(8,128)(2,1)}, u32[]{:S(2)}, u32[]{:S(2)}) collective-permute-start(bf16[640,1280]{1,0:T(8,128)(2,1)} %slice.326), channel_id=1, source_target_pairs={{0,4},{4,0},{8,12},{12,8},{1,5},{5,1},{9,13},{13,9},{2,6},{6,2},{1... | collective-permute-start | bytes 4915208 | tf_op jit(solution)/shard_map/ppermute | solution.py:44
  488.5 37.0 %collective-permute-start.63 = (f32[2,4,160]{2,1,0:T(4,128)S(1)}, f32[2,4,160]{2,1,0:T(4,128)S(1)}, u32[]{:S(2)}, u32[]{:S(2)}) collective-permute-start(f32[2,4,160]{2,1,0:T(4,128)S(1)} %slice_bitcast_fusion.2), channel_id=1, source_target_pairs={{0,4},{4,0},{8,12},{12,8},{1,5},{5,1},{9,13},{13,9},{2,6},{6,2},{1... | collective-permute-start | bytes 15368 | tf_op jit(solution)/shard_map/ppermute | solution.py:44
  523.6 43.0 %collective-permute-start.44 = (bf16[640,640]{1,0:T(8,128)(2,1)}, bf16[640,640]{1,0:T(8,128)(2,1)}, u32[]{:S(2)}, u32[]{:S(2)}) collective-permute-start(bf16[640,640]{1,0:T(8,128)(2,1)} %get-tuple-element.144), channel_id=1, source_target_pairs={{0,4},{4,0},{8,12},{12,8},{1,5},{5,1},{9,13},{13,9},{2,6},{6,2},{1... | collective-permute-start | bytes 2457608 | tf_op jit(solution)/shard_map/ppermute | solution.py:44
  523.8 44.3 %collective-permute-start.45 = (bf16[640,640]{1,0:T(8,128)(2,1)}, bf16[640,640]{1,0:T(8,128)(2,1)}, u32[]{:S(2)}, u32[]{:S(2)}) collective-permute-start(bf16[640,640]{1,0:T(8,128)(2,1)} %get-tuple-element.145), channel_id=1, source_target_pairs={{0,8},{4,12},{8,0},{12,4},{1,9},{5,13},{9,1},{13,5},{2,10},{6,14},... | collective-permute-start | bytes 2457608 | tf_op jit(solution)/shard_map/ppermute | solution.py:44
  525.2 43.3 %collective-permute-start.46 = (bf16[640,640]{1,0:T(8,128)(2,1)}, bf16[640,640]{1,0:T(8,128)(2,1)}, u32[]{:S(2)}, u32[]{:S(2)}) collective-permute-start(bf16[640,640]{1,0:T(8,128)(2,1)} %get-tuple-element.146), channel_id=1, source_target_pairs={{0,12},{4,8},{8,4},{12,0},{1,13},{5,9},{9,5},{13,1},{2,14},{6,10},... | collective-permute-start | bytes 2457608 | tf_op jit(solution)/shard_map/ppermute | solution.py:44
  566.6 43.1 %collective-permute-start.59 = (bf16[640,640]{1,0:T(8,128)(2,1)}, bf16[640,640]{1,0:T(8,128)(2,1)}, u32[]{:S(2)}, u32[]{:S(2)}) collective-permute-start(bf16[640,640]{1,0:T(8,128)(2,1)} %get-tuple-element.172), channel_id=1, source_target_pairs={{0,4},{4,0},{8,12},{12,8},{1,5},{5,1},{9,13},{13,9},{2,6},{6,2},{1... | collective-permute-start | bytes 2457608 | tf_op jit(solution)/shard_map/ppermute | solution.py:44
  566.6 43.1 %collective-permute-start.60 = (bf16[640,640]{1,0:T(8,128)(2,1)}, bf16[640,640]{1,0:T(8,128)(2,1)}, u32[]{:S(2)}, u32[]{:S(2)}) collective-permute-start(bf16[640,640]{1,0:T(8,128)(2,1)} %get-tuple-element.173), channel_id=1, source_target_pairs={{0,8},{4,12},{8,0},{12,4},{1,9},{5,13},{9,1},{13,5},{2,10},{6,14},... | collective-permute-start | bytes 2457608 | tf_op jit(solution)/shard_map/ppermute | solution.py:44
  568.2 41.5 %collective-permute-start.61 = (bf16[640,640]{1,0:T(8,128)(2,1)}, bf16[640,640]{1,0:T(8,128)(2,1)}, u32[]{:S(2)}, u32[]{:S(2)}) collective-permute-start(bf16[640,640]{1,0:T(8,128)(2,1)} %get-tuple-element.174), channel_id=1, source_target_pairs={{0,12},{4,8},{8,4},{12,0},{1,13},{5,9},{9,5},{13,1},{2,14},{6,10},... | collective-permute-start | bytes 2457608 | tf_op jit(solution)/shard_map/ppermute | solution.py:44
  568.5 24.8 %collective-permute-start.65 = (f32[3840]{0:T(1024)S(1)}, f32[3840]{0:T(1024)S(1)}, u32[]{:S(2)}, u32[]{:S(2)}) collective-permute-start(f32[3840]{0:T(1024)S(1)} %fusion.104), channel_id=1, source_target_pairs={{0,2},{1,3},{2,0},{3,1},{4,6},{5,7},{6,4},{7,5},{8,10},{9,11},{10,... | collective-permute-start | bytes 46088 | tf_op jit(solution)/shard_map/ppermute | solution.py:44
  598.5 46.2 %collective-permute-start.48 = (bf16[160,1280]{1,0:T(8,128)(2,1)}, bf16[160,1280]{1,0:T(8,128)(2,1)}, u32[]{:S(2)}, u32[]{:S(2)}) collective-permute-start(bf16[160,1280]{1,0:T(8,128)(2,1)} %broadcast_add_fusion), channel_id=1, source_target_pairs={{0,1},{1,0},{2,3},{3,2},{4,5},{5,4},{6,7},{7,6},{8,9},{9,8},{10,11... | collective-permute-start | bytes 1228808 | tf_op jit(solution)/shard_map/ppermute | solution.py:44
  601.2 46.7 %collective-permute-start.49 = (bf16[160,1280]{1,0:T(8,128)(2,1)}, bf16[160,1280]{1,0:T(8,128)(2,1)}, u32[]{:S(2)}, u32[]{:S(2)}) collective-permute-start(bf16[160,1280]{1,0:T(8,128)(2,1)} %add_convert_fusion.3), channel_id=1, source_target_pairs={{0,2},{1,3},{2,0},{3,1},{4,6},{5,7},{6,4},{7,5},{8,10},{9,11},{10,... | collective-permute-start | bytes 1228808 | tf_op jit(solution)/shard_map/ppermute | solution.py:44
  643.4 32.6 %collective-permute-start.69 = (bf16[4,160,1280]{2,1,0:T(8,128)(2,1)}, bf16[4,160,1280]{2,1,0:T(8,128)(2,1)}, u32[]{:S(2)}, u32[]{:S(2)}) collective-permute-start(bf16[4,160,1280]{2,1,0:T(8,128)(2,1)} %fusion.27), channel_id=1, source_target_pairs={{0,4},{4,0},{8,12},{12,8},{1,5},{5,1},{9,13},{13,9},{2,6},{6,2},{1... | collective-permute-start | bytes 4915208 | tf_op jit(solution)/shard_map/ppermute | solution.py:44
  643.6 30.9 %collective-permute-start.67 = (bf16[160,1280]{1,0:T(8,128)(2,1)S(1)}, bf16[160,1280]{1,0:T(8,128)(2,1)}, u32[]{:S(2)}, u32[]{:S(2)}) collective-permute-start(bf16[160,1280]{1,0:T(8,128)(2,1)S(1)} %copy-done.47), channel_id=1, source_target_pairs={{0,2},{1,3},{2,0},{3,1},{4,6},{5,7},{6,4},{7,5},{8,10},{9,11},{10,... | collective-permute-start | bytes 1228808 | tf_op jit(solution)/shard_map/ppermute | solution.py:44
  644.7 29.8 %collective-permute-start.68 = (bf16[160,1280]{1,0:T(8,128)(2,1)S(1)}, bf16[160,1280]{1,0:T(8,128)(2,1)}, u32[]{:S(2)}, u32[]{:S(2)}) collective-permute-start(bf16[160,1280]{1,0:T(8,128)(2,1)S(1)} %copy-done.45), channel_id=1, source_target_pairs={{0,3},{1,2},{2,1},{3,0},{4,7},{5,6},{6,5},{7,4},{8,11},{9,10},{10,... | collective-permute-start | bytes 1228808 | tf_op jit(solution)/shard_map/ppermute | solution.py:44
  658.8 30.5 %all-to-all-start.1 = ((bf16[8,3,160,160]{3,2,1,0:T(8,128)(2,1)}), bf16[8,3,160,160]{3,2,1,0:T(8,128)(2,1)}, u32[]{:S(2)}, u32[]{:S(2)}) async-start(bf16[8,3,160,160]{3,2,1,0:T(8,128)(2,1)} %pad_maximum_fusion.1), calls=%async_computation.4 | async-start | bytes 3932160 | tf_op jit(solution)/shard_map/all_to_all | solution.py:183
  680.9 25.5 %collective-permute-start.72 = (bf16[160,1280]{1,0:T(8,128)(2,1)S(1)}, bf16[160,1280]{1,0:T(8,128)(2,1)}, u32[]{:S(2)}, u32[]{:S(2)}) collective-permute-start(bf16[160,1280]{1,0:T(8,128)(2,1)S(1)} %get-tuple-element.296), channel_id=1, source_target_pairs={{0,24},{4,28},{8,16},{12,20},{16,8},{20,12},{24,0},{28,4},{1,25},{... | collective-permute-start | bytes 1228808 | tf_op jit(solution)/shard_map/ppermute | solution.py:103
  (157 other events, 1930.3 us)
Sparse Core Ops, SparseCore 0:
  10.5 46.9 all-gather.2
  99.5 97.5 all-gather.4
  479.8 34.4 reduce-scatter.3
  516.6 35.3 reduce-scatter.5
  586.8 53.4 reduce-scatter.7

commit v12 on v11

--- a/solution.py
+++ b/solution.py
@@ -497,6 +497,17 @@
     same = query_hot
     before = ((labels[:, None] >= HDIM) & (labels[:, None] - HDIM <= off_query[None, :])).astype(jnp.float32)
     return hot, jnp.stack([strict, same, before]).astype(jnp.bfloat16)
+
+
+def hold(value, *gates):
+    return pl.pallas_call(
+        lambda *refs: None,
+        in_specs=[ANYWHERE] * (1 + len(gates)),
+        out_specs=ANYWHERE,
+        out_shape=jax.ShapeDtypeStruct(value.shape, value.dtype),
+        input_output_aliases={0: 0},
+        name="hold",
+    )(value, *gates)
 
 
 def head_marks(features):
@@ -933,6 +944,11 @@
     for m in micros:
         hidden_group, hidden_mixed = forwards[m][1][0], forwards[m][1][3]
         top_group, up_low, gate_low = backwards[m][1][:3]
+        if m == last:
+            sent = backwards[0][0][len(backwards[0][0]) // 4]
+            up_low, gate_low, hidden_mixed = (
+                hold(value, sent) for value in (up_low, gate_low, hidden_mixed)
+            )
         joined.append(((up_low, hidden_group), (gate_low, hidden_group), (hidden_mixed, top_group)))
     products = [
         joint_product([joined[m][place] for m in micros]).astype(jnp.bfloat16)

time: 723 us -> 717 us (level)
  waiting for transfers between devices: 194 us -> 175 us
    ppermute x51, waiting for transfers between devices: 156 us -> 142 us  [swap(): lax.ppermute(value, axis, [(place, place ^ bit) for place in range(size)])]
    unnamed x245 -> x219, local copies, waits for them, and re-layouts: 34.4 us -> 34.7 us
  transfers between devices with their start and end apart: 85 -> 85, of which waited for: 32 -> 25; matrix products, arithmetic and copies ran while one was open for 20% -> 23% of each run, Pallas kernels for 26% -> 29%
where the time goes in v12:
time: 717 us; the launch traced here: 709 us
  Pallas kernels  204 us (28%)
  waiting for transfers between devices  175 us (24%)
  local copies, waits for them, and re-layouts  104 us (15%)
  starting transfers between devices  89.3 us (12%)
  other arithmetic  65.9 us (9%)
  matrix products  37.5 us (5%)
  between operations  32.9 us (5%)
    ppermute x51, waiting for transfers between devices, swap(): lax.ppermute(value, axis, [(place, place ^ bit) for place in range(size)])  142 us
    pallas_call x2, Pallas kernels, attend_grad(): pl.pallas_call(lambda *refs: attend_grad_body(count, len(tops), *refs), g...  69.2 us
    ppermute x51, starting transfers between devices, swap(): lax.ppermute(value, axis, [(place, place ^ bit) for place in range(size)])  43 us
    pallas_call x2, Pallas kernels, hidden_backward(): pl.pallas_call(lambda *refs: hidden_grad_body(count, halves, *refs), in_s...  39.2 us
    ppermute x27, starting transfers between devices, hop(): lax.ppermute(value, SPREAD, [(place, place ^ bits) for place in range(8)])  36.4 us
    unnamed x219, local copies, waits for them, and re-layouts  34.7 us
    dot_general x5, matrix products, contract_rows(): lax.dot_general(former, latter, (((0,), (0,)), ((), ())), preferred_eleme...  34.2 us
    pallas_call x2, Pallas kernels, attend(): pl.pallas_call(lambda *refs: attend_body(count, *refs), grid=(keys // KEY...  32.2 us
  transfers between devices with their start and end apart: 85, of which 25 were waited for; matrix products, arithmetic and copies ran while one was open for 23% of the time, Pallas kernels for 29%

profile of v12, /device:TPU:0, one launch (start us, length us, event | category | flops | bytes accessed | tf_op | source)
XLA Modules:
  0.0 708.7 jit_solution(18197316401338861671)
XLA Ops:
  10.9 4.1 collective-permute-start.4
  21.7 4.5 all-to-all-start
  28.1 9.8 %collective-permute-done.1.refs_2_ = bf16[160,1280]{1,0:T(8,128)(2,1)S(1)} collective-permute-done((bf16[160,1280]{1,0:T(8,128)(2,1)S(1)}, bf16[160,1280]{1,0:T(8,128)(2,1)S(1)}, u32[]{:S(2)}, u32[]{:S(2)}) %collective-permute-start.1) | collective-permute-done | bytes 409632 | tf_op jit(solution)/shard_map/ppermute | solution.py:44
  45.7 13.5 %collective-permute-done.13.refs_1_ = bf16[160,1280]{1,0:T(8,128)(2,1)S(1)} collective-permute-done((bf16[160,1280]{1,0:T(8,128)(2,1)S(1)}, bf16[160,1280]{1,0:T(8,128)(2,1)S(1)}, u32[]{:S(2)}, u32[]{:S(2)}) %collective-permute-start.13) | collective-permute-done | bytes 409632 | tf_op jit(solution)/shard_map/ppermute | solution.py:44
  60.4 7.8 %collective-permute-done.2.refs_3_ = bf16[160,1280]{1,0:T(8,128)(2,1)S(1)} collective-permute-done((bf16[160,1280]{1,0:T(8,128)(2,1)S(1)}, bf16[160,1280]{1,0:T(8,128)(2,1)S(1)}, u32[]{:S(2)}, u32[]{:S(2)}) %collective-permute-start.2) | collective-permute-done | bytes 409632 | tf_op jit(solution)/shard_map/ppermute | solution.py:44
  70.1 6.4 project.2
  81.4 10.2 %collective-permute-done.15.refs_3_ = bf16[160,1280]{1,0:T(8,128)(2,1)S(1)} collective-permute-done((bf16[160,1280]{1,0:T(8,128)(2,1)S(1)}, bf16[160,1280]{1,0:T(8,128)(2,1)S(1)}, u32[]{:S(2)}, u32[]{:S(2)}) %collective-permute-start.15) | collective-permute-done | bytes 409632 | tf_op jit(solution)/shard_map/ppermute | solution.py:44
  97.7 4.5 all_gather_reshape.3
  108.3 3.1 fusion.36
  111.4 14.1 %collective-permute-done.8.refs_3_.refs_4_ = bf16[640,640]{1,0:T(8,128)(2,1)} collective-permute-done((bf16[640,640]{1,0:T(8,128)(2,1)}, bf16[640,640]{1,0:T(8,128)(2,1)}, u32[]{:S(2)}, u32[]{:S(2)}) %collective-permute-start.8) | collective-permute-done | bytes 819232 | tf_op jit(solution)/shard_map/ppermute | solution.py:44
  126.2 4.5 reshape.760
  138.5 6.4 project.3
  148.1 16.1 %attend.2 = (bf16[640,320]{1,0:T(8,128)(2,1)S(1)}, f32[8,640]{1,0:T(8,128)S(1)}, bf16[160,1280]{1,0:T(8,128)(2,1)S(1)}, bf16[160,1280]{1,0:T(8,128)(2,1)S(1)}, b...) custom-call(bf16[640,320]{1,0:T(8,128)(2,1)S(1)} %copy-done.9, ...), custom_call_target="tpu_custom_call" | custom-call | tf_op jit(solution)/shard_map/attend/pallas_call | solution.py:345
  167.3 31.7 %collective-permute-done.10 = bf16[160,1280]{1,0:T(8,128)(2,1)S(1)} collective-permute-done((bf16[160,1280]{1,0:T(8,128)(2,1)S(1)}, bf16[160,1280]{1,0:T(8,128)(2,1)S(1)}, u32[]{:S(2)}, u32[]{:S(2)}) %collective-permute-start.10) | collective-permute-done | bytes 409632 | tf_op jit(solution)/shard_map/ppermute | solution.py:44
  204.3 16.1 %attend.3 = (bf16[640,320]{1,0:T(8,128)(2,1)S(1)}, f32[8,640]{1,0:T(8,128)S(1)}, bf16[160,1280]{1,0:T(8,128)(2,1)S(1)}, bf16[160,1280]{1,0:T(8,128)(2,1)S(1)}, b...) custom-call(bf16[640,320]{1,0:T(8,128)(2,1)S(1)} %copy-done.11, ...), custom_call_target="tpu_custom_call" | custom-call | tf_op jit(solution)/shard_map/attend/pallas_call | solution.py:345
  220.6 3.4 collective-permute-done.12
  227.0 5.8 collective-permute-done.19
  241.6 12.4 %collective-permute-done.20 = bf16[160,1280]{1,0:T(8,128)(2,1)S(1)} collective-permute-done((bf16[160,1280]{1,0:T(8,128)(2,1)}, bf16[160,1280]{1,0:T(8,128)(2,1)S(1)}, u32[]{:S(2)}, u32[]{:S(2)}) %collective-permute-start.20) | collective-permute-done | bytes 409632 | tf_op jit(solution)/shard_map/ppermute | solution.py:44
  262.0 5.4 collective-permute-done.24.refs_3_
  267.4 16.0 %hidden.2 = (bf16[160,1280]{1,0:T(8,128)(2,1)S(1)}, bf16[160,1280]{1,0:T(8,128)(2,1)}, bf16[160,1280]{1,0:T(8,128)(2,1)}, bf16[160,1280]{1,0:T(8,128)(2,1)S(1)},...) custom-call(bf16[160,1280]{1,0:T(8,128)(2,1)} %copy-done.88, ...), custom_call_target="tpu_custom_call" | custom-call | tf_op jit(solution)/shard_map/hidden/pallas_call | solution.py:708
  288.9 16.0 %hidden.3 = (bf16[160,1280]{1,0:T(8,128)(2,1)S(1)}, bf16[160,1280]{1,0:T(8,128)(2,1)S(1)}, bf16[160,1280]{1,0:T(8,128)(2,1)S(1)}, bf16[160,1280]{1,0:T(8,128)(2,...) custom-call(bf16[160,1280]{1,0:T(8,128)(2,1)} %copy-done.87, ...), custom_call_target="tpu_custom_call" | custom-call | tf_op jit(solution)/shard_map/hidden/pallas_call | solution.py:708
  320.0 6.3 collective-permute-done.33
  337.6 6.3 collective-permute-done.36.refs_2_
  345.7 19.7 %hidden_grad.2 = (bf16[160,1280]{1,0:T(8,128)(2,1)}, bf16[160,1280]{1,0:T(8,128)(2,1)}, bf16[160,1280]{1,0:T(8,128)(2,1)}, bf16[160,1280]{1,0:T(8,128)(2,1)}, bf...) custom-call(bf16[160,1280]{1,0:T(8,128)(2,1)} %fusion.47.refs_0_, ...), custom_call_target="tpu_custom_call" | custom-call | tf_op jit(solution)/shard_map/hidden_grad/pallas_call | solution.py:784
  372.8 19.5 %hidden_grad.3 = (bf16[160,1280]{1,0:T(8,128)(2,1)}, bf16[160,1280]{1,0:T(8,128)(2,1)}, bf16[160,1280]{1,0:T(8,128)(2,1)}, bf16[160,1280]{1,0:T(8,128)(2,1)}, bf...) custom-call(bf16[160,1280]{1,0:T(8,128)(2,1)} %fusion.48.refs_0_, ...), custom_call_target="tpu_custom_call" | custom-call | tf_op jit(solution)/shard_map/hidden_grad/pallas_call | solution.py:784
  396.0 3.1 multiply_reduce_fusion.7
  414.5 6.4 convolution_convert_fusion.2
  423.9 8.3 %convolution_convert_fusion.1 = bf16[1280,1280]{1,0:T(8,128)(2,1)} fusion(bf16[1280,1280]{1,0:T(8,128)(2,1)S(1)} %copy-done.90, bf16[640,1280]{1,0:T(8,128)(2,1)} %hold.4, bf16[640,1280]{1,0:T(8,128)(2,1)} %get-tuple-element.163), kind=kOutput, calls=%fused_computation.2 | convolution fusion | flops 4202496000 | bytes 9830400 | tf_op jit(solution)/shard_map/dot_general | solution.py:27
  432.3 7.5 %convolution_convert_fusion = bf16[1280,1280]{1,0:T(8,128)(2,1)S(1)} fusion(bf16[640,1280]{1,0:T(8,128)(2,1)} %hold.5, bf16[640,1280]{1,0:T(8,128)(2,1)} %get-tuple-element.165, bf16[640,1280]{1,0:T(8,128)(2,1)} %get-tuple-element.168, bf16[640,1280]{1,0:T(8,128)(2,1)} %get-tuple-element.167), kind=kOutput, calls=%fused_computation.1 | convolution fusion | flops 4209049600 | bytes 9830400 | tf_op jit(solution)/shard_map/dot_general | solution.py:27
  452.0 7.3 %collective-permute-done.43.refs_9_ = bf16[160,1280]{1,0:T(8,128)(2,1)S(1)} collective-permute-done((bf16[160,1280]{1,0:T(8,128)(2,1)S(1)}, bf16[160,1280]{1,0:T(8,128)(2,1)S(1)}, u32[]{:S(2)}, u32[]{:S(2)}) %collective-permute-start.43) | collective-permute-done | bytes 409632 | tf_op jit(solution)/shard_map/ppermute | solution.py:44
  460.5 7.2 %collective-permute-done.58.refs_9_ = bf16[160,1280]{1,0:T(8,128)(2,1)S(1)} collective-permute-done((bf16[160,1280]{1,0:T(8,128)(2,1)S(1)}, bf16[160,1280]{1,0:T(8,128)(2,1)S(1)}, u32[]{:S(2)}, u32[]{:S(2)}) %collective-permute-start.58) | collective-permute-done | bytes 409632 | tf_op jit(solution)/shard_map/ppermute | solution.py:44
  469.6 3.3 fusion.31
  474.8 3.5 collective-permute-done.73
  483.0 34.2 %attend_grad.2 = (f32[640,320]{1,0:T(8,128)}, bf16[640,640]{1,0:T(8,128)(2,1)}, bf16[640,640]{1,0:T(8,128)(2,1)}, bf16[640,640]{1,0:T(8,128)(2,1)}, bf16[640,640]{1,0:T(8,128)(2,1)}, /*index=5*/bf16[640,1280]{1,0:T(8,128)(2,1)}) custom-call(bf16[640,320]{1,0:T(8,128)(2,1)} %copy-done.8, bf16[640,320]{1,0:T(8,128)(2,1)} %copy-done.24, ...), custom_call_target="tpu_custom_call" | custom-call | tf_op jit(solution)/shard_map/attend_grad/pallas_call | solution.py:457
  519.2 35.1 %attend_grad.3 = (f32[640,320]{1,0:T(8,128)}, bf16[640,640]{1,0:T(8,128)(2,1)}, bf16[640,640]{1,0:T(8,128)(2,1)}, bf16[640,640]{1,0:T(8,128)(2,1)}, bf16[640,640]{1,0:T(8,128)(2,1)}, /*index=5*/bf16[640,1280]{1,0:T(8,128)(2,1)}) custom-call(bf16[640,320]{1,0:T(8,128)(2,1)} %copy-done.10, bf16[640,320]{1,0:T(8,128)(2,1)} %copy-done.25, ...), custom_call_target="tpu_custom_call" | custom-call | tf_op jit(solution)/shard_map/attend_grad/pallas_call | solution.py:457
  563.1 9.7 %project_grad.2 = (bf16[640,960]{1,0:T(8,128)(2,1)S(1)}, f32[4,1,640]{2,1,0:T(1,128)S(1)}, bf16[160,1280]{1,0:T(8,128)(2,1)S(1)}, bf16[160,1280]{1,0:T(8,128)(2,...) custom-call(f32[640,320]{1,0:T(8,128)S(1)} %copy-done.21, bf16[640,640]{1,0:T(8,128)(2,1)S(1)} %copy-done.23, ...), custom_call_target="tpu_custom_call" | custom-call | tf_op jit(solution)/shard_map/project_grad/pallas_call | solution.py:632
  578.0 3.2 fusion.35
  581.2 4.3 fusion.20
  607.2 8.8 %project_grad.3 = (bf16[640,960]{1,0:T(8,128)(2,1)S(1)}, f32[4,1,640]{2,1,0:T(1,128)S(1)}, bf16[160,1280]{1,0:T(8,128)(2,1)S(1)}, bf16[160,1280]{1,0:T(8,128)(2,...) custom-call(f32[640,320]{1,0:T(8,128)S(1)} %copy-done.20, bf16[640,640]{1,0:T(8,128)(2,1)S(1)} %copy-done.22, ...), custom_call_target="tpu_custom_call" | custom-call | tf_op jit(solution)/shard_map/project_grad/pallas_call | solution.py:632
  622.0 7.6 %convolution_convert_fusion.3 = bf16[1280,960]{0,1:T(8,128)(2,1)} fusion(bf16[640,1280]{1,0:T(8,128)(2,1)} %copy-done.41, bf16[640,1280]{1,0:T(8,128)(2,1)} %copy-done.40, bf16[640,960]{1,0:T(8,128)(2,1)} %copy-done.43, bf16[640,960]{1,0:T(8,128)(2,1)} %copy-done.42), kind=kOutput, calls=%fused_computation.6 | convolution fusion | flops 3158425600 | bytes 8192000 | tf_op jit(solution)/shard_map/dot_general | solution.py:27
  629.6 4.5 copy.92
  637.2 3.0 collective-permute-start.67
  648.9 3.0 pad_maximum_fusion.1
  651.9 4.7 all-to-all-start.1
  657.9 11.3 %collective-permute-done.68 = bf16[160,1280]{1,0:T(8,128)(2,1)} collective-permute-done((bf16[160,1280]{1,0:T(8,128)(2,1)S(1)}, bf16[160,1280]{1,0:T(8,128)(2,1)}, u32[]{:S(2)}, u32[]{:S(2)}) %collective-permute-start.68) | collective-permute-done | bytes 409632 | tf_op jit(solution)/shard_map/ppermute | solution.py:44
  678.5 3.8 all-to-all-done.1
  682.4 3.5 fusion.79
  692.3 7.2 %collective-permute-done.72 = bf16[160,1280]{1,0:T(8,128)(2,1)} collective-permute-done((bf16[160,1280]{1,0:T(8,128)(2,1)S(1)}, bf16[160,1280]{1,0:T(8,128)(2,1)}, u32[]{:S(2)}, u32[]{:S(2)}) %collective-permute-start.72) | collective-permute-done | bytes 409632 | tf_op jit(solution)/shard_map/ppermute | solution.py:103
  (554 shorter events, 221.8 us)
Async XLA Ops:
  7.2 61.0 %all-gather.3.cloned.1.call-start = ((), (), s32[]{:S(2)}) async-start(), calls=%async_computation.5 | async-start | bytes 3686400 | tf_op jit(solution)/shard_map/all_gather | solution.py:897
  15.0 25.2 %collective-permute-start.3 = (f32[1,2,160]{2,1,0:T(2,128)S(1)}, f32[1,2,160]{2,1,0:T(2,128)S(1)}, u32[]{:S(2)}, u32[]{:S(2)}) collective-permute-start(f32[1,2,160]{2,1,0:T(2,128)S(1)} %maximum_bitcast_fusion.2), channel_id=1, source_target_pairs={{0,1},{1,0},{2,3},{3,2},{4,5},{5,4},{6,7},{7,6},{8,9},{9,8},{10,11... | collective-permute-start | bytes 3848 | tf_op jit(solution)/shard_map/ppermute | solution.py:44
  18.0 42.3 %collective-permute-start = (bf16[160,1280]{1,0:T(8,128)(2,1)S(1)}, bf16[160,1280]{1,0:T(8,128)(2,1)S(1)}, u32[]{:S(2)}, u32[]{:S(2)}) collective-permute-start(bf16[160,1280]{1,0:T(8,128)(2,1)S(1)} %slice_bitcast_fusion.refs_0_), channel_id=1, source_target_pairs={{0,1},{1,0},{2,3},{3,2},{4,5},{5,4},{6,7},{7,6},{8,9},{9,8},{10,11... | collective-permute-start | bytes 1228808 | tf_op jit(solution)/shard_map/ppermute | solution.py:44
  21.7 71.9 %all-to-all-start = ((bf16[8,3,160,160]{3,2,1,0:T(8,128)(2,1)}), bf16[8,3,160,160]{3,2,1,0:T(8,128)(2,1)}, u32[]{:S(2)}, u32[]{:S(2)}) async-start(bf16[8,3,160,160]{3,2,1,0:T(8,128)(2,1)} %pad_maximum_fusion), calls=%async_computation | async-start | bytes 3932160 | tf_op jit(solution)/shard_map/all_to_all | solution.py:131
  26.1 174.9 %all-gather.5.cloned.1.call-start = ((), (), s32[]{:S(2)}) async-start(), calls=%async_computation.6 | async-start | bytes 6144000 | tf_op jit(solution)/shard_map/all_gather | solution.py:144
  39.2 41.7 %collective-permute-start.14 = (bf16[160,1280]{1,0:T(8,128)(2,1)S(1)}, bf16[160,1280]{1,0:T(8,128)(2,1)S(1)}, u32[]{:S(2)}, u32[]{:S(2)}) collective-permute-start(bf16[160,1280]{1,0:T(8,128)(2,1)S(1)} %add_bitcast_fusion.3.refs_0_), channel_id=1, source_target_pairs={{0,2},{1,3},{2,0},{3,1},{4,6},{5,7},{6,4},{7,5},{8,10},{9,11},{10,... | collective-permute-start | bytes 1228808 | tf_op jit(solution)/shard_map/ppermute | solution.py:44
  40.2 27.9 %collective-permute-start.2 = (bf16[160,1280]{1,0:T(8,128)(2,1)S(1)}, bf16[160,1280]{1,0:T(8,128)(2,1)S(1)}, u32[]{:S(2)}, u32[]{:S(2)}) collective-permute-start(bf16[160,1280]{1,0:T(8,128)(2,1)S(1)} %collective-permute-done.1.refs_2_), channel_id=1, source_target_pairs={{0,1},{1,0},{2,3},{3,2},{4,5},{5,4},{6,7},{7,6},{8,9},{9,8},{10,11... | collective-permute-start | bytes 1228808 | tf_op jit(solution)/shard_map/ppermute | solution.py:44
  102.2 495.2 %reduce-scatter.4.cloned.1.call-start = ((), (), s32[]{:S(2)}) async-start(), calls=%async_computation.7 | async-start | bytes 2048000 | tf_op jit(solution)/shard_map/reduce_scatter | solution.py:170
  111.4 36.6 %collective-permute-start.7 = (bf16[640,640]{1,0:T(8,128)(2,1)}, bf16[640,640]{1,0:T(8,128)(2,1)}, u32[]{:S(2)}, u32[]{:S(2)}) collective-permute-start(bf16[640,640]{1,0:T(8,128)(2,1)} %get-tuple-element.115.refs_1_.refs_2_), channel_id=1, source_target_pairs={{0,4},{4,0},{8,12},{12,8},{1,5},{5,1},{9,13},{13,9},{2,6},{6,2},{1... | collective-permute-start | bytes 2457608 | tf_op jit(solution)/shard_map/ppermute | solution.py:44
  165.8 33.2 %collective-permute-start.10 = (bf16[160,1280]{1,0:T(8,128)(2,1)S(1)}, bf16[160,1280]{1,0:T(8,128)(2,1)S(1)}, u32[]{:S(2)}, u32[]{:S(2)}) collective-permute-start(bf16[160,1280]{1,0:T(8,128)(2,1)S(1)} %get-tuple-element.118), channel_id=1, source_target_pairs={{0,1},{1,0},{2,3},{3,2},{4,5},{5,4},{6,7},{7,6},{8,9},{9,8},{10,11... | collective-permute-start | bytes 1228808 | tf_op jit(solution)/shard_map/ppermute | solution.py:44
  166.7 37.5 %collective-permute-start.16 = (bf16[640,640]{1,0:T(8,128)(2,1)}, bf16[640,640]{1,0:T(8,128)(2,1)S(1)}, u32[]{:S(2)}, u32[]{:S(2)}) collective-permute-start(bf16[640,640]{1,0:T(8,128)(2,1)} %get-tuple-element.121.refs_1_.refs_2_), channel_id=1, source_target_pairs={{0,4},{4,0},{8,12},{12,8},{1,5},{5,1},{9,13},{13,9},{2,6},{6,2},{1... | collective-permute-start | bytes 2457608 | tf_op jit(solution)/shard_map/ppermute | solution.py:44
  167.2 37.1 %collective-permute-start.18 = (bf16[640,640]{1,0:T(8,128)(2,1)}, bf16[640,640]{1,0:T(8,128)(2,1)}, u32[]{:S(2)}, u32[]{:S(2)}) collective-permute-start(bf16[640,640]{1,0:T(8,128)(2,1)} %collective-permute-done.17.refs_3_.refs_4_), channel_id=1, source_target_pairs={{0,4},{4,0},{8,12},{12,8},{1,5},{5,1},{9,13},{13,9},{2,6},{6,2},{1... | collective-permute-start | bytes 2457608 | tf_op jit(solution)/shard_map/ppermute | solution.py:44
  201.0 66.4 %collective-permute-start.25 = (bf16[4,3,160,1280]{3,2,1,0:T(8,128)(2,1)}, bf16[4,3,160,1280]{3,2,1,0:T(8,128)(2,1)}, u32[]{:S(2)}, u32[]{:S(2)}) collective-permute-start(bf16[4,3,160,1280]{3,2,1,0:T(8,128)(2,1)} %all-gather.5.cloned.1.call-done.refs_4_), channel_id=1, source_target_pairs={{0,4},{4,0},{8,12},{12,8},{1,5},{5,1},{9,13},{13,9},{2,6},{6,2},{1... | collective-permute-start | bytes 14745608 | tf_op jit(solution)/shard_map/ppermute | solution.py:44
  258.1 28.3 %collective-permute-start.29 = (bf16[160,1280]{1,0:T(8,128)(2,1)S(1)}, bf16[160,1280]{1,0:T(8,128)(2,1)}, u32[]{:S(2)}, u32[]{:S(2)}) collective-permute-start(bf16[160,1280]{1,0:T(8,128)(2,1)S(1)} %multiply_convert_fusion.2.refs_0_), channel_id=1, source_target_pairs={{0,8},{4,12},{8,0},{12,4},{16,24},{20,28},{24,16},{28,20},{1,9},{5... | collective-permute-start | bytes 1228808 | tf_op jit(solution)/shard_map/ppermute | solution.py:103
  259.6 28.6 %collective-permute-start.30 = (bf16[160,1280]{1,0:T(8,128)(2,1)S(1)}, bf16[160,1280]{1,0:T(8,128)(2,1)S(1)}, u32[]{:S(2)}, u32[]{:S(2)}) collective-permute-start(bf16[160,1280]{1,0:T(8,128)(2,1)S(1)} %multiply_convert_fusion.2.refs_0_), channel_id=1, source_target_pairs={{0,16},{4,20},{8,24},{12,28},{16,0},{20,4},{24,8},{28,12},{1,17},{... | collective-permute-start | bytes 1228808 | tf_op jit(solution)/shard_map/ppermute | solution.py:103
  261.1 27.8 %collective-permute-start.31 = (bf16[160,1280]{1,0:T(8,128)(2,1)S(1)}, bf16[160,1280]{1,0:T(8,128)(2,1)}, u32[]{:S(2)}, u32[]{:S(2)}) collective-permute-start(bf16[160,1280]{1,0:T(8,128)(2,1)S(1)} %multiply_convert_fusion.2.refs_0_), channel_id=1, source_target_pairs={{0,24},{4,28},{8,16},{12,20},{16,8},{20,12},{24,0},{28,4},{1,25},{... | collective-permute-start | bytes 1228808 | tf_op jit(solution)/shard_map/ppermute | solution.py:103
  283.4 24.6 %collective-permute-start.26 = (bf16[160,1280]{1,0:T(8,128)(2,1)}, bf16[160,1280]{1,0:T(8,128)(2,1)}, u32[]{:S(2)}, u32[]{:S(2)}) collective-permute-start(bf16[160,1280]{1,0:T(8,128)(2,1)} %get-tuple-element.127), channel_id=1, source_target_pairs={{0,8},{4,12},{8,0},{12,4},{16,24},{20,28},{24,16},{28,20},{1,9},{5... | collective-permute-start | bytes 1228808 | tf_op jit(solution)/shard_map/ppermute | solution.py:103
  284.9 23.6 %collective-permute-start.27 = (bf16[160,1280]{1,0:T(8,128)(2,1)}, bf16[160,1280]{1,0:T(8,128)(2,1)}, u32[]{:S(2)}, u32[]{:S(2)}) collective-permute-start(bf16[160,1280]{1,0:T(8,128)(2,1)} %get-tuple-element.128), channel_id=1, source_target_pairs={{0,16},{4,20},{8,24},{12,28},{16,0},{20,4},{24,8},{28,12},{1,17},{... | collective-permute-start | bytes 1228808 | tf_op jit(solution)/shard_map/ppermute | solution.py:103
  313.7 30.1 %collective-permute-start.36 = (bf16[160,1280]{1,0:T(8,128)(2,1)}, bf16[160,1280]{1,0:T(8,128)(2,1)}, u32[]{:S(2)}, u32[]{:S(2)}) collective-permute-start(bf16[160,1280]{1,0:T(8,128)(2,1)} %fusion.47.refs_0_), channel_id=1, source_target_pairs={{0,16},{4,20},{8,24},{12,28},{16,0},{20,4},{24,8},{28,12},{1,17},{... | collective-permute-start | bytes 1228808 | tf_op jit(solution)/shard_map/ppermute | solution.py:103
  317.6 27.4 %collective-permute-start.37 = (bf16[160,1280]{1,0:T(8,128)(2,1)}, bf16[160,1280]{1,0:T(8,128)(2,1)S(1)}, u32[]{:S(2)}, u32[]{:S(2)}) collective-permute-start(bf16[160,1280]{1,0:T(8,128)(2,1)} %fusion.47.refs_0_), channel_id=1, source_target_pairs={{0,24},{4,28},{8,16},{12,20},{16,8},{20,12},{24,0},{28,4},{1,25},{... | collective-permute-start | bytes 1228808 | tf_op jit(solution)/shard_map/ppermute | solution.py:103
  332.6 34.8 %collective-permute-start.50 = (bf16[160,1280]{1,0:T(8,128)(2,1)}, bf16[160,1280]{1,0:T(8,128)(2,1)S(1)}, u32[]{:S(2)}, u32[]{:S(2)}) collective-permute-start(bf16[160,1280]{1,0:T(8,128)(2,1)} %fusion.48.refs_0_), channel_id=1, source_target_pairs={{0,8},{4,12},{8,0},{12,4},{16,24},{20,28},{24,16},{28,20},{1,9},{5... | collective-permute-start | bytes 1228808 | tf_op jit(solution)/shard_map/ppermute | solution.py:103
  333.9 38.8 %collective-permute-start.51 = (bf16[160,1280]{1,0:T(8,128)(2,1)}, bf16[160,1280]{1,0:T(8,128)(2,1)}, u32[]{:S(2)}, u32[]{:S(2)}) collective-permute-start(bf16[160,1280]{1,0:T(8,128)(2,1)} %fusion.48.refs_0_), channel_id=1, source_target_pairs={{0,16},{4,20},{8,24},{12,28},{16,0},{20,4},{24,8},{28,12},{1,17},{... | collective-permute-start | bytes 1228808 | tf_op jit(solution)/shard_map/ppermute | solution.py:103
  335.2 37.6 %collective-permute-start.52 = (bf16[160,1280]{1,0:T(8,128)(2,1)}, bf16[160,1280]{1,0:T(8,128)(2,1)}, u32[]{:S(2)}, u32[]{:S(2)}) collective-permute-start(bf16[160,1280]{1,0:T(8,128)(2,1)} %fusion.48.refs_0_), channel_id=1, source_target_pairs={{0,24},{4,28},{8,16},{12,20},{16,8},{20,12},{24,0},{28,4},{1,25},{... | collective-permute-start | bytes 1228808 | tf_op jit(solution)/shard_map/ppermute | solution.py:103
  365.4 28.9 %collective-permute-start.38 = (bf16[160,1280]{1,0:T(8,128)(2,1)}, bf16[160,1280]{1,0:T(8,128)(2,1)}, u32[]{:S(2)}, u32[]{:S(2)}) collective-permute-start(bf16[160,1280]{1,0:T(8,128)(2,1)} %get-tuple-element.137), channel_id=1, source_target_pairs={{0,8},{4,12},{8,0},{12,4},{16,24},{20,28},{24,16},{28,20},{1,9},{5... | collective-permute-start | bytes 1228808 | tf_op jit(solution)/shard_map/ppermute | solution.py:103
  366.8 29.1 %collective-permute-start.39 = (bf16[160,1280]{1,0:T(8,128)(2,1)}, bf16[160,1280]{1,0:T(8,128)(2,1)}, u32[]{:S(2)}, u32[]{:S(2)}) collective-permute-start(bf16[160,1280]{1,0:T(8,128)(2,1)} %get-tuple-element.138), channel_id=1, source_target_pairs={{0,16},{4,20},{8,24},{12,28},{16,0},{20,4},{24,8},{28,12},{1,17},{... | collective-permute-start | bytes 1228808 | tf_op jit(solution)/shard_map/ppermute | solution.py:103
  367.4 28.5 %collective-permute-start.40 = (bf16[160,1280]{1,0:T(8,128)(2,1)}, bf16[160,1280]{1,0:T(8,128)(2,1)}, u32[]{:S(2)}, u32[]{:S(2)}) collective-permute-start(bf16[160,1280]{1,0:T(8,128)(2,1)} %get-tuple-element.139), channel_id=1, source_target_pairs={{0,24},{4,28},{8,16},{12,20},{16,8},{20,12},{24,0},{28,4},{1,25},{... | collective-permute-start | bytes 1228808 | tf_op jit(solution)/shard_map/ppermute | solution.py:103
  403.0 41.1 %collective-permute-start.41 = (bf16[160,1280]{1,0:T(8,128)(2,1)}, bf16[160,1280]{1,0:T(8,128)(2,1)}, u32[]{:S(2)}, u32[]{:S(2)}) collective-permute-start(bf16[160,1280]{1,0:T(8,128)(2,1)} %fusion.49.refs_6_), channel_id=1, source_target_pairs={{0,1},{1,0},{2,3},{3,2},{4,5},{5,4},{6,7},{7,6},{8,9},{9,8},{10,11... | collective-permute-start | bytes 1228808 | tf_op jit(solution)/shard_map/ppermute | solution.py:44
  403.0 42.9 %collective-permute-start.42 = (bf16[160,1280]{1,0:T(8,128)(2,1)}, bf16[160,1280]{1,0:T(8,128)(2,1)}, u32[]{:S(2)}, u32[]{:S(2)}) collective-permute-start(bf16[160,1280]{1,0:T(8,128)(2,1)} %fusion.49.refs_6_), channel_id=1, source_target_pairs={{0,2},{1,3},{2,0},{3,1},{4,6},{5,7},{6,4},{7,5},{8,10},{9,11},{10,... | collective-permute-start | bytes 1228808 | tf_op jit(solution)/shard_map/ppermute | solution.py:44
  412.3 34.8 %collective-permute-start.56 = (bf16[160,1280]{1,0:T(8,128)(2,1)}, bf16[160,1280]{1,0:T(8,128)(2,1)}, u32[]{:S(2)}, u32[]{:S(2)}) collective-permute-start(bf16[160,1280]{1,0:T(8,128)(2,1)} %fusion.50.refs_6_), channel_id=1, source_target_pairs={{0,1},{1,0},{2,3},{3,2},{4,5},{5,4},{6,7},{7,6},{8,9},{9,8},{10,11... | collective-permute-start | bytes 1228808 | tf_op jit(solution)/shard_map/ppermute | solution.py:44
  412.3 36.6 %collective-permute-start.57 = (bf16[160,1280]{1,0:T(8,128)(2,1)}, bf16[160,1280]{1,0:T(8,128)(2,1)}, u32[]{:S(2)}, u32[]{:S(2)}) collective-permute-start(bf16[160,1280]{1,0:T(8,128)(2,1)} %fusion.50.refs_6_), channel_id=1, source_target_pairs={{0,2},{1,3},{2,0},{3,1},{4,6},{5,7},{6,4},{7,5},{8,10},{9,11},{10,... | collective-permute-start | bytes 1228808 | tf_op jit(solution)/shard_map/ppermute | solution.py:44
  423.9 45.7 %collective-permute-start.62 = (bf16[640,1280]{1,0:T(8,128)(2,1)}, bf16[640,1280]{1,0:T(8,128)(2,1)}, u32[]{:S(2)}, u32[]{:S(2)}) collective-permute-start(bf16[640,1280]{1,0:T(8,128)(2,1)} %slice.316), channel_id=1, source_target_pairs={{0,4},{4,0},{8,12},{12,8},{1,5},{5,1},{9,13},{13,9},{2,6},{6,2},{1... | collective-permute-start | bytes 4915208 | tf_op jit(solution)/shard_map/ppermute | solution.py:44
  472.9 171.0 %reduce-scatter.6.cloned.1.call-start = ((), (), s32[]{:S(2)}) async-start(), calls=%async_computation.8 | async-start | bytes 2048000 | tf_op jit(solution)/shard_map/reduce_scatter | solution.py:170
  480.1 166.7 %reduce-scatter.8.cloned.1.call-start = ((), (), s32[]{:S(2)}) async-start(), calls=%async_computation.9 | async-start | bytes 2048000 | tf_op jit(solution)/shard_map/reduce_scatter | solution.py:170
  481.4 94.7 %collective-permute-start.74 = (bf16[640,1280]{1,0:T(8,128)(2,1)}, bf16[640,1280]{1,0:T(8,128)(2,1)}, u32[]{:S(2)}, u32[]{:S(2)}) collective-permute-start(bf16[640,1280]{1,0:T(8,128)(2,1)} %slice.326), channel_id=1, source_target_pairs={{0,4},{4,0},{8,12},{12,8},{1,5},{5,1},{9,13},{13,9},{2,6},{6,2},{1... | collective-permute-start | bytes 4915208 | tf_op jit(solution)/shard_map/ppermute | solution.py:44
  482.4 36.6 %collective-permute-start.63 = (f32[2,4,160]{2,1,0:T(4,128)S(1)}, f32[2,4,160]{2,1,0:T(4,128)S(1)}, u32[]{:S(2)}, u32[]{:S(2)}) collective-permute-start(f32[2,4,160]{2,1,0:T(4,128)S(1)} %slice_bitcast_fusion.2), channel_id=1, source_target_pairs={{0,4},{4,0},{8,12},{12,8},{1,5},{5,1},{9,13},{13,9},{2,6},{6,2},{1... | collective-permute-start | bytes 15368 | tf_op jit(solution)/shard_map/ppermute | solution.py:44
  517.1 43.0 %collective-permute-start.44 = (bf16[640,640]{1,0:T(8,128)(2,1)}, bf16[640,640]{1,0:T(8,128)(2,1)}, u32[]{:S(2)}, u32[]{:S(2)}) collective-permute-start(bf16[640,640]{1,0:T(8,128)(2,1)} %get-tuple-element.144), channel_id=1, source_target_pairs={{0,4},{4,0},{8,12},{12,8},{1,5},{5,1},{9,13},{13,9},{2,6},{6,2},{1... | collective-permute-start | bytes 2457608 | tf_op jit(solution)/shard_map/ppermute | solution.py:44
  517.3 44.2 %collective-permute-start.45 = (bf16[640,640]{1,0:T(8,128)(2,1)}, bf16[640,640]{1,0:T(8,128)(2,1)}, u32[]{:S(2)}, u32[]{:S(2)}) collective-permute-start(bf16[640,640]{1,0:T(8,128)(2,1)} %get-tuple-element.145), channel_id=1, source_target_pairs={{0,8},{4,12},{8,0},{12,4},{1,9},{5,13},{9,1},{13,5},{2,10},{6,14},... | collective-permute-start | bytes 2457608 | tf_op jit(solution)/shard_map/ppermute | solution.py:44
  518.7 43.3 %collective-permute-start.46 = (bf16[640,640]{1,0:T(8,128)(2,1)}, bf16[640,640]{1,0:T(8,128)(2,1)}, u32[]{:S(2)}, u32[]{:S(2)}) collective-permute-start(bf16[640,640]{1,0:T(8,128)(2,1)} %get-tuple-element.146), channel_id=1, source_target_pairs={{0,12},{4,8},{8,4},{12,0},{1,13},{5,9},{9,5},{13,1},{2,14},{6,10},... | collective-permute-start | bytes 2457608 | tf_op jit(solution)/shard_map/ppermute | solution.py:44
  560.1 43.4 %collective-permute-start.59 = (bf16[640,640]{1,0:T(8,128)(2,1)}, bf16[640,640]{1,0:T(8,128)(2,1)}, u32[]{:S(2)}, u32[]{:S(2)}) collective-permute-start(bf16[640,640]{1,0:T(8,128)(2,1)} %get-tuple-element.172), channel_id=1, source_target_pairs={{0,4},{4,0},{8,12},{12,8},{1,5},{5,1},{9,13},{13,9},{2,6},{6,2},{1... | collective-permute-start | bytes 2457608 | tf_op jit(solution)/shard_map/ppermute | solution.py:44
  560.1 43.3 %collective-permute-start.60 = (bf16[640,640]{1,0:T(8,128)(2,1)}, bf16[640,640]{1,0:T(8,128)(2,1)}, u32[]{:S(2)}, u32[]{:S(2)}) collective-permute-start(bf16[640,640]{1,0:T(8,128)(2,1)} %get-tuple-element.173), channel_id=1, source_target_pairs={{0,8},{4,12},{8,0},{12,4},{1,9},{5,13},{9,1},{13,5},{2,10},{6,14},... | collective-permute-start | bytes 2457608 | tf_op jit(solution)/shard_map/ppermute | solution.py:44
  561.5 41.9 %collective-permute-start.61 = (bf16[640,640]{1,0:T(8,128)(2,1)}, bf16[640,640]{1,0:T(8,128)(2,1)}, u32[]{:S(2)}, u32[]{:S(2)}) collective-permute-start(bf16[640,640]{1,0:T(8,128)(2,1)} %get-tuple-element.174), channel_id=1, source_target_pairs={{0,12},{4,8},{8,4},{12,0},{1,13},{5,9},{9,5},{13,1},{2,14},{6,10},... | collective-permute-start | bytes 2457608 | tf_op jit(solution)/shard_map/ppermute | solution.py:44
  562.0 25.8 %collective-permute-start.65 = (f32[3840]{0:T(1024)S(1)}, f32[3840]{0:T(1024)S(1)}, u32[]{:S(2)}, u32[]{:S(2)}) collective-permute-start(f32[3840]{0:T(1024)S(1)} %fusion.104), channel_id=1, source_target_pairs={{0,2},{1,3},{2,0},{3,1},{4,6},{5,7},{6,4},{7,5},{8,10},{9,11},{10,... | collective-permute-start | bytes 46088 | tf_op jit(solution)/shard_map/ppermute | solution.py:44
  593.0 47.1 %collective-permute-start.48 = (bf16[160,1280]{1,0:T(8,128)(2,1)}, bf16[160,1280]{1,0:T(8,128)(2,1)}, u32[]{:S(2)}, u32[]{:S(2)}) collective-permute-start(bf16[160,1280]{1,0:T(8,128)(2,1)} %broadcast_add_fusion), channel_id=1, source_target_pairs={{0,1},{1,0},{2,3},{3,2},{4,5},{5,4},{6,7},{7,6},{8,9},{9,8},{10,11... | collective-permute-start | bytes 1228808 | tf_op jit(solution)/shard_map/ppermute | solution.py:44
  597.5 44.2 %collective-permute-start.49 = (bf16[160,1280]{1,0:T(8,128)(2,1)}, bf16[160,1280]{1,0:T(8,128)(2,1)}, u32[]{:S(2)}, u32[]{:S(2)}) collective-permute-start(bf16[160,1280]{1,0:T(8,128)(2,1)} %add_convert_fusion.3), channel_id=1, source_target_pairs={{0,2},{1,3},{2,0},{3,1},{4,6},{5,7},{6,4},{7,5},{8,10},{9,11},{10,... | collective-permute-start | bytes 1228808 | tf_op jit(solution)/shard_map/ppermute | solution.py:44
  637.1 33.6 %collective-permute-start.69 = (bf16[4,160,1280]{2,1,0:T(8,128)(2,1)}, bf16[4,160,1280]{2,1,0:T(8,128)(2,1)}, u32[]{:S(2)}, u32[]{:S(2)}) collective-permute-start(bf16[4,160,1280]{2,1,0:T(8,128)(2,1)} %fusion.27), channel_id=1, source_target_pairs={{0,4},{4,0},{8,12},{12,8},{1,5},{5,1},{9,13},{13,9},{2,6},{6,2},{1... | collective-permute-start | bytes 4915208 | tf_op jit(solution)/shard_map/ppermute | solution.py:44
  640.2 29.0 %collective-permute-start.68 = (bf16[160,1280]{1,0:T(8,128)(2,1)S(1)}, bf16[160,1280]{1,0:T(8,128)(2,1)}, u32[]{:S(2)}, u32[]{:S(2)}) collective-permute-start(bf16[160,1280]{1,0:T(8,128)(2,1)S(1)} %copy-done.45), channel_id=1, source_target_pairs={{0,3},{1,2},{2,1},{3,0},{4,7},{5,6},{6,5},{7,4},{8,11},{9,10},{10,... | collective-permute-start | bytes 1228808 | tf_op jit(solution)/shard_map/ppermute | solution.py:44
  651.9 30.4 %all-to-all-start.1 = ((bf16[8,3,160,160]{3,2,1,0:T(8,128)(2,1)}), bf16[8,3,160,160]{3,2,1,0:T(8,128)(2,1)}, u32[]{:S(2)}, u32[]{:S(2)}) async-start(bf16[8,3,160,160]{3,2,1,0:T(8,128)(2,1)} %pad_maximum_fusion.1), calls=%async_computation.4 | async-start | bytes 3932160 | tf_op jit(solution)/shard_map/all_to_all | solution.py:183
  674.6 24.9 %collective-permute-start.72 = (bf16[160,1280]{1,0:T(8,128)(2,1)S(1)}, bf16[160,1280]{1,0:T(8,128)(2,1)}, u32[]{:S(2)}, u32[]{:S(2)}) collective-permute-start(bf16[160,1280]{1,0:T(8,128)(2,1)S(1)} %get-tuple-element.296), channel_id=1, source_target_pairs={{0,24},{4,28},{8,16},{12,20},{16,8},{20,12},{24,0},{28,4},{1,25},{... | collective-permute-start | bytes 1228808 | tf_op jit(solution)/shard_map/ppermute | solution.py:103
  (144 other events, 1760.2 us)
Sparse Core Ops, SparseCore 0:
  10.5 44.9 all-gather.2
  102.4 97.5 all-gather.4
  473.0 35.5 reduce-scatter.3
  510.9 35.3 reduce-scatter.5
  581.4 52.3 reduce-scatter.7
